TPU v7x, 32 devices: a whole 2x2x4 slice. The times are simulated.
32 devices in a mesh: dp: 16 (over z, x, core), tensor: 2 (over y).
Axes of the slice: x: 2, y: 2, z: 4, core: 2. Of those that a mesh axis runs over, the one named last changes fastest.
Arguments:
- tokens: bfloat16 [16384, 1024], P('dp'), may hold values from -6 to 6
- lengths: int32 [16, 8], replicated, may hold values from 1 to 384, 768 in all within a row
- pairing: int32 [16, 8], P('dp', 'tensor'), may hold values from 0 to 127
- w_qkv: bfloat16 [3, 1024, 1024], P(None, 'dp', 'tensor'), may hold values from -0.1875 to 0.1875
- b_qv: bfloat16 [2, 1024], P(None, 'tensor'), may hold values from -3 to 3
- w_out: bfloat16 [1024, 1024], P('tensor', 'dp'), may hold values from -0.5 to 0.5
- b_out: bfloat16 [1024], replicated, may hold values from -3 to 3
- ln_gain: bfloat16 [2, 1024], replicated, may hold values from 0.5 to 1.5
- ln_bias: bfloat16 [2, 1024], replicated, may hold values from -3 to 3
- w_up: bfloat16 [1024, 4096], P('dp', 'tensor'), may hold values from -0.1875 to 0.1875
- b_up: bfloat16 [4096], P('tensor'), may hold values from -3 to 3
- w_down: bfloat16 [4096, 1024], P('tensor', 'dp'), may hold values from -0.09375 to 0.09375
- b_down: bfloat16 [1024], replicated, may hold values from -3 to 3
- w_proj: bfloat16 [1024, 128], replicated, may hold values from -0.1875 to 0.1875
- cot: bfloat16 [16384, 1024], P(('dp', 'tensor')), may hold values from -6 to 6
Outputs:
- y_out: bfloat16 [16384, 1024], P(('dp', 'tensor'))
- loss: float32 [16, 8], P('dp', 'tensor')
- x_grad: bfloat16 [16384, 1024], P(('dp', 'tensor'))
- w_qkv_grad: float32 [3, 1024, 1024], P(None, 'dp', 'tensor')
- b_qv_grad: float32 [2, 1024], P(None, 'tensor')
- w_out_grad: float32 [1024, 1024], P('tensor', 'dp')
- b_out_grad: float32 [1024], replicated
- ln_gain_grad: float32 [2, 1024], replicated
- ln_bias_grad: float32 [2, 1024], replicated
- w_up_grad: float32 [1024, 4096], P('dp', 'tensor')
- b_up_grad: float32 [4096], P('tensor')
- w_down_grad: float32 [4096, 1024], P('tensor', 'dp')
- b_down_grad: float32 [1024], replicated
- w_proj_grad: float32 [1024, 128], replicated
Inputs may be any that keep to these rules, and one draw needn't show every extreme that they name: lengths[r] are the token counts of row r's 8 documents, which follow its 8 queries of 32 tokens; each row sums to 768 and its largest is 384. pairing[r, q] numbers a document over all rows: its row times 8 plus its place in that row.
All inputs are finite; a program needn't handle non-finite values.
Results may differ from a plain program's by a relative error of at most 0.02.
Values may be sent and summed in bfloat16 or wider, within the bound.
No kernel may reach another device: no remote copies, remote signals or barrier semaphores. Data moves between devices by JAX's collectives and lax.ppermute only.
A program may use at most 192 MiB of HBM per device.

v0:
```python
from functools import partial

import jax
import jax.numpy as jnp
from jax import lax
from jax.sharding import PartitionSpec as P

HEAD_DIM = 64
QLEN = 32
NQ_ROW = 8
NDOC = 8


EPS_NORM = 1e-05
EPS_EMBED = 1e-06
POOL_TEMP = 0.1
LOSS_TEMP = 0.1
FULL_PRECISION = lax.Precision.HIGHEST
MASKED_SCORE = -1e30


def shortened(shard):

    def short(part):
        return part.astype(jnp.bfloat16) if part.dtype == jnp.float32 else part

    return jax.tree.map(short, shard)


def contract_rows(left, right, precision=None):
    return lax.dot_general(
        left,
        right,
        (((0,), (0,)), ((), ())),
        precision=precision,
        preferred_element_type=jnp.float32,
    )


def contract_cols(left, right, precision=None):
    return lax.dot_general(
        left,
        right,
        (((1,), (1,)), ((), ())),
        precision=precision,
        preferred_element_type=jnp.float32,
    )


def norm_forward(value, gain, shift):
    centred = value - jnp.mean(value, axis=1, keepdims=True)
    rstd = lax.rsqrt(jnp.mean(centred * centred, axis=1, keepdims=True) + EPS_NORM)
    unit = centred * rstd
    return (unit * gain + shift, unit, rstd)


def norm_backward(grad, unit, rstd, gain):
    scaled = grad * gain
    return rstd * (
        scaled
        - jnp.mean(scaled, axis=1, keepdims=True)
        - unit * jnp.mean(scaled * unit, axis=1, keepdims=True)
    )


def segments_of(row_lengths, token_count):
    position = jnp.arange(token_count, dtype=jnp.int32)
    query_span = NQ_ROW * QLEN
    ends = jnp.cumsum(row_lengths)
    passed = jnp.sum((position[:, None] - query_span >= ends[None, :]).astype(jnp.int32), axis=1)
    return jnp.where(position < query_span, position // QLEN, NQ_ROW + passed)


def normalize_cut(raw, width):
    part = raw[:, :width]
    scale = lax.rsqrt(jnp.sum(part * part, axis=1, keepdims=True) + EPS_EMBED)
    return (part * scale, part, scale)


def normalize_back(grad, part, scale, full_width):
    result = scale * grad - part * (scale * scale * scale) * jnp.sum(
        part * grad, axis=1, keepdims=True
    )
    return jnp.pad(result, ((0, 0), (0, full_width - grad.shape[1])))


def masked_scores(query_block, key_rows, block_segments, segments):
    scores = jnp.einsum(
        "qhd,khd->hqk", query_block, key_rows, preferred_element_type=jnp.float32
    ) * HEAD_DIM ** (-0.5)
    return jnp.where((block_segments[:, None] == segments[None, :])[None], scores, MASKED_SCORE)


def attend_forward(query_rows, key_rows, value_rows, segments, block_rows):
    token_count = query_rows.shape[0]

    def one_block(block_start):
        query_block = lax.dynamic_slice_in_dim(query_rows, block_start, block_rows, 0)
        block_segments = lax.dynamic_slice_in_dim(segments, block_start, block_rows, 0)
        scores = masked_scores(query_block, key_rows, block_segments, segments)
        highest = jnp.max(scores, axis=2, keepdims=True)
        expo = jnp.exp(scores - highest)
        totals = jnp.sum(expo, axis=2, keepdims=True)
        weights = (expo / totals).astype(jnp.bfloat16)
        mixed = jnp.einsum("hqk,khd->qhd", weights, value_rows, preferred_element_type=jnp.float32)
        return (mixed.astype(jnp.bfloat16), (highest + jnp.log(totals))[:, :, 0])

    starts = jnp.arange(token_count // block_rows, dtype=jnp.int32) * block_rows
    mixed, log_totals = lax.map(one_block, starts)
    return (mixed.reshape(token_count, -1), log_totals)


def attend_backward(query_rows, key_rows, value_rows, segments, log_totals, grad_mixed, block_rows):
    token_count, local_heads, head_size = query_rows.shape
    scale = HEAD_DIM ** (-0.5)
    grad_heads = grad_mixed.reshape(token_count, local_heads, head_size)

    def one_block(carried, inputs):
        grad_keys, grad_values = carried
        block_start, block_lse = inputs
        query_block = lax.dynamic_slice_in_dim(query_rows, block_start, block_rows, 0)
        grad_block = lax.dynamic_slice_in_dim(grad_heads, block_start, block_rows, 0)
        block_segments = lax.dynamic_slice_in_dim(segments, block_start, block_rows, 0)
        scores = masked_scores(query_block, key_rows, block_segments, segments)
        probs = jnp.exp(scores - block_lse[:, :, None])
        grad_probs = jnp.einsum(
            "qhd,khd->hqk", grad_block, value_rows, preferred_element_type=jnp.float32
        )
        inner = jnp.sum(probs * grad_probs, axis=2, keepdims=True)
        grad_scores = (probs * (grad_probs - inner)).astype(jnp.bfloat16)
        grad_query = (
            jnp.einsum("hqk,khd->qhd", grad_scores, key_rows, preferred_element_type=jnp.float32)
            * scale
        )
        grad_keys = (
            grad_keys
            + jnp.einsum(
                "hqk,qhd->khd", grad_scores, query_block, preferred_element_type=jnp.float32
            )
            * scale
        )
        grad_values = grad_values + jnp.einsum(
            "hqk,qhd->khd",
            probs.astype(jnp.bfloat16),
            grad_block,
            preferred_element_type=jnp.float32,
        )
        return ((grad_keys, grad_values), grad_query)

    starts = jnp.arange(token_count // block_rows, dtype=jnp.int32) * block_rows
    zero_rows = jnp.zeros(key_rows.shape, jnp.float32)
    (grad_keys, grad_values), grad_queries = lax.scan(
        one_block, (zero_rows, zero_rows), (starts, log_totals)
    )
    flat_width = local_heads * head_size
    return (
        grad_queries.reshape(token_count, flat_width),
        grad_keys.reshape(token_count, flat_width),
        grad_values.reshape(token_count, flat_width),
    )


def local(
    tokens,
    lengths,
    pairing,
    w_qkv,
    b_qv,
    w_out,
    b_out,
    ln_gain,
    ln_bias,
    w_up,
    b_up,
    w_down,
    b_down,
    w_proj,
    cot,
):
    tensor_count = lax.axis_size("tensor")
    tensor_index = lax.axis_index("tensor")
    data_index = lax.axis_index("dp")
    token_count = tokens.shape[0]
    share_rows = token_count // tensor_count
    block_rows = min(512, token_count)
    own_start = tensor_index * share_rows
    full_qkv, full_out, full_up, full_down = (
        lax.all_gather(w_qkv, "dp", axis=1, tiled=True),
        lax.all_gather(w_out, "dp", axis=1, tiled=True),
        lax.all_gather(w_up, "dp", axis=0, tiled=True),
        lax.all_gather(w_down, "dp", axis=1, tiled=True),
    )
    head_width = full_qkv.shape[2]
    local_heads = head_width // HEAD_DIM
    row_lengths = lax.dynamic_index_in_dim(lengths, data_index, 0, keepdims=False)
    segments = segments_of(row_lengths, token_count)
    projected = jnp.einsum("td,kdw->ktw", tokens, full_qkv, preferred_element_type=jnp.float32)
    qv_bias = b_qv.astype(jnp.float32)
    query_rows = (
        (projected[0] + qv_bias[0]).astype(jnp.bfloat16).reshape(token_count, local_heads, HEAD_DIM)
    )
    key_rows = projected[1].astype(jnp.bfloat16).reshape(token_count, local_heads, HEAD_DIM)
    value_rows = (
        (projected[2] + qv_bias[1]).astype(jnp.bfloat16).reshape(token_count, local_heads, HEAD_DIM)
    )
    mixed, log_totals = attend_forward(query_rows, key_rows, value_rows, segments, block_rows)
    attn_terms = jnp.dot(mixed, full_out, preferred_element_type=jnp.float32)
    attn_sum = lax.psum_scatter(
        attn_terms.astype(jnp.bfloat16), "tensor", scatter_dimension=0, tiled=True
    ).astype(jnp.float32)
    own_tokens = lax.dynamic_slice_in_dim(tokens, own_start, share_rows, 0).astype(jnp.float32)
    gains = ln_gain.astype(jnp.float32)
    shifts = ln_bias.astype(jnp.float32)
    normed, unit_one, rstd_one = norm_forward(
        own_tokens + attn_sum + b_out.astype(jnp.float32), gains[0], shifts[0]
    )
    normed_all = lax.all_gather(normed.astype(jnp.bfloat16), "tensor", axis=0, tiled=True)
    up_value = jnp.dot(normed_all, full_up, preferred_element_type=jnp.float32) + b_up.astype(
        jnp.float32
    )
    activation = jax.nn.gelu(up_value, approximate=False).astype(jnp.bfloat16)
    ffn_terms = jnp.dot(activation, full_down, preferred_element_type=jnp.float32)
    ffn_sum = lax.psum_scatter(
        ffn_terms.astype(jnp.bfloat16), "tensor", scatter_dimension=0, tiled=True
    ).astype(jnp.float32)
    result, unit_two, rstd_two = norm_forward(
        normed + ffn_sum + b_down.astype(jnp.float32), gains[1], shifts[1]
    )
    result_low = result.astype(jnp.bfloat16)
    embed = jnp.dot(result_low, w_proj, preferred_element_type=jnp.float32).astype(jnp.bfloat16)
    embed_all = lax.all_gather(embed, ("dp", "tensor"), axis=0, tiled=True)
    row_count = lengths.shape[0]
    proj_width = w_proj.shape[1]
    widths = (proj_width, 3 * proj_width // 4, proj_width // 2)
    per_device = pairing.shape[1]
    query_count = per_device * QLEN
    query_span = NQ_ROW * QLEN
    emb_rows = embed_all.reshape(row_count, token_count, proj_width)
    my_row = lax.dynamic_index_in_dim(emb_rows, data_index, 0, keepdims=False)
    query_raw = lax.dynamic_slice_in_dim(my_row, tensor_index * query_count, query_count, 0).astype(
        jnp.float32
    )
    query_levels = [normalize_cut(query_raw, width) for width in widths]
    query_units = [level_parts[0].astype(jnp.bfloat16) for level_parts in query_levels]
    doc_numbers = jnp.arange(NDOC, dtype=jnp.int32)

    def row_pool(carried, inputs):
        row_emb, lengths_row = inputs
        row_hot = (
            segments_of(lengths_row, token_count)[:, None] == NQ_ROW + doc_numbers[None, :]
        ).astype(jnp.float32)
        row_raw = row_emb.astype(jnp.float32)
        pooled_list = []
        sums_list = []
        for width, query_unit in zip(widths, query_units):
            doc_unit = normalize_cut(row_raw, width)[0].astype(jnp.bfloat16)
            expo = jnp.exp(contract_cols(query_unit, doc_unit) / POOL_TEMP)
            sums = jnp.dot(expo, row_hot, precision=FULL_PRECISION)
            pooled = POOL_TEMP * jnp.log(sums / lengths_row.astype(jnp.float32))
            pooled_list.append(jnp.sum(pooled.reshape(per_device, QLEN, NDOC), axis=1))
            sums_list.append(sums)
        return (carried, (jnp.stack(pooled_list), jnp.stack(sums_list)))

    _, (row_scores, row_sums) = lax.scan(row_pool, 0, (emb_rows, lengths))
    logits = (
        jnp.transpose(row_scores, (2, 1, 0, 3)).reshape(per_device, 3, row_count * NDOC) / LOSS_TEMP
    )
    own_pairs = pairing[0]
    target = jnp.take_along_axis(
        logits, jnp.broadcast_to(own_pairs[:, None, None], (per_device, 3, 1)), axis=2
    )[:, :, 0]
    loss_out = jnp.sum(jax.nn.logsumexp(logits, axis=2) - target, axis=1).reshape(1, per_device)
    picked = (
        jnp.arange(row_count * NDOC, dtype=jnp.int32)[None, None, :] == own_pairs[:, None, None]
    ).astype(jnp.float32)
    grad_logits = (jax.nn.softmax(logits, axis=2) - picked) / LOSS_TEMP
    grad_rows = jnp.transpose(grad_logits.reshape(per_device, 3, row_count, NDOC), (2, 1, 0, 3))
    coefficient = jnp.repeat(grad_rows, QLEN, axis=2) / row_sums

    def row_back(carried, inputs):
        row_emb, lengths_row, row_coef = inputs
        row_hot = (
            segments_of(lengths_row, token_count)[:, None] == NQ_ROW + doc_numbers[None, :]
        ).astype(jnp.float32)
        row_raw = row_emb.astype(jnp.float32)
        new_carried = []
        row_grad = jnp.zeros((token_count, proj_width), jnp.float32)
        for level_index in range(3):
            width = widths[level_index]
            doc_unit_f, doc_part, doc_scale = normalize_cut(row_raw, width)
            doc_unit = doc_unit_f.astype(jnp.bfloat16)
            expo = jnp.exp(contract_cols(query_units[level_index], doc_unit) / POOL_TEMP)
            spread = contract_cols(row_coef[level_index], row_hot, FULL_PRECISION)
            grad_sim = (expo * spread).astype(jnp.bfloat16)
            new_carried.append(
                carried[level_index]
                + jnp.dot(grad_sim, doc_unit, preferred_element_type=jnp.float32)
            )
        return (tuple(new_carried), row_grad)

    zero_query = tuple((jnp.zeros((query_count, width), jnp.float32) for width in widths))
    query_grads, doc_grads = lax.scan(row_back, zero_query, (emb_rows, lengths, coefficient))
    grad_query = jnp.zeros((query_count, proj_width), jnp.float32)
    for level_index in range(3):
        level_parts = query_levels[level_index]
        grad_query = grad_query + normalize_back(
            query_grads[level_index], level_parts[1], level_parts[2], proj_width
        )
    coef_mine = jnp.transpose(coefficient, (2, 1, 0, 3)).reshape(query_count, 3, row_count * NDOC)
    coef_all, grad_query_all = (
        lax.all_gather(shortened(coef_mine), ("dp", "tensor"), axis=0, tiled=True).astype(
            coef_mine.dtype
        ),
        lax.all_gather(
            grad_query.astype(jnp.bfloat16), ("dp", "tensor"), axis=0, tiled=True
        ).astype(grad_query.dtype),
    )
    own_raw = embed.astype(jnp.float32)
    own_segments = lax.dynamic_slice_in_dim(segments, own_start, share_rows, 0)
    own_docs = jnp.where(own_segments >= NQ_ROW, data_index * NDOC + own_segments - NQ_ROW, -1)
    own_hot = (own_docs[:, None] == jnp.arange(row_count * NDOC, dtype=jnp.int32)[None, :]).astype(
        jnp.float32
    )
    queries_all = (
        emb_rows[:, :query_span].reshape(row_count * query_span, proj_width).astype(jnp.float32)
    )
    grad_embed = jnp.zeros((share_rows, proj_width), jnp.float32)
    for level_index in range(3):
        width = widths[level_index]
        query_unit_all = normalize_cut(queries_all, width)[0].astype(jnp.bfloat16)
        doc_unit_f, doc_part, doc_scale = normalize_cut(own_raw, width)
        expo = jnp.exp(contract_cols(query_unit_all, doc_unit_f.astype(jnp.bfloat16)) / POOL_TEMP)
        spread = contract_cols(coef_all[:, level_index], own_hot, FULL_PRECISION)
        grad_sim = (expo * spread).astype(jnp.bfloat16)
        grad_doc = contract_rows(grad_sim, query_unit_all)
        grad_embed = grad_embed + normalize_back(grad_doc, doc_part, doc_scale, proj_width)
    row_query_grads = lax.dynamic_slice_in_dim(
        grad_query_all, data_index * query_span, query_span, 0
    )
    padded = jnp.pad(row_query_grads, ((0, token_count - query_span), (0, 0)))
    grad_embed = grad_embed + lax.dynamic_slice_in_dim(padded, own_start, share_rows, 0)
    proj_float = w_proj.astype(jnp.float32)
    grad_result = cot.astype(jnp.float32) + contract_cols(grad_embed, proj_float, FULL_PRECISION)
    proj_grad = contract_rows(result_low.astype(jnp.float32), grad_embed, FULL_PRECISION)
    gain_two = jnp.sum(grad_result * unit_two, axis=0)
    shift_two = jnp.sum(grad_result, axis=0)
    grad_second = norm_backward(grad_result, unit_two, rstd_two, gains[1])
    grad_ffn = grad_second.astype(jnp.bfloat16)
    down_bias = jnp.sum(grad_ffn.astype(jnp.float32), axis=0)
    grad_ffn_all = lax.all_gather(grad_ffn, "tensor", axis=0, tiled=True)
    grad_act = contract_cols(grad_ffn_all, full_down)
    down_grad = contract_rows(activation, grad_ffn_all)
    _, gelu_pull = jax.vjp(partial(jax.nn.gelu, approximate=False), up_value)
    grad_up = gelu_pull(grad_act)[0].astype(jnp.bfloat16)
    up_bias = jnp.sum(grad_up.astype(jnp.float32), axis=0)
    up_grad = contract_rows(normed_all, grad_up)
    normed_terms = contract_cols(grad_up, full_up)
    grad_normed = (
        lax.psum_scatter(
            normed_terms.astype(jnp.bfloat16), "tensor", scatter_dimension=0, tiled=True
        ).astype(jnp.float32)
        + grad_second
    )
    gain_one = jnp.sum(grad_normed * unit_one, axis=0)
    shift_one = jnp.sum(grad_normed, axis=0)
    grad_first = norm_backward(grad_normed, unit_one, rstd_one, gains[0])
    grad_attn = grad_first.astype(jnp.bfloat16)
    out_bias = jnp.sum(grad_attn.astype(jnp.float32), axis=0)
    grad_attn_all = lax.all_gather(grad_attn, "tensor", axis=0, tiled=True)
    out_grad = contract_rows(mixed, grad_attn_all)
    grad_mixed = contract_cols(grad_attn_all, full_out).astype(jnp.bfloat16)
    grad_q, grad_k, grad_v = attend_backward(
        query_rows, key_rows, value_rows, segments, log_totals, grad_mixed, block_rows
    )
    stacked_grads = jnp.stack(
        [grad_q.astype(jnp.bfloat16), grad_k.astype(jnp.bfloat16), grad_v.astype(jnp.bfloat16)]
    )
    qkv_grad = jnp.einsum("td,ktw->kdw", tokens, stacked_grads, preferred_element_type=jnp.float32)
    input_terms = jnp.einsum(
        "ktw,kdw->td", stacked_grads, full_qkv, preferred_element_type=jnp.float32
    )
    grad_input = (
        lax.psum_scatter(
            input_terms.astype(jnp.bfloat16), "tensor", scatter_dimension=0, tiled=True
        ).astype(jnp.float32)
        + grad_first
    )
    qv_grad = jnp.stack(
        [
            jnp.sum(stacked_grads[0].astype(jnp.float32), axis=0),
            jnp.sum(stacked_grads[2].astype(jnp.float32), axis=0),
        ]
    )
    qkv_part, out_part, up_part, down_part = (
        lax.psum_scatter(
            qkv_grad.astype(jnp.bfloat16), "dp", scatter_dimension=1, tiled=True
        ).astype(jnp.float32),
        lax.psum_scatter(
            out_grad.astype(jnp.bfloat16), "dp", scatter_dimension=1, tiled=True
        ).astype(jnp.float32),
        lax.psum_scatter(
            up_grad.astype(jnp.bfloat16), "dp", scatter_dimension=0, tiled=True
        ).astype(jnp.float32),
        lax.psum_scatter(
            down_grad.astype(jnp.bfloat16), "dp", scatter_dimension=1, tiled=True
        ).astype(jnp.float32),
    )
    gain_sum, shift_sum, out_bias_sum, down_bias_sum, proj_sum = lax.psum(
        (
            jnp.stack([gain_one, gain_two]),
            jnp.stack([shift_one, shift_two]),
            out_bias,
            down_bias,
            proj_grad,
        ),
        ("dp", "tensor"),
    )
    qv_sum, up_bias_sum = lax.psum((qv_grad, up_bias), "dp")
    return (
        result_low,
        loss_out,
        grad_input.astype(jnp.bfloat16),
        qkv_part,
        qv_sum,
        out_part,
        out_bias_sum,
        gain_sum,
        shift_sum,
        up_part,
        up_bias_sum,
        down_part,
        down_bias_sum,
        proj_sum,
    )


def solution(mesh):
    return jax.shard_map(
        local,
        mesh=mesh,
        in_specs=(
            P("dp", None),
            P(),
            P("dp", "tensor"),
            P(None, "dp", "tensor"),
            P(None, "tensor"),
            P("tensor", "dp"),
            P(),
            P(),
            P(),
            P("dp", "tensor"),
            P("tensor"),
            P("tensor", "dp"),
            P(),
            P(),
            P(("dp", "tensor"), None),
        ),
        out_specs=(
            P(("dp", "tensor"), None),
            P("dp", "tensor"),
            P(("dp", "tensor"), None),
            P(None, "dp", "tensor"),
            P(None, "tensor"),
            P("tensor", "dp"),
            P(),
            P(),
            P(),
            P("dp", "tensor"),
            P("tensor"),
            P("tensor", "dp"),
            P(),
            P(),
        ),
        check_vma=False,
    )
```

profile of v0, /device:TPU:1, one launch (start us, length us, event | category | flops | bytes accessed | tf_op | source)
XLA Modules:
  0.0 1435.9 jit_solution(2835645235980154128)
XLA Ops:
  10.8 47.2 %all-gather.11.cloned.1.call-done = bf16[3,1024,512]{2,1,0:T(8,128)(2,1)} async-done(((bf16[3,64,512]{2,1,0:T(8,128)(2,1)}), bf16[3,1024,512]{2,1,0:T(8,128)(2,1)}) %all-gather.11.cloned.1.call-update) | async-done | bytes 3145744 | tf_op jit(solution)/shard_map/all_gather | solution.py:188
  58.0 6.0 convolution_bitcast_fusion
  65.0 33.8 %while.59 = (s32[]{:T(128)}, bf16[2,512,8,64]{1,3,2,0:T(8,128)(2,1)}, f32[2,8,512]{2,1,0:T(8,128)S(1)}, s32[2]{0:T(128)S(1)}, s32[1024]{0:T(1024)S(1)}, /*index=...) while((s32[]{:T(128)}, ...), condition=%wide.region_5.6_spmd, body=%wide.region_2.5_spmd.sunk | while | flops 1124855808 | bytes 55716516 | solution.py:109
  68.5 3.6 fusion.236
  72.1 4.2 fusion.237
  76.4 5.8 fusion.238
  85.2 3.6 fusion.236
  88.8 4.2 fusion.237
  93.1 5.8 fusion.238
  98.9 3.1 copy.156
  103.3 4.2 convolution_convert_fusion.4
  108.3 29.7 %reduce-scatter.8.cloned.1.call-done = bf16[512,1024]{1,0:T(8,128)(2,1)} async-done(((bf16[1024,1024]{1,0:T(8,128)(2,1)}), bf16[512,1024]{1,0:T(8,128)(2,1)}) %reduce-scatter.8.cloned.1.call-update) | async-done | bytes 1048592 | tf_op jit(solution)/shard_map/reduce_scatter | solution.py:208
  144.1 47.3 %all-gather.17.cloned.1.call-done = bf16[1024,2048]{1,0:T(8,128)(2,1)} async-done(((bf16[64,2048]{1,0:T(8,128)(2,1)}), bf16[1024,2048]{1,0:T(8,128)(2,1)}) %all-gather.17.cloned.1.call-update) | async-done | bytes 4194320 | tf_op jit(solution)/shard_map/all_gather | solution.py:190
  191.4 33.3 %all-gather.15.cloned.1.call-done = bf16[1024,1024]{1,0:T(8,128)(2,1)} async-done(((bf16[512,1024]{1,0:T(8,128)(2,1)}), bf16[1024,1024]{1,0:T(8,128)(2,1)}) %all-gather.15.cloned.1.call-update) | async-done | bytes 2097168 | tf_op jit(solution)/shard_map/all_gather | solution.py:217
  224.6 26.3 %multiply_convert_fusion.19 = (bf16[1024,2048]{1,0:T(8,128)(2,1)}, f32[1024,2048]{1,0:T(8,128)}, f32[1024,2048]{1,0:T(8,128)}) fusion(f32[2048]{0:T(1024)S(1)} %convert_element_type.390, bf16[1024,1024]{1,0:T(8,128)(2,1)} %all-gather.15.cloned.1.call-done, bf16[1024,2048]{1,0:T(8,128)(2,1)} %all-gather.17.cloned.1.call-done), kind=kOutput, calls=%fused_computation.161 | convolution fusion | flops 4433379328 | bytes 27271168 | tf_op jit(solution)/shard_map/dot_general | solution.py:218
  251.0 27.1 %all-gather.19.cloned.1.call-done = bf16[2048,1024]{0,1:T(8,128)(2,1)} async-done(((bf16[2048,64]{0,1:T(8,128)(2,1)}), bf16[2048,1024]{0,1:T(8,128)(2,1)}) %all-gather.19.cloned.1.call-update) | async-done | bytes 4194320 | tf_op jit(solution)/shard_map/all_gather | solution.py:191
  278.0 9.4 convolution_convert_fusion.3
  287.5 30.0 %reduce-scatter.10.cloned.1.call-done = bf16[512,1024]{1,0:T(8,128)(2,1)} async-done(((bf16[1024,1024]{1,0:T(8,128)(2,1)}), bf16[512,1024]{1,0:T(8,128)(2,1)}) %reduce-scatter.10.cloned.1.call-update) | async-done | bytes 1048592 | tf_op jit(solution)/shard_map/reduce_scatter | solution.py:223
  323.9 64.3 %all-gather.21.cloned.1.call-done = bf16[16384,128]{0,1:T(8,128)(2,1)} async-done(((bf16[512,128]{0,1:T(8,128)(2,1)}), bf16[16384,128]{0,1:T(8,128)(2,1)}) %all-gather.21.cloned.1.call-update) | async-done | bytes 4194320 | tf_op jit(solution)/shard_map/all_gather | solution.py:231
  388.2 6.6 copy.157
  397.8 135.9 %while.60 = (s32[]{:T(128)}, f32[16,3,4,8]{3,2,1,0:T(4,128)S(1)}, f32[16,3,128,8]{2,3,0,1:T(8,128)}, bf16[16,1024,128]{2,1,0:T(8,128)(2,1)}, bf16[128,128]{1,0:T...) while((s32[]{:T(128)}, f32[16,3,4,8]{3,2,1,0:T(4,128)S(1)}, ...), condition=%wide.region_24.25_spmd.clone, body=%wide.region_15.24_spmd.clone.sunk | while | flops 115288232 | bytes 6425197 | solution.py:264
  538.1 140.2 %while.61 = (s32[]{:T(128)}, f32[128,128]{1,0:T(8,128)S(1)}, f32[128,96]{0,1:T(8,128)S(1)}, f32[128,64]{0,1:T(8,128)S(1)}, bf16[16,1024,128]{2,1,0:T(8,128)(2,1)...) while((s32[]{:T(128)}, f32[128,128]{1,0:T(8,128)S(1)}, ...), condition=%wide.region_44.45_spmd.clone, body=%wide.region_38.44_spmd.clone.sunk | while | flops 192351296 | bytes 11119501 | solution.py:302
  688.3 4.4 fusion.95
  692.8 4.0 fusion.102
  696.8 4.0 fusion.100
  700.8 25.3 %all-gather.25.cloned.1.call-done = bf16[4096,128]{0,1:T(8,128)(2,1)} async-done(((bf16[128,128]{0,1:T(8,128)(2,1)}), bf16[4096,128]{0,1:T(8,128)(2,1)}) %all-gather.25.cloned.1.call-update) | async-done | bytes 1048592 | tf_op jit(solution)/shard_map/all_gather | solution.py:314
  727.6 60.9 %all-gather.23.cloned.1.call-done = bf16[4096,3,128]{0,2,1:T(8,128)(2,1)} async-done(((bf16[128,3,128]{0,2,1:T(8,128)(2,1)}), bf16[4096,3,128]{0,2,1:T(8,128)(2,1)}) %all-gather.23.cloned.1.call-update) | async-done | bytes 3145744 | tf_op jit(solution)/shard_map/all_gather | solution.py:311
  788.5 5.0 multiply_convert_fusion.18
  804.0 2.7 multiply_reduce_fusion.7
  809.2 30.8 %all-gather.27.cloned.1.call-done = bf16[1024,1024]{1,0:T(8,128)(2,1)} async-done(((bf16[512,1024]{1,0:T(8,128)(2,1)}), bf16[1024,1024]{1,0:T(8,128)(2,1)}) %all-gather.27.cloned.1.call-update) | async-done | bytes 2097168 | tf_op jit(solution)/shard_map/all_gather | solution.py:350
  840.0 13.9 convert_reduce_fusion.2
  855.8 5.8 convolution_convert_fusion.2
  861.6 31.9 %reduce-scatter.12.cloned.1.call-done = bf16[512,1024]{1,0:T(8,128)(2,1)} async-done(((bf16[1024,1024]{1,0:T(8,128)(2,1)}), bf16[512,1024]{1,0:T(8,128)(2,1)}) %reduce-scatter.12.cloned.1.call-update) | async-done | bytes 1048592 | tf_op jit(solution)/shard_map/reduce_scatter | solution.py:359
  893.6 3.6 multiply_reduce_fusion.8
  897.1 3.3 convert_reduce_fusion.4
  900.5 9.3 convolution_convert_fusion
  911.6 8.3 convolution_convert_fusion.1
  920.0 13.7 all-gather.29.cloned.1.call-done
  933.7 4.2 convolution_convert_fusion.6
  937.9 123.0 %while.62 = (s32[]{:T(128)}, f32[1024,8,64]{0,2,1:T(8,128)}, f32[1024,8,64]{0,2,1:T(8,128)}, bf16[2,512,8,64]{1,3,2,0:T(8,128)(2,1)}, s32[2]{0:T(128)S(1)}, /*in...) while((s32[]{:T(128)}, f32[1024,8,64]{0,2,1:T(8,128)}, ...), condition=%wide.region_55.56_spmd.clone, body=%wide.region_53.55_spmd.clone.sunk | while | flops 2725507072 | bytes 212953888 | solution.py:152
  940.9 10.2 fusion.281
  951.5 13.4 multiply_reduce_fusion.41
  965.0 15.4 %multiply_convert_fusion.54 = bf16[8,512,1024]{2,1,0:T(8,128)(2,1)} fusion(f32[8,512,1024]{2,1,0:T(8,128)} %get-tuple-element.1026, f32[8,512,1024]{2,1,0:T(8,128)} %fusion.281, f32[8,512]{1,0:T(8,128)S(1)} %get-tuple-element.1027), kind=kLoop, calls=%fused_computation.133.clone.1 | loop fusion | flops 12582912 | bytes 41959424 | tf_op jit(solution)/shard_map/while/body/eval_jaxpr/convert_element_type | solution.py:130
  980.4 7.0 bitcast_add_fusion.4
  987.3 7.7 fusion.282
  995.0 4.2 bitcast_add_fusion.5
  1001.7 9.3 fusion.281
  1011.5 13.0 multiply_reduce_fusion.41
  1024.5 16.0 %multiply_convert_fusion.54 = bf16[8,512,1024]{2,1,0:T(8,128)(2,1)} fusion(f32[8,512,1024]{2,1,0:T(8,128)} %get-tuple-element.1026, f32[8,512,1024]{2,1,0:T(8,128)} %fusion.281, f32[8,512]{1,0:T(8,128)S(1)} %get-tuple-element.1027), kind=kLoop, calls=%fused_computation.133.clone.1 | loop fusion | flops 12582912 | bytes 41959424 | tf_op jit(solution)/shard_map/while/body/eval_jaxpr/convert_element_type | solution.py:130
  1040.6 7.8 bitcast_add_fusion.4
  1048.4 7.7 fusion.282
  1056.1 4.8 bitcast_add_fusion.5
  1060.9 3.5 copy.189
  1064.4 4.3 reshape.754
  1073.4 6.0 convert_bitcast_fusion.1
  1079.4 5.8 copy.183
  1086.4 3.9 convolution_convert_fusion.5
  1090.4 7.0 bitcast_convert_fusion.2
  1101.0 3.0 fusion.134
  1104.1 40.5 %all-reduce.6 = (f32[1024]{0:T(1024)}, f32[2,1024]{1,0:T(2,128)}, f32[2,1024]{1,0:T(2,128)}, f32[1024]{0:T(1024)}) all-reduce(f32[1024]{0:T(1024)S(1)} %copy-done.62, f32[2,1024]{1,0:T(2,128)S(1)} %pad_maximum_fusion.3, f32[2,1024]{1,0:T(2,128)S(1)} %pad_maximum_fusion.4, ...), channel_id=1, replica_groups=mesh['dp'=16,'tensor'=2] {'dp','tensor'}, use_global_device_ids=true, to_apply=%region_63.64 | all-reduce | flops 6144 | bytes 49152 | tf_op jit(solution)/shard_map/psum | solution.py:408
  1146.2 57.0 %all-reduce.7 = (f32[2,512]{1,0:T(2,128)}, f32[2048]{0:T(1024)}) all-reduce(f32[2,512]{1,0:T(2,128)S(1)} %pad_maximum_fusion.5, f32[2048]{0:T(1024)S(1)} %copy-done.73), channel_id=1, replica_groups=mesh['dp'=16,'tensor'=2] {'dp'}, use_global_device_ids=true, to_apply=%region_60.61 | all-reduce | flops 3072 | bytes 24576 | tf_op jit(solution)/shard_map/psum | solution.py:418
  1208.6 51.0 %reduce-scatter.16.cloned.1.call-done = bf16[512,64]{0,1:T(8,128)(2,1)} async-done(((bf16[512,1024]{0,1:T(8,128)(2,1)}), bf16[512,64]{0,1:T(8,128)(2,1)}) %reduce-scatter.16.cloned.1.call-update) | async-done | bytes 65552 | tf_op jit(solution)/shard_map/reduce_scatter | solution.py:398
  1261.1 33.4 %reduce-scatter.14.cloned.1.call-done = bf16[512,1024]{1,0:T(8,128)(2,1)} async-done(((bf16[1024,1024]{1,0:T(8,128)(2,1)}), bf16[512,1024]{1,0:T(8,128)(2,1)}) %reduce-scatter.14.cloned.1.call-update) | async-done | bytes 1048592 | tf_op jit(solution)/shard_map/reduce_scatter | solution.py:383
  1297.0 130.4 %all-reduce.11.cloned.1.call-done = f32[1024,128]{1,0:T(8,128)} async-done(((f32[1024,128]{1,0:T(8,128)}), f32[1024,128]{1,0:T(8,128)}) %all-reduce.11.cloned.1.call-update) | async-done | bytes 524304 | tf_op jit(solution)/shard_map/psum | solution.py:408
  (1289 shorter events, 351.2 us)
Async XLA Ops:
  7.2 315.3 %copy-start = (bf16[1024,128]{1,0:T(8,128)(2,1)S(1)}, bf16[1024,128]{1,0:T(8,128)(2,1)}, u32[]{:S(2)}) copy-start(bf16[1024,128]{1,0:T(8,128)(2,1)} %param.36) | copy-start | bytes 786436
  7.2 50.8 %all-gather.11.cloned.1.call-start = ((), (), s32[]{:S(2)}) async-start(), calls=%async_computation.7 | async-start | bytes 3342336 | tf_op jit(solution)/shard_map/all_gather | solution.py:188
  7.9 95.3 %all-gather.13.cloned.1.call-start = ((), (), s32[]{:S(2)}) async-start(), calls=%async_computation.8 | async-start | bytes 1114112 | tf_op jit(solution)/shard_map/all_gather | solution.py:189
  8.7 129.3 %reduce-scatter.8.cloned.1.call-start = ((), (), s32[]{:S(2)}) async-start(), calls=%async_computation.9 | async-start | bytes 3145728 | tf_op jit(solution)/shard_map/reduce_scatter | solution.py:208
  98.9 8.6 copy-start.3
  98.9 8.6 copy-start.6
  98.9 8.6 copy-start.8
  98.9 8.6 copy-start.40
  98.9 8.6 copy-start.86
  107.5 32.5 %copy-start.14 = (bf16[1024,1024]{1,0:T(8,128)(2,1)S(1)}, bf16[1024,1024]{1,0:T(8,128)(2,1)}, u32[]{:S(2)}) copy-start(bf16[1024,1024]{1,0:T(8,128)(2,1)} %param.23) | copy-start | bytes 6291460
  107.6 83.8 %all-gather.17.cloned.1.call-start = ((), (), s32[]{:S(2)}) async-start(), calls=%async_computation.11 | async-start | bytes 4456448 | tf_op jit(solution)/shard_map/all_gather | solution.py:190
  108.1 116.5 %all-gather.15.cloned.1.call-start = ((), (), s32[]{:S(2)}) async-start(), calls=%async_computation.10 | async-start | bytes 3145728 | tf_op jit(solution)/shard_map/all_gather | solution.py:217
  108.3 211.9 %copy-start.42 = (f32[1,1024]{1,0:T(1,128)}, f32[1,1024]{1,0:T(1,128)S(1)}, u32[]{:S(2)}) copy-start(f32[1,1024]{1,0:T(1,128)S(1)} %get-tuple-element.754) | copy-start | bytes 12292
  108.3 35.8 %copy-start.77 = (bf16[2048]{0:T(1024)(128)(2,1)S(1)}, bf16[2048]{0:T(1024)(128)(2,1)}, u32[]{:S(2)}) copy-start(bf16[2048]{0:T(1024)(128)(2,1)} %param.33) | copy-start | bytes 12292
  141.8 175.7 %copy-start.48 = (f32[512]{0:T(512)}, f32[512]{0:T(512)S(1)}, u32[]{:S(2)}) copy-start(f32[512]{0:T(512)S(1)} %add_rsqrt_fusion.12) | copy-start | bytes 6148
  143.4 134.6 %all-gather.19.cloned.1.call-start = ((), (), s32[]{:S(2)}) async-start(), calls=%async_computation.12 | async-start | bytes 4456448 | tf_op jit(solution)/shard_map/all_gather | solution.py:191
  144.0 173.5 %reduce-scatter.10.cloned.1.call-start = ((), (), s32[]{:S(2)}) async-start(), calls=%async_computation.13 | async-start | bytes 3145728 | tf_op jit(solution)/shard_map/reduce_scatter | solution.py:223
  144.1 106.9 %copy-start.71 = (f32[2048]{0:T(1024)}, f32[2048]{0:T(1024)S(1)}, u32[]{:S(2)}) copy-start(f32[2048]{0:T(1024)S(1)} %convert_element_type.390) | copy-start | bytes 24580
  278.0 9.4 copy-start.79
  287.4 100.8 %all-gather.21.cloned.1.call-start = ((), (), s32[]{:S(2)}) async-start(), calls=%async_computation.14 | async-start | bytes 4325376 | tf_op jit(solution)/shard_map/all_gather | solution.py:231
  323.6 356.9 %copy-start.16 = (f32[512,128]{0,1:T(8,128)}, f32[512,128]{0,1:T(8,128)S(1)}, u32[]{:S(2)}) copy-start(f32[512,128]{0,1:T(8,128)S(1)} %get-tuple-element.771) | copy-start | bytes 786436
  323.6 402.5 %all-gather.25.cloned.1.call-start = ((), (), s32[]{:S(2)}) async-start(), calls=%async_computation.16 | async-start | bytes 1081344 | tf_op jit(solution)/shard_map/all_gather | solution.py:314
  538.1 140.4 %copy-start.82 = (f32[128]{0:T(128)S(1)}, f32[128]{0:T(128)}, u32[]{:S(2)}) copy-start(f32[128]{0:T(128)} %get-tuple-element.766) | copy-start | bytes 1540
  538.1 140.4 %copy-start.80 = (f32[128]{0:T(128)S(1)}, f32[128]{0:T(128)}, u32[]{:S(2)}) copy-start(f32[128]{0:T(128)} %get-tuple-element.768) | copy-start | bytes 1540
  538.1 140.4 %copy-start.81 = (f32[128]{0:T(128)S(1)}, f32[128]{0:T(128)}, u32[]{:S(2)}) copy-start(f32[128]{0:T(128)} %get-tuple-element.764) | copy-start | bytes 1540
  538.1 142.4 %copy-start.25 = (bf16[512,128]{0,1:T(8,128)(2,1)S(1)}, bf16[512,128]{0,1:T(8,128)(2,1)}, u32[]{:S(2)}) copy-start(bf16[512,128]{0,1:T(8,128)(2,1)} %get-tuple-element.772) | copy-start | bytes 393220
  679.2 109.3 %all-gather.23.cloned.1.call-start = ((), (), s32[]{:S(2)}) async-start(), calls=%async_computation.15 | async-start | bytes 3244032 | tf_op jit(solution)/shard_map/all_gather | solution.py:311
  679.8 160.2 %all-gather.27.cloned.1.call-start = ((), (), s32[]{:S(2)}) async-start(), calls=%async_computation.17 | async-start | bytes 3145728 | tf_op jit(solution)/shard_map/all_gather | solution.py:350
  681.2 7.1 copy-start.57
  681.8 15.0 %copy-start.55 = (f32[512]{0:T(512)}, f32[512]{0:T(512)S(1)}, u32[]{:S(2)}) copy-start(f32[512]{0:T(512)S(1)} %get-tuple-element.761) | copy-start | bytes 6148
  682.4 10.4 copy-start.53
  686.9 9.9 copy-start.38
  788.5 7.4 copy-start.26
  806.6 33.4 %copy-start.72 = (f32[2048]{0:T(1024)S(1)}, f32[2048]{0:T(1024)}, u32[]{:S(2)}) copy-start(f32[2048]{0:T(1024)} %copy-done.71) | copy-start | bytes 24580
  809.0 84.6 %reduce-scatter.12.cloned.1.call-start = ((), (), s32[]{:S(2)}) async-start(), calls=%async_computation.18 | async-start | bytes 3145728 | tf_op jit(solution)/shard_map/reduce_scatter | solution.py:359
  840.0 15.8 %copy-start.83 = (bf16[1024,2048]{1,0:T(8,128)(2,1)S(1)}, bf16[1024,2048]{1,0:T(8,128)(2,1)}, u32[]{:S(2)}) copy-start(bf16[1024,2048]{1,0:T(8,128)(2,1)} %all-gather.17.cloned.1.call-done) | copy-start | bytes 12582916
  855.8 37.8 %copy-start.49 = (f32[512]{0:T(512)S(1)}, f32[512]{0:T(512)}, u32[]{:S(2)}) copy-start(f32[512]{0:T(512)} %copy-done.48) | copy-start | bytes 6148
  861.6 72.1 %all-gather.29.cloned.1.call-start = ((), (), s32[]{:S(2)}) async-start(), calls=%async_computation.19 | async-start | bytes 3145728 | tf_op jit(solution)/shard_map/all_gather | solution.py:369
  900.4 302.7 %reduce-scatter.20.cloned.1.call-start = ((), (), s32[]{:S(2)}) async-start(), calls=%async_computation.23 | async-start | bytes 4456448 | tf_op jit(solution)/shard_map/reduce_scatter | solution.py:404
  909.9 295.1 %reduce-scatter.18.cloned.1.call-start = ((), (), s32[]{:S(2)}) async-start(), calls=%async_computation.22 | async-start | bytes 4456448 | tf_op jit(solution)/shard_map/reduce_scatter | solution.py:401
  919.9 18.0 %copy-start.4 = (bf16[1024,8,64]{0,2,1:T(8,128)(2,1)S(1)}, bf16[1024,8,64]{0,2,1:T(8,128)(2,1)}, u32[]{:S(2)}) copy-start(bf16[1024,8,64]{0,2,1:T(8,128)(2,1)} %copy-done.3) | copy-start | bytes 3145732
  919.9 18.0 %copy-start.7 = (bf16[1024,8,64]{0,2,1:T(8,128)(2,1)S(1)}, bf16[1024,8,64]{0,2,1:T(8,128)(2,1)}, u32[]{:S(2)}) copy-start(bf16[1024,8,64]{0,2,1:T(8,128)(2,1)} %copy-done.6) | copy-start | bytes 3145732
  919.9 18.0 %copy-start.41 = (f32[2,8,512]{2,1,0:T(8,128)S(1)}, f32[2,8,512]{2,1,0:T(8,128)}, u32[]{:S(2)}) copy-start(f32[2,8,512]{2,1,0:T(8,128)} %copy-done.40) | copy-start | bytes 98308
  919.9 18.0 %copy-start.87 = (s32[2]{0:T(128)S(1)}, s32[2]{0:T(128)}, u32[]{:S(2)}) copy-start(s32[2]{0:T(128)} %copy-done.86) | copy-start | bytes 28
  920.0 286.8 %all-reduce.13.cloned.1.call-start = ((), (), s32[]{:S(2)}) async-start(), calls=%async_computation.25 | async-start | bytes 8388608
  940.9 10.7 copy-start.9
  980.4 14.6 %copy-start.2 = (f32[8,512,1024]{2,1,0:T(8,128)S(1)}, f32[8,512,1024]{2,1,0:T(8,128)}, u32[]{:S(2)}) copy-start(f32[8,512,1024]{2,1,0:T(8,128)} %get-tuple-element.1026) | copy-start | bytes 50331652 | tf_op jit(solution)/shard_map/while
  1001.7 9.8 copy-start.9
  1040.6 15.5 %copy-start.2 = (f32[8,512,1024]{2,1,0:T(8,128)S(1)}, f32[8,512,1024]{2,1,0:T(8,128)}, u32[]{:S(2)}) copy-start(f32[8,512,1024]{2,1,0:T(8,128)} %get-tuple-element.1026) | copy-start | bytes 50331652 | tf_op jit(solution)/shard_map/while
  1064.4 7.5 copy-start.5
  1085.2 174.3 %reduce-scatter.16.cloned.1.call-start = ((), (), s32[]{:S(2)}) async-start(), calls=%async_computation.21 | async-start | bytes 1114112 | tf_op jit(solution)/shard_map/reduce_scatter | solution.py:398
  1090.3 7.3 copy-start.76
  1090.3 7.8 copy-start.85
  1090.3 9.0 copy-start.33
  1090.3 204.1 %reduce-scatter.14.cloned.1.call-start = ((), (), s32[]{:S(2)}) async-start(), calls=%async_computation.20 | async-start | bytes 3145728 | tf_op jit(solution)/shard_map/reduce_scatter | solution.py:383
  1097.4 6.5 copy-start.67
  1097.5 6.5 copy-start.60
  1097.5 6.5 copy-start.66
  1097.5 6.5 copy-start.59
  1097.5 6.5 copy-start.62
  1097.5 48.6 %copy-start.73 = (f32[2048]{0:T(1024)S(1)}, f32[2048]{0:T(1024)}, u32[]{:S(2)}) copy-start(f32[2048]{0:T(1024)} %get-tuple-element.730) | copy-start | bytes 24580
  1097.5 329.8 %all-reduce.11.cloned.1.call-start = ((), (), s32[]{:S(2)}) async-start(), calls=%async_computation.24 | async-start | bytes 1048576 | tf_op jit(solution)/shard_map/psum | solution.py:408
  1099.5 195.0 %copy-start.21 = (f32[512,1024]{1,0:T(8,128)S(1)}, f32[512,1024]{1,0:T(8,128)}, u32[]{:S(2)}) copy-start(f32[512,1024]{1,0:T(8,128)} %get-tuple-element.729) | copy-start | bytes 6291460
  1146.2 283.1 %copy-start.1 = (bf16[1024,128]{1,0:T(8,128)(2,1)S(1)}, bf16[1024,128]{1,0:T(8,128)(2,1)}, u32[]{:S(2)}) copy-start(bf16[1024,128]{1,0:T(8,128)(2,1)} %param.36) | copy-start | bytes 786436
  (78 other events, 273.3 us)
Sparse Core Ops, SparseCore 0:
  10.2 47.6 all-gather.10
  60.1 36.7 all-gather.12
  107.7 30.2 reduce-scatter.7
  140.2 51.1 all-gather.16
  193.4 31.1 all-gather.14
  226.9 51.1 all-gather.18
  287.6 29.8 reduce-scatter.9
  323.8 64.4 all-gather.20
  679.3 46.7 all-gather.24
  729.4 59.0 all-gather.22
  809.1 30.8 all-gather.26
  861.7 31.8 reduce-scatter.11
  900.6 33.1 all-gather.28
  937.9 71.3 reduce-scatter.19
  1013.0 70.9 reduce-scatter.17
  1088.0 111.5 all-reduce.12
  1203.7 55.7 reduce-scatter.15
  1261.7 32.6 reduce-scatter.13
  1300.3 127.0 all-reduce.10
where the time goes:
time: 1450 us; the launch traced here: 1440 us
  waiting for transfers between devices  659 us (45%)
  matrix products  396 us (27%)
  other arithmetic  197 us (14%)
  blocking collectives  97.5 us (7%)
  local copies, waits for them, and re-layouts  56.1 us (4%)
  between operations  16.2 us (1%)
    dot_general x154, matrix products, contract_cols(): lax.dot_general(left, right, (((1,), (1,)), ((), ())), precision=precisio...  133 us
    psum x1, waiting for transfers between devices, local(): lax.psum((jnp.stack([gain_one, gain_two]), jnp.stack([shift_one, shift_tw...  130 us
    all_gather x1, waiting for transfers between devices, local(): embed_all = lax.all_gather(embed, ('dp', 'tensor'), axis=0, tiled=True)  64.3 us
    all_gather x1, waiting for transfers between devices, local(): lax.all_gather(shortened(coef_mine), ('dp', 'tensor'), axis=0, tiled=True)  60.9 us
    psum x1, blocking collectives, local(): qv_sum, up_bias_sum = lax.psum((qv_grad, up_bias), 'dp')  57 us
    reduce_sum x105, other arithmetic, normalize_cut(): scale = lax.rsqrt(jnp.sum(part * part, axis=1, keepdims=True) + EPS_EMBED)  54 us
    reduce_scatter x1, waiting for transfers between devices, local(): lax.psum_scatter(out_grad.astype(jnp.bfloat16), 'dp', scatter_dimension=1...  51 us
    all_gather x1, waiting for transfers between devices, local(): lax.all_gather(w_up, 'dp', axis=0, tiled=True)  47.3 us
  transfers between devices with their start and end apart: 19, of which 15 were waited for; matrix products, arithmetic and copies ran while one was open for 20% of the time, Pallas kernels for 0%

commit v1 on v0

--- a/solution.py
+++ b/solution.py
@@ -3,7 +3,9 @@
 import jax
 import jax.numpy as jnp
 from jax import lax
-from jax.sharding import PartitionSpec as P
+from jax.experimental import pallas as pl
+from jax.experimental.pallas import tpu as pltpu
+from jax.sharding import Mesh, PartitionSpec as P
 
 HEAD_DIM = 64
 QLEN = 32
@@ -434,42 +436,421 @@
     )
 
 
+SWAP = [(0, 1), (1, 0)]
+TURN = [(0, 0), (1, 2), (2, 1), (3, 3)]
+RING_UP = [(0, 1), (1, 2), (2, 3), (3, 0)]
+RING_DOWN = [(1, 0), (2, 1), (3, 2), (0, 3)]
+BF = jnp.bfloat16
+F32 = jnp.float32
+
+
+def dot(left, right):
+    return jnp.dot(left, right, preferred_element_type=F32)
+
+
+def turn(value):
+    return lax.ppermute(value, ("c", "y"), TURN)
+
+
+def swap(value, axis):
+    return lax.ppermute(value, axis, SWAP)
+
+
+def up(value):
+    return lax.ppermute(value, "z", RING_UP)
+
+
+def down(value):
+    return lax.ppermute(value, "z", RING_DOWN)
+
+
+def pair_up(first, second, own_index, axis):
+    return jnp.where(
+        own_index == 0, jnp.stack([first, second], axis), jnp.stack([second, first], axis)
+    )
+
+
+def gather_z(value, z):
+    below, above = up(value), down(value)
+    half = value.shape[-2] // 2
+    far_low = up(below[..., :half, :])
+    far_high = down(above[..., half:, :])
+    far = jnp.concatenate([far_low, far_high], axis=-2)
+    whole = jnp.zeros((4,) + value.shape, value.dtype)
+    for offset, part in ((0, value), (3, below), (1, above), (2, far)):
+        whole = lax.dynamic_update_index_in_dim(whole, part, (z + offset) % 4, 0)
+    return whole
+
+
+def gather_blocks(value, order, z, x, y):
+    done = []
+    for axis in order:
+        if axis == "z":
+            value = gather_z(value, z)
+        else:
+            place = sum(1 for name in done if "zxy".index(name) < "zxy".index(axis))
+            value = pair_up(value, swap(value, axis), {"x": x, "y": y}[axis], place)
+        done.append(axis)
+    return value.reshape(-1, value.shape[-1])
+
+
+def sum_pair(blocks, axis_name, own_index, axis):
+    theirs = lax.dynamic_index_in_dim(blocks, 1 - own_index, axis, keepdims=False)
+    mine = lax.dynamic_index_in_dim(blocks, own_index, axis, keepdims=False)
+    return mine.astype(F32) + swap(theirs.astype(BF), axis_name).astype(F32)
+
+
+def sum_ring(block_of, z):
+    far = block_of((z + 2) % 4).astype(BF)
+    half = far.shape[0] // 2
+    from_below = up(far[:half])
+    from_above = down(far[half:])
+    pad = ((0, half),) + ((0, 0),) * (far.ndim - 1)
+    pad_high = ((half, 0),) + ((0, 0),) * (far.ndim - 1)
+    after = block_of((z + 1) % 4) + jnp.pad(from_below, pad).astype(F32)
+    before = block_of((z + 3) % 4) + jnp.pad(from_above, pad_high).astype(F32)
+    got_up = up(after.astype(BF))
+    got_down = down(before.astype(BF))
+    return block_of(z) + got_up.astype(F32) + got_down.astype(F32)
+
+
+def weight_sum(left, right, order, z, x, y):
+    width = right.shape[1]
+    if order[0] == "z":
+
+        def block_of(place):
+            return contract_rows(lax.dynamic_slice_in_dim(left, place * 256, 256, 1), right)
+
+        own = sum_ring(block_of, z).reshape(2, 2, 64, width)
+        own = sum_pair(own, "y", y, 1)
+        own = sum_pair(own, "x", x, 0)
+    else:
+
+        def half_of(x_place):
+            columns = [
+                lax.dynamic_slice_in_dim(left, step * 256 + x_place * 128, 128, 1)
+                for step in range(4)
+            ]
+            return contract_rows(jnp.concatenate(columns, axis=1), right)
+
+        theirs = swap(half_of(1 - x).astype(BF), "x")
+        own = half_of(x) + theirs.astype(F32)
+        own = sum_pair(own.reshape(4, 2, 64, width), "y", y, 1)
+        own = sum_ring(lambda place: lax.dynamic_index_in_dim(own, place, 0, keepdims=False), z)
+    return turn(own.astype(BF)).astype(F32)
+
+
+def sum_chips(value, steps):
+    for step in steps:
+        if step == "0":
+            value = value + lax.ppermute(value, "z", [(0, 1), (1, 0), (2, 3), (3, 2)])
+        elif step == "1":
+            value = value + lax.ppermute(value, "z", [(0, 3), (3, 0), (1, 2), (2, 1)])
+        else:
+            value = value + swap(value, step)
+    return value
+
+
+def rows_of(value, start, count):
+    return lax.dynamic_slice_in_dim(value, start, count, 0)
+
+
+def local_chip(
+    tokens,
+    lengths,
+    pairing,
+    w_qkv,
+    b_qv,
+    w_out,
+    b_out,
+    ln_gain,
+    ln_bias,
+    w_up,
+    b_up,
+    w_down,
+    b_down,
+    w_proj,
+    cot,
+):
+    z, x, c, y = (lax.axis_index(name) for name in ("z", "x", "c", "y"))
+    chip = 4 * z + 2 * x + y
+    token_count, width = tokens.shape
+    share = token_count // 2
+    own_start, other_start = c * share, (1 - c) * share
+    gains, shifts = ln_gain.astype(F32), ln_bias.astype(F32)
+
+    qkv_rows = jnp.concatenate([w_qkv[0], w_qkv[1], w_qkv[2]], axis=1)
+    full_qkv = gather_blocks(turn(qkv_rows), "xyz", z, x, y)
+    row = jnp.where(c == y, tokens, swap(tokens, "c"))
+    bias = turn(jnp.concatenate([b_qv.reshape(-1), b_up])[None])[0].astype(F32)
+    full_out = gather_blocks(turn(w_out.T), "xyz", z, x, y)
+    full_up = gather_blocks(turn(w_up), "zyx", z, x, y)
+    full_down = gather_blocks(turn(w_down.T), "xyz", z, x, y)
+    own_cot = turn(cot)
+    all_pairs = lax.all_gather(pairing, ("z", "x", "c", "y"), axis=0, tiled=False)
+
+    half_width = w_qkv.shape[2]
+    local_heads = half_width // HEAD_DIM
+    q_bias, v_bias, up_shift = (
+        bias[:half_width],
+        bias[half_width : 2 * half_width],
+        bias[2 * half_width :],
+    )
+    row_lengths = lax.dynamic_index_in_dim(lengths, chip, 0, keepdims=False)
+    segments = segments_of(row_lengths, token_count)
+    projected = dot(row, full_qkv)
+    heads_shape = (token_count, local_heads, HEAD_DIM)
+    query_rows = (projected[:, :half_width] + q_bias).astype(BF).reshape(heads_shape)
+    key_rows = projected[:, half_width : 2 * half_width].astype(BF).reshape(heads_shape)
+    value_rows = (projected[:, 2 * half_width :] + v_bias).astype(BF).reshape(heads_shape)
+    mixed, log_totals = attend_forward(query_rows, key_rows, value_rows, segments, 512)
+
+    def row_sum(left, weight_t, transposed):
+        times = contract_cols if transposed else dot
+        theirs = swap(times(left(1), weight_t).astype(BF), "c")
+        return times(left(0), weight_t) + theirs.astype(F32)
+
+    def mixed_half(which):
+        return rows_of(mixed, other_start if which else own_start, share)
+
+    attn_sum = row_sum(mixed_half, full_out, True)
+    own_tokens = rows_of(row, own_start, share).astype(F32)
+    normed, unit_one, rstd_one = norm_forward(
+        own_tokens + attn_sum + b_out.astype(F32), gains[0], shifts[0]
+    )
+    normed_low = normed.astype(BF)
+    normed_all = jnp.concatenate([normed_low, swap(normed_low, "c")], axis=0)
+    up_value = dot(normed_all, full_up) + up_shift
+    activation = jax.nn.gelu(up_value, approximate=False).astype(BF)
+    ffn_sum = row_sum(
+        lambda which: activation[which * share : (which + 1) * share], full_down, True
+    )
+    result, unit_two, rstd_two = norm_forward(
+        normed + ffn_sum + b_down.astype(F32), gains[1], shifts[1]
+    )
+    result_low = result.astype(BF)
+    y_out = turn(result_low)
+    embed = dot(result_low, w_proj).astype(BF)
+
+    other_embed = swap(embed, "c")
+    row_embed = jnp.where(
+        c == 0,
+        jnp.concatenate([embed, other_embed], axis=0),
+        jnp.concatenate([other_embed, embed], axis=0),
+    )
+    query_span = NQ_ROW * QLEN
+    half_span = query_span // 2
+    half_queries = NQ_ROW // 2
+    own_queries = rows_of(row_embed, c * half_span, half_span)
+    chips = ("z", "x", "y")
+    chip_count = lengths.shape[0]
+    queries = lax.all_to_all(
+        jnp.broadcast_to(own_queries[None], (chip_count,) + own_queries.shape), chips, 0, 0
+    ).reshape(chip_count * half_span, -1)
+    proj_width = w_proj.shape[1]
+    widths = (proj_width, 3 * proj_width // 4, proj_width // 2)
+    doc_raw = row_embed[query_span:].astype(F32)
+    query_raw = queries.astype(F32)
+    hot = (
+        segments[query_span:, None] == NQ_ROW + jnp.arange(NDOC, dtype=jnp.int32)[None, :]
+    ).astype(F32)
+    query_levels = [normalize_cut(query_raw, cut) for cut in widths]
+    doc_levels = [normalize_cut(doc_raw, cut) for cut in widths]
+    sums_list = []
+    for cut in range(3):
+        expo = jnp.exp(
+            contract_cols(query_levels[cut][0].astype(BF), doc_levels[cut][0].astype(BF))
+            / POOL_TEMP
+        )
+        sums_list.append(jnp.dot(expo, hot, precision=FULL_PRECISION))
+    sums = jnp.stack(sums_list)
+    pooled = POOL_TEMP * jnp.log(sums / row_lengths.astype(F32))
+    query_total = chip_count * half_queries
+    own_logits = jnp.sum(pooled.reshape(3, query_total, QLEN, NDOC), axis=2) / LOSS_TEMP
+    chip_logits = lax.all_to_all(
+        jnp.broadcast_to(own_logits[None], (chip_count,) + own_logits.shape), chips, 0, 0
+    )
+    logits = jnp.transpose(chip_logits, (1, 2, 0, 3)).reshape(3, query_total, chip_count * NDOC)
+    pairs = lax.dynamic_index_in_dim(
+        all_pairs.reshape(chip_count, 2, half_queries), c, 1, keepdims=False
+    ).reshape(query_total)
+    picked = (
+        jnp.arange(chip_count * NDOC, dtype=jnp.int32)[None, :] == pairs[:, None]
+    ).astype(F32)
+    highest = jnp.max(logits, axis=2, keepdims=True)
+    shares = jnp.exp(logits - highest)
+    total = jnp.sum(shares, axis=2, keepdims=True)
+    losses = jnp.sum(
+        (highest + jnp.log(total))[:, :, 0] - jnp.sum(logits * picked, axis=2), axis=0
+    ).reshape(chip_count, half_queries)
+    losses = jnp.where(c == y, losses, swap(losses, "c"))
+    loss_out = rows_of(losses, 4 * z + 2 * x + c, 1)
+    grad_logits = (shares / total - picked) / LOSS_TEMP
+    own_grad = lax.dynamic_slice_in_dim(grad_logits, chip * NDOC, NDOC, 2)
+    coefficient = jnp.repeat(own_grad, QLEN, axis=1) / sums
+    query_grad = jnp.zeros((chip_count * half_span, proj_width), F32)
+    doc_grad = jnp.zeros((token_count - query_span, proj_width), F32)
+    for cut in range(3):
+        query_unit_f, query_part, query_scale = query_levels[cut]
+        doc_unit_f, doc_part, doc_scale = doc_levels[cut]
+        query_unit, doc_unit = query_unit_f.astype(BF), doc_unit_f.astype(BF)
+        expo = jnp.exp(contract_cols(query_unit, doc_unit) / POOL_TEMP)
+        spread = contract_cols(coefficient[cut], hot, FULL_PRECISION)
+        grad_sim = (expo * spread).astype(BF)
+        query_grad = query_grad + normalize_back(
+            dot(grad_sim, doc_unit), query_part, query_scale, proj_width
+        )
+        doc_grad = doc_grad + normalize_back(
+            contract_rows(grad_sim, query_unit), doc_part, doc_scale, proj_width
+        )
+    grad_blocks = lax.all_to_all(
+        query_grad.astype(BF).reshape(chip_count, half_span, proj_width), chips, 0, 0
+    )
+    own_query_grad = jnp.sum(grad_blocks.astype(F32), axis=0)
+    row_grad = jnp.concatenate([jnp.zeros((query_span, proj_width), F32), doc_grad], axis=0)
+    row_grad = lax.dynamic_update_slice_in_dim(row_grad, own_query_grad, c * half_span, 0)
+    grad_embed = rows_of(row_grad, own_start, share) + swap(
+        rows_of(row_grad, other_start, share), "c"
+    )
+
+    proj_low = w_proj
+    grad_embed_low = grad_embed.astype(BF)
+    grad_embed_rest = (grad_embed - grad_embed_low.astype(F32)).astype(BF)
+    grad_result = own_cot.astype(F32) + (
+        contract_cols(grad_embed_low, proj_low) + contract_cols(grad_embed_rest, proj_low)
+    )
+    proj_grad = contract_rows(result_low, grad_embed_low) + contract_rows(
+        result_low, grad_embed_rest
+    )
+    gain_two = jnp.sum(grad_result * unit_two, axis=0)
+    shift_two = jnp.sum(grad_result, axis=0)
+    grad_second = norm_backward(grad_result, unit_two, rstd_two, gains[1])
+    grad_ffn = grad_second.astype(BF)
+    down_bias = jnp.sum(grad_ffn.astype(F32), axis=0)
+    grad_ffn_all = jnp.concatenate([grad_ffn, swap(grad_ffn, "c")], axis=0)
+    down_part = weight_sum(grad_ffn_all, activation, "zyx", z, x, y)
+    grad_act = dot(grad_ffn_all, full_down)
+    _, gelu_pull = jax.vjp(partial(jax.nn.gelu, approximate=False), up_value)
+    grad_up = gelu_pull(grad_act)[0].astype(BF)
+    up_bias = jnp.sum(grad_up.astype(F32), axis=0)
+    up_part = weight_sum(normed_all, grad_up, "xyz", z, x, y)
+    grad_normed = (
+        row_sum(lambda which: grad_up[which * share : (which + 1) * share], full_up, True)
+        + grad_second
+    )
+    gain_one = jnp.sum(grad_normed * unit_one, axis=0)
+    shift_one = jnp.sum(grad_normed, axis=0)
+    grad_first = norm_backward(grad_normed, unit_one, rstd_one, gains[0])
+    grad_attn = grad_first.astype(BF)
+    out_bias = jnp.sum(grad_attn.astype(F32), axis=0)
+    other_attn = swap(grad_attn, "c")
+    grad_attn_all = jnp.where(
+        c == 0,
+        jnp.concatenate([grad_attn, other_attn], axis=0),
+        jnp.concatenate([other_attn, grad_attn], axis=0),
+    )
+    out_part = weight_sum(grad_attn_all, mixed, "zyx", z, x, y)
+    grad_mixed = dot(grad_attn_all, full_out).astype(BF)
+    grad_q, grad_k, grad_v = attend_backward(
+        query_rows, key_rows, value_rows, segments, log_totals, grad_mixed, 512
+    )
+    grads = jnp.concatenate([grad_q.astype(BF), grad_k.astype(BF), grad_v.astype(BF)], axis=1)
+    qkv_part = weight_sum(row, grads, "zyx", z, x, y)
+    grad_input = turn(
+        (
+            row_sum(
+                lambda which: rows_of(grads, other_start if which else own_start, share),
+                full_qkv,
+                True,
+            )
+            + grad_first
+        ).astype(BF)
+    )
+
+    half_sums = jnp.concatenate(
+        [
+            jnp.sum(grads[:, :half_width].astype(F32), axis=0),
+            jnp.sum(grads[:, 2 * half_width :].astype(F32), axis=0),
+            up_bias,
+        ]
+    ).reshape(-1, 128)
+    half_sums = sum_chips(half_sums, "xy01")
+    half_sums = jnp.where(c == y, half_sums, swap(half_sums, "c")).reshape(-1)
+    shared = jnp.stack([gain_one, gain_two, shift_one, shift_two, out_bias, down_bias])
+    shared = sum_chips(shared, "cxy01")
+    proj_sum = sum_chips(proj_grad, "cxy01")
+    return (
+        y_out,
+        loss_out,
+        grad_input,
+        jnp.stack([qkv_part[:, k * half_width : (k + 1) * half_width] for k in range(3)]),
+        half_sums[: 2 * half_width].reshape(2, half_width),
+        out_part.T,
+        shared[4],
+        shared[0:2],
+        shared[2:4],
+        up_part,
+        half_sums[2 * half_width :],
+        down_part.T,
+        shared[5],
+        proj_sum,
+    )
+
+
+IN_SPECS = (
+    P("dp", None),
+    P(),
+    P("dp", "tensor"),
+    P(None, "dp", "tensor"),
+    P(None, "tensor"),
+    P("tensor", "dp"),
+    P(),
+    P(),
+    P(),
+    P("dp", "tensor"),
+    P("tensor"),
+    P("tensor", "dp"),
+    P(),
+    P(),
+    P(("dp", "tensor"), None),
+)
+OUT_SPECS = (
+    P(("dp", "tensor"), None),
+    P("dp", "tensor"),
+    P(("dp", "tensor"), None),
+    P(None, "dp", "tensor"),
+    P(None, "tensor"),
+    P("tensor", "dp"),
+    P(),
+    P(),
+    P(),
+    P("dp", "tensor"),
+    P("tensor"),
+    P("tensor", "dp"),
+    P(),
+    P(),
+)
+
+
 def solution(mesh):
+    if mesh.devices.shape != (16, 2):
+        return jax.shard_map(
+            local, mesh=mesh, in_specs=IN_SPECS, out_specs=OUT_SPECS, check_vma=False
+        )
+    names = {"dp": ("z", "x", "c"), "tensor": ("y",)}
+
+    def respec(spec):
+        parts = []
+        for entry in spec:
+            axes = () if entry is None else entry if isinstance(entry, tuple) else (entry,)
+            parts.append(tuple(name for axis in axes for name in names[axis]) or None)
+        return P(*parts)
+
+    chips = Mesh(mesh.devices.reshape(4, 2, 2, 2), ("z", "x", "c", "y"))
     return jax.shard_map(
-        local,
-        mesh=mesh,
-        in_specs=(
-            P("dp", None),
-            P(),
-            P("dp", "tensor"),
-            P(None, "dp", "tensor"),
-            P(None, "tensor"),
-            P("tensor", "dp"),
-            P(),
-            P(),
-            P(),
-            P("dp", "tensor"),
-            P("tensor"),
-            P("tensor", "dp"),
-            P(),
-            P(),
-            P(("dp", "tensor"), None),
-        ),
-        out_specs=(
-            P(("dp", "tensor"), None),
-            P("dp", "tensor"),
-            P(("dp", "tensor"), None),
-            P(None, "dp", "tensor"),
-            P(None, "tensor"),
-            P("tensor", "dp"),
-            P(),
-            P(),
-            P(),
-            P("dp", "tensor"),
-            P("tensor"),
-            P("tensor", "dp"),
-            P(),
-            P(),
-        ),
+        local_chip,
+        mesh=chips,
+        in_specs=tuple(respec(spec) for spec in IN_SPECS),
+        out_specs=tuple(respec(spec) for spec in OUT_SPECS),
         check_vma=False,
     )

time: 1450 us -> 916 us (0.63)
  waiting for transfers between devices: 659 us -> 273 us
  matrix products: 396 us -> 246 us
  starting transfers between devices: 0.95 us -> 140 us
  other arithmetic: 197 us -> 98.4 us
  blocking collectives: 97.5 us -> 68.3 us
    all_gather x10 -> x0, waiting for transfers between devices: 350 us -> none  [the longest x1 64.3 us: local(): embed_all = lax.all_gather(embed, ('dp', 'tensor'), axis=0, tiled=True)]
    ppermute x0 -> x86, waiting for transfers between devices: none -> 253 us  [the longest x16 80.7 us: up(): return lax.ppermute(value, 'z', RING_UP)]
    reduce_scatter x7 -> x0, waiting for transfers between devices: 176 us -> none  [the longest x1 51 us: local(): lax.psum_scatter(out_grad.astype(jnp.bfloat16), 'dp', scatter_dimension=1...]
    psum x1 -> x0, waiting for transfers between devices: 130 us -> none  [local(): lax.psum((jnp.stack([gain_one, gain_two]), jnp.stack([shift_one, shift_tw...]
    ppermute x0 -> x86, starting transfers between devices: none -> 127 us  [the longest x12 39.4 us: turn(): return lax.ppermute(value, ('c', 'y'), TURN)]
    psum x2 -> x0, blocking collectives: 97.5 us -> none  [the longest x1 57 us: local(): qv_sum, up_bias_sum = lax.psum((qv_grad, up_bias), 'dp')]
    dot_general x154 -> x16, matrix products: 133 us -> 45.5 us  [contract_cols(): lax.dot_general(left, right, (((1,), (1,)), ((), ())), precision=precisio...]
    dot_general x103 -> x11, matrix products: 131 us -> 59.6 us  [the longest x8 48.8 us: dot(): return jnp.dot(left, right, preferred_element_type=F32)]
  transfers between devices with their start and end apart: 19 -> 89, of which waited for: 15 -> 36; matrix products, arithmetic and copies ran while one was open for 20% -> 40% of each run, Pallas kernels for 0% -> 0%
where the time goes in v1:
time: 916 us; the launch traced here: 907 us
  waiting for transfers between devices  273 us (30%)
  matrix products  246 us (27%)
  starting transfers between devices  140 us (15%)
  other arithmetic  98.4 us (11%)
  local copies, waits for them, and re-layouts  69.2 us (8%)
  blocking collectives  68.3 us (7%)
    ppermute x16, waiting for transfers between devices, up(): return lax.ppermute(value, 'z', RING_UP)  80.7 us
    all_gather x1, blocking collectives, local_chip(): lax.all_gather(pairing, ('z', 'x', 'c', 'y'), axis=0, tiled=False)  68.3 us
    ppermute x16, waiting for transfers between devices, down(): return lax.ppermute(value, 'z', RING_DOWN)  62.7 us
    ppermute x3, waiting for transfers between devices, sum_chips(): value = value + lax.ppermute(value, 'z', [(0, 1), (1, 0), (2, 3), (3, 2)])  57.2 us
    dot_general x8, matrix products, dot(): return jnp.dot(left, right, preferred_element_type=F32)  48.8 us
    dot_general x16, matrix products, contract_cols(): lax.dot_general(left, right, (((1,), (1,)), ((), ())), precision=precisio...  45.5 us
    ppermute x36, waiting for transfers between devices, swap(): return lax.ppermute(value, axis, SWAP)  39.8 us
    ppermute x12, starting transfers between devices, turn(): return lax.ppermute(value, ('c', 'y'), TURN)  39.4 us
  transfers between devices with their start and end apart: 89, of which 36 were waited for; matrix products, arithmetic and copies ran while one was open for 40% of the time, Pallas kernels for 0%

profile of v1, /device:TPU:1, one launch (start us, length us, event | category | flops | bytes accessed | tf_op | source)
XLA Modules:
  0.0 907.0 jit_solution(3095779246425554687)
XLA Ops:
  1.6 4.5 collective-permute-start.1
  28.6 4.2 collective-permute-done.11
  39.1 5.6 collective-permute-done.26
  47.9 5.8 collective-permute-done.19
  53.7 4.9 collective-permute-done.20
  62.2 3.7 collective-permute-done.21
  75.9 6.4 collective-permute-done.27
  84.5 6.4 collective-permute-done.4
  90.9 15.2 %collective-permute-done.5 = bf16[2,2,64,1536]{3,2,1,0:T(8,128)(2,1)S(1)} collective-permute-done((bf16[2,2,64,1536]{3,2,1,0:T(8,128)(2,1)S(1)}, bf16[2,2,64,1536]{3,2,1,0:T(8,128)(2,1)S(1)}, u32[]{:S(2)}, u32[]{:S(2)}) %collective-permute-start.5) | collective-permute-done | bytes 786464 | tf_op jit(solution)/shard_map/ppermute | solution.py:464
  113.7 47.5 %collective-permute-done.6 = bf16[2,2,32,1536]{3,2,1,0:T(8,128)(2,1)S(1)} collective-permute-done((bf16[2,2,32,1536]{3,2,1,0:T(8,128)(2,1)S(1)}, bf16[2,2,32,1536]{3,2,1,0:T(8,128)(2,1)S(1)}, u32[]{:S(2)}, u32[]{:S(2)}) %collective-permute-start.6) | collective-permute-done | bytes 393248 | tf_op jit(solution)/shard_map/ppermute | solution.py:460
  162.4 5.5 collective-permute-done.7
  178.0 33.4 %while.27 = (s32[]{:T(128)}, bf16[2,512,8,64]{1,3,2,0:T(8,128)(2,1)}, f32[2,8,512]{2,1,0:T(8,128)S(1)}, s32[2]{0:T(128)S(1)}, s32[1024]{0:T(1024)S(1)}, /*index=...) while((s32[]{:T(128)}, ...), condition=%wide.region_5.6_spmd, body=%wide.region_2.5_spmd.sunk | while | flops 1124855808 | bytes 55716516 | solution.py:111
  184.6 4.2 fusion.297
  188.9 5.8 fusion.298
  201.3 4.2 fusion.297
  205.6 5.8 fusion.298
  229.1 5.7 collective-permute-done.30
  234.9 11.6 %collective-permute-done.31 = bf16[2,2,32,2048]{3,2,1,0:T(8,128)(2,1)S(1)} collective-permute-done((bf16[2,2,32,2048]{3,2,1,0:T(8,128)(2,1)S(1)}, bf16[2,2,32,2048]{3,2,1,0:T(8,128)(2,1)S(1)}, u32[]{:S(2)}, u32[]{:S(2)}) %collective-permute-start.31) | collective-permute-done | bytes 524320 | tf_op jit(solution)/shard_map/ppermute | solution.py:464
  246.6 4.0 maximum_select_fusion
  250.7 25.2 %multiply_convert_fusion.1 = (bf16[1024,2048]{1,0:T(8,128)(2,1)S(1)}, f32[1024,2048]{1,0:T(8,128)}, f32[1024,2048]{1,0:T(8,128)}) fusion(f32[2048]{0:T(1024)S(1)} %bitcast.449, bf16[1024,2048]{1,0:T(8,128)(2,1)S(1)} %bitcast.367, bf16[512,1024]{1,0:T(8,128)(2,1)S(1)} %collective-permute-done.17, bf16[512,1024]{1,0:T(8,128)(2,1)S(1)} %fusion.56), kind=kOutput, calls=%fused_computation.41 | convolution fusion | flops 4437573632 | bytes 27271168 | tf_op jit(solution)/shard_map/dot_general | solution.py:448
  281.7 68.3 %all-gather.1 = s32[32,1,4]{2,1,0:T(1,128)S(1)} all-gather(s32[1,1,4]{2,1,0:T(1,128)S(1)} %bitcast.457), channel_id=2, replica_groups=mesh['z'=4,'x'=2,'c'=2,'y'=2] {'z','x','c','y'}, dimensions={0}, use_global_device_ids=true | all-gather | bytes 528 | tf_op jit(solution)/shard_map/all_gather | solution.py:590
  350.3 5.8 fusion.221
  363.3 4.0 all-to-all-start
  369.6 10.5 %all-to-all-done = bf16[16,128,128]{2,1,0:T(8,128)(2,1)S(1)} async-done(((bf16[16,128,128]{2,1,0:T(8,128)(2,1)}), bf16[16,128,128]{2,1,0:T(8,128)(2,1)S(1)}, u32[]{:S(2)}, u32[]{:S(2)}) %all-to-all-start) | async-done | bytes 524320 | tf_op jit(solution)/shard_map/all_to_all | solution.py:647
  404.3 3.7 fusion.34
  412.7 5.3 all-to-all-start.1
  419.3 5.3 all-to-all-done.1
  438.3 5.8 multiply_convert_fusion.4
  444.1 6.8 multiply_convert_fusion.3
  451.0 3.7 multiply_convert_fusion.2
  466.5 4.2 all-to-all-start.2
  477.8 3.8 all-to-all-done.2
  484.4 5.3 collective-permute-start.37
  502.3 14.0 %convert_reduce_fusion = (f32[2048]{0:T(1024)}, bf16[1024,2048]{1,0:T(8,128)(2,1)S(1)}) fusion(f32[1024,2048]{1,0:T(8,128)} %get-tuple-element.235, bf16[1024,2048]{1,0:T(8,128)(2,1)} %bitcast.372, bf16[512,1024]{1,0:T(8,128)(2,1)S(1)} %collective-permute-done.38, bf16[512,1024]{1,0:T(8,128)(2,1)} %get-tuple-element.225, ...), kind=kOutput, calls=%fused_computation.39 | convolution fusion | flops 4334811136 | bytes 27279360 | tf_op jit(solution)/shard_map/dot_general | solution.py:448
  542.0 3.7 fusion.42
  547.8 4.8 collective-permute-done.76
  559.1 40.5 %collective-permute-done.65 = f32[6,1024]{1,0:T(8,128)S(1)} collective-permute-done((f32[6,1024]{1,0:T(8,128)S(1)}, f32[6,1024]{1,0:T(8,128)S(1)}, u32[]{:S(2)}, u32[]{:S(2)}) %collective-permute-start.65) | collective-permute-done | bytes 24608 | tf_op jit(solution)/shard_map/ppermute | solution.py:546
  600.1 3.7 convolution_convert_fusion
  604.8 6.4 collective-permute-done.84
  619.9 7.0 collective-permute-done.85
  632.3 9.1 %collective-permute-start.55 = (bf16[128,512]{1,0:T(8,128)(2,1)}, bf16[128,512]{1,0:T(8,128)(2,1)}, u32[]{:S(2)}, u32[]{:S(2)}) collective-permute-start(bf16[128,512]{1,0:T(8,128)(2,1)} %get-tuple-element.263), channel_id=1, source_target_pairs={{0,8},{8,16},{16,24},{24,0},{1,9},{9,17},{17,25},{25,1},{2,10},{10... | collective-permute-start | bytes 393224 | tf_op jit(solution)/shard_map/ppermute | solution.py:460
  641.7 119.2 %while.28 = (s32[]{:T(128)}, f32[1024,8,64]{0,2,1:T(8,128)}, f32[1024,8,64]{0,2,1:T(8,128)}, bf16[2,512,8,64]{1,3,2,0:T(8,128)(2,1)}, s32[2]{0:T(128)S(1)}, /*in...) while((s32[]{:T(128)}, f32[1024,8,64]{0,2,1:T(8,128)}, ...), condition=%wide.region_34.35_spmd.clone, body=%wide.region_32.34_spmd.clone.sunk | while | flops 2725507072 | bytes 212953888 | solution.py:154
  644.3 9.4 %fusion.308 = f32[8,512,1024]{2,1,0:T(8,128)} fusion(bf16[1024,8,64]{0,2,1:T(8,128)(2,1)S(1)} %get-tuple-element.506, bf16[1024,8,64]{0,2,1:T(8,128)(2,1)} %get-tuple-element.505, s32[]{:T(128)S(6)} %select_n.604), kind=kOutput, calls=%fused_computation.28.clone.1 | convolution fusion | flops 536870912 | bytes 18350084 | tf_op jit(solution)/shard_map/while/body/eval_jaxpr/qhd,khd->hqk/dot_general | solution.py:128
  654.1 13.0 %multiply_reduce_fusion.23 = (f32[8,512]{1,0:T(8,128)S(1)}, f32[8,512,1024]{2,1,0:T(8,128)}) fusion(f32[8,512,1024]{2,1,0:T(8,128)} %fusion.308, f32[8,512]{1,0:T(8,128)S(1)} %dynamic-slice_bitcast_fusion.2, bf16[1024,8,64]{0,2,1:T(8,128)(2,1)S(1)} %get-tuple-element.503, bf16[1024,8,64]{0,2,1:T(8,128)(2,1)S(1)} %copy-done.10, s32[]{:T(128)S(6)} %select_n.604, ...), kind=kOutput, calls=%fused_computation.17.clone.1 | convolution fusion | flops 557838336 | bytes 35684356 | tf_op jit(solution)/shard_map/while/body/eval_jaxpr/qhd,khd->hqk/dot_general | solution.py:90
  667.2 14.9 %multiply_convert_fusion.22 = bf16[8,512,1024]{2,1,0:T(8,128)(2,1)} fusion(f32[8,512,1024]{2,1,0:T(8,128)} %get-tuple-element.433, f32[8,512,1024]{2,1,0:T(8,128)} %fusion.308, f32[8,512]{1,0:T(8,128)S(1)} %get-tuple-element.434), kind=kLoop, calls=%fused_computation.16.clone.1 | loop fusion | flops 12582912 | bytes 41959424 | tf_op jit(solution)/shard_map/while/body/eval_jaxpr/convert_element_type | solution.py:132
  682.0 6.7 bitcast_add_fusion.14
  688.7 7.6 fusion.309
  696.3 4.2 bitcast_add_fusion.15
  703.0 9.3 %fusion.308 = f32[8,512,1024]{2,1,0:T(8,128)} fusion(bf16[1024,8,64]{0,2,1:T(8,128)(2,1)S(1)} %get-tuple-element.506, bf16[1024,8,64]{0,2,1:T(8,128)(2,1)} %get-tuple-element.505, s32[]{:T(128)S(6)} %select_n.604), kind=kOutput, calls=%fused_computation.28.clone.1 | convolution fusion | flops 536870912 | bytes 18350084 | tf_op jit(solution)/shard_map/while/body/eval_jaxpr/qhd,khd->hqk/dot_general | solution.py:128
  712.8 13.0 %multiply_reduce_fusion.23 = (f32[8,512]{1,0:T(8,128)S(1)}, f32[8,512,1024]{2,1,0:T(8,128)}) fusion(f32[8,512,1024]{2,1,0:T(8,128)} %fusion.308, f32[8,512]{1,0:T(8,128)S(1)} %dynamic-slice_bitcast_fusion.2, bf16[1024,8,64]{0,2,1:T(8,128)(2,1)S(1)} %get-tuple-element.503, bf16[1024,8,64]{0,2,1:T(8,128)(2,1)S(1)} %copy-done.10, s32[]{:T(128)S(6)} %select_n.604, ...), kind=kOutput, calls=%fused_computation.17.clone.1 | convolution fusion | flops 557838336 | bytes 35684356 | tf_op jit(solution)/shard_map/while/body/eval_jaxpr/qhd,khd->hqk/dot_general | solution.py:90
  725.9 14.9 %multiply_convert_fusion.22 = bf16[8,512,1024]{2,1,0:T(8,128)(2,1)} fusion(f32[8,512,1024]{2,1,0:T(8,128)} %get-tuple-element.433, f32[8,512,1024]{2,1,0:T(8,128)} %fusion.308, f32[8,512]{1,0:T(8,128)S(1)} %get-tuple-element.434), kind=kLoop, calls=%fused_computation.16.clone.1 | loop fusion | flops 12582912 | bytes 41959424 | tf_op jit(solution)/shard_map/while/body/eval_jaxpr/convert_element_type | solution.py:132
  740.7 7.2 bitcast_add_fusion.14
  748.0 7.6 fusion.309
  755.6 4.9 bitcast_add_fusion.15
  780.3 4.3 convert_add_fusion
  788.3 10.4 %collective-permute-done.52 = f32[24,128]{1,0:T(8,128)S(1)} collective-permute-done((f32[24,128]{1,0:T(8,128)S(1)}, f32[24,128]{1,0:T(8,128)S(1)}, u32[]{:S(2)}, u32[]{:S(2)}) %collective-permute-start.52) | collective-permute-done | bytes 12320 | tf_op jit(solution)/shard_map/ppermute | solution.py:546
  811.1 4.2 collective-permute-done.79
  820.2 4.9 collective-permute-done.58
  825.1 3.9 collective-permute-start.80
  834.3 14.6 %collective-permute-done.59 = bf16[2,64,512]{2,1,0:T(8,128)(2,1)S(1)} collective-permute-done((bf16[2,64,512]{2,1,0:T(8,128)(2,1)S(1)}, bf16[2,64,512]{2,1,0:T(8,128)(2,1)S(1)}, u32[]{:S(2)}, u32[]{:S(2)}) %collective-permute-start.59) | collective-permute-done | bytes 131104 | tf_op jit(solution)/shard_map/ppermute | solution.py:456
  852.5 5.1 collective-permute-start.61
  861.4 9.2 %collective-permute-done.46 = bf16[256,1536]{1,0:T(8,128)(2,1)S(1)} collective-permute-done((bf16[256,1536]{1,0:T(8,128)(2,1)S(1)}, bf16[256,1536]{1,0:T(8,128)(2,1)S(1)}, u32[]{:S(2)}, u32[]{:S(2)}) %collective-permute-start.46) | collective-permute-done | bytes 786464 | tf_op jit(solution)/shard_map/ppermute | solution.py:464
  875.9 5.2 collective-permute-start.42
  885.7 5.4 collective-permute-done.70
  (692 shorter events, 317.0 us)
Async XLA Ops:
  1.6 25.7 %collective-permute-start.1 = (bf16[64,1536]{1,0:T(8,128)(2,1)S(1)}, bf16[64,1536]{1,0:T(8,128)(2,1)S(1)}, u32[]{:S(2)}, u32[]{:S(2)}) collective-permute-start(bf16[64,1536]{1,0:T(8,128)(2,1)S(1)} %pad_maximum_fusion.10), channel_id=1, source_target_pairs={{0,0},{1,2},{2,1},{3,3},{4,4},{5,6},{6,5},{7,7},{8,8},{9,10},{10,9... | collective-permute-start | bytes 589832 | tf_op jit(solution)/shard_map/ppermute | solution.py:452
  6.2 161.9 %collective-permute-start = (bf16[1024,1024]{1,0:T(8,128)(2,1)}, bf16[1024,1024]{1,0:T(8,128)(2,1)S(1)}, u32[]{:S(2)}, u32[]{:S(2)}) collective-permute-start(bf16[1024,1024]{1,0:T(8,128)(2,1)} %param.19), channel_id=1, source_target_pairs={{0,2},{2,0},{1,3},{3,1},{4,6},{6,4},{5,7},{7,5},{8,10},{10,8},{9,1... | collective-permute-start | bytes 6291464 | tf_op jit(solution)/shard_map/ppermute | solution.py:456
  7.7 12.7 %collective-permute-start.8 = (bf16[1,3072]{1,0:T(2,128)(2,1)S(1)}, bf16[1,3072]{1,0:T(2,128)(2,1)S(1)}, u32[]{:S(2)}, u32[]{:S(2)}) collective-permute-start(bf16[1,3072]{1,0:T(2,128)(2,1)S(1)} %broadcast_in_dim.170), channel_id=1, source_target_pairs={{0,0},{1,2},{2,1},{3,3},{4,4},{5,6},{6,5},{7,7},{8,8},{9,10},{10,9... | collective-permute-start | bytes 18440 | tf_op jit(solution)/shard_map/ppermute | solution.py:452
  9.6 14.4 %collective-permute-start.9 = (bf16[64,512]{1,0:T(8,128)(2,1)}, bf16[64,512]{1,0:T(8,128)(2,1)S(1)}, u32[]{:S(2)}, u32[]{:S(2)}) collective-permute-start(bf16[64,512]{1,0:T(8,128)(2,1)} %bitcast.461), channel_id=1, source_target_pairs={{0,0},{1,2},{2,1},{3,3},{4,4},{5,6},{6,5},{7,7},{8,8},{9,10},{10,9... | collective-permute-start | bytes 196616 | tf_op jit(solution)/shard_map/ppermute | solution.py:452
  13.2 20.9 %collective-permute-start.18 = (bf16[64,2048]{1,0:T(8,128)(2,1)}, bf16[64,2048]{1,0:T(8,128)(2,1)}, u32[]{:S(2)}, u32[]{:S(2)}) collective-permute-start(bf16[64,2048]{1,0:T(8,128)(2,1)} %param.28), channel_id=1, source_target_pairs={{0,0},{1,2},{2,1},{3,3},{4,4},{5,6},{6,5},{7,7},{8,8},{9,10},{10,9... | collective-permute-start | bytes 786440 | tf_op jit(solution)/shard_map/ppermute | solution.py:452
  20.4 17.2 %collective-permute-start.25 = (bf16[64,2048]{1,0:T(8,128)(2,1)}, bf16[64,2048]{1,0:T(8,128)(2,1)S(1)}, u32[]{:S(2)}, u32[]{:S(2)}) collective-permute-start(bf16[64,2048]{1,0:T(8,128)(2,1)} %bitcast.460), channel_id=1, source_target_pairs={{0,0},{1,2},{2,1},{3,3},{4,4},{5,6},{6,5},{7,7},{8,8},{9,10},{10,9... | collective-permute-start | bytes 786440 | tf_op jit(solution)/shard_map/ppermute | solution.py:452
  32.8 14.9 %collective-permute-start.12 = (bf16[2,2,64,512]{3,2,1,0:T(8,128)(2,1)S(1)}, bf16[2,2,64,512]{3,2,1,0:T(8,128)(2,1)S(1)}, u32[]{:S(2)}, u32[]{:S(2)}) collective-permute-start(bf16[2,2,64,512]{3,2,1,0:T(8,128)(2,1)S(1)} %maximum_select_fusion.12), channel_id=1, source_target_pairs={{0,8},{8,16},{16,24},{24,0},{1,9},{9,17},{17,25},{25,1},{2,10},{10... | collective-permute-start | bytes 786440 | tf_op jit(solution)/shard_map/ppermute | solution.py:460
  34.2 26.4 %collective-permute-start.13 = (bf16[2,2,64,512]{3,2,1,0:T(8,128)(2,1)S(1)}, bf16[2,2,64,512]{3,2,1,0:T(8,128)(2,1)S(1)}, u32[]{:S(2)}, u32[]{:S(2)}) collective-permute-start(bf16[2,2,64,512]{3,2,1,0:T(8,128)(2,1)S(1)} %maximum_select_fusion.12), channel_id=1, source_target_pairs={{8,0},{16,8},{24,16},{0,24},{9,1},{17,9},{25,17},{1,25},{10,2},{18... | collective-permute-start | bytes 786440 | tf_op jit(solution)/shard_map/ppermute | solution.py:464
  37.6 16.1 %collective-permute-start.19 = (bf16[64,2048]{1,0:T(8,128)(2,1)}, bf16[64,2048]{1,0:T(8,128)(2,1)S(1)}, u32[]{:S(2)}, u32[]{:S(2)}) collective-permute-start(bf16[64,2048]{1,0:T(8,128)(2,1)} %collective-permute-done.18), channel_id=1, source_target_pairs={{0,8},{8,16},{16,24},{24,0},{1,9},{9,17},{17,25},{25,1},{2,10},{10... | collective-permute-start | bytes 786440 | tf_op jit(solution)/shard_map/ppermute | solution.py:460
  44.7 13.9 %collective-permute-start.20 = (bf16[64,2048]{1,0:T(8,128)(2,1)}, bf16[64,2048]{1,0:T(8,128)(2,1)S(1)}, u32[]{:S(2)}, u32[]{:S(2)}) collective-permute-start(bf16[64,2048]{1,0:T(8,128)(2,1)} %collective-permute-done.18), channel_id=1, source_target_pairs={{8,0},{16,8},{24,16},{0,24},{9,1},{17,9},{25,17},{1,25},{10,2},{18... | collective-permute-start | bytes 786440 | tf_op jit(solution)/shard_map/ppermute | solution.py:464
  47.8 21.7 %collective-permute-start.3 = (bf16[2,64,1536]{2,1,0:T(8,128)(2,1)S(1)}, bf16[2,64,1536]{2,1,0:T(8,128)(2,1)S(1)}, u32[]{:S(2)}, u32[]{:S(2)}) collective-permute-start(bf16[2,64,1536]{2,1,0:T(8,128)(2,1)S(1)} %maximum_select_fusion.10), channel_id=1, source_target_pairs={{0,1},{1,0},{2,3},{3,2},{4,5},{5,4},{6,7},{7,6},{8,9},{9,8},{10,11... | collective-permute-start | bytes 1179656 | tf_op jit(solution)/shard_map/ppermute | solution.py:456
  53.6 17.5 %collective-permute-start.14 = (bf16[2,2,32,512]{3,2,1,0:T(8,128)(2,1)S(1)}, bf16[2,2,32,512]{3,2,1,0:T(8,128)(2,1)S(1)}, u32[]{:S(2)}, u32[]{:S(2)}) collective-permute-start(bf16[2,2,32,512]{3,2,1,0:T(8,128)(2,1)S(1)} %slice.239), channel_id=1, source_target_pairs={{0,8},{8,16},{16,24},{24,0},{1,9},{9,17},{17,25},{25,1},{2,10},{10... | collective-permute-start | bytes 393224 | tf_op jit(solution)/shard_map/ppermute | solution.py:460
  69.4 12.8 %collective-permute-start.27 = (bf16[2,64,2048]{2,1,0:T(8,128)(2,1)S(1)}, bf16[2,64,2048]{2,1,0:T(8,128)(2,1)S(1)}, u32[]{:S(2)}, u32[]{:S(2)}) collective-permute-start(bf16[2,64,2048]{2,1,0:T(8,128)(2,1)S(1)} %maximum_select_fusion.8), channel_id=1, source_target_pairs={{0,1},{1,0},{2,3},{3,2},{4,5},{5,4},{6,7},{7,6},{8,9},{9,8},{10,11... | collective-permute-start | bytes 1572872 | tf_op jit(solution)/shard_map/ppermute | solution.py:456
  69.5 36.9 %collective-permute-start.23 = (bf16[4,64,2048]{2,1,0:T(8,128)(2,1)S(1)}, bf16[4,64,2048]{2,1,0:T(8,128)(2,1)S(1)}, u32[]{:S(2)}, u32[]{:S(2)}) collective-permute-start(bf16[4,64,2048]{2,1,0:T(8,128)(2,1)S(1)} %fusion.144), channel_id=1, source_target_pairs={{0,1},{1,0},{2,3},{3,2},{4,5},{5,4},{6,7},{7,6},{8,9},{9,8},{10,11... | collective-permute-start | bytes 3145736 | tf_op jit(solution)/shard_map/ppermute | solution.py:456
  71.1 19.8 %collective-permute-start.4 = (bf16[2,2,64,1536]{3,2,1,0:T(8,128)(2,1)S(1)}, bf16[2,2,64,1536]{3,2,1,0:T(8,128)(2,1)S(1)}, u32[]{:S(2)}, u32[]{:S(2)}) collective-permute-start(bf16[2,2,64,1536]{3,2,1,0:T(8,128)(2,1)S(1)} %maximum_select_fusion.6), channel_id=1, source_target_pairs={{0,8},{8,16},{16,24},{24,0},{1,9},{9,17},{17,25},{25,1},{2,10},{10... | collective-permute-start | bytes 2359304 | tf_op jit(solution)/shard_map/ppermute | solution.py:460
  71.5 34.7 %collective-permute-start.5 = (bf16[2,2,64,1536]{3,2,1,0:T(8,128)(2,1)S(1)}, bf16[2,2,64,1536]{3,2,1,0:T(8,128)(2,1)S(1)}, u32[]{:S(2)}, u32[]{:S(2)}) collective-permute-start(bf16[2,2,64,1536]{3,2,1,0:T(8,128)(2,1)S(1)} %maximum_select_fusion.6), channel_id=1, source_target_pairs={{8,0},{16,8},{24,16},{0,24},{9,1},{17,9},{25,17},{1,25},{10,2},{18... | collective-permute-start | bytes 2359304 | tf_op jit(solution)/shard_map/ppermute | solution.py:464
  83.4 134.8 %collective-permute-start.28 = (bf16[2,2,64,2048]{3,2,1,0:T(8,128)(2,1)}, bf16[2,2,64,2048]{3,2,1,0:T(8,128)(2,1)}, u32[]{:S(2)}, u32[]{:S(2)}) collective-permute-start(bf16[2,2,64,2048]{3,2,1,0:T(8,128)(2,1)} %maximum_select_fusion.4), channel_id=1, source_target_pairs={{0,8},{8,16},{16,24},{24,0},{1,9},{9,17},{17,25},{25,1},{2,10},{10... | collective-permute-start | bytes 3145736 | tf_op jit(solution)/shard_map/ppermute | solution.py:460
  90.9 128.8 %collective-permute-start.29 = (bf16[2,2,64,2048]{3,2,1,0:T(8,128)(2,1)}, bf16[2,2,64,2048]{3,2,1,0:T(8,128)(2,1)}, u32[]{:S(2)}, u32[]{:S(2)}) collective-permute-start(bf16[2,2,64,2048]{3,2,1,0:T(8,128)(2,1)} %maximum_select_fusion.4), channel_id=1, source_target_pairs={{8,0},{16,8},{24,16},{0,24},{9,1},{17,9},{25,17},{1,25},{10,2},{18... | collective-permute-start | bytes 3145736 | tf_op jit(solution)/shard_map/ppermute | solution.py:464
  106.2 55.0 %collective-permute-start.6 = (bf16[2,2,32,1536]{3,2,1,0:T(8,128)(2,1)S(1)}, bf16[2,2,32,1536]{3,2,1,0:T(8,128)(2,1)S(1)}, u32[]{:S(2)}, u32[]{:S(2)}) collective-permute-start(bf16[2,2,32,1536]{3,2,1,0:T(8,128)(2,1)S(1)} %slice.232), channel_id=1, source_target_pairs={{0,8},{8,16},{16,24},{24,0},{1,9},{9,17},{17,25},{25,1},{2,10},{10... | collective-permute-start | bytes 1179656 | tf_op jit(solution)/shard_map/ppermute | solution.py:460
  106.4 61.6 %collective-permute-start.7 = (bf16[2,2,32,1536]{3,2,1,0:T(8,128)(2,1)S(1)}, bf16[2,2,32,1536]{3,2,1,0:T(8,128)(2,1)S(1)}, u32[]{:S(2)}, u32[]{:S(2)}) collective-permute-start(bf16[2,2,32,1536]{3,2,1,0:T(8,128)(2,1)S(1)} %slice.233), channel_id=1, source_target_pairs={{8,0},{16,8},{24,16},{0,24},{9,1},{17,9},{25,17},{1,25},{10,2},{18... | collective-permute-start | bytes 1179656 | tf_op jit(solution)/shard_map/ppermute | solution.py:464
  161.2 85.4 %collective-permute-start.24 = (bf16[4,2,64,2048]{3,2,1,0:T(8,128)(2,1)}, bf16[4,2,64,2048]{3,2,1,0:T(8,128)(2,1)}, u32[]{:S(2)}, u32[]{:S(2)}) collective-permute-start(bf16[4,2,64,2048]{3,2,1,0:T(8,128)(2,1)} %maximum_select_fusion.1), channel_id=1, source_target_pairs={{0,4},{4,0},{1,5},{5,1},{2,6},{6,2},{3,7},{7,3},{8,12},{12,8},{9,1... | collective-permute-start | bytes 6291464 | tf_op jit(solution)/shard_map/ppermute | solution.py:456
  219.5 15.4 %collective-permute-start.30 = (bf16[2,2,32,2048]{3,2,1,0:T(8,128)(2,1)S(1)}, bf16[2,2,32,2048]{3,2,1,0:T(8,128)(2,1)S(1)}, u32[]{:S(2)}, u32[]{:S(2)}) collective-permute-start(bf16[2,2,32,2048]{3,2,1,0:T(8,128)(2,1)S(1)} %slice.247), channel_id=1, source_target_pairs={{0,8},{8,16},{16,24},{24,0},{1,9},{9,17},{17,25},{25,1},{2,10},{10... | collective-permute-start | bytes 1572872 | tf_op jit(solution)/shard_map/ppermute | solution.py:460
  221.1 25.4 %collective-permute-start.31 = (bf16[2,2,32,2048]{3,2,1,0:T(8,128)(2,1)S(1)}, bf16[2,2,32,2048]{3,2,1,0:T(8,128)(2,1)S(1)}, u32[]{:S(2)}, u32[]{:S(2)}) collective-permute-start(bf16[2,2,32,2048]{3,2,1,0:T(8,128)(2,1)S(1)} %slice.248), channel_id=1, source_target_pairs={{8,0},{16,8},{24,16},{0,24},{9,1},{17,9},{25,17},{1,25},{10,2},{18... | collective-permute-start | bytes 1572872 | tf_op jit(solution)/shard_map/ppermute | solution.py:464
  227.1 23.5 %collective-permute-start.17 = (bf16[512,1024]{1,0:T(8,128)(2,1)S(1)}, bf16[512,1024]{1,0:T(8,128)(2,1)S(1)}, u32[]{:S(2)}, u32[]{:S(2)}) collective-permute-start(bf16[512,1024]{1,0:T(8,128)(2,1)S(1)} %fusion.56), channel_id=1, source_target_pairs={{0,2},{2,0},{1,3},{3,1},{4,6},{6,4},{5,7},{7,5},{8,10},{10,8},{9,1... | collective-permute-start | bytes 3145736 | tf_op jit(solution)/shard_map/ppermute | solution.py:456
  279.3 70.9 %collective-permute-start.32 = (bf16[512,1024]{1,0:T(8,128)(2,1)}, bf16[512,1024]{1,0:T(8,128)(2,1)}, u32[]{:S(2)}, u32[]{:S(2)}) collective-permute-start(bf16[512,1024]{1,0:T(8,128)(2,1)} %fusion.68), channel_id=1, source_target_pairs={{0,2},{2,0},{1,3},{3,1},{4,6},{6,4},{5,7},{7,5},{8,10},{10,8},{9,1... | collective-permute-start | bytes 3145736 | tf_op jit(solution)/shard_map/ppermute | solution.py:456
  279.8 212.6 %collective-permute-start.36 = (bf16[512,1024]{1,0:T(8,128)(2,1)}, bf16[512,1024]{1,0:T(8,128)(2,1)}, u32[]{:S(2)}, u32[]{:S(2)}) collective-permute-start(bf16[512,1024]{1,0:T(8,128)(2,1)} %param.33), channel_id=1, source_target_pairs={{0,0},{1,2},{2,1},{3,3},{4,4},{5,6},{6,5},{7,7},{8,8},{9,10},{10,9... | collective-permute-start | bytes 3145736 | tf_op jit(solution)/shard_map/ppermute | solution.py:452
  363.3 16.9 %all-to-all-start = ((bf16[16,128,128]{2,1,0:T(8,128)(2,1)}), bf16[16,128,128]{2,1,0:T(8,128)(2,1)S(1)}, u32[]{:S(2)}, u32[]{:S(2)}) async-start(bf16[16,128,128]{2,1,0:T(8,128)(2,1)} %broadcast_in_dim.184), calls=%async_computation | async-start | bytes 1048576 | tf_op jit(solution)/shard_map/all_to_all | solution.py:647
  412.7 11.9 %all-to-all-start.1 = ((f32[16,1,1536]{2,1,0:T(1,128)}), f32[16,1,1536]{2,1,0:T(1,128)}, u32[]{:S(2)}, u32[]{:S(2)}) async-start(f32[16,1,1536]{2,1,0:T(1,128)} %reshape.1045), calls=%async_computation.1 | async-start | bytes 196608 | tf_op jit(solution)/shard_map/all_to_all | solution.py:670
  466.5 15.1 %all-to-all-start.2 = ((bf16[16,128,128]{2,1,0:T(8,128)(2,1)}), bf16[16,128,128]{2,1,0:T(8,128)(2,1)}, u32[]{:S(2)}, u32[]{:S(2)}) async-start(bf16[16,128,128]{2,1,0:T(8,128)(2,1)} %bitcast.405), calls=%async_computation.2 | async-start | bytes 1048576 | tf_op jit(solution)/shard_map/all_to_all | solution.py:706
  499.0 22.5 %collective-permute-start.33 = (bf16[512,1024]{1,0:T(8,128)(2,1)S(1)}, bf16[512,1024]{1,0:T(8,128)(2,1)S(1)}, u32[]{:S(2)}, u32[]{:S(2)}) collective-permute-start(bf16[512,1024]{1,0:T(8,128)(2,1)S(1)} %add_convert_fusion.2), channel_id=1, source_target_pairs={{0,0},{1,2},{2,1},{3,3},{4,4},{5,6},{6,5},{7,7},{8,8},{9,10},{10,9... | collective-permute-start | bytes 3145736 | tf_op jit(solution)/shard_map/ppermute | solution.py:452
  502.1 19.4 %collective-permute-start.81 = (f32[1024,128]{1,0:T(8,128)S(1)}, f32[1024,128]{1,0:T(8,128)S(1)}, u32[]{:S(2)}, u32[]{:S(2)}) collective-permute-start(f32[1024,128]{1,0:T(8,128)S(1)} %convolution_add_fusion.6), channel_id=1, source_target_pairs={{0,2},{2,0},{1,3},{3,1},{4,6},{6,4},{5,7},{7,5},{8,10},{10,8},{9,1... | collective-permute-start | bytes 1572872 | tf_op jit(solution)/shard_map/ppermute | solution.py:456
  518.6 11.6 %collective-permute-start.39 = (bf16[512,1024]{1,0:T(8,128)(2,1)S(1)}, bf16[512,1024]{1,0:T(8,128)(2,1)S(1)}, u32[]{:S(2)}, u32[]{:S(2)}) collective-permute-start(bf16[512,1024]{1,0:T(8,128)(2,1)S(1)} %fusion.71), channel_id=1, source_target_pairs={{0,2},{2,0},{1,3},{3,1},{4,6},{6,4},{5,7},{7,5},{8,10},{10,8},{9,1... | collective-permute-start | bytes 3145736 | tf_op jit(solution)/shard_map/ppermute | solution.py:456
  521.6 15.4 %collective-permute-start.82 = (f32[1024,128]{1,0:T(8,128)S(1)}, f32[1024,128]{1,0:T(8,128)S(1)}, u32[]{:S(2)}, u32[]{:S(2)}) collective-permute-start(f32[1024,128]{1,0:T(8,128)S(1)} %add.762), channel_id=1, source_target_pairs={{0,4},{4,0},{1,5},{5,1},{2,6},{6,2},{3,7},{7,3},{8,12},{12,8},{9,1... | collective-permute-start | bytes 1572872 | tf_op jit(solution)/shard_map/ppermute | solution.py:456
  526.8 15.2 %collective-permute-start.74 = (bf16[128,2048]{1,0:T(8,128)(2,1)}, bf16[128,2048]{1,0:T(8,128)(2,1)}, u32[]{:S(2)}, u32[]{:S(2)}) collective-permute-start(bf16[128,2048]{1,0:T(8,128)(2,1)} %get-tuple-element.254), channel_id=1, source_target_pairs={{0,8},{8,16},{16,24},{24,0},{1,9},{9,17},{17,25},{25,1},{2,10},{10... | collective-permute-start | bytes 1572872 | tf_op jit(solution)/shard_map/ppermute | solution.py:460
  527.8 24.8 %collective-permute-start.76 = (bf16[128,2048]{1,0:T(8,128)(2,1)}, bf16[128,2048]{1,0:T(8,128)(2,1)}, u32[]{:S(2)}, u32[]{:S(2)}) collective-permute-start(bf16[128,2048]{1,0:T(8,128)(2,1)} %get-tuple-element.255), channel_id=1, source_target_pairs={{8,0},{16,8},{24,16},{0,24},{9,1},{17,9},{25,17},{1,25},{10,2},{18... | collective-permute-start | bytes 1572872 | tf_op jit(solution)/shard_map/ppermute | solution.py:464
  536.9 20.1 %collective-permute-start.35 = (f32[16,4]{1,0:T(8,128)S(1)}, f32[16,4]{1,0:T(8,128)S(1)}, u32[]{:S(2)}, u32[]{:S(2)}) collective-permute-start(f32[16,4]{1,0:T(8,128)S(1)} %reshape.1019), channel_id=1, source_target_pairs={{0,2},{2,0},{1,3},{3,1},{4,6},{6,4},{5,7},{7,5},{8,10},{10,8},{9,1... | collective-permute-start | bytes 776 | tf_op jit(solution)/shard_map/ppermute | solution.py:456
  537.1 20.5 %collective-permute-start.83 = (f32[1024,128]{1,0:T(8,128)S(1)}, f32[1024,128]{1,0:T(8,128)S(1)}, u32[]{:S(2)}, u32[]{:S(2)}) collective-permute-start(f32[1024,128]{1,0:T(8,128)S(1)} %add.763), channel_id=1, source_target_pairs={{0,1},{1,0},{2,3},{3,2},{4,5},{5,4},{6,7},{7,6},{8,9},{9,8},{10,11... | collective-permute-start | bytes 1572872 | tf_op jit(solution)/shard_map/ppermute | solution.py:456
  545.6 68.3 %collective-permute-start.75 = (bf16[256,2048]{1,0:T(8,128)(2,1)S(1)}, bf16[256,2048]{1,0:T(8,128)(2,1)S(1)}, u32[]{:S(2)}, u32[]{:S(2)}) collective-permute-start(bf16[256,2048]{1,0:T(8,128)(2,1)S(1)} %fusion.42), channel_id=1, source_target_pairs={{0,8},{8,16},{16,24},{24,0},{1,9},{9,17},{17,25},{25,1},{2,10},{10... | collective-permute-start | bytes 3145736 | tf_op jit(solution)/shard_map/ppermute | solution.py:460
  555.0 58.9 %collective-permute-start.77 = (bf16[256,2048]{1,0:T(8,128)(2,1)S(1)}, bf16[256,2048]{1,0:T(8,128)(2,1)S(1)}, u32[]{:S(2)}, u32[]{:S(2)}) collective-permute-start(bf16[256,2048]{1,0:T(8,128)(2,1)S(1)} %fusion.43), channel_id=1, source_target_pairs={{8,0},{16,8},{24,16},{0,24},{9,1},{17,9},{25,17},{1,25},{10,2},{18... | collective-permute-start | bytes 3145736 | tf_op jit(solution)/shard_map/ppermute | solution.py:464
  556.9 42.6 %collective-permute-start.65 = (f32[6,1024]{1,0:T(8,128)S(1)}, f32[6,1024]{1,0:T(8,128)S(1)}, u32[]{:S(2)}, u32[]{:S(2)}) collective-permute-start(f32[6,1024]{1,0:T(8,128)S(1)} %add.731), channel_id=1, source_target_pairs={{0,8},{8,0},{16,24},{24,16},{1,9},{9,1},{17,25},{25,17},{2,10},{10... | collective-permute-start | bytes 73736 | tf_op jit(solution)/shard_map/ppermute | solution.py:546
  557.6 53.7 %collective-permute-start.84 = (f32[1024,128]{1,0:T(8,128)S(1)}, f32[1024,128]{1,0:T(8,128)S(1)}, u32[]{:S(2)}, u32[]{:S(2)}) collective-permute-start(f32[1024,128]{1,0:T(8,128)S(1)} %add.764), channel_id=1, source_target_pairs={{0,8},{8,0},{16,24},{24,16},{1,9},{9,1},{17,25},{25,17},{2,10},{10... | collective-permute-start | bytes 1572872 | tf_op jit(solution)/shard_map/ppermute | solution.py:546
  599.5 12.2 %collective-permute-start.66 = (f32[6,1024]{1,0:T(8,128)S(1)}, f32[6,1024]{1,0:T(8,128)S(1)}, u32[]{:S(2)}, u32[]{:S(2)}) collective-permute-start(f32[6,1024]{1,0:T(8,128)S(1)} %add.732), channel_id=1, source_target_pairs={{0,24},{24,0},{8,16},{16,8},{1,25},{25,1},{9,17},{17,9},{2,26},{26... | collective-permute-start | bytes 73736 | tf_op jit(solution)/shard_map/ppermute | solution.py:548
  603.8 175.1 %collective-permute-start.67 = (bf16[512,2048]{1,0:T(8,128)(2,1)}, bf16[512,2048]{1,0:T(8,128)(2,1)}, u32[]{:S(2)}, u32[]{:S(2)}) collective-permute-start(bf16[512,2048]{1,0:T(8,128)(2,1)} %convolution_convert_fusion), channel_id=1, source_target_pairs={{0,4},{4,0},{1,5},{5,1},{2,6},{6,2},{3,7},{7,3},{8,12},{12,8},{9,1... | collective-permute-start | bytes 6291464 | tf_op jit(solution)/shard_map/ppermute | solution.py:456
  611.2 16.5 %collective-permute-start.40 = (bf16[512,1024]{1,0:T(8,128)(2,1)S(1)}, bf16[512,1024]{1,0:T(8,128)(2,1)S(1)}, u32[]{:S(2)}, u32[]{:S(2)}) collective-permute-start(bf16[512,1024]{1,0:T(8,128)(2,1)S(1)} %get-tuple-element.228), channel_id=1, source_target_pairs={{0,2},{2,0},{1,3},{3,1},{4,6},{6,4},{5,7},{7,5},{8,10},{10,8},{9,1... | collective-permute-start | bytes 3145736 | tf_op jit(solution)/shard_map/ppermute | solution.py:456
  611.7 15.2 %collective-permute-start.85 = (f32[1024,128]{1,0:T(8,128)S(1)}, f32[1024,128]{1,0:T(8,128)S(1)}, u32[]{:S(2)}, u32[]{:S(2)}) collective-permute-start(f32[1024,128]{1,0:T(8,128)S(1)} %add.765), channel_id=1, source_target_pairs={{0,24},{24,0},{8,16},{16,8},{1,25},{25,1},{9,17},{17,9},{2,26},{26... | collective-permute-start | bytes 1572872 | tf_op jit(solution)/shard_map/ppermute | solution.py:548
  618.4 168.2 %collective-permute-start.78 = (bf16[2,64,2048]{2,1,0:T(8,128)(2,1)}, bf16[2,64,2048]{2,1,0:T(8,128)(2,1)}, u32[]{:S(2)}, u32[]{:S(2)}) collective-permute-start(bf16[2,64,2048]{2,1,0:T(8,128)(2,1)} %fusion.108), channel_id=1, source_target_pairs={{0,1},{1,0},{2,3},{3,2},{4,5},{5,4},{6,7},{7,6},{8,9},{9,8},{10,11... | collective-permute-start | bytes 1572872 | tf_op jit(solution)/shard_map/ppermute | solution.py:456
  632.3 175.2 %collective-permute-start.55 = (bf16[128,512]{1,0:T(8,128)(2,1)}, bf16[128,512]{1,0:T(8,128)(2,1)}, u32[]{:S(2)}, u32[]{:S(2)}) collective-permute-start(bf16[128,512]{1,0:T(8,128)(2,1)} %get-tuple-element.263), channel_id=1, source_target_pairs={{0,8},{8,16},{16,24},{24,0},{1,9},{9,17},{17,25},{25,1},{2,10},{10... | collective-permute-start | bytes 393224 | tf_op jit(solution)/shard_map/ppermute | solution.py:460
  641.4 168.1 %collective-permute-start.57 = (bf16[128,512]{1,0:T(8,128)(2,1)}, bf16[128,512]{1,0:T(8,128)(2,1)}, u32[]{:S(2)}, u32[]{:S(2)}) collective-permute-start(bf16[128,512]{1,0:T(8,128)(2,1)} %get-tuple-element.264), channel_id=1, source_target_pairs={{8,0},{16,8},{24,16},{0,24},{9,1},{17,9},{25,17},{1,25},{10,2},{18... | collective-permute-start | bytes 393224 | tf_op jit(solution)/shard_map/ppermute | solution.py:464
  777.4 52.1 %collective-permute-start.43 = (bf16[128,1536]{1,0:T(8,128)(2,1)}, bf16[128,1536]{1,0:T(8,128)(2,1)}, u32[]{:S(2)}, u32[]{:S(2)}) collective-permute-start(bf16[128,1536]{1,0:T(8,128)(2,1)} %get-tuple-element.256), channel_id=1, source_target_pairs={{0,8},{8,16},{16,24},{24,0},{1,9},{9,17},{17,25},{25,1},{2,10},{10... | collective-permute-start | bytes 1179656 | tf_op jit(solution)/shard_map/ppermute | solution.py:460
  784.7 47.1 %collective-permute-start.45 = (bf16[128,1536]{1,0:T(8,128)(2,1)}, bf16[128,1536]{1,0:T(8,128)(2,1)}, u32[]{:S(2)}, u32[]{:S(2)}) collective-permute-start(bf16[128,1536]{1,0:T(8,128)(2,1)} %get-tuple-element.257), channel_id=1, source_target_pairs={{8,0},{16,8},{24,16},{0,24},{9,1},{17,9},{25,17},{1,25},{10,2},{18... | collective-permute-start | bytes 1179656 | tf_op jit(solution)/shard_map/ppermute | solution.py:464
  786.6 12.1 %collective-permute-start.52 = (f32[24,128]{1,0:T(8,128)S(1)}, f32[24,128]{1,0:T(8,128)S(1)}, u32[]{:S(2)}, u32[]{:S(2)}) collective-permute-start(f32[24,128]{1,0:T(8,128)S(1)} %fusion.274), channel_id=1, source_target_pairs={{0,8},{8,0},{16,24},{24,16},{1,9},{9,1},{17,25},{25,17},{2,10},{10... | collective-permute-start | bytes 36872 | tf_op jit(solution)/shard_map/ppermute | solution.py:546
  806.0 66.8 %collective-permute-start.41 = (bf16[512,1024]{1,0:T(8,128)(2,1)}, bf16[512,1024]{1,0:T(8,128)(2,1)}, u32[]{:S(2)}, u32[]{:S(2)}) collective-permute-start(bf16[512,1024]{1,0:T(8,128)(2,1)} %fusion.65), channel_id=1, source_target_pairs={{0,2},{2,0},{1,3},{3,1},{4,6},{6,4},{5,7},{7,5},{8,10},{10,8},{9,1... | collective-permute-start | bytes 3145736 | tf_op jit(solution)/shard_map/ppermute | solution.py:456
  818.8 38.7 %collective-permute-start.68 = (bf16[4,64,2048]{2,1,0:T(8,128)(2,1)S(1)}, bf16[4,64,2048]{2,1,0:T(8,128)(2,1)S(1)}, u32[]{:S(2)}, u32[]{:S(2)}) collective-permute-start(bf16[4,64,2048]{2,1,0:T(8,128)(2,1)S(1)} %copy-done.69), channel_id=1, source_target_pairs={{0,1},{1,0},{2,3},{3,2},{4,5},{5,4},{6,7},{7,6},{8,9},{9,8},{10,11... | collective-permute-start | bytes 3145736 | tf_op jit(solution)/shard_map/ppermute | solution.py:456
  825.1 23.9 %collective-permute-start.80 = (bf16[64,2048]{1,0:T(8,128)(2,1)S(1)}, bf16[64,2048]{1,0:T(8,128)(2,1)S(1)}, u32[]{:S(2)}, u32[]{:S(2)}) collective-permute-start(bf16[64,2048]{1,0:T(8,128)(2,1)S(1)} %fusion.117), channel_id=1, source_target_pairs={{0,0},{1,2},{2,1},{3,3},{4,4},{5,6},{6,5},{7,7},{8,8},{9,10},{10,9... | collective-permute-start | bytes 786440 | tf_op jit(solution)/shard_map/ppermute | solution.py:452
  829.5 19.4 %collective-permute-start.59 = (bf16[2,64,512]{2,1,0:T(8,128)(2,1)S(1)}, bf16[2,64,512]{2,1,0:T(8,128)(2,1)S(1)}, u32[]{:S(2)}, u32[]{:S(2)}) collective-permute-start(bf16[2,64,512]{2,1,0:T(8,128)(2,1)S(1)} %fusion.158), channel_id=1, source_target_pairs={{0,1},{1,0},{2,3},{3,2},{4,5},{5,4},{6,7},{7,6},{8,9},{9,8},{10,11... | collective-permute-start | bytes 393224 | tf_op jit(solution)/shard_map/ppermute | solution.py:456
  831.7 28.1 %collective-permute-start.44 = (bf16[256,1536]{1,0:T(8,128)(2,1)S(1)}, bf16[256,1536]{1,0:T(8,128)(2,1)S(1)}, u32[]{:S(2)}, u32[]{:S(2)}) collective-permute-start(bf16[256,1536]{1,0:T(8,128)(2,1)S(1)} %fusion.40), channel_id=1, source_target_pairs={{0,8},{8,16},{16,24},{24,0},{1,9},{9,17},{17,25},{25,1},{2,10},{10... | collective-permute-start | bytes 2359304 | tf_op jit(solution)/shard_map/ppermute | solution.py:460
  848.9 21.7 %collective-permute-start.46 = (bf16[256,1536]{1,0:T(8,128)(2,1)S(1)}, bf16[256,1536]{1,0:T(8,128)(2,1)S(1)}, u32[]{:S(2)}, u32[]{:S(2)}) collective-permute-start(bf16[256,1536]{1,0:T(8,128)(2,1)S(1)} %fusion.41), channel_id=1, source_target_pairs={{8,0},{16,8},{24,16},{0,24},{9,1},{17,9},{25,17},{1,25},{10,2},{18... | collective-permute-start | bytes 2359304 | tf_op jit(solution)/shard_map/ppermute | solution.py:464
  852.5 47.4 %collective-permute-start.61 = (bf16[64,512]{1,0:T(8,128)(2,1)S(1)}, bf16[64,512]{1,0:T(8,128)(2,1)S(1)}, u32[]{:S(2)}, u32[]{:S(2)}) collective-permute-start(bf16[64,512]{1,0:T(8,128)(2,1)S(1)} %fusion.159), channel_id=1, source_target_pairs={{0,0},{1,2},{2,1},{3,3},{4,4},{5,6},{6,5},{7,7},{8,8},{9,10},{10,9... | collective-permute-start | bytes 196616 | tf_op jit(solution)/shard_map/ppermute | solution.py:452
  858.0 23.1 %collective-permute-start.69 = (bf16[32,2048]{1,0:T(8,128)(2,1)S(1)}, bf16[32,2048]{1,0:T(8,128)(2,1)S(1)}, u32[]{:S(2)}, u32[]{:S(2)}) collective-permute-start(bf16[32,2048]{1,0:T(8,128)(2,1)S(1)} %get-tuple-element.261), channel_id=1, source_target_pairs={{0,8},{8,16},{16,24},{24,0},{1,9},{9,17},{17,25},{25,1},{2,10},{10... | collective-permute-start | bytes 393224 | tf_op jit(solution)/shard_map/ppermute | solution.py:460
  859.8 21.3 %collective-permute-start.71 = (bf16[32,2048]{1,0:T(8,128)(2,1)S(1)}, bf16[32,2048]{1,0:T(8,128)(2,1)S(1)}, u32[]{:S(2)}, u32[]{:S(2)}) collective-permute-start(bf16[32,2048]{1,0:T(8,128)(2,1)S(1)} %get-tuple-element.262), channel_id=1, source_target_pairs={{8,0},{16,8},{24,16},{0,24},{9,1},{17,9},{25,17},{1,25},{10,2},{18... | collective-permute-start | bytes 393224 | tf_op jit(solution)/shard_map/ppermute | solution.py:464
  871.8 12.7 %collective-permute-start.47 = (bf16[2,64,1536]{2,1,0:T(8,128)(2,1)S(1)}, bf16[2,64,1536]{2,1,0:T(8,128)(2,1)S(1)}, u32[]{:S(2)}, u32[]{:S(2)}) collective-permute-start(bf16[2,64,1536]{2,1,0:T(8,128)(2,1)S(1)} %fusion.132), channel_id=1, source_target_pairs={{0,1},{1,0},{2,3},{3,2},{4,5},{5,4},{6,7},{7,6},{8,9},{9,8},{10,11... | collective-permute-start | bytes 1179656 | tf_op jit(solution)/shard_map/ppermute | solution.py:456
  875.9 29.0 %collective-permute-start.42 = (bf16[512,1024]{1,0:T(8,128)(2,1)S(1)}, bf16[512,1024]{1,0:T(8,128)(2,1)S(1)}, u32[]{:S(2)}, u32[]{:S(2)}) collective-permute-start(bf16[512,1024]{1,0:T(8,128)(2,1)S(1)} %add_convert_fusion.1), channel_id=1, source_target_pairs={{0,0},{1,2},{2,1},{3,3},{4,4},{5,6},{6,5},{7,7},{8,8},{9,10},{10,9... | collective-permute-start | bytes 3145736 | tf_op jit(solution)/shard_map/ppermute | solution.py:452
  881.3 12.9 %collective-permute-start.72 = (bf16[64,2048]{1,0:T(8,128)(2,1)S(1)}, bf16[64,2048]{1,0:T(8,128)(2,1)S(1)}, u32[]{:S(2)}, u32[]{:S(2)}) collective-permute-start(bf16[64,2048]{1,0:T(8,128)(2,1)S(1)} %get-tuple-element.243), channel_id=1, source_target_pairs={{8,0},{16,8},{24,16},{0,24},{9,1},{17,9},{25,17},{1,25},{10,2},{18... | collective-permute-start | bytes 786440 | tf_op jit(solution)/shard_map/ppermute | solution.py:464
  884.6 11.5 %collective-permute-start.48 = (bf16[64,1536]{1,0:T(8,128)(2,1)S(1)}, bf16[64,1536]{1,0:T(8,128)(2,1)S(1)}, u32[]{:S(2)}, u32[]{:S(2)}) collective-permute-start(bf16[64,1536]{1,0:T(8,128)(2,1)S(1)} %fusion.145), channel_id=1, source_target_pairs={{0,4},{4,0},{1,5},{5,1},{2,6},{6,2},{3,7},{7,3},{8,12},{12,8},{9,1... | collective-permute-start | bytes 589832 | tf_op jit(solution)/shard_map/ppermute | solution.py:456
  (168 other events, 2385.0 us)

commit v2 on v1

--- a/solution.py
+++ b/solution.py
@@ -494,6 +494,18 @@
     return value.reshape(-1, value.shape[-1])
 
 
+def gather_split(value, z, x, y):
+    value = gather_z(value, z)
+    half = value.shape[-1] // 2
+    parts = []
+    for part, order in ((value[..., :half], "xy"), (value[..., half:], "yx")):
+        for step, axis in enumerate(order):
+            place = 1 if axis == "x" or step == 0 else 2
+            part = pair_up(part, swap(part, axis), {"x": x, "y": y}[axis], place)
+        parts.append(part.reshape(-1, half))
+    return parts
+
+
 def sum_pair(blocks, axis_name, own_index, axis):
     theirs = lax.dynamic_index_in_dim(blocks, 1 - own_index, axis, keepdims=False)
     mine = lax.dynamic_index_in_dim(blocks, own_index, axis, keepdims=False)
@@ -540,19 +552,424 @@
     return turn(own.astype(BF)).astype(F32)
 
 
+def sum_other(value, step):
+    if step == "0":
+        return lax.ppermute(value, "z", [(0, 1), (1, 0), (2, 3), (3, 2)])
+    if step == "1":
+        return lax.ppermute(value, "z", [(0, 3), (3, 0), (1, 2), (2, 1)])
+    return swap(value, step)
+
+
 def sum_chips(value, steps):
     for step in steps:
-        if step == "0":
-            value = value + lax.ppermute(value, "z", [(0, 1), (1, 0), (2, 3), (3, 2)])
-        elif step == "1":
-            value = value + lax.ppermute(value, "z", [(0, 3), (3, 0), (1, 2), (2, 1)])
-        else:
-            value = value + swap(value, step)
+        value = value + sum_other(value, step)
     return value
+
+
+def tile_bounds(row_lengths, token_count):
+    ends = jnp.cumsum(row_lengths)
+    span = NQ_ROW * QLEN
+    first = jnp.arange(token_count // TILE, dtype=jnp.int32) * TILE - span
+    last = first + TILE - 1
+    begin = jnp.max(jnp.where(ends[None, :] <= first[:, None], ends[None, :], 0), axis=1)
+    end = jnp.min(jnp.where(ends[None, :] > last[:, None], ends[None, :], token_count), axis=1)
+    low = jnp.where(first < 0, 0, (begin + span) // TILE)
+    high = jnp.where(first < 0, 1, (end + span + TILE - 1) // TILE)
+    return jnp.stack([low, high]).astype(jnp.int32)
 
 
 def rows_of(value, start, count):
     return lax.dynamic_slice_in_dim(value, start, count, 0)
+
+
+TILE = 256
+NEG = -1e30
+
+
+def exact(left, right, dims):
+    return lax.dot_general(left, right, (dims, ((), ())), preferred_element_type=F32)
+
+
+def head_masks(value):
+    lane = lax.broadcasted_iota(jnp.int32, value.shape, 1)
+    zero = jnp.zeros_like(value)
+    return (jnp.where(lane < HEAD_DIM, value, zero), jnp.where(lane < HEAD_DIM, zero, value))
+
+
+def fill_bias(seg_col, seg_row, bias):
+    for start in range(0, bias.shape[0], TILE):
+        rows = slice(start, start + TILE)
+        bias[rows, :] = jnp.where(seg_col[rows, :] == seg_row[...], 0.0, NEG)
+
+
+def attend_kernel(bounds, q_ref, k_ref, v_ref, seg_col, seg_row, out_ref, lse_ref, bias, held):
+    @pl.when(pl.program_id(0) == 0)
+    def _():
+        fill_bias(seg_col, seg_row, bias)
+
+    for block in range(q_ref.shape[0] // TILE):
+        own = slice(block * TILE, (block + 1) * TILE)
+        queries = head_masks(q_ref[own, :] * HEAD_DIM**-0.5)
+
+        def score(step, highest):
+            rows = pl.ds(pl.multiple_of(step * TILE, TILE), TILE)
+            keys, shift = k_ref[rows, :], bias[rows, own]
+            fresh = []
+            for head in range(2):
+                scores = exact(keys, queries[head], ((1,), (1,))) + shift
+                held[head, rows, :] = scores
+                fresh.append(jnp.maximum(highest[head], jnp.max(scores, axis=0, keepdims=True)))
+            return tuple(fresh)
+
+        low = jnp.full((1, TILE), NEG, F32)
+        highest = lax.fori_loop(bounds[0, block], bounds[1, block], score, (low, low))
+
+        def mix(step, carried):
+            rows = pl.ds(pl.multiple_of(step * TILE, TILE), TILE)
+            values = v_ref[rows, :]
+            fresh = []
+            for head in range(2):
+                total, mixed = carried[head]
+                expo = jnp.exp(held[head, rows, :] - highest[head])
+                fresh.append(
+                    (
+                        total + jnp.sum(expo, axis=0, keepdims=True),
+                        mixed + exact(values, expo.astype(BF), ((0,), (0,))),
+                    )
+                )
+            return tuple(fresh)
+
+        start = (jnp.zeros((1, TILE), F32), jnp.zeros((2 * HEAD_DIM, TILE), F32))
+        parts = lax.fori_loop(bounds[0, block], bounds[1, block], mix, (start, start))
+        mixed = jnp.concatenate(
+            [parts[0][1][:HEAD_DIM] / parts[0][0], parts[1][1][HEAD_DIM:] / parts[1][0]], axis=0
+        )
+        out_ref[own, :] = jnp.transpose(mixed).astype(BF)
+        for head in range(2):
+            lse_ref[0, head : head + 1, own] = highest[head] + jnp.log(parts[head][0])
+
+
+def attend(bounds, qkv, seg_col, seg_row):
+    count, wide = qkv.shape
+    pairs = wide // 3 // 128
+    column = lambda shift: pl.BlockSpec((count, 128), lambda i: (0, shift + i))
+    whole = lambda shape: pl.BlockSpec(shape, lambda i: (0, 0))
+    return pl.pallas_call(
+        attend_kernel,
+        grid=(pairs,),
+        in_specs=[
+            pl.BlockSpec(memory_space=pltpu.SMEM),
+            column(0),
+            column(pairs),
+            column(2 * pairs),
+            whole((count, 1)),
+            whole((1, count)),
+        ],
+        out_specs=[column(0), pl.BlockSpec((1, 8, count), lambda i: (i, 0, 0))],
+        out_shape=[
+            jax.ShapeDtypeStruct((count, wide // 3), BF),
+            jax.ShapeDtypeStruct((pairs, 8, count), F32),
+        ],
+        scratch_shapes=[pltpu.VMEM((count, count), F32), pltpu.VMEM((2, count, TILE), F32)],
+        compiler_params=pltpu.CompilerParams(vmem_limit_bytes=40 << 20),
+        cost_estimate=pl.CostEstimate(
+            flops=4 * pairs * count * count * 128,
+            transcendentals=pairs * count * count,
+            bytes_accessed=4 * count * wide * 2,
+        ),
+    )(bounds, qkv, qkv, qkv, seg_col, seg_row)
+
+
+def attend_back_kernel(
+    bounds, q_ref, k_ref, v_ref, out_ref, grad_ref, lse_ref, seg_col, seg_row,
+    grads_ref, sums_ref, bias, key_sum, value_sum,
+):
+    pair = pl.program_id(0)
+
+    @pl.when(pair == 0)
+    def _():
+        fill_bias(seg_col, seg_row, bias)
+
+    key_sum[...] = jnp.zeros_like(key_sum)
+    value_sum[...] = jnp.zeros_like(value_sum)
+    columns = [
+        pl.ds(pl.multiple_of(part * (grads_ref.shape[1] // 3) + pair * 128, 128), 128) for part in range(3)
+    ]
+    query_total = jnp.zeros((1, 128), F32)
+    picks = head_masks(jnp.ones((8, 128), BF))
+    for block in range(q_ref.shape[0] // TILE):
+        own = slice(block * TILE, (block + 1) * TILE)
+        queries = head_masks(q_ref[own, :] * HEAD_DIM**-0.5)
+        grads = head_masks(grad_ref[own, :])
+        product = grad_ref[own, :].astype(F32) * out_ref[own, :].astype(F32)
+        product_high = product.astype(BF)
+        product_low = (product - product_high.astype(F32)).astype(BF)
+        inner = [
+            (
+                exact(picks[head], product_high, ((1,), (1,)))
+                + exact(picks[head], product_low, ((1,), (1,)))
+            )[0:1]
+            for head in range(2)
+        ]
+        lse = [lse_ref[0, head : head + 1, own] for head in range(2)]
+
+        def step_of(step, carried):
+            rows = pl.ds(pl.multiple_of(step * TILE, TILE), TILE)
+            keys, values, shift = k_ref[rows, :], v_ref[rows, :], bias[rows, own]
+            fresh = []
+            key_add = jnp.zeros((TILE, 128), F32)
+            value_add = jnp.zeros((TILE, 128), F32)
+            for head in range(2):
+                scores = exact(keys, queries[head], ((1,), (1,))) + shift
+                probs = jnp.exp(scores - lse[head])
+                grad_probs = exact(values, grads[head], ((1,), (1,)))
+                grad_scores = (probs * (grad_probs - inner[head])).astype(BF)
+                value_add = value_add + exact(probs.astype(BF), grads[head], ((1,), (0,)))
+                key_add = key_add + exact(grad_scores, queries[head], ((1,), (0,)))
+                fresh.append(carried[head] + exact(keys, grad_scores, ((0,), (0,))))
+            key_sum[rows, :] += key_add
+            value_sum[rows, :] += value_add
+            return tuple(fresh)
+
+        start = jnp.zeros((2 * HEAD_DIM, TILE), F32)
+        parts = lax.fori_loop(bounds[0, block], bounds[1, block], step_of, (start, start))
+        grad_query = jnp.concatenate([parts[0][:HEAD_DIM], parts[1][HEAD_DIM:]], axis=0)
+        grad_query = jnp.transpose(grad_query * HEAD_DIM**-0.5).astype(BF)
+        grads_ref[own, columns[0]] = grad_query
+        query_total = query_total + jnp.sum(grad_query.astype(F32), axis=0, keepdims=True)
+    grad_value = value_sum[...].astype(BF)
+    grads_ref[:, columns[1]] = key_sum[...].astype(BF)
+    grads_ref[:, columns[2]] = grad_value
+    sums_ref[0, 0:1, :] = query_total
+    sums_ref[0, 1:2, :] = jnp.sum(grad_value.astype(F32), axis=0, keepdims=True)
+
+
+def attend_back(bounds, qkv, mixed, grad_mixed, lse, seg_col, seg_row):
+    count, wide = qkv.shape
+    pairs = wide // 3 // 128
+    column = lambda shift: pl.BlockSpec((count, 128), lambda i: (0, shift + i))
+    whole = lambda shape: pl.BlockSpec(shape, lambda i: (0, 0))
+    return pl.pallas_call(
+        attend_back_kernel,
+        grid=(pairs,),
+        in_specs=[
+            pl.BlockSpec(memory_space=pltpu.SMEM),
+            column(0),
+            column(pairs),
+            column(2 * pairs),
+            column(0),
+            column(0),
+            pl.BlockSpec((1, 8, count), lambda i: (i, 0, 0)),
+            whole((count, 1)),
+            whole((1, count)),
+        ],
+        out_specs=[whole((count, wide)), pl.BlockSpec((1, 8, 128), lambda i: (i, 0, 0))],
+        out_shape=[
+            jax.ShapeDtypeStruct((count, wide), BF),
+            jax.ShapeDtypeStruct((pairs, 8, 128), F32),
+        ],
+        scratch_shapes=[
+            pltpu.VMEM((count, count), F32),
+            pltpu.VMEM((count, 128), F32),
+            pltpu.VMEM((count, 128), F32),
+        ],
+        compiler_params=pltpu.CompilerParams(vmem_limit_bytes=40 << 20),
+        cost_estimate=pl.CostEstimate(
+            flops=10 * pairs * count * count * 128,
+            transcendentals=pairs * count * count,
+            bytes_accessed=8 * count * wide * 2,
+        ),
+    )(bounds, qkv, qkv, qkv, mixed, grad_mixed, lse, seg_col, seg_row)
+
+
+ERFC = (
+    -1.26551223, 1.00002368, 0.37409196, 0.09678418, -0.18628806,
+    0.27886807, -1.13520398, 1.48851587, -0.82215223, 0.17087277,
+)
+
+
+def gelu_pair(value):
+    size = jnp.abs(value) * 0.5**0.5
+    ratio = 1.0 / (1.0 + 0.5 * size)
+    series = jnp.full_like(value, ERFC[-1])
+    for factor in ERFC[-2::-1]:
+        series = series * ratio + factor
+    bell = jnp.exp(-size * size)
+    tail = 0.5 * ratio * bell * jnp.exp(series)
+    phi = jnp.where(value < 0.0, tail, 1.0 - tail)
+    return (value * phi, phi + value * bell * 0.3989422804014327)
+
+
+def expand_kernel(x_ref, w_ref, b_ref, act_ref, slope_ref):
+    rows = 256
+    for start in range(0, x_ref.shape[0], rows):
+        part = slice(start, start + rows)
+        value = exact(x_ref[part, :], w_ref[...], ((1,), (0,))) + b_ref[...]
+        active, slope = gelu_pair(value)
+        act_ref[part, :] = active.astype(BF)
+        slope_ref[part, :] = slope.astype(BF)
+
+
+def expand(value, weight, shift):
+    count, depth = value.shape
+    width = weight.shape[1]
+    tile = 256
+    return pl.pallas_call(
+        expand_kernel,
+        grid=(width // tile,),
+        in_specs=[
+            pl.BlockSpec((count, depth), lambda i: (0, 0)),
+            pl.BlockSpec((depth, tile), lambda i: (0, i)),
+            pl.BlockSpec((1, tile), lambda i: (0, i)),
+        ],
+        out_specs=[pl.BlockSpec((count, tile), lambda i: (0, i))] * 2,
+        out_shape=[jax.ShapeDtypeStruct((count, width), BF)] * 2,
+        compiler_params=pltpu.CompilerParams(vmem_limit_bytes=32 << 20),
+        cost_estimate=pl.CostEstimate(
+            flops=2 * count * depth * width,
+            transcendentals=3 * count * width,
+            bytes_accessed=2 * (count * depth + depth * width + 2 * count * width),
+        ),
+    )(value, weight, shift)
+
+
+def cut_levels(raw, cuts):
+    lane = lax.broadcasted_iota(jnp.int32, raw.shape, 1)
+    levels = []
+    for cut in cuts:
+        part = jnp.where(lane < cut, raw, 0.0)
+        scale = lax.rsqrt(jnp.sum(part * part, axis=1, keepdims=True) + EPS_EMBED)
+        levels.append(((part * scale).astype(BF), part, scale))
+    return levels
+
+
+def pool_kernel(cuts, span, q_ref, d_ref, seg_ref, out_ref, units, hot):
+    @pl.when(pl.program_id(0) == 0)
+    def _():
+        raw = d_ref[span:, :].astype(F32)
+        for level, parts in enumerate(cut_levels(raw, cuts)):
+            units[level] = parts[0]
+        doc = lax.broadcasted_iota(jnp.int32, hot.shape, 0)
+        hot[...] = (seg_ref[:, span:] == NQ_ROW + doc).astype(F32).astype(BF)
+
+    levels = cut_levels(q_ref[...].astype(F32), cuts)
+    for level in range(len(cuts)):
+        similar = exact(units[level], levels[level][0], ((1,), (1,)))
+        expo = jnp.exp(similar * (1.0 / POOL_TEMP))
+        high = expo.astype(BF)
+        rest = (expo - high.astype(F32)).astype(BF)
+        out_ref[level * NDOC : (level + 1) * NDOC, :] = exact(
+            hot[...], high, ((1,), (0,))
+        ) + exact(hot[...], rest, ((1,), (0,)))
+
+
+def pool(cuts, span, queries, row_embed, seg_row):
+    count, width = queries.shape
+    tokens = row_embed.shape[0]
+    whole = lambda shape: pl.BlockSpec(shape, lambda i: (0, 0))
+    return pl.pallas_call(
+        partial(pool_kernel, cuts, span),
+        grid=(count // TILE,),
+        in_specs=[
+            pl.BlockSpec((TILE, width), lambda i: (i, 0)),
+            whole((tokens, width)),
+            whole((1, tokens)),
+        ],
+        out_specs=pl.BlockSpec((len(cuts) * NDOC, TILE), lambda i: (0, i)),
+        out_shape=jax.ShapeDtypeStruct((len(cuts) * NDOC, count), F32),
+        scratch_shapes=[
+            pltpu.VMEM((len(cuts), tokens - span, width), BF),
+            pltpu.VMEM((NDOC, tokens - span), BF),
+        ],
+        compiler_params=pltpu.CompilerParams(vmem_limit_bytes=32 << 20),
+        cost_estimate=pl.CostEstimate(
+            flops=2 * len(cuts) * count * tokens * 256,
+            transcendentals=len(cuts) * count * tokens,
+            bytes_accessed=2 * (count + tokens) * width,
+        ),
+    )(queries, row_embed, seg_row)
+
+
+def level_back(grad, part, scale):
+    return scale * grad - part * (scale * scale * scale) * jnp.sum(
+        part * grad, axis=1, keepdims=True
+    )
+
+
+def pool_back_kernel(
+    cuts, span, q_ref, d_ref, seg_ref, coef_ref, q_out, d_out, units, units_t, hot, sums
+):
+    step = pl.program_id(0)
+
+    @pl.when(step == 0)
+    def _():
+        raw = d_ref[span:, :].astype(F32)
+        for level, parts in enumerate(cut_levels(raw, cuts)):
+            units[level] = parts[0]
+            units_t[level] = jnp.transpose(parts[0])
+        doc = lax.broadcasted_iota(jnp.int32, hot.shape, 0)
+        wanted = NQ_ROW + jnp.where(doc < NDOC, doc, doc - NDOC)
+        hot[...] = (seg_ref[:, span:] == wanted).astype(F32).astype(BF)
+        sums[...] = jnp.zeros_like(sums)
+
+    levels = cut_levels(q_ref[...].astype(F32), cuts)
+    total = jnp.zeros(q_ref.shape, F32)
+    for level in range(len(cuts)):
+        unit, part, scale = levels[level]
+        similar = exact(units[level], unit, ((1,), (1,)))
+        coef = coef_ref[level * NDOC : (level + 1) * NDOC, :]
+        high = coef.astype(BF).astype(F32)
+        both = jnp.concatenate([high, coef - high], axis=0).astype(BF)
+        spread = exact(hot[...], both, ((0,), (0,)))
+        grad = (jnp.exp(similar * (1.0 / POOL_TEMP)) * spread).astype(BF)
+        sums[level] += exact(grad, unit, ((1,), (0,)))
+        grad_unit = jnp.transpose(exact(units_t[level], grad, ((1,), (0,))))
+        total = total + level_back(grad_unit, part, scale)
+    q_out[...] = total.astype(BF)
+
+    @pl.when(step == pl.num_programs(0) - 1)
+    def _():
+        raw = d_ref[span:, :].astype(F32)
+        result = jnp.zeros(raw.shape, F32)
+        for level, parts in enumerate(cut_levels(raw, cuts)):
+            lane = lax.broadcasted_iota(jnp.int32, raw.shape, 1)
+            grad = jnp.where(lane < cuts[level], sums[level], 0.0)
+            result = result + level_back(grad, parts[1], parts[2])
+        d_out[...] = result
+
+
+def pool_back(cuts, span, queries, row_embed, seg_row, coef):
+    count, width = queries.shape
+    tokens = row_embed.shape[0]
+    docs = tokens - span
+    whole = lambda shape: pl.BlockSpec(shape, lambda i: (0, 0))
+    return pl.pallas_call(
+        partial(pool_back_kernel, cuts, span),
+        grid=(count // TILE,),
+        in_specs=[
+            pl.BlockSpec((TILE, width), lambda i: (i, 0)),
+            whole((tokens, width)),
+            whole((1, tokens)),
+            pl.BlockSpec((len(cuts) * NDOC, TILE), lambda i: (0, i)),
+        ],
+        out_specs=[pl.BlockSpec((TILE, width), lambda i: (i, 0)), whole((docs, width))],
+        out_shape=[
+            jax.ShapeDtypeStruct((count, width), BF),
+            jax.ShapeDtypeStruct((docs, width), F32),
+        ],
+        scratch_shapes=[
+            pltpu.VMEM((len(cuts), docs, width), BF),
+            pltpu.VMEM((len(cuts), width, docs), BF),
+            pltpu.VMEM((2 * NDOC, docs), BF),
+            pltpu.VMEM((len(cuts), docs, width), F32),
+        ],
+        compiler_params=pltpu.CompilerParams(vmem_limit_bytes=32 << 20),
+        cost_estimate=pl.CostEstimate(
+            flops=2 * len(cuts) * count * docs * 512,
+            transcendentals=len(cuts) * count * docs,
+            bytes_accessed=4 * (count + tokens) * width,
+        ),
+    )(queries, row_embed, seg_row, coef)
 
 
 def local_chip(
@@ -579,31 +996,36 @@
     own_start, other_start = c * share, (1 - c) * share
     gains, shifts = ln_gain.astype(F32), ln_bias.astype(F32)
 
+    half_width = w_qkv.shape[2]
     qkv_rows = jnp.concatenate([w_qkv[0], w_qkv[1], w_qkv[2]], axis=1)
     full_qkv = gather_blocks(turn(qkv_rows), "xyz", z, x, y)
     row = jnp.where(c == y, tokens, swap(tokens, "c"))
-    bias = turn(jnp.concatenate([b_qv.reshape(-1), b_up])[None])[0].astype(F32)
-    full_out = gather_blocks(turn(w_out.T), "xyz", z, x, y)
-    full_up = gather_blocks(turn(w_up), "zyx", z, x, y)
+    bias = turn(jnp.concatenate([b_qv.reshape(-1), b_up])[None].astype(F32))
+    mid_rows = turn(jnp.concatenate([w_up, w_out.T], axis=1))
+    up_wide = w_up.shape[1]
+    full_mid = gather_blocks(mid_rows, "zyx", z, x, y)
+    full_up, full_out = full_mid[:, :up_wide], full_mid[:, up_wide:]
     full_down = gather_blocks(turn(w_down.T), "xyz", z, x, y)
     own_cot = turn(cot)
-    all_pairs = lax.all_gather(pairing, ("z", "x", "c", "y"), axis=0, tiled=False)
-
-    half_width = w_qkv.shape[2]
-    local_heads = half_width // HEAD_DIM
-    q_bias, v_bias, up_shift = (
-        bias[:half_width],
-        bias[half_width : 2 * half_width],
-        bias[2 * half_width :],
-    )
+    half_queries = NQ_ROW // 2
+    chip_count = lengths.shape[0]
+    query_total = chip_count * half_queries
+    pairs = lax.dynamic_update_slice_in_dim(
+        jnp.zeros((1, query_total), F32), turn(pairing).astype(F32), chip * half_queries, 1
+    )
+    pairs = sum_chips(pairs, "xy01").astype(jnp.int32)
+
     row_lengths = lax.dynamic_index_in_dim(lengths, chip, 0, keepdims=False)
     segments = segments_of(row_lengths, token_count)
-    projected = dot(row, full_qkv)
-    heads_shape = (token_count, local_heads, HEAD_DIM)
-    query_rows = (projected[:, :half_width] + q_bias).astype(BF).reshape(heads_shape)
-    key_rows = projected[:, half_width : 2 * half_width].astype(BF).reshape(heads_shape)
-    value_rows = (projected[:, 2 * half_width :] + v_bias).astype(BF).reshape(heads_shape)
-    mixed, log_totals = attend_forward(query_rows, key_rows, value_rows, segments, 512)
+    seg_col, seg_row = segments[:, None], segments[None, :]
+    query_span = NQ_ROW * QLEN
+    bounds = tile_bounds(row_lengths, token_count)
+    qkv_bias = jnp.concatenate(
+        [bias[:, :half_width], jnp.zeros_like(bias[:, :half_width]), bias[:, half_width : 2 * half_width]],
+        axis=1,
+    )
+    qkv = (dot(row, full_qkv) + qkv_bias).astype(BF)
+    mixed, lse = attend(bounds, qkv, seg_col, seg_row)
 
     def row_sum(left, weight_t, transposed):
         times = contract_cols if transposed else dot
@@ -620,8 +1042,7 @@
     )
     normed_low = normed.astype(BF)
     normed_all = jnp.concatenate([normed_low, swap(normed_low, "c")], axis=0)
-    up_value = dot(normed_all, full_up) + up_shift
-    activation = jax.nn.gelu(up_value, approximate=False).astype(BF)
+    activation, slope = expand(normed_all, full_up, bias[:, 2 * half_width :])
     ffn_sum = row_sum(
         lambda which: activation[which * share : (which + 1) * share], full_down, True
     )
@@ -638,73 +1059,52 @@
         jnp.concatenate([embed, other_embed], axis=0),
         jnp.concatenate([other_embed, embed], axis=0),
     )
-    query_span = NQ_ROW * QLEN
     half_span = query_span // 2
-    half_queries = NQ_ROW // 2
     own_queries = rows_of(row_embed, c * half_span, half_span)
     chips = ("z", "x", "y")
-    chip_count = lengths.shape[0]
     queries = lax.all_to_all(
         jnp.broadcast_to(own_queries[None], (chip_count,) + own_queries.shape), chips, 0, 0
     ).reshape(chip_count * half_span, -1)
     proj_width = w_proj.shape[1]
-    widths = (proj_width, 3 * proj_width // 4, proj_width // 2)
-    doc_raw = row_embed[query_span:].astype(F32)
-    query_raw = queries.astype(F32)
-    hot = (
-        segments[query_span:, None] == NQ_ROW + jnp.arange(NDOC, dtype=jnp.int32)[None, :]
+    cuts = (proj_width, 3 * proj_width // 4, proj_width // 2)
+    sums = pool(cuts, query_span, queries, row_embed, seg_row)
+    doc_sizes = jnp.tile(row_lengths.astype(F32), 3)[:, None]
+    group = (
+        jnp.arange(query_total * QLEN, dtype=jnp.int32)[:, None] // QLEN
+        == jnp.arange(query_total, dtype=jnp.int32)[None, :]
     ).astype(F32)
-    query_levels = [normalize_cut(query_raw, cut) for cut in widths]
-    doc_levels = [normalize_cut(doc_raw, cut) for cut in widths]
-    sums_list = []
-    for cut in range(3):
-        expo = jnp.exp(
-            contract_cols(query_levels[cut][0].astype(BF), doc_levels[cut][0].astype(BF))
-            / POOL_TEMP
+    pooled = POOL_TEMP * jnp.log(sums / doc_sizes)
+    logits = jnp.dot(pooled, group, precision=FULL_PRECISION) / LOSS_TEMP
+    logits = logits.reshape(3, NDOC, query_total)
+    doc_numbers = chip * NDOC + jnp.arange(NDOC, dtype=jnp.int32)
+    picked = (doc_numbers[:, None] == pairs).astype(F32)
+    own_high = jnp.max(logits, axis=1)
+    own_lse = own_high + jnp.log(jnp.sum(jnp.exp(logits - own_high[:, None]), axis=1))
+    own_target = jnp.sum(logits * picked, axis=1)
+    notes = jnp.pad(jnp.concatenate([own_lse, own_target], axis=1), ((0, 5), (0, 0)))
+    notes = lax.all_to_all(
+        jnp.broadcast_to(notes[None], (chip_count,) + notes.shape), chips, 0, 0
+    )
+    chip_lse = notes[:, :3, :query_total]
+    high = jnp.max(chip_lse, axis=0)
+    all_lse = high + jnp.log(jnp.sum(jnp.exp(chip_lse - high), axis=0))
+    target = jnp.sum(notes[:, :3, query_total:], axis=0)
+    losses = jnp.sum(all_lse - target, axis=0).reshape(chip_count, half_queries)
+    grad_logits = (jnp.exp(logits - all_lse[:, None]) - picked) / LOSS_TEMP
+    coefficient = (
+        lax.dot_general(
+            grad_logits.reshape(3 * NDOC, query_total),
+            group,
+            (((1,), (1,)), ((), ())),
+            precision=FULL_PRECISION,
         )
-        sums_list.append(jnp.dot(expo, hot, precision=FULL_PRECISION))
-    sums = jnp.stack(sums_list)
-    pooled = POOL_TEMP * jnp.log(sums / row_lengths.astype(F32))
-    query_total = chip_count * half_queries
-    own_logits = jnp.sum(pooled.reshape(3, query_total, QLEN, NDOC), axis=2) / LOSS_TEMP
-    chip_logits = lax.all_to_all(
-        jnp.broadcast_to(own_logits[None], (chip_count,) + own_logits.shape), chips, 0, 0
-    )
-    logits = jnp.transpose(chip_logits, (1, 2, 0, 3)).reshape(3, query_total, chip_count * NDOC)
-    pairs = lax.dynamic_index_in_dim(
-        all_pairs.reshape(chip_count, 2, half_queries), c, 1, keepdims=False
-    ).reshape(query_total)
-    picked = (
-        jnp.arange(chip_count * NDOC, dtype=jnp.int32)[None, :] == pairs[:, None]
-    ).astype(F32)
-    highest = jnp.max(logits, axis=2, keepdims=True)
-    shares = jnp.exp(logits - highest)
-    total = jnp.sum(shares, axis=2, keepdims=True)
-    losses = jnp.sum(
-        (highest + jnp.log(total))[:, :, 0] - jnp.sum(logits * picked, axis=2), axis=0
-    ).reshape(chip_count, half_queries)
+        / sums
+    )
     losses = jnp.where(c == y, losses, swap(losses, "c"))
     loss_out = rows_of(losses, 4 * z + 2 * x + c, 1)
-    grad_logits = (shares / total - picked) / LOSS_TEMP
-    own_grad = lax.dynamic_slice_in_dim(grad_logits, chip * NDOC, NDOC, 2)
-    coefficient = jnp.repeat(own_grad, QLEN, axis=1) / sums
-    query_grad = jnp.zeros((chip_count * half_span, proj_width), F32)
-    doc_grad = jnp.zeros((token_count - query_span, proj_width), F32)
-    for cut in range(3):
-        query_unit_f, query_part, query_scale = query_levels[cut]
-        doc_unit_f, doc_part, doc_scale = doc_levels[cut]
-        query_unit, doc_unit = query_unit_f.astype(BF), doc_unit_f.astype(BF)
-        expo = jnp.exp(contract_cols(query_unit, doc_unit) / POOL_TEMP)
-        spread = contract_cols(coefficient[cut], hot, FULL_PRECISION)
-        grad_sim = (expo * spread).astype(BF)
-        query_grad = query_grad + normalize_back(
-            dot(grad_sim, doc_unit), query_part, query_scale, proj_width
-        )
-        doc_grad = doc_grad + normalize_back(
-            contract_rows(grad_sim, query_unit), doc_part, doc_scale, proj_width
-        )
+    query_grad, doc_grad = pool_back(cuts, query_span, queries, row_embed, seg_row, coefficient)
     grad_blocks = lax.all_to_all(
-        query_grad.astype(BF).reshape(chip_count, half_span, proj_width), chips, 0, 0
+        query_grad.reshape(chip_count, half_span, proj_width), chips, 0, 0
     )
     own_query_grad = jnp.sum(grad_blocks.astype(F32), axis=0)
     row_grad = jnp.concatenate([jnp.zeros((query_span, proj_width), F32), doc_grad], axis=0)
@@ -729,9 +1129,7 @@
     down_bias = jnp.sum(grad_ffn.astype(F32), axis=0)
     grad_ffn_all = jnp.concatenate([grad_ffn, swap(grad_ffn, "c")], axis=0)
     down_part = weight_sum(grad_ffn_all, activation, "zyx", z, x, y)
-    grad_act = dot(grad_ffn_all, full_down)
-    _, gelu_pull = jax.vjp(partial(jax.nn.gelu, approximate=False), up_value)
-    grad_up = gelu_pull(grad_act)[0].astype(BF)
+    grad_up = (dot(grad_ffn_all, full_down) * slope.astype(F32)).astype(BF)
     up_bias = jnp.sum(grad_up.astype(F32), axis=0)
     up_part = weight_sum(normed_all, grad_up, "xyz", z, x, y)
     grad_normed = (
@@ -751,10 +1149,7 @@
     )
     out_part = weight_sum(grad_attn_all, mixed, "zyx", z, x, y)
     grad_mixed = dot(grad_attn_all, full_out).astype(BF)
-    grad_q, grad_k, grad_v = attend_backward(
-        query_rows, key_rows, value_rows, segments, log_totals, grad_mixed, 512
-    )
-    grads = jnp.concatenate([grad_q.astype(BF), grad_k.astype(BF), grad_v.astype(BF)], axis=1)
+    grads, grad_sums = attend_back(bounds, qkv, mixed, grad_mixed, lse, seg_col, seg_row)
     qkv_part = weight_sum(row, grads, "zyx", z, x, y)
     grad_input = turn(
         (
@@ -768,17 +1163,18 @@
     )
 
     half_sums = jnp.concatenate(
-        [
-            jnp.sum(grads[:, :half_width].astype(F32), axis=0),
-            jnp.sum(grads[:, 2 * half_width :].astype(F32), axis=0),
-            up_bias,
-        ]
+        [grad_sums[:, 0].reshape(-1), grad_sums[:, 1].reshape(-1), up_bias]
     ).reshape(-1, 128)
     half_sums = sum_chips(half_sums, "xy01")
     half_sums = jnp.where(c == y, half_sums, swap(half_sums, "c")).reshape(-1)
     shared = jnp.stack([gain_one, gain_two, shift_one, shift_two, out_bias, down_bias])
     shared = sum_chips(shared, "cxy01")
-    proj_sum = sum_chips(proj_grad, "cxy01")
+    proj_half = rows_of(proj_grad, own_start, share) + swap(
+        rows_of(proj_grad, other_start, share), "c"
+    )
+    for step in ("x", "y", "0", "1"):
+        proj_half = proj_half + sum_other(proj_half.astype(BF), step).astype(F32)
+    proj_sum = pair_up(proj_half, swap(proj_half, "c"), c, 0).reshape(width, -1)
     return (
         y_out,
         loss_out,

time: 916 us -> 680 us (0.74)
  matrix products: 246 us -> 70 us
  Pallas kernels: 0 us -> 89.5 us
  waiting for transfers between devices: 273 us -> 213 us
  blocking collectives: 68.3 us -> 9.33 us
  other arithmetic: 98.4 us -> 47.8 us
  starting transfers between devices: 140 us -> 190 us
  local copies, waits for them, and re-layouts: 69.2 us -> 44.3 us
    dot_general x17 -> x2, matrix products: 113 us -> 1.34 us  [the longest x1 0.73 us: local_chip(): lax.dot_general(grad_logits.reshape(3 * NDOC, query_total), group, (((1,)...]
    pallas_call x0 -> x5, Pallas kernels: none -> 89.5 us  [the longest x1 27 us: attend_back(): pl.pallas_call(attend_back_kernel, grid=(pairs,), in_specs=[pl.BlockSpec(...]
    all_gather x1 -> x0, blocking collectives: 68.3 us -> none  [local_chip(): lax.all_gather(pairing, ('z', 'x', 'c', 'y'), axis=0, tiled=False)]
    dot_general x8 -> x4, matrix products: 48.8 us -> 16.6 us  [dot(): return jnp.dot(left, right, preferred_element_type=F32)]
    ppermute x6 -> x8, waiting for transfers between devices: 67.4 us -> 38.8 us  [the longest x4 38.2 us: sum_other(): return lax.ppermute(value, 'z', [(0, 1), (1, 0), (2, 3), (3, 2)])]
    convert_element_type x11 -> x9, other arithmetic: 33.5 us -> 8.31 us  [the longest x4 4.31 us: local_chip(): proj_half = proj_half + sum_other(proj_half.astype(BF), step).astype(F32)]
    ppermute x36 -> x37, starting transfers between devices: 39.4 us -> 62.6 us  [swap(): return lax.ppermute(value, axis, SWAP)]
    dot_general x16 -> x10, matrix products: 45.5 us -> 23.6 us  [contract_cols(): lax.dot_general(left, right, (((1,), (1,)), ((), ())), precision=precisio...]
  transfers between devices with their start and end apart: 89 -> 87, of which waited for: 36 -> 37; matrix products, arithmetic and copies ran while one was open for 40% -> 20% of each run, Pallas kernels for 0% -> 7%
where the time goes in v2:
time: 680 us; the launch traced here: 667 us
  waiting for transfers between devices  213 us (31%)
  starting transfers between devices  190 us (28%)
  Pallas kernels  89.5 us (13%)
  matrix products  70 us (10%)
  other arithmetic  47.8 us (7%)
  local copies, waits for them, and re-layouts  44.3 us (7%)
  blocking collectives  9.33 us (1%)
    ppermute x14, waiting for transfers between devices, up(): return lax.ppermute(value, 'z', RING_UP)  65.4 us
    ppermute x37, starting transfers between devices, swap(): return lax.ppermute(value, axis, SWAP)  62.6 us
    ppermute x37, waiting for transfers between devices, swap(): return lax.ppermute(value, axis, SWAP)  50.2 us
    ppermute x14, waiting for transfers between devices, down(): return lax.ppermute(value, 'z', RING_DOWN)  45.1 us
    ppermute x14, starting transfers between devices, down(): return lax.ppermute(value, 'z', RING_DOWN)  43.9 us
    ppermute x12, starting transfers between devices, turn(): return lax.ppermute(value, ('c', 'y'), TURN)  39.4 us
    ppermute x4, waiting for transfers between devices, sum_other(): return lax.ppermute(value, 'z', [(0, 1), (1, 0), (2, 3), (3, 2)])  38.2 us
    dot_general x16, matrix products, contract_rows(): lax.dot_general(left, right, (((0,), (0,)), ((), ())), precision=precisio...  28.4 us
  transfers between devices with their start and end apart: 87, of which 37 were waited for; matrix products, arithmetic and copies ran while one was open for 20% of the time, Pallas kernels for 7%

profile of v2, /device:TPU:1, one launch (start us, length us, event | category | flops | bytes accessed | tf_op | source)
XLA Modules:
  0.0 667.1 jit_solution(9211529645132879388)
XLA Ops:
  1.6 4.5 collective-permute-start.1
  10.5 3.6 collective-permute-start.9
  29.1 2.5 collective-permute-done.10
  31.6 3.0 collective-permute-done.11
  37.9 3.3 collective-permute-start.5
  45.0 3.1 collective-permute-start.14
  50.2 7.5 %collective-permute-done.4 = bf16[2,2,64,1536]{3,2,1,0:T(8,128)(2,1)S(1)} collective-permute-done((bf16[2,2,64,1536]{3,2,1,0:T(8,128)(2,1)S(1)}, bf16[2,2,64,1536]{3,2,1,0:T(8,128)(2,1)S(1)}, u32[]{:S(2)}, u32[]{:S(2)}) %collective-permute-start.4) | collective-permute-done | bytes 786464 | tf_op jit(solution)/shard_map/ppermute | solution.py:460
  57.7 18.1 %collective-permute-start.6 = (bf16[2,2,32,1536]{3,2,1,0:T(8,128)(2,1)S(1)}, bf16[2,2,32,1536]{3,2,1,0:T(8,128)(2,1)S(1)}, u32[]{:S(2)}, u32[]{:S(2)}) collective-permute-start(bf16[2,2,32,1536]{3,2,1,0:T(8,128)(2,1)S(1)} %slice.187), channel_id=1, source_target_pairs={{0,8},{8,16},{16,24},{24,0},{1,9},{9,17},{17,25},{25,1},{2,10},{10... | collective-permute-start | bytes 1179656 | tf_op jit(solution)/shard_map/ppermute | solution.py:460
  79.2 26.3 %collective-permute-done.6 = bf16[2,2,32,1536]{3,2,1,0:T(8,128)(2,1)S(1)} collective-permute-done((bf16[2,2,32,1536]{3,2,1,0:T(8,128)(2,1)S(1)}, bf16[2,2,32,1536]{3,2,1,0:T(8,128)(2,1)S(1)}, u32[]{:S(2)}, u32[]{:S(2)}) %collective-permute-start.6) | collective-permute-done | bytes 393248 | tf_op jit(solution)/shard_map/ppermute | solution.py:460
  105.5 11.9 %collective-permute-start.22 = (bf16[2,2,64,2048]{3,2,1,0:T(8,128)(2,1)}, bf16[2,2,64,2048]{3,2,1,0:T(8,128)(2,1)}, u32[]{:S(2)}, u32[]{:S(2)}) collective-permute-start(bf16[2,2,64,2048]{3,2,1,0:T(8,128)(2,1)} %maximum_select_fusion.4), channel_id=1, source_target_pairs={{8,0},{16,8},{24,16},{0,24},{9,1},{17,9},{25,17},{1,25},{10,2},{18... | collective-permute-start | bytes 3145736 | tf_op jit(solution)/shard_map/ppermute | solution.py:464
  120.2 3.6 add_convert_fusion.q_ref.k_ref.v_ref
  123.9 19.2 %shard_map.254 = (bf16[1024,512]{1,0:T(8,128)(2,1)S(1)}, f32[4,8,1024]{2,1,0:T(8,128)S(1)}) custom-call(s32[2,4]{1,0:T(2,128)S(1)} %pad_add_fusion.bounds, bf16[1024,1536]{1,0:T(8,128)(2,1)S(1)} %add_convert_fusion.q_ref.k_ref.v_ref, bf16[1024,1536]{1,0:T(8,128)(2,1)S(1)} %add_convert_fusion.q_ref.k_ref.v_ref, ...), custom_call_target="tpu_custom_call" | custom-call | flops 2147483648 | bytes 12582912 | tf_op jit(solution)/shard_map/pallas_call | solution.py:657
  143.8 32.1 %collective-permute-done.15 = bf16[4,2,64,2560]{3,2,1,0:T(8,128)(2,1)S(1)} collective-permute-done((bf16[4,2,64,2560]{3,2,1,0:T(8,128)(2,1)S(1)}, bf16[4,2,64,2560]{3,2,1,0:T(8,128)(2,1)S(1)}, u32[]{:S(2)}, u32[]{:S(2)}) %collective-permute-start.15) | collective-permute-done | bytes 2621472 | tf_op jit(solution)/shard_map/ppermute | solution.py:456
  188.3 3.4 collective-permute-start.24
  198.1 4.3 collective-permute-done.23
  202.4 11.2 %collective-permute-done.24 = bf16[2,2,32,2048]{3,2,1,0:T(8,128)(2,1)S(1)} collective-permute-done((bf16[2,2,32,2048]{3,2,1,0:T(8,128)(2,1)S(1)}, bf16[2,2,32,2048]{3,2,1,0:T(8,128)(2,1)S(1)}, u32[]{:S(2)}, u32[]{:S(2)}) %collective-permute-start.24) | collective-permute-done | bytes 524320 | tf_op jit(solution)/shard_map/ppermute | solution.py:464
  216.1 17.6 %shard_map.255 = (bf16[1024,2048]{1,0:T(8,128)(2,1)S(1)}, bf16[1024,2048]{1,0:T(8,128)(2,1)S(1)}) custom-call(bf16[1024,1024]{1,0:T(8,128)(2,1)S(1)} %pad_maximum_fusion.x_ref, bf16[1024,2048]{1,0:T(8,128)(2,1)S(1)} %slice.196.w_ref, f32[1,2048]{1,0:T(1,128)S(1)} %slice.197.b_ref), custom_call_target="tpu_custom_call" | custom-call | flops 4294967296 | bytes 14680064 | tf_op jit(solution)/shard_map/pallas_call | solution.py:817
  239.2 2.7 fusion.177
  248.8 4.2 all-to-all-start
  253.0 4.1 collective-permute-start.28
  267.1 2.5 collective-permute-done.30
  274.5 3.2 collective-permute-start.32
  283.9 10.0 %shard_map.256 = f32[24,2048]{1,0:T(8,128)S(1)} custom-call(bf16[2048,128]{1,0:T(8,128)(2,1)} %bitcast.46.q_ref, bf16[1024,128]{1,0:T(8,128)(2,1)S(1)} %copy-done.16, s32[1,1024]{1,0:T(1,128)S(1)} %compare_select_fusion.seg_row.seg_ref), custom_call_target="tpu_custom_call" | custom-call | flops 3221225472 | bytes 786432 | tf_op jit(solution)/shard_map/pallas_call | solution.py:870
  294.6 9.3 %all_to_all.15 = f32[16,8,128]{2,1,0:T(8,128)S(1)} all-to-all(f32[16,8,128]{2,1,0:T(8,128)S(1)} %broadcast_in_dim.129), channel_id=1, replica_groups=mesh['z'=4,'x'=2,'c'=2,'y'=2] {'z','x','y'}, dimensions={0} | all-to-all | bytes 131072 | tf_op jit(solution)/shard_map/all_to_all | solution.py:1085
  305.3 15.8 %shard_map.257 = (bf16[2048,128]{1,0:T(8,128)(2,1)S(1)}, f32[768,128]{1,0:T(8,128)S(1)}) custom-call(bf16[2048,128]{1,0:T(8,128)(2,1)} %bitcast.46.q_ref, bf16[1024,128]{1,0:T(8,128)(2,1)S(1)} %copy-done.17, s32[1,1024]{1,0:T(1,128)S(1)} %compare_select_fusion.seg_row.seg_ref, f32[24,2048]{1,0:T(8,128)S(1)} %convolution_divide_fusion.coef_ref), custom_call_target="tpu_custom_call" | custom-call | flops 4831838208 | bytes 1572864 | tf_op jit(solution)/shard_map/pallas_call | solution.py:946
  322.6 4.2 all-to-all-start.2
  328.7 7.8 %all-to-all-done.2 = bf16[16,128,128]{2,1,0:T(8,128)(2,1)} async-done(((bf16[16,128,128]{2,1,0:T(8,128)(2,1)}), bf16[16,128,128]{2,1,0:T(8,128)(2,1)}, u32[]{:S(2)}, u32[]{:S(2)}) %all-to-all-start.2) | async-done | bytes 524320 | tf_op jit(solution)/shard_map/all_to_all | solution.py:1106
  340.0 8.5 %collective-permute-start.35 = (f32[512,128]{1,0:T(8,128)}, f32[512,128]{1,0:T(8,128)}, u32[]{:S(2)}, u32[]{:S(2)}) collective-permute-start(f32[512,128]{1,0:T(8,128)} %constant_dynamic-slice_fusion.2), channel_id=1, source_target_pairs={{0,2},{2,0},{1,3},{3,1},{4,6},{6,4},{5,7},{7,5},{8,10},{10,8},{9,1... | collective-permute-start | bytes 786440 | tf_op jit(solution)/shard_map/ppermute | solution.py:456
  348.5 3.0 collective-permute-start.34
  351.5 2.9 collective-permute-start.26
  357.7 13.3 %collective-permute-start.79 = (f32[512,128]{1,0:T(8,128)S(1)}, f32[512,128]{1,0:T(8,128)S(1)}, u32[]{:S(2)}, u32[]{:S(2)}) collective-permute-start(f32[512,128]{1,0:T(8,128)S(1)} %constant_dynamic-slice_fusion), channel_id=1, source_target_pairs={{0,2},{2,0},{1,3},{3,1},{4,6},{6,4},{5,7},{7,5},{8,10},{10,8},{9,1... | collective-permute-start | bytes 786440 | tf_op jit(solution)/shard_map/ppermute | solution.py:456
  371.5 3.1 multiply_reduce_fusion
  374.6 2.9 convert_reduce_fusion.1
  391.4 8.6 %convert_reduce_fusion = (f32[2048]{0:T(1024)S(1)}, bf16[1024,2048]{1,0:T(8,128)(2,1)S(1)}) fusion(bf16[1024,2048]{1,0:T(8,128)(2,1)} %copy-done.18, bf16[1024,2048]{1,0:T(8,128)(2,1)} %bitcast.269, bf16[512,1024]{1,0:T(8,128)(2,1)} %collective-permute-done.36, bf16[512,1024]{1,0:T(8,128)(2,1)} %get-tuple-element.47), kind=kOutput, calls=%fused_computation | convolution fusion | flops 4309645312 | bytes 14688256 | tf_op jit(solution)/shard_map/dot_general | solution.py:448
  411.1 3.0 collective-permute-start.74
  414.1 3.6 multiply_reduce_fusion.1
  417.8 2.9 convert_reduce_fusion.2
  426.5 3.8 fusion.4
  430.9 4.6 collective-permute-done.74
  435.5 2.5 fusion.5
  440.0 4.1 collective-permute-start.63
  447.5 35.8 %collective-permute-done.63 = f32[6,1024]{1,0:T(8,128)S(1)} collective-permute-done((f32[6,1024]{1,0:T(8,128)S(1)}, f32[6,1024]{1,0:T(8,128)S(1)}, u32[]{:S(2)}, u32[]{:S(2)}) %collective-permute-start.63) | collective-permute-done | bytes 24608 | tf_op jit(solution)/shard_map/ppermute | solution.py:557
  483.4 3.2 collective-permute-start.64
  487.4 2.8 collective-permute-start.38
  494.9 3.3 convolution_convert_fusion.3.grad_ref
  498.2 27.0 %shard_map.258 = (bf16[1024,1536]{1,0:T(8,128)(2,1)S(1)}, f32[4,8,128]{2,1,0:T(8,128)S(1)}) custom-call(s32[2,4]{1,0:T(2,128)S(1)} %pad_add_fusion.bounds, bf16[1024,1536]{1,0:T(8,128)(2,1)S(1)} %add_convert_fusion.q_ref.k_ref.v_ref, bf16[1024,1536]{1,0:T(8,128)(2,1)S(1)} %add_convert_fusion.q_ref.k_ref.v_ref, ...), custom_call_target="tpu_custom_call" | custom-call | flops 5368709120 | bytes 25165824 | tf_op jit(solution)/shard_map/pallas_call | solution.py:752
  525.2 6.1 collective-permute-start.48
  533.6 2.8 fusion.21
  538.0 2.5 convert_add_fusion
  547.3 3.3 collective-permute-start.55
  551.1 4.6 collective-permute-start.52
  557.9 3.3 collective-permute-start.43
  564.3 3.3 collective-permute-start.56
  568.6 14.7 %collective-permute-done.54 = bf16[256,512]{1,0:T(8,128)(2,1)S(1)} collective-permute-done((bf16[256,512]{1,0:T(8,128)(2,1)S(1)}, bf16[256,512]{1,0:T(8,128)(2,1)S(1)}, u32[]{:S(2)}, u32[]{:S(2)}) %collective-permute-start.54) | collective-permute-done | bytes 262176 | tf_op jit(solution)/shard_map/ppermute | solution.py:460
  585.0 3.2 collective-permute-done.56
  588.2 2.7 collective-permute-start.78
  601.7 5.0 collective-permute-start.59
  608.6 4.8 collective-permute-done.42
  613.5 19.8 %collective-permute-done.44 = bf16[256,1536]{1,0:T(8,128)(2,1)S(1)} collective-permute-done((bf16[256,1536]{1,0:T(8,128)(2,1)S(1)}, bf16[256,1536]{1,0:T(8,128)(2,1)S(1)}, u32[]{:S(2)}, u32[]{:S(2)}) %collective-permute-start.44) | collective-permute-done | bytes 786464 | tf_op jit(solution)/shard_map/ppermute | solution.py:464
  636.4 4.1 collective-permute-start.40
  640.9 3.0 collective-permute-start.70
  645.3 5.3 collective-permute-done.68
  653.0 2.6 collective-permute-start.71
  655.6 3.0 collective-permute-start.47
  (485 shorter events, 192.2 us)
Async XLA Ops:
  1.6 17.2 %collective-permute-start.1 = (bf16[64,1536]{1,0:T(8,128)(2,1)S(1)}, bf16[64,1536]{1,0:T(8,128)(2,1)S(1)}, u32[]{:S(2)}, u32[]{:S(2)}) collective-permute-start(bf16[64,1536]{1,0:T(8,128)(2,1)S(1)} %pad_maximum_fusion.7), channel_id=1, source_target_pairs={{0,0},{1,2},{2,1},{3,3},{4,4},{5,6},{6,5},{7,7},{8,8},{9,10},{10,9... | collective-permute-start | bytes 589832 | tf_op jit(solution)/shard_map/ppermute | solution.py:452
  7.6 11.2 %collective-permute-start.8 = (f32[1,3072]{1,0:T(1,128)S(1)}, f32[1,3072]{1,0:T(1,128)S(1)}, u32[]{:S(2)}, u32[]{:S(2)}) collective-permute-start(f32[1,3072]{1,0:T(1,128)S(1)} %maximum_convert_fusion), channel_id=1, source_target_pairs={{0,0},{1,2},{2,1},{3,3},{4,4},{5,6},{6,5},{7,7},{8,8},{9,10},{10,9... | collective-permute-start | bytes 36872 | tf_op jit(solution)/shard_map/ppermute | solution.py:452
  10.5 13.1 %collective-permute-start.9 = (bf16[64,2560]{1,0:T(8,128)(2,1)S(1)}, bf16[64,2560]{1,0:T(8,128)(2,1)S(1)}, u32[]{:S(2)}, u32[]{:S(2)}) collective-permute-start(bf16[64,2560]{1,0:T(8,128)(2,1)S(1)} %pad_maximum_fusion.6), channel_id=1, source_target_pairs={{0,0},{1,2},{2,1},{3,3},{4,4},{5,6},{6,5},{7,7},{8,8},{9,10},{10,9... | collective-permute-start | bytes 983048 | tf_op jit(solution)/shard_map/ppermute | solution.py:452
  14.2 8.2 %collective-permute-start.18 = (bf16[64,2048]{1,0:T(8,128)(2,1)}, bf16[64,2048]{1,0:T(8,128)(2,1)S(1)}, u32[]{:S(2)}, u32[]{:S(2)}) collective-permute-start(bf16[64,2048]{1,0:T(8,128)(2,1)} %bitcast.329), channel_id=1, source_target_pairs={{0,0},{1,2},{2,1},{3,3},{4,4},{5,6},{6,5},{7,7},{8,8},{9,10},{10,9... | collective-permute-start | bytes 786440 | tf_op jit(solution)/shard_map/ppermute | solution.py:452
  18.8 8.2 %collective-permute-start.2 = (bf16[64,1536]{1,0:T(8,128)(2,1)S(1)}, bf16[64,1536]{1,0:T(8,128)(2,1)S(1)}, u32[]{:S(2)}, u32[]{:S(2)}) collective-permute-start(bf16[64,1536]{1,0:T(8,128)(2,1)S(1)} %collective-permute-done.1), channel_id=1, source_target_pairs={{0,4},{4,0},{1,5},{5,1},{2,6},{6,2},{3,7},{7,3},{8,12},{12,8},{9,1... | collective-permute-start | bytes 589832 | tf_op jit(solution)/shard_map/ppermute | solution.py:456
  23.6 7.9 %collective-permute-start.10 = (bf16[64,2560]{1,0:T(8,128)(2,1)S(1)}, bf16[64,2560]{1,0:T(8,128)(2,1)S(1)}, u32[]{:S(2)}, u32[]{:S(2)}) collective-permute-start(bf16[64,2560]{1,0:T(8,128)(2,1)S(1)} %collective-permute-done.9), channel_id=1, source_target_pairs={{0,8},{8,16},{16,24},{24,0},{1,9},{9,17},{17,25},{25,1},{2,10},{10... | collective-permute-start | bytes 983048 | tf_op jit(solution)/shard_map/ppermute | solution.py:460
  24.9 9.7 %collective-permute-start.11 = (bf16[64,2560]{1,0:T(8,128)(2,1)S(1)}, bf16[64,2560]{1,0:T(8,128)(2,1)S(1)}, u32[]{:S(2)}, u32[]{:S(2)}) collective-permute-start(bf16[64,2560]{1,0:T(8,128)(2,1)S(1)} %collective-permute-done.9), channel_id=1, source_target_pairs={{8,0},{16,8},{24,16},{0,24},{9,1},{17,9},{25,17},{1,25},{10,2},{18... | collective-permute-start | bytes 983048 | tf_op jit(solution)/shard_map/ppermute | solution.py:464
  27.1 10.5 %collective-permute-start.3 = (bf16[2,64,1536]{2,1,0:T(8,128)(2,1)S(1)}, bf16[2,64,1536]{2,1,0:T(8,128)(2,1)S(1)}, u32[]{:S(2)}, u32[]{:S(2)}) collective-permute-start(bf16[2,64,1536]{2,1,0:T(8,128)(2,1)S(1)} %maximum_select_fusion.11), channel_id=1, source_target_pairs={{0,1},{1,0},{2,3},{3,2},{4,5},{5,4},{6,7},{7,6},{8,9},{9,8},{10,11... | collective-permute-start | bytes 1179656 | tf_op jit(solution)/shard_map/ppermute | solution.py:456
  27.7 21.2 %collective-permute-start.20 = (bf16[2,64,2048]{2,1,0:T(8,128)(2,1)S(1)}, bf16[2,64,2048]{2,1,0:T(8,128)(2,1)S(1)}, u32[]{:S(2)}, u32[]{:S(2)}) collective-permute-start(bf16[2,64,2048]{2,1,0:T(8,128)(2,1)S(1)} %maximum_select_fusion.8), channel_id=1, source_target_pairs={{0,1},{1,0},{2,3},{3,2},{4,5},{5,4},{6,7},{7,6},{8,9},{9,8},{10,11... | collective-permute-start | bytes 1572872 | tf_op jit(solution)/shard_map/ppermute | solution.py:456
  31.6 10.0 %collective-permute-start.12 = (bf16[32,2560]{1,0:T(8,128)(2,1)S(1)}, bf16[32,2560]{1,0:T(8,128)(2,1)S(1)}, u32[]{:S(2)}, u32[]{:S(2)}) collective-permute-start(bf16[32,2560]{1,0:T(8,128)(2,1)S(1)} %slice.191), channel_id=1, source_target_pairs={{0,8},{8,16},{16,24},{24,0},{1,9},{9,17},{17,25},{25,1},{2,10},{10... | collective-permute-start | bytes 491528 | tf_op jit(solution)/shard_map/ppermute | solution.py:460
  34.7 10.3 %collective-permute-start.13 = (bf16[32,2560]{1,0:T(8,128)(2,1)S(1)}, bf16[32,2560]{1,0:T(8,128)(2,1)S(1)}, u32[]{:S(2)}, u32[]{:S(2)}) collective-permute-start(bf16[32,2560]{1,0:T(8,128)(2,1)S(1)} %slice.192), channel_id=1, source_target_pairs={{8,0},{16,8},{24,16},{0,24},{9,1},{17,9},{25,17},{1,25},{10,2},{18... | collective-permute-start | bytes 491528 | tf_op jit(solution)/shard_map/ppermute | solution.py:464
  37.8 19.9 %collective-permute-start.4 = (bf16[2,2,64,1536]{3,2,1,0:T(8,128)(2,1)S(1)}, bf16[2,2,64,1536]{3,2,1,0:T(8,128)(2,1)S(1)}, u32[]{:S(2)}, u32[]{:S(2)}) collective-permute-start(bf16[2,2,64,1536]{3,2,1,0:T(8,128)(2,1)S(1)} %maximum_select_fusion.6), channel_id=1, source_target_pairs={{0,8},{8,16},{16,24},{24,0},{1,9},{9,17},{17,25},{25,1},{2,10},{10... | collective-permute-start | bytes 2359304 | tf_op jit(solution)/shard_map/ppermute | solution.py:460
  37.9 38.9 %collective-permute-start.5 = (bf16[2,2,64,1536]{3,2,1,0:T(8,128)(2,1)S(1)}, bf16[2,2,64,1536]{3,2,1,0:T(8,128)(2,1)S(1)}, u32[]{:S(2)}, u32[]{:S(2)}) collective-permute-start(bf16[2,2,64,1536]{3,2,1,0:T(8,128)(2,1)S(1)} %maximum_select_fusion.6), channel_id=1, source_target_pairs={{8,0},{16,8},{24,16},{0,24},{9,1},{17,9},{25,17},{1,25},{10,2},{18... | collective-permute-start | bytes 2359304 | tf_op jit(solution)/shard_map/ppermute | solution.py:464
  42.7 76.0 %collective-permute-start = (bf16[1024,1024]{1,0:T(8,128)(2,1)S(1)}, bf16[1024,1024]{1,0:T(8,128)(2,1)S(1)}, u32[]{:S(2)}, u32[]{:S(2)}) collective-permute-start(bf16[1024,1024]{1,0:T(8,128)(2,1)S(1)} %copy-done.47), channel_id=1, source_target_pairs={{0,2},{2,0},{1,3},{3,1},{4,6},{6,4},{5,7},{7,5},{8,10},{10,8},{9,1... | collective-permute-start | bytes 6291464 | tf_op jit(solution)/shard_map/ppermute | solution.py:456
  45.0 72.5 %collective-permute-start.14 = (bf16[4,64,2560]{2,1,0:T(8,128)(2,1)S(1)}, bf16[4,64,2560]{2,1,0:T(8,128)(2,1)S(1)}, u32[]{:S(2)}, u32[]{:S(2)}) collective-permute-start(bf16[4,64,2560]{2,1,0:T(8,128)(2,1)S(1)} %fusion.95), channel_id=1, source_target_pairs={{0,1},{1,0},{2,3},{3,2},{4,5},{5,4},{6,7},{7,6},{8,9},{9,8},{10,11... | collective-permute-start | bytes 3932168 | tf_op jit(solution)/shard_map/ppermute | solution.py:456
  50.1 135.4 %collective-permute-start.21 = (bf16[2,2,64,2048]{3,2,1,0:T(8,128)(2,1)}, bf16[2,2,64,2048]{3,2,1,0:T(8,128)(2,1)}, u32[]{:S(2)}, u32[]{:S(2)}) collective-permute-start(bf16[2,2,64,2048]{3,2,1,0:T(8,128)(2,1)} %maximum_select_fusion.4), channel_id=1, source_target_pairs={{0,8},{8,16},{16,24},{24,0},{1,9},{9,17},{17,25},{25,1},{2,10},{10... | collective-permute-start | bytes 3145736 | tf_op jit(solution)/shard_map/ppermute | solution.py:460
  57.7 47.8 %collective-permute-start.6 = (bf16[2,2,32,1536]{3,2,1,0:T(8,128)(2,1)S(1)}, bf16[2,2,32,1536]{3,2,1,0:T(8,128)(2,1)S(1)}, u32[]{:S(2)}, u32[]{:S(2)}) collective-permute-start(bf16[2,2,32,1536]{3,2,1,0:T(8,128)(2,1)S(1)} %slice.187), channel_id=1, source_target_pairs={{0,8},{8,16},{16,24},{24,0},{1,9},{9,17},{17,25},{25,1},{2,10},{10... | collective-permute-start | bytes 1179656 | tf_op jit(solution)/shard_map/ppermute | solution.py:460
  76.8 40.6 %collective-permute-start.7 = (bf16[2,2,32,1536]{3,2,1,0:T(8,128)(2,1)S(1)}, bf16[2,2,32,1536]{3,2,1,0:T(8,128)(2,1)S(1)}, u32[]{:S(2)}, u32[]{:S(2)}) collective-permute-start(bf16[2,2,32,1536]{3,2,1,0:T(8,128)(2,1)S(1)} %slice.188), channel_id=1, source_target_pairs={{8,0},{16,8},{24,16},{0,24},{9,1},{17,9},{25,17},{1,25},{10,2},{18... | collective-permute-start | bytes 1179656 | tf_op jit(solution)/shard_map/ppermute | solution.py:464
  105.5 81.5 %collective-permute-start.22 = (bf16[2,2,64,2048]{3,2,1,0:T(8,128)(2,1)}, bf16[2,2,64,2048]{3,2,1,0:T(8,128)(2,1)}, u32[]{:S(2)}, u32[]{:S(2)}) collective-permute-start(bf16[2,2,64,2048]{3,2,1,0:T(8,128)(2,1)} %maximum_select_fusion.4), channel_id=1, source_target_pairs={{8,0},{16,8},{24,16},{0,24},{9,1},{17,9},{25,17},{1,25},{10,2},{18... | collective-permute-start | bytes 3145736 | tf_op jit(solution)/shard_map/ppermute | solution.py:464
  118.0 57.9 %collective-permute-start.15 = (bf16[4,2,64,2560]{3,2,1,0:T(8,128)(2,1)S(1)}, bf16[4,2,64,2560]{3,2,1,0:T(8,128)(2,1)S(1)}, u32[]{:S(2)}, u32[]{:S(2)}) collective-permute-start(bf16[4,2,64,2560]{3,2,1,0:T(8,128)(2,1)S(1)} %maximum_select_fusion.1), channel_id=1, source_target_pairs={{0,4},{4,0},{1,5},{5,1},{2,6},{6,2},{3,7},{7,3},{8,12},{12,8},{9,1... | collective-permute-start | bytes 7864328 | tf_op jit(solution)/shard_map/ppermute | solution.py:456
  179.8 12.0 %collective-permute-start.16 = (bf16[512,1024]{1,0:T(8,128)(2,1)}, bf16[512,1024]{1,0:T(8,128)(2,1)}, u32[]{:S(2)}, u32[]{:S(2)}) collective-permute-start(bf16[512,1024]{1,0:T(8,128)(2,1)} %convolution_convert_fusion.4), channel_id=1, source_target_pairs={{0,2},{2,0},{1,3},{3,1},{4,6},{6,4},{5,7},{7,5},{8,10},{10,8},{9,1... | collective-permute-start | bytes 3145736 | tf_op jit(solution)/shard_map/ppermute | solution.py:456
  187.0 15.5 %collective-permute-start.23 = (bf16[2,2,32,2048]{3,2,1,0:T(8,128)(2,1)S(1)}, bf16[2,2,32,2048]{3,2,1,0:T(8,128)(2,1)S(1)}, u32[]{:S(2)}, u32[]{:S(2)}) collective-permute-start(bf16[2,2,32,2048]{3,2,1,0:T(8,128)(2,1)S(1)} %slice.198), channel_id=1, source_target_pairs={{0,8},{8,16},{16,24},{24,0},{1,9},{9,17},{17,25},{25,1},{2,10},{10... | collective-permute-start | bytes 1572872 | tf_op jit(solution)/shard_map/ppermute | solution.py:460
  188.3 25.3 %collective-permute-start.24 = (bf16[2,2,32,2048]{3,2,1,0:T(8,128)(2,1)S(1)}, bf16[2,2,32,2048]{3,2,1,0:T(8,128)(2,1)S(1)}, u32[]{:S(2)}, u32[]{:S(2)}) collective-permute-start(bf16[2,2,32,2048]{3,2,1,0:T(8,128)(2,1)S(1)} %slice.199), channel_id=1, source_target_pairs={{8,0},{16,8},{24,16},{0,24},{9,1},{17,9},{25,17},{1,25},{10,2},{18... | collective-permute-start | bytes 1572872 | tf_op jit(solution)/shard_map/ppermute | solution.py:464
  194.8 19.7 %collective-permute-start.17 = (bf16[512,1024]{1,0:T(8,128)(2,1)S(1)}, bf16[512,1024]{1,0:T(8,128)(2,1)S(1)}, u32[]{:S(2)}, u32[]{:S(2)}) collective-permute-start(bf16[512,1024]{1,0:T(8,128)(2,1)S(1)} %fusion.14), channel_id=1, source_target_pairs={{0,2},{2,0},{1,3},{3,1},{4,6},{6,4},{5,7},{7,5},{8,10},{10,8},{9,1... | collective-permute-start | bytes 3145736 | tf_op jit(solution)/shard_map/ppermute | solution.py:456
  248.8 34.1 %all-to-all-start = ((bf16[16,128,128]{2,1,0:T(8,128)(2,1)}), bf16[16,128,128]{2,1,0:T(8,128)(2,1)}, u32[]{:S(2)}, u32[]{:S(2)}) async-start(bf16[16,128,128]{2,1,0:T(8,128)(2,1)} %broadcast_in_dim.127), calls=%async_computation | async-start | bytes 1048576 | tf_op jit(solution)/shard_map/all_to_all | solution.py:1065
  322.6 13.9 %all-to-all-start.2 = ((bf16[16,128,128]{2,1,0:T(8,128)(2,1)}), bf16[16,128,128]{2,1,0:T(8,128)(2,1)}, u32[]{:S(2)}, u32[]{:S(2)}) async-start(bf16[16,128,128]{2,1,0:T(8,128)(2,1)} %bitcast.250), calls=%async_computation.2 | async-start | bytes 1048576 | tf_op jit(solution)/shard_map/all_to_all | solution.py:1106
  340.0 14.4 %collective-permute-start.35 = (f32[512,128]{1,0:T(8,128)}, f32[512,128]{1,0:T(8,128)}, u32[]{:S(2)}, u32[]{:S(2)}) collective-permute-start(f32[512,128]{1,0:T(8,128)} %constant_dynamic-slice_fusion.2), channel_id=1, source_target_pairs={{0,2},{2,0},{1,3},{3,1},{4,6},{6,4},{5,7},{7,5},{8,10},{10,8},{9,1... | collective-permute-start | bytes 786440 | tf_op jit(solution)/shard_map/ppermute | solution.py:456
  348.5 23.0 %collective-permute-start.34 = (bf16[512,1024]{1,0:T(8,128)(2,1)}, bf16[512,1024]{1,0:T(8,128)(2,1)}, u32[]{:S(2)}, u32[]{:S(2)}) collective-permute-start(bf16[512,1024]{1,0:T(8,128)(2,1)} %param.29), channel_id=1, source_target_pairs={{0,0},{1,2},{2,1},{3,3},{4,4},{5,6},{6,5},{7,7},{8,8},{9,10},{10,9... | collective-permute-start | bytes 3145736 | tf_op jit(solution)/shard_map/ppermute | solution.py:452
  351.5 36.4 %collective-permute-start.26 = (bf16[512,1024]{1,0:T(8,128)(2,1)}, bf16[512,1024]{1,0:T(8,128)(2,1)}, u32[]{:S(2)}, u32[]{:S(2)}) collective-permute-start(bf16[512,1024]{1,0:T(8,128)(2,1)} %copy-done.25), channel_id=1, source_target_pairs={{0,0},{1,2},{2,1},{3,3},{4,4},{5,6},{6,5},{7,7},{8,8},{9,10},{10,9... | collective-permute-start | bytes 3145736 | tf_op jit(solution)/shard_map/ppermute | solution.py:452
  357.7 20.4 %collective-permute-start.79 = (f32[512,128]{1,0:T(8,128)S(1)}, f32[512,128]{1,0:T(8,128)S(1)}, u32[]{:S(2)}, u32[]{:S(2)}) collective-permute-start(f32[512,128]{1,0:T(8,128)S(1)} %constant_dynamic-slice_fusion), channel_id=1, source_target_pairs={{0,2},{2,0},{1,3},{3,1},{4,6},{6,4},{5,7},{7,5},{8,10},{10,8},{9,1... | collective-permute-start | bytes 786440 | tf_op jit(solution)/shard_map/ppermute | solution.py:456
  377.6 13.8 %collective-permute-start.36 = (bf16[512,1024]{1,0:T(8,128)(2,1)}, bf16[512,1024]{1,0:T(8,128)(2,1)}, u32[]{:S(2)}, u32[]{:S(2)}) collective-permute-start(bf16[512,1024]{1,0:T(8,128)(2,1)} %get-tuple-element.47), channel_id=1, source_target_pairs={{0,2},{2,0},{1,3},{3,1},{4,6},{6,4},{5,7},{7,5},{8,10},{10,8},{9,1... | collective-permute-start | bytes 3145736 | tf_op jit(solution)/shard_map/ppermute | solution.py:456
  390.5 13.9 %collective-permute-start.82 = (bf16[512,128]{1,0:T(8,128)(2,1)S(1)}, bf16[512,128]{1,0:T(8,128)(2,1)S(1)}, u32[]{:S(2)}, u32[]{:S(2)}) collective-permute-start(bf16[512,128]{1,0:T(8,128)(2,1)S(1)} %fusion.162), channel_id=1, source_target_pairs={{0,8},{8,0},{16,24},{24,16},{1,9},{9,1},{17,25},{25,17},{2,10},{10... | collective-permute-start | bytes 393224 | tf_op jit(solution)/shard_map/ppermute | solution.py:557
  402.4 11.7 %collective-permute-start.37 = (bf16[512,1024]{1,0:T(8,128)(2,1)S(1)}, bf16[512,1024]{1,0:T(8,128)(2,1)S(1)}, u32[]{:S(2)}, u32[]{:S(2)}) collective-permute-start(bf16[512,1024]{1,0:T(8,128)(2,1)S(1)} %fusion.27), channel_id=1, source_target_pairs={{0,2},{2,0},{1,3},{3,1},{4,6},{6,4},{5,7},{7,5},{8,10},{10,8},{9,1... | collective-permute-start | bytes 3145736 | tf_op jit(solution)/shard_map/ppermute | solution.py:456
  406.1 17.2 %collective-permute-start.83 = (bf16[512,128]{1,0:T(8,128)(2,1)}, bf16[512,128]{1,0:T(8,128)(2,1)}, u32[]{:S(2)}, u32[]{:S(2)}) collective-permute-start(bf16[512,128]{1,0:T(8,128)(2,1)} %fusion.110), channel_id=1, source_target_pairs={{0,24},{24,0},{8,16},{16,8},{1,25},{25,1},{9,17},{17,9},{2,26},{26... | collective-permute-start | bytes 393224 | tf_op jit(solution)/shard_map/ppermute | solution.py:559
  410.6 15.9 %collective-permute-start.72 = (bf16[128,2048]{1,0:T(8,128)(2,1)}, bf16[128,2048]{1,0:T(8,128)(2,1)}, u32[]{:S(2)}, u32[]{:S(2)}) collective-permute-start(bf16[128,2048]{1,0:T(8,128)(2,1)} %get-tuple-element.68), channel_id=1, source_target_pairs={{0,8},{8,16},{16,24},{24,0},{1,9},{9,17},{17,25},{25,1},{2,10},{10... | collective-permute-start | bytes 1572872 | tf_op jit(solution)/shard_map/ppermute | solution.py:460
  411.1 24.4 %collective-permute-start.74 = (bf16[128,2048]{1,0:T(8,128)(2,1)}, bf16[128,2048]{1,0:T(8,128)(2,1)}, u32[]{:S(2)}, u32[]{:S(2)}) collective-permute-start(bf16[128,2048]{1,0:T(8,128)(2,1)} %get-tuple-element.69), channel_id=1, source_target_pairs={{8,0},{16,8},{24,16},{0,24},{9,1},{17,9},{25,17},{1,25},{10,2},{18... | collective-permute-start | bytes 1572872 | tf_op jit(solution)/shard_map/ppermute | solution.py:464
  424.4 62.1 %collective-permute-start.84 = (f32[512,128]{1,0:T(8,128)S(1)}, f32[512,128]{1,0:T(8,128)S(1)}, u32[]{:S(2)}, u32[]{:S(2)}) collective-permute-start(f32[512,128]{1,0:T(8,128)S(1)} %convert_add_fusion.1), channel_id=1, source_target_pairs={{0,2},{2,0},{1,3},{3,1},{4,6},{6,4},{5,7},{7,5},{8,10},{10,8},{9,1... | collective-permute-start | bytes 786440 | tf_op jit(solution)/shard_map/ppermute | solution.py:456
  430.3 61.1 %collective-permute-start.73 = (bf16[256,2048]{1,0:T(8,128)(2,1)S(1)}, bf16[256,2048]{1,0:T(8,128)(2,1)S(1)}, u32[]{:S(2)}, u32[]{:S(2)}) collective-permute-start(bf16[256,2048]{1,0:T(8,128)(2,1)S(1)} %fusion.4), channel_id=1, source_target_pairs={{0,8},{8,16},{16,24},{24,0},{1,9},{9,17},{17,25},{25,1},{2,10},{10... | collective-permute-start | bytes 3145736 | tf_op jit(solution)/shard_map/ppermute | solution.py:460
  430.4 9.5 %collective-permute-start.62 = (f32[6,1024]{1,0:T(8,128)S(1)}, f32[6,1024]{1,0:T(8,128)S(1)}, u32[]{:S(2)}, u32[]{:S(2)}) collective-permute-start(f32[6,1024]{1,0:T(8,128)S(1)} %add.709), channel_id=1, source_target_pairs={{0,1},{1,0},{2,3},{3,2},{4,5},{5,4},{6,7},{7,6},{8,9},{9,8},{10,11... | collective-permute-start | bytes 73736 | tf_op jit(solution)/shard_map/ppermute | solution.py:456
  438.0 53.4 %collective-permute-start.75 = (bf16[256,2048]{1,0:T(8,128)(2,1)S(1)}, bf16[256,2048]{1,0:T(8,128)(2,1)S(1)}, u32[]{:S(2)}, u32[]{:S(2)}) collective-permute-start(bf16[256,2048]{1,0:T(8,128)(2,1)S(1)} %fusion.5), channel_id=1, source_target_pairs={{8,0},{16,8},{24,16},{0,24},{9,1},{17,9},{25,17},{1,25},{10,2},{18... | collective-permute-start | bytes 3145736 | tf_op jit(solution)/shard_map/ppermute | solution.py:464
  440.0 43.4 %collective-permute-start.63 = (f32[6,1024]{1,0:T(8,128)S(1)}, f32[6,1024]{1,0:T(8,128)S(1)}, u32[]{:S(2)}, u32[]{:S(2)}) collective-permute-start(f32[6,1024]{1,0:T(8,128)S(1)} %add.710), channel_id=1, source_target_pairs={{0,8},{8,0},{16,24},{24,16},{1,9},{9,1},{17,25},{25,17},{2,10},{10... | collective-permute-start | bytes 73736 | tf_op jit(solution)/shard_map/ppermute | solution.py:557
  446.5 90.0 %collective-permute-start.65 = (bf16[512,2048]{1,0:T(8,128)(2,1)S(1)}, bf16[512,2048]{1,0:T(8,128)(2,1)S(1)}, u32[]{:S(2)}, u32[]{:S(2)}) collective-permute-start(bf16[512,2048]{1,0:T(8,128)(2,1)S(1)} %convolution_convert_fusion), channel_id=1, source_target_pairs={{0,4},{4,0},{1,5},{5,1},{2,6},{6,2},{3,7},{7,3},{8,12},{12,8},{9,1... | collective-permute-start | bytes 6291464 | tf_op jit(solution)/shard_map/ppermute | solution.py:456
  493.8 42.6 %collective-permute-start.76 = (bf16[2,64,2048]{2,1,0:T(8,128)(2,1)S(1)}, bf16[2,64,2048]{2,1,0:T(8,128)(2,1)S(1)}, u32[]{:S(2)}, u32[]{:S(2)}) collective-permute-start(bf16[2,64,2048]{2,1,0:T(8,128)(2,1)S(1)} %fusion.66), channel_id=1, source_target_pairs={{0,1},{1,0},{2,3},{3,2},{4,5},{5,4},{6,7},{7,6},{8,9},{9,8},{10,11... | collective-permute-start | bytes 1572872 | tf_op jit(solution)/shard_map/ppermute | solution.py:456
  525.2 15.8 %collective-permute-start.48 = (f32[24,128]{1,0:T(8,128)S(1)}, f32[24,128]{1,0:T(8,128)S(1)}, u32[]{:S(2)}, u32[]{:S(2)}) collective-permute-start(f32[24,128]{1,0:T(8,128)S(1)} %maximum_bitcast_fusion.3), channel_id=1, source_target_pairs={{0,4},{4,0},{1,5},{5,1},{2,6},{6,2},{3,7},{7,3},{8,12},{12,8},{9,1... | collective-permute-start | bytes 36872 | tf_op jit(solution)/shard_map/ppermute | solution.py:456
  541.2 23.1 %collective-permute-start.77 = (bf16[64,2048]{1,0:T(8,128)(2,1)S(1)}, bf16[64,2048]{1,0:T(8,128)(2,1)}, u32[]{:S(2)}, u32[]{:S(2)}) collective-permute-start(bf16[64,2048]{1,0:T(8,128)(2,1)S(1)} %fusion.104), channel_id=1, source_target_pairs={{0,4},{4,0},{1,5},{5,1},{2,6},{6,2},{3,7},{7,3},{8,12},{12,8},{9,1... | collective-permute-start | bytes 786440 | tf_op jit(solution)/shard_map/ppermute | solution.py:456
  544.9 61.9 %collective-permute-start.66 = (bf16[4,64,2048]{2,1,0:T(8,128)(2,1)}, bf16[4,64,2048]{2,1,0:T(8,128)(2,1)}, u32[]{:S(2)}, u32[]{:S(2)}) collective-permute-start(bf16[4,64,2048]{2,1,0:T(8,128)(2,1)} %fusion.37), channel_id=1, source_target_pairs={{0,1},{1,0},{2,3},{3,2},{4,5},{5,4},{6,7},{7,6},{8,9},{9,8},{10,11... | collective-permute-start | bytes 3145736 | tf_op jit(solution)/shard_map/ppermute | solution.py:456
  547.3 10.6 %collective-permute-start.53 = (bf16[128,512]{1,0:T(8,128)(2,1)}, bf16[128,512]{1,0:T(8,128)(2,1)}, u32[]{:S(2)}, u32[]{:S(2)}) collective-permute-start(bf16[128,512]{1,0:T(8,128)(2,1)} %get-tuple-element.77), channel_id=1, source_target_pairs={{0,8},{8,16},{16,24},{24,0},{1,9},{9,17},{17,25},{25,1},{2,10},{10... | collective-permute-start | bytes 393224 | tf_op jit(solution)/shard_map/ppermute | solution.py:460
  547.3 15.3 %collective-permute-start.55 = (bf16[128,512]{1,0:T(8,128)(2,1)S(1)}, bf16[128,512]{1,0:T(8,128)(2,1)}, u32[]{:S(2)}, u32[]{:S(2)}) collective-permute-start(bf16[128,512]{1,0:T(8,128)(2,1)S(1)} %get-tuple-element.78), channel_id=1, source_target_pairs={{8,0},{16,8},{24,16},{0,24},{9,1},{17,9},{25,17},{1,25},{10,2},{18... | collective-permute-start | bytes 393224 | tf_op jit(solution)/shard_map/ppermute | solution.py:464
  556.7 34.8 %collective-permute-start.41 = (bf16[128,1536]{1,0:T(8,128)(2,1)}, bf16[128,1536]{1,0:T(8,128)(2,1)}, u32[]{:S(2)}, u32[]{:S(2)}) collective-permute-start(bf16[128,1536]{1,0:T(8,128)(2,1)} %get-tuple-element.70), channel_id=1, source_target_pairs={{0,8},{8,16},{16,24},{24,0},{1,9},{9,17},{17,25},{25,1},{2,10},{10... | collective-permute-start | bytes 1179656 | tf_op jit(solution)/shard_map/ppermute | solution.py:460
  557.9 35.7 %collective-permute-start.43 = (bf16[128,1536]{1,0:T(8,128)(2,1)}, bf16[128,1536]{1,0:T(8,128)(2,1)S(1)}, u32[]{:S(2)}, u32[]{:S(2)}) collective-permute-start(bf16[128,1536]{1,0:T(8,128)(2,1)} %get-tuple-element.71), channel_id=1, source_target_pairs={{8,0},{16,8},{24,16},{0,24},{9,1},{17,9},{25,17},{1,25},{10,2},{18... | collective-permute-start | bytes 1179656 | tf_op jit(solution)/shard_map/ppermute | solution.py:464
  562.7 20.6 %collective-permute-start.54 = (bf16[256,512]{1,0:T(8,128)(2,1)S(1)}, bf16[256,512]{1,0:T(8,128)(2,1)S(1)}, u32[]{:S(2)}, u32[]{:S(2)}) collective-permute-start(bf16[256,512]{1,0:T(8,128)(2,1)S(1)} %fusion.35), channel_id=1, source_target_pairs={{0,8},{8,16},{16,24},{24,0},{1,9},{9,17},{17,25},{25,1},{2,10},{10... | collective-permute-start | bytes 786440 | tf_op jit(solution)/shard_map/ppermute | solution.py:460
  564.3 23.9 %collective-permute-start.56 = (bf16[256,512]{1,0:T(8,128)(2,1)S(1)}, bf16[256,512]{1,0:T(8,128)(2,1)S(1)}, u32[]{:S(2)}, u32[]{:S(2)}) collective-permute-start(bf16[256,512]{1,0:T(8,128)(2,1)S(1)} %fusion.36), channel_id=1, source_target_pairs={{8,0},{16,8},{24,16},{0,24},{9,1},{17,9},{25,17},{1,25},{10,2},{18... | collective-permute-start | bytes 786440 | tf_op jit(solution)/shard_map/ppermute | solution.py:464
  583.3 51.3 %collective-permute-start.39 = (bf16[512,1024]{1,0:T(8,128)(2,1)S(1)}, bf16[512,1024]{1,0:T(8,128)(2,1)S(1)}, u32[]{:S(2)}, u32[]{:S(2)}) collective-permute-start(bf16[512,1024]{1,0:T(8,128)(2,1)S(1)} %copy-done.79), channel_id=1, source_target_pairs={{0,2},{2,0},{1,3},{3,1},{4,6},{6,4},{5,7},{7,5},{8,10},{10,8},{9,1... | collective-permute-start | bytes 3145736 | tf_op jit(solution)/shard_map/ppermute | solution.py:456
  588.2 10.0 %collective-permute-start.78 = (bf16[64,2048]{1,0:T(8,128)(2,1)S(1)}, bf16[64,2048]{1,0:T(8,128)(2,1)S(1)}, u32[]{:S(2)}, u32[]{:S(2)}) collective-permute-start(bf16[64,2048]{1,0:T(8,128)(2,1)S(1)} %fusion.75), channel_id=1, source_target_pairs={{0,0},{1,2},{2,1},{3,3},{4,4},{5,6},{6,5},{7,7},{8,8},{9,10},{10,9... | collective-permute-start | bytes 786440 | tf_op jit(solution)/shard_map/ppermute | solution.py:452
  593.6 19.8 %collective-permute-start.42 = (bf16[256,1536]{1,0:T(8,128)(2,1)S(1)}, bf16[256,1536]{1,0:T(8,128)(2,1)S(1)}, u32[]{:S(2)}, u32[]{:S(2)}) collective-permute-start(bf16[256,1536]{1,0:T(8,128)(2,1)S(1)} %fusion.2), channel_id=1, source_target_pairs={{0,8},{8,16},{16,24},{24,0},{1,9},{9,17},{17,25},{25,1},{2,10},{10... | collective-permute-start | bytes 2359304 | tf_op jit(solution)/shard_map/ppermute | solution.py:460
  597.0 36.3 %collective-permute-start.44 = (bf16[256,1536]{1,0:T(8,128)(2,1)S(1)}, bf16[256,1536]{1,0:T(8,128)(2,1)S(1)}, u32[]{:S(2)}, u32[]{:S(2)}) collective-permute-start(bf16[256,1536]{1,0:T(8,128)(2,1)S(1)} %fusion.3), channel_id=1, source_target_pairs={{8,0},{16,8},{24,16},{0,24},{9,1},{17,9},{25,17},{1,25},{10,2},{18... | collective-permute-start | bytes 2359304 | tf_op jit(solution)/shard_map/ppermute | solution.py:464
  601.7 56.9 %collective-permute-start.59 = (bf16[64,512]{1,0:T(8,128)(2,1)S(1)}, bf16[64,512]{1,0:T(8,128)(2,1)S(1)}, u32[]{:S(2)}, u32[]{:S(2)}) collective-permute-start(bf16[64,512]{1,0:T(8,128)(2,1)S(1)} %fusion.112), channel_id=1, source_target_pairs={{0,0},{1,2},{2,1},{3,3},{4,4},{5,6},{6,5},{7,7},{8,8},{9,10},{10,9... | collective-permute-start | bytes 196616 | tf_op jit(solution)/shard_map/ppermute | solution.py:452
  608.3 32.2 %collective-permute-start.67 = (bf16[32,2048]{1,0:T(8,128)(2,1)S(1)}, bf16[32,2048]{1,0:T(8,128)(2,1)S(1)}, u32[]{:S(2)}, u32[]{:S(2)}) collective-permute-start(bf16[32,2048]{1,0:T(8,128)(2,1)S(1)} %get-tuple-element.75), channel_id=1, source_target_pairs={{0,8},{8,16},{16,24},{24,0},{1,9},{9,17},{17,25},{25,1},{2,10},{10... | collective-permute-start | bytes 393224 | tf_op jit(solution)/shard_map/ppermute | solution.py:460
  613.5 27.1 %collective-permute-start.69 = (bf16[32,2048]{1,0:T(8,128)(2,1)S(1)}, bf16[32,2048]{1,0:T(8,128)(2,1)S(1)}, u32[]{:S(2)}, u32[]{:S(2)}) collective-permute-start(bf16[32,2048]{1,0:T(8,128)(2,1)S(1)} %get-tuple-element.76), channel_id=1, source_target_pairs={{8,0},{16,8},{24,16},{0,24},{9,1},{17,9},{25,17},{1,25},{10,2},{18... | collective-permute-start | bytes 393224 | tf_op jit(solution)/shard_map/ppermute | solution.py:464
  634.4 10.0 %collective-permute-start.45 = (bf16[2,64,1536]{2,1,0:T(8,128)(2,1)S(1)}, bf16[2,64,1536]{2,1,0:T(8,128)(2,1)S(1)}, u32[]{:S(2)}, u32[]{:S(2)}) collective-permute-start(bf16[2,64,1536]{2,1,0:T(8,128)(2,1)S(1)} %fusion.93), channel_id=1, source_target_pairs={{0,1},{1,0},{2,3},{3,2},{4,5},{5,4},{6,7},{7,6},{8,9},{9,8},{10,11... | collective-permute-start | bytes 1179656 | tf_op jit(solution)/shard_map/ppermute | solution.py:456
  636.4 27.2 %collective-permute-start.40 = (bf16[512,1024]{1,0:T(8,128)(2,1)S(1)}, bf16[512,1024]{1,0:T(8,128)(2,1)S(1)}, u32[]{:S(2)}, u32[]{:S(2)}) collective-permute-start(bf16[512,1024]{1,0:T(8,128)(2,1)S(1)} %add_convert_fusion.1), channel_id=1, source_target_pairs={{0,0},{1,2},{2,1},{3,3},{4,4},{5,6},{6,5},{7,7},{8,8},{9,10},{10,9... | collective-permute-start | bytes 3145736 | tf_op jit(solution)/shard_map/ppermute | solution.py:452
  640.6 9.9 %collective-permute-start.68 = (bf16[64,2048]{1,0:T(8,128)(2,1)S(1)}, bf16[64,2048]{1,0:T(8,128)(2,1)S(1)}, u32[]{:S(2)}, u32[]{:S(2)}) collective-permute-start(bf16[64,2048]{1,0:T(8,128)(2,1)S(1)} %get-tuple-element.58), channel_id=1, source_target_pairs={{0,8},{8,16},{16,24},{24,0},{1,9},{9,17},{17,25},{25,1},{2,10},{10... | collective-permute-start | bytes 786440 | tf_op jit(solution)/shard_map/ppermute | solution.py:460
  640.9 11.9 %collective-permute-start.70 = (bf16[64,2048]{1,0:T(8,128)(2,1)S(1)}, bf16[64,2048]{1,0:T(8,128)(2,1)S(1)}, u32[]{:S(2)}, u32[]{:S(2)}) collective-permute-start(bf16[64,2048]{1,0:T(8,128)(2,1)S(1)} %get-tuple-element.59), channel_id=1, source_target_pairs={{8,0},{16,8},{24,16},{0,24},{9,1},{17,9},{25,17},{1,25},{10,2},{18... | collective-permute-start | bytes 786440 | tf_op jit(solution)/shard_map/ppermute | solution.py:464
  644.5 11.0 %collective-permute-start.46 = (bf16[64,1536]{1,0:T(8,128)(2,1)S(1)}, bf16[64,1536]{1,0:T(8,128)(2,1)S(1)}, u32[]{:S(2)}, u32[]{:S(2)}) collective-permute-start(bf16[64,1536]{1,0:T(8,128)(2,1)S(1)} %fusion.105), channel_id=1, source_target_pairs={{0,4},{4,0},{1,5},{5,1},{2,6},{6,2},{3,7},{7,3},{8,12},{12,8},{9,1... | collective-permute-start | bytes 589832 | tf_op jit(solution)/shard_map/ppermute | solution.py:456
  (108 other events, 1305.0 us)

commit v3 on v2

--- a/solution.py
+++ b/solution.py
@@ -482,34 +482,44 @@
     return whole
 
 
-def gather_blocks(value, order, z, x, y):
-    done = []
-    for axis in order:
-        if axis == "z":
-            value = gather_z(value, z)
-        else:
-            place = sum(1 for name in done if "zxy".index(name) < "zxy".index(axis))
-            value = pair_up(value, swap(value, axis), {"x": x, "y": y}[axis], place)
-        done.append(axis)
+def gather_c(value, c, y, axis):
+    got = lax.ppermute(value, ("c", "y"), [(2, 0), (1, 3), (0, 1), (3, 2)])
+    cross = lax.ppermute(value, ("c", "y"), [(2, 1), (1, 2)])
+    first = jnp.where(c == y, value, got)
+    second = jnp.where(c == y, got, cross)
+    return pair_up(first, second, c, axis)
+
+
+def gather_x(value, x, axis):
+    return pair_up(value, swap(value, "x"), x, axis)
+
+
+def flat(value):
     return value.reshape(-1, value.shape[-1])
 
 
-def gather_split(value, z, x, y):
-    value = gather_z(value, z)
-    half = value.shape[-1] // 2
-    parts = []
-    for part, order in ((value[..., :half], "xy"), (value[..., half:], "yx")):
-        for step, axis in enumerate(order):
-            place = 1 if axis == "x" or step == 0 else 2
-            part = pair_up(part, swap(part, axis), {"x": x, "y": y}[axis], place)
-        parts.append(part.reshape(-1, half))
-    return parts
-
-
-def sum_pair(blocks, axis_name, own_index, axis):
-    theirs = lax.dynamic_index_in_dim(blocks, 1 - own_index, axis, keepdims=False)
-    mine = lax.dynamic_index_in_dim(blocks, own_index, axis, keepdims=False)
-    return mine.astype(F32) + swap(theirs.astype(BF), axis_name).astype(F32)
+def tie(value, *others):
+    return lax.optimization_barrier((value,) + others)[0]
+
+
+def sum_c(blocks, c, y):
+    axis = blocks.ndim - 3
+    mine = lax.dynamic_index_in_dim(blocks, c, axis, keepdims=False)
+    other = lax.dynamic_index_in_dim(blocks, 1 - c, axis, keepdims=False)
+    other_low = other.astype(BF)
+    got = lax.ppermute(
+        jnp.where(c == y, other_low, mine.astype(BF)),
+        ("c", "y"),
+        [(0, 2), (3, 1), (1, 0), (2, 3)],
+    )
+    cross = lax.ppermute(other_low, ("c", "y"), [(1, 2), (2, 1)])
+    return got.astype(F32) + jnp.where(c == y, mine, cross.astype(F32))
+
+
+def sum_x(blocks, x, axis):
+    theirs = lax.dynamic_index_in_dim(blocks, 1 - x, axis, keepdims=False)
+    mine = lax.dynamic_index_in_dim(blocks, x, axis, keepdims=False)
+    return mine.astype(F32) + swap(theirs.astype(BF), "x").astype(F32)
 
 
 def sum_ring(block_of, z):
@@ -526,30 +536,12 @@
     return block_of(z) + got_up.astype(F32) + got_down.astype(F32)
 
 
-def weight_sum(left, right, order, z, x, y):
-    width = right.shape[1]
-    if order[0] == "z":
-
-        def block_of(place):
-            return contract_rows(lax.dynamic_slice_in_dim(left, place * 256, 256, 1), right)
-
-        own = sum_ring(block_of, z).reshape(2, 2, 64, width)
-        own = sum_pair(own, "y", y, 1)
-        own = sum_pair(own, "x", x, 0)
-    else:
-
-        def half_of(x_place):
-            columns = [
-                lax.dynamic_slice_in_dim(left, step * 256 + x_place * 128, 128, 1)
-                for step in range(4)
-            ]
-            return contract_rows(jnp.concatenate(columns, axis=1), right)
-
-        theirs = swap(half_of(1 - x).astype(BF), "x")
-        own = half_of(x) + theirs.astype(F32)
-        own = sum_pair(own.reshape(4, 2, 64, width), "y", y, 1)
-        own = sum_ring(lambda place: lax.dynamic_index_in_dim(own, place, 0, keepdims=False), z)
-    return turn(own.astype(BF)).astype(F32)
+def weight_sum_z(left, right, z, x, c, y):
+    def block_of(place):
+        return contract_rows(lax.dynamic_slice_in_dim(left, place * 256, 256, 1), right)
+
+    own = sum_ring(block_of, z).reshape(2, 2, 64, right.shape[1])
+    return sum_c(sum_x(own, x, 0), c, y)
 
 
 def sum_other(value, step):
@@ -800,26 +792,32 @@
     return (value * phi, phi + value * bell * 0.3989422804014327)
 
 
-def expand_kernel(x_ref, w_ref, b_ref, act_ref, slope_ref):
-    rows = 256
-    for start in range(0, x_ref.shape[0], rows):
-        part = slice(start, start + rows)
-        value = exact(x_ref[part, :], w_ref[...], ((1,), (0,))) + b_ref[...]
-        active, slope = gelu_pair(value)
-        act_ref[part, :] = active.astype(BF)
-        slope_ref[part, :] = slope.astype(BF)
-
-
-def expand(value, weight, shift):
+def expand_kernel(left_tiles, x_ref, left_ref, right_ref, b_ref, act_ref, slope_ref):
+    def fill(w_ref):
+        rows = 256
+        for start in range(0, x_ref.shape[0], rows):
+            part = slice(start, start + rows)
+            value = exact(x_ref[part, :], w_ref[...], ((1,), (0,))) + b_ref[...]
+            active, slope = gelu_pair(value)
+            act_ref[part, :] = active.astype(BF)
+            slope_ref[part, :] = slope.astype(BF)
+
+    pl.when(pl.program_id(0) < left_tiles)(lambda: fill(left_ref))
+    pl.when(pl.program_id(0) >= left_tiles)(lambda: fill(right_ref))
+
+
+def expand(value, left, right, shift):
     count, depth = value.shape
-    width = weight.shape[1]
+    width = shift.shape[1]
     tile = 256
+    left_tiles = left.shape[1] // tile
     return pl.pallas_call(
-        expand_kernel,
+        partial(expand_kernel, left_tiles),
         grid=(width // tile,),
         in_specs=[
             pl.BlockSpec((count, depth), lambda i: (0, 0)),
-            pl.BlockSpec((depth, tile), lambda i: (0, i)),
+            pl.BlockSpec((depth, tile), lambda i: (0, jnp.minimum(i, left_tiles - 1))),
+            pl.BlockSpec((depth, tile), lambda i: (0, jnp.maximum(i - left_tiles, 0))),
             pl.BlockSpec((1, tile), lambda i: (0, i)),
         ],
         out_specs=[pl.BlockSpec((count, tile), lambda i: (0, i))] * 2,
@@ -830,7 +828,7 @@
             transcendentals=3 * count * width,
             bytes_accessed=2 * (count * depth + depth * width + 2 * count * width),
         ),
-    )(value, weight, shift)
+    )(value, left, right, shift)
 
 
 def cut_levels(raw, cuts):
@@ -997,23 +995,38 @@
     gains, shifts = ln_gain.astype(F32), ln_bias.astype(F32)
 
     half_width = w_qkv.shape[2]
+    up_wide = w_up.shape[1]
+    left_wide = (up_wide + half_width) // 2
     qkv_rows = jnp.concatenate([w_qkv[0], w_qkv[1], w_qkv[2]], axis=1)
-    full_qkv = gather_blocks(turn(qkv_rows), "xyz", z, x, y)
+    mid_rows = jnp.concatenate([w_up, w_out.T], axis=1)
+    qkv_rows = gather_c(qkv_rows, c, y, 0)
+    mid_rows = gather_z(mid_rows, z)
+    down_rows = gather_c(w_down.T, c, y, 0)
+    qkv_rows = gather_x(qkv_rows, x, 0)
+    down_rows = gather_x(down_rows, x, 0)
+    mid_left = gather_x(mid_rows[..., :left_wide], x, 1)
+    mid_right = gather_c(mid_rows[..., left_wide:], c, y, 1)
+    full_qkv = flat(gather_z(qkv_rows, z))
+    mid_left = flat(gather_c(mid_left, c, y, 2))
+    mid_right = flat(gather_x(mid_right, x, 1))
+    full_out = mid_right[:, up_wide - left_wide :]
+    full_down = flat(gather_z(down_rows, z))
     row = jnp.where(c == y, tokens, swap(tokens, "c"))
-    bias = turn(jnp.concatenate([b_qv.reshape(-1), b_up])[None].astype(F32))
-    mid_rows = turn(jnp.concatenate([w_up, w_out.T], axis=1))
-    up_wide = w_up.shape[1]
-    full_mid = gather_blocks(mid_rows, "zyx", z, x, y)
-    full_up, full_out = full_mid[:, :up_wide], full_mid[:, up_wide:]
-    full_down = gather_blocks(turn(w_down.T), "xyz", z, x, y)
+    bias = jnp.concatenate([b_qv.reshape(-1), b_up])[None].astype(F32)
+    bias = jnp.where(c == y, bias, swap(bias, "y"))
     own_cot = turn(cot)
     half_queries = NQ_ROW // 2
     chip_count = lengths.shape[0]
     query_total = chip_count * half_queries
     pairs = lax.dynamic_update_slice_in_dim(
-        jnp.zeros((1, query_total), F32), turn(pairing).astype(F32), chip * half_queries, 1
-    )
-    pairs = sum_chips(pairs, "xy01").astype(jnp.int32)
+        jnp.zeros((1, 2 * query_total), F32),
+        pairing.astype(F32),
+        ((4 * z + 2 * x + c) * 2 + y) * half_queries,
+        1,
+    )
+    pairs = sum_chips(pairs, "cxy01").reshape(chip_count, 2, half_queries)
+    pairs = lax.dynamic_index_in_dim(pairs, c, 1, keepdims=False).reshape(1, query_total)
+    pairs = pairs.astype(jnp.int32)
 
     row_lengths = lax.dynamic_index_in_dim(lengths, chip, 0, keepdims=False)
     segments = segments_of(row_lengths, token_count)
@@ -1026,6 +1039,7 @@
     )
     qkv = (dot(row, full_qkv) + qkv_bias).astype(BF)
     mixed, lse = attend(bounds, qkv, seg_col, seg_row)
+    mixed, own_cot, pairs = lax.optimization_barrier((mixed, own_cot, pairs))
 
     def row_sum(left, weight_t, transposed):
         times = contract_cols if transposed else dot
@@ -1042,7 +1056,7 @@
     )
     normed_low = normed.astype(BF)
     normed_all = jnp.concatenate([normed_low, swap(normed_low, "c")], axis=0)
-    activation, slope = expand(normed_all, full_up, bias[:, 2 * half_width :])
+    activation, slope = expand(normed_all, mid_left, mid_right, bias[:, 2 * half_width :])
     ffn_sum = row_sum(
         lambda which: activation[which * share : (which + 1) * share], full_down, True
     )
@@ -1128,14 +1142,18 @@
     grad_ffn = grad_second.astype(BF)
     down_bias = jnp.sum(grad_ffn.astype(F32), axis=0)
     grad_ffn_all = jnp.concatenate([grad_ffn, swap(grad_ffn, "c")], axis=0)
-    down_part = weight_sum(grad_ffn_all, activation, "zyx", z, x, y)
+    down_part = weight_sum_z(grad_ffn_all, activation, z, x, c, y)
     grad_up = (dot(grad_ffn_all, full_down) * slope.astype(F32)).astype(BF)
     up_bias = jnp.sum(grad_up.astype(F32), axis=0)
-    up_part = weight_sum(normed_all, grad_up, "xyz", z, x, y)
-    grad_normed = (
-        row_sum(lambda which: grad_up[which * share : (which + 1) * share], full_up, True)
-        + grad_second
-    )
+    up_part = weight_sum_z(normed_all, grad_up, z, x, c, y)
+    def normed_terms(which):
+        part = grad_up[which * share : (which + 1) * share]
+        return contract_cols(part[:, :left_wide], mid_left) + contract_cols(
+            part[:, left_wide:], mid_right[:, : up_wide - left_wide]
+        )
+
+    other_terms = swap(normed_terms(1).astype(BF), "c")
+    grad_normed = normed_terms(0) + other_terms.astype(F32) + grad_second
     gain_one = jnp.sum(grad_normed * unit_one, axis=0)
     shift_one = jnp.sum(grad_normed, axis=0)
     grad_first = norm_backward(grad_normed, unit_one, rstd_one, gains[0])
@@ -1147,10 +1165,10 @@
         jnp.concatenate([grad_attn, other_attn], axis=0),
         jnp.concatenate([other_attn, grad_attn], axis=0),
     )
-    out_part = weight_sum(grad_attn_all, mixed, "zyx", z, x, y)
+    out_part = weight_sum_z(grad_attn_all, mixed, z, x, c, y)
     grad_mixed = dot(grad_attn_all, full_out).astype(BF)
     grads, grad_sums = attend_back(bounds, qkv, mixed, grad_mixed, lse, seg_col, seg_row)
-    qkv_part = weight_sum(row, grads, "zyx", z, x, y)
+    qkv_part = weight_sum_z(row, grads, z, x, c, y)
     grad_input = turn(
         (
             row_sum(
@@ -1162,13 +1180,16 @@
         ).astype(BF)
     )
 
+    shared = jnp.stack([gain_one, gain_two, shift_one, shift_two, out_bias, down_bias])
     half_sums = jnp.concatenate(
         [grad_sums[:, 0].reshape(-1), grad_sums[:, 1].reshape(-1), up_bias]
-    ).reshape(-1, 128)
-    half_sums = sum_chips(half_sums, "xy01")
-    half_sums = jnp.where(c == y, half_sums, swap(half_sums, "c")).reshape(-1)
-    shared = jnp.stack([gain_one, gain_two, shift_one, shift_two, out_bias, down_bias])
-    shared = sum_chips(shared, "cxy01")
+    )
+    small = jnp.concatenate([shared.reshape(-1), half_sums]).reshape(-1, 128)
+    small = sum_chips(small, "xy01")
+    other_small = swap(small, "c")
+    shared_rows = 6 * width // 128
+    shared = (small[:shared_rows] + other_small[:shared_rows]).reshape(6, width)
+    half_sums = jnp.where(c == y, small[shared_rows:], other_small[shared_rows:]).reshape(-1)
     proj_half = rows_of(proj_grad, own_start, share) + swap(
         rows_of(proj_grad, other_start, share), "c"
     )

time: 680 us -> 727 us (1.069)
  waiting for transfers between devices: 213 us -> 293 us
  starting transfers between devices: 190 us -> 167 us
  local copies, waits for them, and re-layouts: 44.3 us -> 34.6 us
    ppermute x14, waiting for transfers between devices: 65.4 us -> 119 us  [up(): return lax.ppermute(value, 'z', RING_UP)]
    ppermute x14, waiting for transfers between devices: 45.1 us -> 92.9 us  [down(): return lax.ppermute(value, 'z', RING_DOWN)]
    ppermute x0 -> x16, starting transfers between devices: none -> 41.8 us  [the longest x4 15.8 us: gather_c(): got = lax.ppermute(value, ('c', 'y'), [(2, 0), (1, 3), (0, 1), (3, 2)])]
    ppermute x12 -> x3, starting transfers between devices: 39.4 us -> 6.45 us  [turn(): return lax.ppermute(value, ('c', 'y'), TURN)]
    ppermute x37 -> x30, waiting for transfers between devices: 50.2 us -> 22.3 us  [swap(): return lax.ppermute(value, axis, SWAP)]
    ppermute x37 -> x30, starting transfers between devices: 62.6 us -> 38.4 us  [swap(): return lax.ppermute(value, axis, SWAP)]
    ppermute x0 -> x16, waiting for transfers between devices: none -> 18.1 us  [the longest x4 5.43 us: sum_c(): cross = lax.ppermute(other_low, ('c', 'y'), [(1, 2), (2, 1)])]
    ppermute x4 -> x3, waiting for transfers between devices: 38.2 us -> 20.8 us  [sum_other(): return lax.ppermute(value, 'z', [(0, 1), (1, 0), (2, 3), (3, 2)])]
  transfers between devices with their start and end apart: 87 -> 85, of which waited for: 37 -> 41; matrix products, arithmetic and copies ran while one was open for 20% -> 18% of each run, Pallas kernels for 7% -> 6%
where the time goes in v3:
time: 727 us; the launch traced here: 716 us
  waiting for transfers between devices  293 us (40%)
  starting transfers between devices  167 us (23%)
  Pallas kernels  90.1 us (12%)
  matrix products  75.4 us (10%)
  other arithmetic  42.5 us (6%)
  local copies, waits for them, and re-layouts  34.6 us (5%)
  blocking collectives  11.7 us (2%)
    ppermute x14, waiting for transfers between devices, up(): return lax.ppermute(value, 'z', RING_UP)  119 us
    ppermute x14, waiting for transfers between devices, down(): return lax.ppermute(value, 'z', RING_DOWN)  92.9 us
    ppermute x14, starting transfers between devices, down(): return lax.ppermute(value, 'z', RING_DOWN)  41.5 us
    ppermute x30, starting transfers between devices, swap(): return lax.ppermute(value, axis, SWAP)  38.4 us
    dot_general x18, matrix products, contract_rows(): lax.dot_general(left, right, (((0,), (0,)), ((), ())), precision=precisio...  35 us
    pallas_call x1, Pallas kernels, attend_back(): pl.pallas_call(attend_back_kernel, grid=(pairs,), in_specs=[pl.BlockSpec(...  27.1 us
    ppermute x14, starting transfers between devices, up(): return lax.ppermute(value, 'z', RING_UP)  22.7 us
    dot_general x12, matrix products, contract_cols(): lax.dot_general(left, right, (((1,), (1,)), ((), ())), precision=precisio...  22.3 us
  transfers between devices with their start and end apart: 85, of which 41 were waited for; matrix products, arithmetic and copies ran while one was open for 18% of the time, Pallas kernels for 6%

profile of v3, /device:TPU:1, one launch (start us, length us, event | category | flops | bytes accessed | tf_op | source)
XLA Modules:
  0.0 716.3 jit_solution(14177169577903300333)
XLA Ops:
  8.6 3.2 collective-permute-start.2
  39.0 6.3 collective-permute-start.27
  50.8 3.3 collective-permute-done.28
  55.9 3.3 collective-permute-start.18
  59.2 3.6 collective-permute-done.17
  63.0 2.9 collective-permute-start.20
  67.1 3.3 collective-permute-done.29
  73.1 4.1 collective-permute-done.19
  79.7 2.9 collective-permute-start.31
  83.4 4.0 collective-permute-done.4
  87.5 14.9 %collective-permute-start.6 = (bf16[2,2,32,1536]{3,2,1,0:T(8,128)(2,1)S(1)}, bf16[2,2,32,1536]{3,2,1,0:T(8,128)(2,1)S(1)}, u32[]{:S(2)}, u32[]{:S(2)}) collective-permute-start(bf16[2,2,32,1536]{3,2,1,0:T(8,128)(2,1)S(1)} %slice.228), channel_id=1, source_target_pairs={{0,8},{8,16},{16,24},{24,0},{1,9},{9,17},{17,25},{25,1},{2,10},{10... | collective-permute-start | bytes 1179656 | tf_op jit(solution)/shard_map/ppermute | solution.py:460
  104.8 52.3 %collective-permute-done.6 = bf16[2,2,32,1536]{3,2,1,0:T(8,128)(2,1)S(1)} collective-permute-done((bf16[2,2,32,1536]{3,2,1,0:T(8,128)(2,1)S(1)}, bf16[2,2,32,1536]{3,2,1,0:T(8,128)(2,1)S(1)}, u32[]{:S(2)}, u32[]{:S(2)}) %collective-permute-start.6) | collective-permute-done | bytes 393248 | tf_op jit(solution)/shard_map/ppermute | solution.py:460
  158.8 8.9 %collective-permute-done.7 = bf16[2,2,32,1536]{3,2,1,0:T(8,128)(2,1)S(1)} collective-permute-done((bf16[2,2,32,1536]{3,2,1,0:T(8,128)(2,1)S(1)}, bf16[2,2,32,1536]{3,2,1,0:T(8,128)(2,1)S(1)}, u32[]{:S(2)}, u32[]{:S(2)}) %collective-permute-start.7) | collective-permute-done | bytes 393248 | tf_op jit(solution)/shard_map/ppermute | solution.py:464
  170.4 8.5 %collective-permute-start.25 = (bf16[4,2,64,1280]{3,2,0,1:T(8,128)(2,1)S(1)}, bf16[4,2,64,1280]{3,2,0,1:T(8,128)(2,1)}, u32[]{:S(2)}, u32[]{:S(2)}) collective-permute-start(bf16[4,2,64,1280]{3,2,0,1:T(8,128)(2,1)S(1)} %maximum_select_fusion.4), channel_id=1, source_target_pairs={{2,0},{1,3},{0,1},{3,2},{6,4},{5,7},{4,5},{7,6},{10,8},{9,11},{8,9... | collective-permute-start | bytes 3932168 | tf_op jit(solution)/shard_map/ppermute | solution.py:486
  182.8 3.6 add_convert_fusion.q_ref.k_ref.v_ref
  186.4 19.1 %shard_map.254 = (bf16[1024,512]{1,0:T(8,128)(2,1)S(1)}, f32[4,8,1024]{2,1,0:T(8,128)S(1)}) custom-call(s32[2,4]{1,0:T(2,128)S(1)} %pad_add_fusion.bounds, bf16[1024,1536]{1,0:T(8,128)(2,1)S(1)} %add_convert_fusion.q_ref.k_ref.v_ref, bf16[1024,1536]{1,0:T(8,128)(2,1)S(1)} %add_convert_fusion.q_ref.k_ref.v_ref, ...), custom_call_target="tpu_custom_call" | custom-call | flops 2147483648 | bytes 12582912 | tf_op jit(solution)/shard_map/pallas_call | solution.py:649
  205.6 7.6 %collective-permute-start.33 = (bf16[2,2,32,2048]{3,2,1,0:T(8,128)(2,1)S(1)}, bf16[2,2,32,2048]{3,2,1,0:T(8,128)(2,1)S(1)}, u32[]{:S(2)}, u32[]{:S(2)}) collective-permute-start(bf16[2,2,32,2048]{3,2,1,0:T(8,128)(2,1)S(1)} %copy-done.49), channel_id=1, source_target_pairs={{8,0},{16,8},{24,16},{0,24},{9,1},{17,9},{25,17},{1,25},{10,2},{18... | collective-permute-start | bytes 1572872 | tf_op jit(solution)/shard_map/ppermute | solution.py:464
  216.8 7.6 %collective-permute-done.33 = bf16[2,2,32,2048]{3,2,1,0:T(8,128)(2,1)S(1)} collective-permute-done((bf16[2,2,32,2048]{3,2,1,0:T(8,128)(2,1)S(1)}, bf16[2,2,32,2048]{3,2,1,0:T(8,128)(2,1)S(1)}, u32[]{:S(2)}, u32[]{:S(2)}) %collective-permute-start.33) | collective-permute-done | bytes 524320 | tf_op jit(solution)/shard_map/ppermute | solution.py:464
  232.4 18.1 %shard_map.255 = (bf16[1024,2048]{1,0:T(8,128)(2,1)S(1)}, bf16[1024,2048]{1,0:T(8,128)(2,1)S(1)}) custom-call(bf16[1024,1024]{1,0:T(8,128)(2,1)S(1)} %pad_maximum_fusion.x_ref, bf16[1024,1280]{1,0:T(8,128)(2,1)S(1)} %bitcast.275, bf16[1024,1280]{1,0:T(8,128)(2,1)S(1)} %bitcast.271, f32[1,2048]{1,0:T(1,128)S(1)} %slice.239.b_ref), custom_call_target="tpu_custom_call" | custom-call | flops 4294967296 | bytes 14680064 | tf_op jit(solution)/shard_map/pallas_call | solution.py:814
  255.7 2.8 fusion.187
  265.3 5.4 all-to-all-start
  275.4 8.2 %all-to-all-done = bf16[16,128,128]{2,1,0:T(8,128)(2,1)} async-done(((bf16[16,128,128]{2,1,0:T(8,128)(2,1)}), bf16[16,128,128]{2,1,0:T(8,128)(2,1)}, u32[]{:S(2)}, u32[]{:S(2)}) %all-to-all-start) | async-done | bytes 524320 | tf_op jit(solution)/shard_map/all_to_all | solution.py:1079
  284.6 10.0 %shard_map.256 = f32[24,2048]{1,0:T(8,128)S(1)} custom-call(bf16[2048,128]{1,0:T(8,128)(2,1)} %bitcast.51.q_ref, bf16[1024,128]{1,0:T(8,128)(2,1)S(1)} %copy-done.18, s32[1,1024]{1,0:T(1,128)S(1)} %compare_select_fusion.seg_row.seg_ref), custom_call_target="tpu_custom_call" | custom-call | flops 3221225472 | bytes 786432 | tf_op jit(solution)/shard_map/pallas_call | solution.py:868
  295.3 11.7 %all_to_all.15 = f32[16,8,128]{2,1,0:T(8,128)S(1)} all-to-all(f32[16,8,128]{2,1,0:T(8,128)S(1)} %broadcast_in_dim.129), channel_id=1, replica_groups=mesh['z'=4,'x'=2,'c'=2,'y'=2] {'z','x','y'}, dimensions={0} | all-to-all | bytes 131072 | tf_op jit(solution)/shard_map/all_to_all | solution.py:1099
  308.4 15.8 %shard_map.257 = (bf16[2048,128]{1,0:T(8,128)(2,1)S(1)}, f32[768,128]{1,0:T(8,128)S(1)}) custom-call(bf16[2048,128]{1,0:T(8,128)(2,1)} %bitcast.51.q_ref, bf16[1024,128]{1,0:T(8,128)(2,1)S(1)} %copy-done.19, s32[1,1024]{1,0:T(1,128)S(1)} %compare_select_fusion.seg_row.seg_ref, f32[24,2048]{1,0:T(8,128)S(1)} %convolution_divide_fusion.coef_ref), custom_call_target="tpu_custom_call" | custom-call | flops 4831838208 | bytes 1572864 | tf_op jit(solution)/shard_map/pallas_call | solution.py:944
  325.7 4.4 all-to-all-start.2
  332.0 8.6 %all-to-all-done.2 = bf16[16,128,128]{2,1,0:T(8,128)(2,1)} async-done(((bf16[16,128,128]{2,1,0:T(8,128)(2,1)}), bf16[16,128,128]{2,1,0:T(8,128)(2,1)}, u32[]{:S(2)}, u32[]{:S(2)}) %all-to-all-start.2) | async-done | bytes 524320 | tf_op jit(solution)/shard_map/all_to_all | solution.py:1120
  343.4 5.7 collective-permute-start.38
  353.7 7.4 %collective-permute-start.77 = (f32[512,128]{1,0:T(8,128)S(1)}, f32[512,128]{1,0:T(8,128)S(1)}, u32[]{:S(2)}, u32[]{:S(2)}) collective-permute-start(f32[512,128]{1,0:T(8,128)S(1)} %constant_dynamic-slice_fusion.1), channel_id=1, source_target_pairs={{0,2},{2,0},{1,3},{3,1},{4,6},{6,4},{5,7},{7,5},{8,10},{10,8},{9,1... | collective-permute-start | bytes 786440 | tf_op jit(solution)/shard_map/ppermute | solution.py:456
  361.1 3.1 multiply_reduce_fusion
  365.3 3.5 collective-permute-done.78
  370.5 2.9 convert_reduce_fusion.1
  375.5 2.8 collective-permute-done.80
  389.6 8.7 %convert_reduce_fusion = (f32[2048]{0:T(1024)S(1)}, bf16[1024,2048]{1,0:T(8,128)(2,1)S(1)}) fusion(bf16[1024,2048]{1,0:T(8,128)(2,1)} %copy-done.20, bf16[1024,2048]{1,0:T(8,128)(2,1)} %bitcast.287, bf16[512,1024]{1,0:T(8,128)(2,1)} %collective-permute-done.39, bf16[512,1024]{1,0:T(8,128)(2,1)} %get-tuple-element.59), kind=kOutput, calls=%fused_computation | convolution fusion | flops 4309645312 | bytes 14688256 | tf_op jit(solution)/shard_map/dot_general | solution.py:448
  409.4 3.3 collective-permute-start.65
  415.8 4.1 collective-permute-done.70
  419.9 3.3 fusion.7
  423.2 6.7 collective-permute-done.72
  429.9 3.3 fusion.8
  435.2 7.2 %collective-permute-done.63 = bf16[128,2048]{1,0:T(8,128)(2,1)S(1)} collective-permute-done((bf16[128,2048]{1,0:T(8,128)(2,1)S(1)}, bf16[128,2048]{1,0:T(8,128)(2,1)S(1)}, u32[]{:S(2)}, u32[]{:S(2)}) %collective-permute-start.63) | collective-permute-done | bytes 524320 | tf_op jit(solution)/shard_map/ppermute | solution.py:460
  444.8 7.6 %collective-permute-done.65 = bf16[128,2048]{1,0:T(8,128)(2,1)S(1)} collective-permute-done((bf16[128,2048]{1,0:T(8,128)(2,1)S(1)}, bf16[128,2048]{1,0:T(8,128)(2,1)S(1)}, u32[]{:S(2)}, u32[]{:S(2)}) %collective-permute-start.65) | collective-permute-done | bytes 524320 | tf_op jit(solution)/shard_map/ppermute | solution.py:464
  462.7 13.6 %collective-permute-done.71 = bf16[256,2048]{1,0:T(8,128)(2,1)} collective-permute-done((bf16[256,2048]{1,0:T(8,128)(2,1)}, bf16[256,2048]{1,0:T(8,128)(2,1)}, u32[]{:S(2)}, u32[]{:S(2)}) %collective-permute-start.71) | collective-permute-done | bytes 1048608 | tf_op jit(solution)/shard_map/ppermute | solution.py:460
  476.3 21.1 %collective-permute-done.73 = bf16[256,2048]{1,0:T(8,128)(2,1)} collective-permute-done((bf16[256,2048]{1,0:T(8,128)(2,1)}, bf16[256,2048]{1,0:T(8,128)(2,1)}, u32[]{:S(2)}, u32[]{:S(2)}) %collective-permute-start.73) | collective-permute-done | bytes 1048608 | tf_op jit(solution)/shard_map/ppermute | solution.py:464
  497.4 4.4 fusion.2
  502.9 18.3 %collective-permute-done.64 = bf16[256,2048]{1,0:T(8,128)(2,1)} collective-permute-done((bf16[256,2048]{1,0:T(8,128)(2,1)}, bf16[256,2048]{1,0:T(8,128)(2,1)}, u32[]{:S(2)}, u32[]{:S(2)}) %collective-permute-start.64) | collective-permute-done | bytes 1048608 | tf_op jit(solution)/shard_map/ppermute | solution.py:460
  521.2 21.1 %collective-permute-done.66 = bf16[256,2048]{1,0:T(8,128)(2,1)} collective-permute-done((bf16[256,2048]{1,0:T(8,128)(2,1)}, bf16[256,2048]{1,0:T(8,128)(2,1)}, u32[]{:S(2)}, u32[]{:S(2)}) %collective-permute-start.66) | collective-permute-done | bytes 1048608 | tf_op jit(solution)/shard_map/ppermute | solution.py:464
  542.4 2.8 fusion.1
  547.4 3.2 convolution_convert_fusion.3.grad_ref
  551.2 27.1 %shard_map.258 = (bf16[1024,1536]{1,0:T(8,128)(2,1)S(1)}, f32[4,8,128]{2,1,0:T(8,128)S(1)}) custom-call(s32[2,4]{1,0:T(2,128)S(1)} %pad_add_fusion.bounds, bf16[1024,1536]{1,0:T(8,128)(2,1)S(1)} %add_convert_fusion.q_ref.k_ref.v_ref, bf16[1024,1536]{1,0:T(8,128)(2,1)S(1)} %add_convert_fusion.q_ref.k_ref.v_ref, ...), custom_call_target="tpu_custom_call" | custom-call | flops 5368709120 | bytes 25165824 | tf_op jit(solution)/shard_map/pallas_call | solution.py:744
  581.5 2.8 fusion.18
  586.9 4.8 collective-permute-start.58
  592.7 3.3 collective-permute-start.46
  600.2 15.5 %collective-permute-done.53 = f32[72,128]{1,0:T(8,128)S(1)} collective-permute-done((f32[72,128]{1,0:T(8,128)S(1)}, f32[72,128]{1,0:T(8,128)S(1)}, u32[]{:S(2)}, u32[]{:S(2)}) %collective-permute-start.53) | collective-permute-done | bytes 36896 | tf_op jit(solution)/shard_map/ppermute | solution.py:549
  623.5 3.5 collective-permute-start.76
  635.3 4.9 collective-permute-done.57
  640.2 3.4 collective-permute-done.59
  657.8 4.3 collective-permute-start.62
  662.1 10.5 %collective-permute-done.45 = bf16[256,1536]{1,0:T(8,128)(2,1)S(1)} collective-permute-done((bf16[256,1536]{1,0:T(8,128)(2,1)S(1)}, bf16[256,1536]{1,0:T(8,128)(2,1)S(1)}, u32[]{:S(2)}, u32[]{:S(2)}) %collective-permute-start.45) | collective-permute-done | bytes 786464 | tf_op jit(solution)/shard_map/ppermute | solution.py:460
  672.6 14.5 %collective-permute-done.47 = bf16[256,1536]{1,0:T(8,128)(2,1)S(1)} collective-permute-done((bf16[256,1536]{1,0:T(8,128)(2,1)S(1)}, bf16[256,1536]{1,0:T(8,128)(2,1)S(1)}, u32[]{:S(2)}, u32[]{:S(2)}) %collective-permute-start.47) | collective-permute-done | bytes 786464 | tf_op jit(solution)/shard_map/ppermute | solution.py:464
  688.5 3.1 add_convert_fusion.1
  694.0 4.5 collective-permute-done.48
  698.7 4.8 collective-permute-start.50
  704.2 3.7 collective-permute-done.49
  707.9 4.0 collective-permute-done.50
  (470 shorter events, 199.7 us)
Async XLA Ops:
  1.8 54.0 %collective-permute-start.15 = (bf16[64,2560]{1,0:T(8,128)(2,1)S(1)}, bf16[64,2560]{1,0:T(8,128)(2,1)S(1)}, u32[]{:S(2)}, u32[]{:S(2)}) collective-permute-start(bf16[64,2560]{1,0:T(8,128)(2,1)S(1)} %pad_maximum_fusion.6), channel_id=1, source_target_pairs={{0,8},{8,16},{16,24},{24,0},{1,9},{9,17},{17,25},{25,1},{2,10},{10... | collective-permute-start | bytes 983048 | tf_op jit(solution)/shard_map/ppermute | solution.py:460
  3.9 51.9 %collective-permute-start.16 = (bf16[64,2560]{1,0:T(8,128)(2,1)S(1)}, bf16[64,2560]{1,0:T(8,128)(2,1)S(1)}, u32[]{:S(2)}, u32[]{:S(2)}) collective-permute-start(bf16[64,2560]{1,0:T(8,128)(2,1)S(1)} %pad_maximum_fusion.6), channel_id=1, source_target_pairs={{8,0},{16,8},{24,16},{0,24},{9,1},{17,9},{25,17},{1,25},{10,2},{18... | collective-permute-start | bytes 983048 | tf_op jit(solution)/shard_map/ppermute | solution.py:464
  7.7 38.4 %collective-permute-start.1 = (bf16[64,1536]{1,0:T(8,128)(2,1)}, bf16[64,1536]{1,0:T(8,128)(2,1)S(1)}, u32[]{:S(2)}, u32[]{:S(2)}) collective-permute-start(bf16[64,1536]{1,0:T(8,128)(2,1)} %pad_maximum_fusion.7), channel_id=1, source_target_pairs={{2,0},{1,3},{0,1},{3,2},{6,4},{5,7},{4,5},{7,6},{10,8},{9,11},{8,9... | collective-permute-start | bytes 589832 | tf_op jit(solution)/shard_map/ppermute | solution.py:486
  8.6 39.4 %collective-permute-start.2 = (bf16[64,1536]{1,0:T(8,128)(2,1)}, bf16[64,1536]{1,0:T(8,128)(2,1)}, u32[]{:S(2)}, u32[]{:S(2)}) collective-permute-start(bf16[64,1536]{1,0:T(8,128)(2,1)} %pad_maximum_fusion.7), channel_id=1, source_target_pairs={{2,1},{1,2},{6,5},{5,6},{10,9},{9,10},{14,13},{13,14},{18,17},{17,... | collective-permute-start | bytes 589832 | tf_op jit(solution)/shard_map/ppermute | solution.py:487
  14.2 8.1 %collective-permute-start.10 = (f32[1,128]{1,0:T(1,128)}, f32[1,128]{1,0:T(1,128)}, u32[]{:S(2)}, u32[]{:S(2)}) collective-permute-start(f32[1,128]{1,0:T(1,128)} %dynamic_update_slice.51), channel_id=1, source_target_pairs={{0,2},{2,0},{1,3},{3,1},{4,6},{6,4},{5,7},{7,5},{8,10},{10,8},{9,1... | collective-permute-start | bytes 1544 | tf_op jit(solution)/shard_map/ppermute | solution.py:456
  39.0 10.4 %collective-permute-start.27 = (bf16[64,2048]{1,0:T(8,128)(2,1)S(1)}, bf16[64,2048]{1,0:T(8,128)(2,1)S(1)}, u32[]{:S(2)}, u32[]{:S(2)}) collective-permute-start(bf16[64,2048]{1,0:T(8,128)(2,1)S(1)} %bitcast.303), channel_id=1, source_target_pairs={{2,0},{1,3},{0,1},{3,2},{6,4},{5,7},{4,5},{7,6},{10,8},{9,11},{8,9... | collective-permute-start | bytes 786440 | tf_op jit(solution)/shard_map/ppermute | solution.py:486
  48.0 134.4 %collective-permute-start = (bf16[1024,1024]{1,0:T(8,128)(2,1)}, bf16[1024,1024]{1,0:T(8,128)(2,1)S(1)}, u32[]{:S(2)}, u32[]{:S(2)}) collective-permute-start(bf16[1024,1024]{1,0:T(8,128)(2,1)} %param.15), channel_id=1, source_target_pairs={{0,2},{2,0},{1,3},{3,1},{4,6},{6,4},{5,7},{7,5},{8,10},{10,8},{9,1... | collective-permute-start | bytes 6291464 | tf_op jit(solution)/shard_map/ppermute | solution.py:456
  49.3 16.6 %collective-permute-start.3 = (bf16[2,64,1536]{2,1,0:T(8,128)(2,1)S(1)}, bf16[2,64,1536]{2,1,0:T(8,128)(2,1)S(1)}, u32[]{:S(2)}, u32[]{:S(2)}) collective-permute-start(bf16[2,64,1536]{2,1,0:T(8,128)(2,1)S(1)} %maximum_select_fusion.13), channel_id=1, source_target_pairs={{0,4},{4,0},{1,5},{5,1},{2,6},{6,2},{3,7},{7,3},{8,12},{12,8},{9,1... | collective-permute-start | bytes 1179656 | tf_op jit(solution)/shard_map/ppermute | solution.py:456
  54.2 16.2 %collective-permute-start.29 = (bf16[2,64,2048]{2,1,0:T(8,128)(2,1)S(1)}, bf16[2,64,2048]{2,1,0:T(8,128)(2,1)S(1)}, u32[]{:S(2)}, u32[]{:S(2)}) collective-permute-start(bf16[2,64,2048]{2,1,0:T(8,128)(2,1)S(1)} %maximum_select_fusion.10), channel_id=1, source_target_pairs={{0,4},{4,0},{1,5},{5,1},{2,6},{6,2},{3,7},{7,3},{8,12},{12,8},{9,1... | collective-permute-start | bytes 1572872 | tf_op jit(solution)/shard_map/ppermute | solution.py:456
  62.9 14.2 %collective-permute-start.19 = (bf16[4,64,1280]{2,1,0:T(8,128)(2,1)S(1)}, bf16[4,64,1280]{2,1,0:T(8,128)(2,1)S(1)}, u32[]{:S(2)}, u32[]{:S(2)}) collective-permute-start(bf16[4,64,1280]{2,1,0:T(8,128)(2,1)S(1)} %slice.234), channel_id=1, source_target_pairs={{2,0},{1,3},{0,1},{3,2},{6,4},{5,7},{4,5},{7,6},{10,8},{9,11},{8,9... | collective-permute-start | bytes 1966088 | tf_op jit(solution)/shard_map/ppermute | solution.py:486
  63.0 16.7 %collective-permute-start.20 = (bf16[4,64,1280]{2,1,0:T(8,128)(2,1)S(1)}, bf16[4,64,1280]{2,1,0:T(8,128)(2,1)S(1)}, u32[]{:S(2)}, u32[]{:S(2)}) collective-permute-start(bf16[4,64,1280]{2,1,0:T(8,128)(2,1)S(1)} %slice.234), channel_id=1, source_target_pairs={{2,1},{1,2},{6,5},{5,6},{10,9},{9,10},{14,13},{13,14},{18,17},{17,... | collective-permute-start | bytes 1966088 | tf_op jit(solution)/shard_map/ppermute | solution.py:487
  66.0 21.4 %collective-permute-start.4 = (bf16[2,2,64,1536]{3,2,1,0:T(8,128)(2,1)S(1)}, bf16[2,2,64,1536]{3,2,1,0:T(8,128)(2,1)S(1)}, u32[]{:S(2)}, u32[]{:S(2)}) collective-permute-start(bf16[2,2,64,1536]{3,2,1,0:T(8,128)(2,1)S(1)} %maximum_select_fusion.8), channel_id=1, source_target_pairs={{0,8},{8,16},{16,24},{24,0},{1,9},{9,17},{17,25},{25,1},{2,10},{10... | collective-permute-start | bytes 2359304 | tf_op jit(solution)/shard_map/ppermute | solution.py:460
  70.4 34.0 %collective-permute-start.5 = (bf16[2,2,64,1536]{3,2,1,0:T(8,128)(2,1)S(1)}, bf16[2,2,64,1536]{3,2,1,0:T(8,128)(2,1)S(1)}, u32[]{:S(2)}, u32[]{:S(2)}) collective-permute-start(bf16[2,2,64,1536]{3,2,1,0:T(8,128)(2,1)S(1)} %maximum_select_fusion.8), channel_id=1, source_target_pairs={{8,0},{16,8},{24,16},{0,24},{9,1},{17,9},{25,17},{1,25},{10,2},{18... | collective-permute-start | bytes 2359304 | tf_op jit(solution)/shard_map/ppermute | solution.py:464
  77.2 93.2 %collective-permute-start.30 = (bf16[2,2,64,2048]{3,2,1,0:T(8,128)(2,1)S(1)}, bf16[2,2,64,2048]{3,2,1,0:T(8,128)(2,1)S(1)}, u32[]{:S(2)}, u32[]{:S(2)}) collective-permute-start(bf16[2,2,64,2048]{3,2,1,0:T(8,128)(2,1)S(1)} %maximum_select_fusion.6), channel_id=1, source_target_pairs={{0,8},{8,16},{16,24},{24,0},{1,9},{9,17},{17,25},{25,1},{2,10},{10... | collective-permute-start | bytes 3145736 | tf_op jit(solution)/shard_map/ppermute | solution.py:460
  79.7 100.0 %collective-permute-start.31 = (bf16[2,2,64,2048]{3,2,1,0:T(8,128)(2,1)S(1)}, bf16[2,2,64,2048]{3,2,1,0:T(8,128)(2,1)S(1)}, u32[]{:S(2)}, u32[]{:S(2)}) collective-permute-start(bf16[2,2,64,2048]{3,2,1,0:T(8,128)(2,1)S(1)} %maximum_select_fusion.6), channel_id=1, source_target_pairs={{8,0},{16,8},{24,16},{0,24},{9,1},{17,9},{25,17},{1,25},{10,2},{18... | collective-permute-start | bytes 3145736 | tf_op jit(solution)/shard_map/ppermute | solution.py:464
  87.5 69.7 %collective-permute-start.6 = (bf16[2,2,32,1536]{3,2,1,0:T(8,128)(2,1)S(1)}, bf16[2,2,32,1536]{3,2,1,0:T(8,128)(2,1)S(1)}, u32[]{:S(2)}, u32[]{:S(2)}) collective-permute-start(bf16[2,2,32,1536]{3,2,1,0:T(8,128)(2,1)S(1)} %slice.228), channel_id=1, source_target_pairs={{0,8},{8,16},{16,24},{24,0},{1,9},{9,17},{17,25},{25,1},{2,10},{10... | collective-permute-start | bytes 1179656 | tf_op jit(solution)/shard_map/ppermute | solution.py:460
  104.4 65.3 %collective-permute-start.24 = (bf16[4,64,1280]{2,1,0:T(8,128)(2,1)S(1)}, bf16[4,64,1280]{2,1,0:T(8,128)(2,1)S(1)}, u32[]{:S(2)}, u32[]{:S(2)}) collective-permute-start(bf16[4,64,1280]{2,1,0:T(8,128)(2,1)S(1)} %get-tuple-element.75), channel_id=1, source_target_pairs={{0,4},{4,0},{1,5},{5,1},{2,6},{6,2},{3,7},{7,3},{8,12},{12,8},{9,1... | collective-permute-start | bytes 1966088 | tf_op jit(solution)/shard_map/ppermute | solution.py:456
  157.1 10.6 %collective-permute-start.7 = (bf16[2,2,32,1536]{3,2,1,0:T(8,128)(2,1)S(1)}, bf16[2,2,32,1536]{3,2,1,0:T(8,128)(2,1)S(1)}, u32[]{:S(2)}, u32[]{:S(2)}) collective-permute-start(bf16[2,2,32,1536]{3,2,1,0:T(8,128)(2,1)S(1)} %slice.229), channel_id=1, source_target_pairs={{8,0},{16,8},{24,16},{0,24},{9,1},{17,9},{25,17},{1,25},{10,2},{18... | collective-permute-start | bytes 1179656 | tf_op jit(solution)/shard_map/ppermute | solution.py:464
  167.7 37.9 %collective-permute-start.9 = (bf16[512,1024]{1,0:T(8,128)(2,1)}, bf16[512,1024]{1,0:T(8,128)(2,1)}, u32[]{:S(2)}, u32[]{:S(2)}) collective-permute-start(bf16[512,1024]{1,0:T(8,128)(2,1)} %param.29), channel_id=1, source_target_pairs={{0,0},{1,2},{2,1},{3,3},{4,4},{5,6},{6,5},{7,7},{8,8},{9,10},{10,9... | collective-permute-start | bytes 3145736 | tf_op jit(solution)/shard_map/ppermute | solution.py:452
  169.7 43.5 %collective-permute-start.21 = (bf16[4,2,64,1280]{3,2,1,0:T(8,128)(2,1)S(1)}, bf16[4,2,64,1280]{3,2,1,0:T(8,128)(2,1)}, u32[]{:S(2)}, u32[]{:S(2)}) collective-permute-start(bf16[4,2,64,1280]{3,2,1,0:T(8,128)(2,1)S(1)} %maximum_select_fusion.3), channel_id=1, source_target_pairs={{0,4},{4,0},{1,5},{5,1},{2,6},{6,2},{3,7},{7,3},{8,12},{12,8},{9,1... | collective-permute-start | bytes 3932168 | tf_op jit(solution)/shard_map/ppermute | solution.py:456
  170.4 57.5 %collective-permute-start.25 = (bf16[4,2,64,1280]{3,2,0,1:T(8,128)(2,1)S(1)}, bf16[4,2,64,1280]{3,2,0,1:T(8,128)(2,1)}, u32[]{:S(2)}, u32[]{:S(2)}) collective-permute-start(bf16[4,2,64,1280]{3,2,0,1:T(8,128)(2,1)S(1)} %maximum_select_fusion.4), channel_id=1, source_target_pairs={{2,0},{1,3},{0,1},{3,2},{6,4},{5,7},{4,5},{7,6},{10,8},{9,11},{8,9... | collective-permute-start | bytes 3932168 | tf_op jit(solution)/shard_map/ppermute | solution.py:486
  179.7 48.1 %collective-permute-start.26 = (bf16[4,2,64,1280]{3,2,0,1:T(8,128)(2,1)S(1)}, bf16[4,2,64,1280]{3,2,0,1:T(8,128)(2,1)}, u32[]{:S(2)}, u32[]{:S(2)}) collective-permute-start(bf16[4,2,64,1280]{3,2,0,1:T(8,128)(2,1)S(1)} %maximum_select_fusion.4), channel_id=1, source_target_pairs={{2,1},{1,2},{6,5},{5,6},{10,9},{9,10},{14,13},{13,14},{18,17},{17,... | collective-permute-start | bytes 3932168 | tf_op jit(solution)/shard_map/ppermute | solution.py:487
  182.4 34.4 %collective-permute-start.32 = (bf16[2,2,32,2048]{3,2,1,0:T(8,128)(2,1)}, bf16[2,2,32,2048]{3,2,1,0:T(8,128)(2,1)S(1)}, u32[]{:S(2)}, u32[]{:S(2)}) collective-permute-start(bf16[2,2,32,2048]{3,2,1,0:T(8,128)(2,1)} %slice.240), channel_id=1, source_target_pairs={{0,8},{8,16},{16,24},{24,0},{1,9},{9,17},{17,25},{25,1},{2,10},{10... | collective-permute-start | bytes 1572872 | tf_op jit(solution)/shard_map/ppermute | solution.py:460
  205.6 18.8 %collective-permute-start.33 = (bf16[2,2,32,2048]{3,2,1,0:T(8,128)(2,1)S(1)}, bf16[2,2,32,2048]{3,2,1,0:T(8,128)(2,1)S(1)}, u32[]{:S(2)}, u32[]{:S(2)}) collective-permute-start(bf16[2,2,32,2048]{3,2,1,0:T(8,128)(2,1)S(1)} %copy-done.49), channel_id=1, source_target_pairs={{8,0},{16,8},{24,16},{0,24},{9,1},{17,9},{25,17},{1,25},{10,2},{18... | collective-permute-start | bytes 1572872 | tf_op jit(solution)/shard_map/ppermute | solution.py:464
  216.0 8.6 %collective-permute-start.22 = (bf16[512,1024]{1,0:T(8,128)(2,1)S(1)}, bf16[512,1024]{1,0:T(8,128)(2,1)S(1)}, u32[]{:S(2)}, u32[]{:S(2)}) collective-permute-start(bf16[512,1024]{1,0:T(8,128)(2,1)S(1)} %convolution_convert_fusion.4), channel_id=1, source_target_pairs={{0,2},{2,0},{1,3},{3,1},{4,6},{6,4},{5,7},{7,5},{8,10},{10,8},{9,1... | collective-permute-start | bytes 3145736 | tf_op jit(solution)/shard_map/ppermute | solution.py:456
  265.3 18.3 %all-to-all-start = ((bf16[16,128,128]{2,1,0:T(8,128)(2,1)}), bf16[16,128,128]{2,1,0:T(8,128)(2,1)}, u32[]{:S(2)}, u32[]{:S(2)}) async-start(bf16[16,128,128]{2,1,0:T(8,128)(2,1)} %broadcast_in_dim.128), calls=%async_computation | async-start | bytes 1048576 | tf_op jit(solution)/shard_map/all_to_all | solution.py:1079
  325.7 14.9 %all-to-all-start.2 = ((bf16[16,128,128]{2,1,0:T(8,128)(2,1)}), bf16[16,128,128]{2,1,0:T(8,128)(2,1)}, u32[]{:S(2)}, u32[]{:S(2)}) async-start(bf16[16,128,128]{2,1,0:T(8,128)(2,1)} %bitcast.278), calls=%async_computation.2 | async-start | bytes 1048576 | tf_op jit(solution)/shard_map/all_to_all | solution.py:1120
  349.2 34.6 %collective-permute-start.35 = (bf16[512,1024]{1,0:T(8,128)(2,1)}, bf16[512,1024]{1,0:T(8,128)(2,1)}, u32[]{:S(2)}, u32[]{:S(2)}) collective-permute-start(bf16[512,1024]{1,0:T(8,128)(2,1)} %copy-done.27), channel_id=1, source_target_pairs={{0,0},{1,2},{2,1},{3,3},{4,4},{5,6},{6,5},{7,7},{8,8},{9,10},{10,9... | collective-permute-start | bytes 3145736 | tf_op jit(solution)/shard_map/ppermute | solution.py:452
  353.7 10.5 %collective-permute-start.77 = (f32[512,128]{1,0:T(8,128)S(1)}, f32[512,128]{1,0:T(8,128)S(1)}, u32[]{:S(2)}, u32[]{:S(2)}) collective-permute-start(f32[512,128]{1,0:T(8,128)S(1)} %constant_dynamic-slice_fusion.1), channel_id=1, source_target_pairs={{0,2},{2,0},{1,3},{3,1},{4,6},{6,4},{5,7},{7,5},{8,10},{10,8},{9,1... | collective-permute-start | bytes 786440 | tf_op jit(solution)/shard_map/ppermute | solution.py:456
  373.4 16.2 %collective-permute-start.39 = (bf16[512,1024]{1,0:T(8,128)(2,1)}, bf16[512,1024]{1,0:T(8,128)(2,1)}, u32[]{:S(2)}, u32[]{:S(2)}) collective-permute-start(bf16[512,1024]{1,0:T(8,128)(2,1)} %get-tuple-element.59), channel_id=1, source_target_pairs={{0,2},{2,0},{1,3},{3,1},{4,6},{6,4},{5,7},{7,5},{8,10},{10,8},{9,1... | collective-permute-start | bytes 3145736 | tf_op jit(solution)/shard_map/ppermute | solution.py:456
  387.1 26.6 %collective-permute-start.82 = (f32[512,128]{1,0:T(8,128)S(1)}, f32[512,128]{1,0:T(8,128)S(1)}, u32[]{:S(2)}, u32[]{:S(2)}) collective-permute-start(f32[512,128]{1,0:T(8,128)S(1)} %convert_add_fusion), channel_id=1, source_target_pairs={{0,2},{2,0},{1,3},{3,1},{4,6},{6,4},{5,7},{7,5},{8,10},{10,8},{9,1... | collective-permute-start | bytes 786440 | tf_op jit(solution)/shard_map/ppermute | solution.py:456
  404.5 15.4 %collective-permute-start.70 = (bf16[128,2048]{1,0:T(8,128)(2,1)S(1)}, bf16[128,2048]{1,0:T(8,128)(2,1)S(1)}, u32[]{:S(2)}, u32[]{:S(2)}) collective-permute-start(bf16[128,2048]{1,0:T(8,128)(2,1)S(1)} %get-tuple-element.80), channel_id=1, source_target_pairs={{0,8},{8,16},{16,24},{24,0},{1,9},{9,17},{17,25},{25,1},{2,10},{10... | collective-permute-start | bytes 1572872 | tf_op jit(solution)/shard_map/ppermute | solution.py:460
  405.3 24.6 %collective-permute-start.72 = (bf16[128,2048]{1,0:T(8,128)(2,1)S(1)}, bf16[128,2048]{1,0:T(8,128)(2,1)S(1)}, u32[]{:S(2)}, u32[]{:S(2)}) collective-permute-start(bf16[128,2048]{1,0:T(8,128)(2,1)S(1)} %get-tuple-element.81), channel_id=1, source_target_pairs={{8,0},{16,8},{24,16},{0,24},{9,1},{17,9},{25,17},{1,25},{10,2},{18... | collective-permute-start | bytes 1572872 | tf_op jit(solution)/shard_map/ppermute | solution.py:464
  409.4 33.0 %collective-permute-start.63 = (bf16[128,2048]{1,0:T(8,128)(2,1)S(1)}, bf16[128,2048]{1,0:T(8,128)(2,1)S(1)}, u32[]{:S(2)}, u32[]{:S(2)}) collective-permute-start(bf16[128,2048]{1,0:T(8,128)(2,1)S(1)} %get-tuple-element.82), channel_id=1, source_target_pairs={{0,8},{8,16},{16,24},{24,0},{1,9},{9,17},{17,25},{25,1},{2,10},{10... | collective-permute-start | bytes 1572872 | tf_op jit(solution)/shard_map/ppermute | solution.py:460
  409.4 42.9 %collective-permute-start.65 = (bf16[128,2048]{1,0:T(8,128)(2,1)S(1)}, bf16[128,2048]{1,0:T(8,128)(2,1)S(1)}, u32[]{:S(2)}, u32[]{:S(2)}) collective-permute-start(bf16[128,2048]{1,0:T(8,128)(2,1)S(1)} %get-tuple-element.83), channel_id=1, source_target_pairs={{8,0},{16,8},{24,16},{0,24},{9,1},{17,9},{25,17},{1,25},{10,2},{18... | collective-permute-start | bytes 1572872 | tf_op jit(solution)/shard_map/ppermute | solution.py:464
  413.7 42.9 %collective-permute-start.40 = (bf16[512,1024]{1,0:T(8,128)(2,1)S(1)}, bf16[512,1024]{1,0:T(8,128)(2,1)S(1)}, u32[]{:S(2)}, u32[]{:S(2)}) collective-permute-start(bf16[512,1024]{1,0:T(8,128)(2,1)S(1)} %add_convert_fusion.2), channel_id=1, source_target_pairs={{0,2},{2,0},{1,3},{3,1},{4,6},{6,4},{5,7},{7,5},{8,10},{10,8},{9,1... | collective-permute-start | bytes 3145736 | tf_op jit(solution)/shard_map/ppermute | solution.py:456
  423.2 53.1 %collective-permute-start.71 = (bf16[256,2048]{1,0:T(8,128)(2,1)}, bf16[256,2048]{1,0:T(8,128)(2,1)}, u32[]{:S(2)}, u32[]{:S(2)}) collective-permute-start(bf16[256,2048]{1,0:T(8,128)(2,1)} %fusion.7), channel_id=1, source_target_pairs={{0,8},{8,16},{16,24},{24,0},{1,9},{9,17},{17,25},{25,1},{2,10},{10... | collective-permute-start | bytes 3145736 | tf_op jit(solution)/shard_map/ppermute | solution.py:460
  433.2 64.2 %collective-permute-start.73 = (bf16[256,2048]{1,0:T(8,128)(2,1)}, bf16[256,2048]{1,0:T(8,128)(2,1)}, u32[]{:S(2)}, u32[]{:S(2)}) collective-permute-start(bf16[256,2048]{1,0:T(8,128)(2,1)} %fusion.8), channel_id=1, source_target_pairs={{8,0},{16,8},{24,16},{0,24},{9,1},{17,9},{25,17},{1,25},{10,2},{18... | collective-permute-start | bytes 3145736 | tf_op jit(solution)/shard_map/ppermute | solution.py:464
  444.7 76.5 %collective-permute-start.64 = (bf16[256,2048]{1,0:T(8,128)(2,1)}, bf16[256,2048]{1,0:T(8,128)(2,1)}, u32[]{:S(2)}, u32[]{:S(2)}) collective-permute-start(bf16[256,2048]{1,0:T(8,128)(2,1)} %fusion.5), channel_id=1, source_target_pairs={{0,8},{8,16},{16,24},{24,0},{1,9},{9,17},{17,25},{25,1},{2,10},{10... | collective-permute-start | bytes 3145736 | tf_op jit(solution)/shard_map/ppermute | solution.py:460
  454.6 87.7 %collective-permute-start.66 = (bf16[256,2048]{1,0:T(8,128)(2,1)}, bf16[256,2048]{1,0:T(8,128)(2,1)}, u32[]{:S(2)}, u32[]{:S(2)}) collective-permute-start(bf16[256,2048]{1,0:T(8,128)(2,1)} %fusion.6), channel_id=1, source_target_pairs={{8,0},{16,8},{24,16},{0,24},{9,1},{17,9},{25,17},{1,25},{10,2},{18... | collective-permute-start | bytes 3145736 | tf_op jit(solution)/shard_map/ppermute | solution.py:464
  461.1 85.2 %collective-permute-start.41 = (bf16[512,1024]{1,0:T(8,128)(2,1)}, bf16[512,1024]{1,0:T(8,128)(2,1)S(1)}, u32[]{:S(2)}, u32[]{:S(2)}) collective-permute-start(bf16[512,1024]{1,0:T(8,128)(2,1)} %get-tuple-element.62), channel_id=1, source_target_pairs={{0,2},{2,0},{1,3},{3,1},{4,6},{6,4},{5,7},{7,5},{8,10},{10,8},{9,1... | collective-permute-start | bytes 3145736 | tf_op jit(solution)/shard_map/ppermute | solution.py:456
  501.9 90.7 %collective-permute-start.74 = (bf16[2,64,2048]{2,1,0:T(8,128)(2,1)S(1)}, bf16[2,64,2048]{2,1,0:T(8,128)(2,1)S(1)}, u32[]{:S(2)}, u32[]{:S(2)}) collective-permute-start(bf16[2,64,2048]{2,1,0:T(8,128)(2,1)S(1)} %fusion.50), channel_id=1, source_target_pairs={{0,4},{4,0},{1,5},{5,1},{2,6},{6,2},{3,7},{7,3},{8,12},{12,8},{9,1... | collective-permute-start | bytes 1572872 | tf_op jit(solution)/shard_map/ppermute | solution.py:456
  545.3 47.4 %collective-permute-start.67 = (bf16[2,64,2048]{2,1,0:T(8,128)(2,1)S(1)}, bf16[2,64,2048]{2,1,0:T(8,128)(2,1)S(1)}, u32[]{:S(2)}, u32[]{:S(2)}) collective-permute-start(bf16[2,64,2048]{2,1,0:T(8,128)(2,1)S(1)} %fusion.49), channel_id=1, source_target_pairs={{0,4},{4,0},{1,5},{5,1},{2,6},{6,2},{3,7},{7,3},{8,12},{12,8},{9,1... | collective-permute-start | bytes 1572872 | tf_op jit(solution)/shard_map/ppermute | solution.py:456
  584.4 11.8 %collective-permute-start.51 = (f32[72,128]{1,0:T(8,128)S(1)}, f32[72,128]{1,0:T(8,128)S(1)}, u32[]{:S(2)}, u32[]{:S(2)}) collective-permute-start(f32[72,128]{1,0:T(8,128)S(1)} %maximum_bitcast_fusion.3), channel_id=1, source_target_pairs={{0,4},{4,0},{1,5},{5,1},{2,6},{6,2},{3,7},{7,3},{8,12},{12,8},{9,1... | collective-permute-start | bytes 110600 | tf_op jit(solution)/shard_map/ppermute | solution.py:456
  584.9 31.5 %collective-permute-start.56 = (bf16[128,512]{1,0:T(8,128)(2,1)S(1)}, bf16[128,512]{1,0:T(8,128)(2,1)S(1)}, u32[]{:S(2)}, u32[]{:S(2)}) collective-permute-start(bf16[128,512]{1,0:T(8,128)(2,1)S(1)} %get-tuple-element.99), channel_id=1, source_target_pairs={{0,8},{8,16},{16,24},{24,0},{1,9},{9,17},{17,25},{25,1},{2,10},{10... | collective-permute-start | bytes 393224 | tf_op jit(solution)/shard_map/ppermute | solution.py:460
  586.9 35.1 %collective-permute-start.58 = (bf16[128,512]{1,0:T(8,128)(2,1)S(1)}, bf16[128,512]{1,0:T(8,128)(2,1)S(1)}, u32[]{:S(2)}, u32[]{:S(2)}) collective-permute-start(bf16[128,512]{1,0:T(8,128)(2,1)S(1)} %get-tuple-element.100), channel_id=1, source_target_pairs={{8,0},{16,8},{24,16},{0,24},{9,1},{17,9},{25,17},{1,25},{10,2},{18... | collective-permute-start | bytes 393224 | tf_op jit(solution)/shard_map/ppermute | solution.py:464
  592.6 55.0 %collective-permute-start.44 = (bf16[128,1536]{1,0:T(8,128)(2,1)}, bf16[128,1536]{1,0:T(8,128)(2,1)}, u32[]{:S(2)}, u32[]{:S(2)}) collective-permute-start(bf16[128,1536]{1,0:T(8,128)(2,1)} %get-tuple-element.84), channel_id=1, source_target_pairs={{0,8},{8,16},{16,24},{24,0},{1,9},{9,17},{17,25},{25,1},{2,10},{10... | collective-permute-start | bytes 1179656 | tf_op jit(solution)/shard_map/ppermute | solution.py:460
  592.7 58.6 %collective-permute-start.46 = (bf16[128,1536]{1,0:T(8,128)(2,1)}, bf16[128,1536]{1,0:T(8,128)(2,1)}, u32[]{:S(2)}, u32[]{:S(2)}) collective-permute-start(bf16[128,1536]{1,0:T(8,128)(2,1)} %get-tuple-element.85), channel_id=1, source_target_pairs={{8,0},{16,8},{24,16},{0,24},{9,1},{17,9},{25,17},{1,25},{10,2},{18... | collective-permute-start | bytes 1179656 | tf_op jit(solution)/shard_map/ppermute | solution.py:464
  599.4 16.4 %collective-permute-start.53 = (f32[72,128]{1,0:T(8,128)S(1)}, f32[72,128]{1,0:T(8,128)S(1)}, u32[]{:S(2)}, u32[]{:S(2)}) collective-permute-start(f32[72,128]{1,0:T(8,128)S(1)} %fusion.226), channel_id=1, source_target_pairs={{0,8},{8,0},{16,24},{24,16},{1,9},{9,1},{17,25},{25,17},{2,10},{10... | collective-permute-start | bytes 110600 | tf_op jit(solution)/shard_map/ppermute | solution.py:549
  615.8 72.7 %collective-permute-start.42 = (bf16[512,1024]{1,0:T(8,128)(2,1)}, bf16[512,1024]{1,0:T(8,128)(2,1)}, u32[]{:S(2)}, u32[]{:S(2)}) collective-permute-start(bf16[512,1024]{1,0:T(8,128)(2,1)} %fusion.18), channel_id=1, source_target_pairs={{0,2},{2,0},{1,3},{3,1},{4,6},{6,4},{5,7},{7,5},{8,10},{10,8},{9,1... | collective-permute-start | bytes 3145736 | tf_op jit(solution)/shard_map/ppermute | solution.py:456
  621.1 9.1 %collective-permute-start.75 = (bf16[64,2048]{1,0:T(8,128)(2,1)}, bf16[64,2048]{1,0:T(8,128)(2,1)}, u32[]{:S(2)}, u32[]{:S(2)}) collective-permute-start(bf16[64,2048]{1,0:T(8,128)(2,1)} %get-tuple-element.52), channel_id=1, source_target_pairs={{0,2},{3,1},{1,0},{2,3},{4,6},{7,5},{5,4},{6,7},{8,10},{11,9},{9,8... | collective-permute-start | bytes 786440 | tf_op jit(solution)/shard_map/ppermute | solution.py:510
  630.2 10.0 %collective-permute-start.57 = (bf16[256,512]{1,0:T(8,128)(2,1)}, bf16[256,512]{1,0:T(8,128)(2,1)S(1)}, u32[]{:S(2)}, u32[]{:S(2)}) collective-permute-start(bf16[256,512]{1,0:T(8,128)(2,1)} %fusion.35), channel_id=1, source_target_pairs={{0,8},{8,16},{16,24},{24,0},{1,9},{9,17},{17,25},{25,1},{2,10},{10... | collective-permute-start | bytes 786440 | tf_op jit(solution)/shard_map/ppermute | solution.py:460
  631.5 12.0 %collective-permute-start.59 = (bf16[256,512]{1,0:T(8,128)(2,1)}, bf16[256,512]{1,0:T(8,128)(2,1)S(1)}, u32[]{:S(2)}, u32[]{:S(2)}) collective-permute-start(bf16[256,512]{1,0:T(8,128)(2,1)} %fusion.36), channel_id=1, source_target_pairs={{8,0},{16,8},{24,16},{0,24},{9,1},{17,9},{25,17},{1,25},{10,2},{18... | collective-permute-start | bytes 786440 | tf_op jit(solution)/shard_map/ppermute | solution.py:464
  640.2 14.2 %collective-permute-start.68 = (bf16[64,2048]{1,0:T(8,128)(2,1)}, bf16[64,2048]{1,0:T(8,128)(2,1)S(1)}, u32[]{:S(2)}, u32[]{:S(2)}) collective-permute-start(bf16[64,2048]{1,0:T(8,128)(2,1)} %get-tuple-element.54), channel_id=1, source_target_pairs={{0,2},{3,1},{1,0},{2,3},{4,6},{7,5},{5,4},{6,7},{8,10},{11,9},{9,8... | collective-permute-start | bytes 786440 | tf_op jit(solution)/shard_map/ppermute | solution.py:510
  643.6 13.2 %collective-permute-start.69 = (bf16[64,2048]{1,0:T(8,128)(2,1)S(1)}, bf16[64,2048]{1,0:T(8,128)(2,1)S(1)}, u32[]{:S(2)}, u32[]{:S(2)}) collective-permute-start(bf16[64,2048]{1,0:T(8,128)(2,1)S(1)} %get-tuple-element.55), channel_id=1, source_target_pairs={{1,2},{2,1},{5,6},{6,5},{9,10},{10,9},{13,14},{14,13},{17,18},{18,... | collective-permute-start | bytes 786440 | tf_op jit(solution)/shard_map/ppermute | solution.py:515
  647.7 10.0 %collective-permute-start.60 = (bf16[2,64,512]{2,1,0:T(8,128)(2,1)S(1)}, bf16[2,64,512]{2,1,0:T(8,128)(2,1)S(1)}, u32[]{:S(2)}, u32[]{:S(2)}) collective-permute-start(bf16[2,64,512]{2,1,0:T(8,128)(2,1)S(1)} %fusion.101), channel_id=1, source_target_pairs={{0,4},{4,0},{1,5},{5,1},{2,6},{6,2},{3,7},{7,3},{8,12},{12,8},{9,1... | collective-permute-start | bytes 393224 | tf_op jit(solution)/shard_map/ppermute | solution.py:456
  651.3 21.2 %collective-permute-start.45 = (bf16[256,1536]{1,0:T(8,128)(2,1)S(1)}, bf16[256,1536]{1,0:T(8,128)(2,1)S(1)}, u32[]{:S(2)}, u32[]{:S(2)}) collective-permute-start(bf16[256,1536]{1,0:T(8,128)(2,1)S(1)} %fusion.3), channel_id=1, source_target_pairs={{0,8},{8,16},{16,24},{24,0},{1,9},{9,17},{17,25},{25,1},{2,10},{10... | collective-permute-start | bytes 2359304 | tf_op jit(solution)/shard_map/ppermute | solution.py:460
  654.4 32.6 %collective-permute-start.47 = (bf16[256,1536]{1,0:T(8,128)(2,1)S(1)}, bf16[256,1536]{1,0:T(8,128)(2,1)S(1)}, u32[]{:S(2)}, u32[]{:S(2)}) collective-permute-start(bf16[256,1536]{1,0:T(8,128)(2,1)S(1)} %fusion.4), channel_id=1, source_target_pairs={{8,0},{16,8},{24,16},{0,24},{9,1},{17,9},{25,17},{1,25},{10,2},{18... | collective-permute-start | bytes 2359304 | tf_op jit(solution)/shard_map/ppermute | solution.py:464
  657.7 45.8 %collective-permute-start.61 = (bf16[64,512]{1,0:T(8,128)(2,1)S(1)}, bf16[64,512]{1,0:T(8,128)(2,1)S(1)}, u32[]{:S(2)}, u32[]{:S(2)}) collective-permute-start(bf16[64,512]{1,0:T(8,128)(2,1)S(1)} %get-tuple-element.56), channel_id=1, source_target_pairs={{0,2},{3,1},{1,0},{2,3},{4,6},{7,5},{5,4},{6,7},{8,10},{11,9},{9,8... | collective-permute-start | bytes 196616 | tf_op jit(solution)/shard_map/ppermute | solution.py:510
  657.8 45.7 %collective-permute-start.62 = (bf16[64,512]{1,0:T(8,128)(2,1)S(1)}, bf16[64,512]{1,0:T(8,128)(2,1)S(1)}, u32[]{:S(2)}, u32[]{:S(2)}) collective-permute-start(bf16[64,512]{1,0:T(8,128)(2,1)S(1)} %get-tuple-element.57), channel_id=1, source_target_pairs={{1,2},{2,1},{5,6},{6,5},{9,10},{10,9},{13,14},{14,13},{17,18},{18,... | collective-permute-start | bytes 196616 | tf_op jit(solution)/shard_map/ppermute | solution.py:515
  688.2 10.3 %collective-permute-start.48 = (bf16[2,64,1536]{2,1,0:T(8,128)(2,1)S(1)}, bf16[2,64,1536]{2,1,0:T(8,128)(2,1)S(1)}, u32[]{:S(2)}, u32[]{:S(2)}) collective-permute-start(bf16[2,64,1536]{2,1,0:T(8,128)(2,1)S(1)} %fusion.83), channel_id=1, source_target_pairs={{0,4},{4,0},{1,5},{5,1},{2,6},{6,2},{3,7},{7,3},{8,12},{12,8},{9,1... | collective-permute-start | bytes 1179656 | tf_op jit(solution)/shard_map/ppermute | solution.py:456
  691.6 21.2 %collective-permute-start.43 = (bf16[512,1024]{1,0:T(8,128)(2,1)S(1)}, bf16[512,1024]{1,0:T(8,128)(2,1)S(1)}, u32[]{:S(2)}, u32[]{:S(2)}) collective-permute-start(bf16[512,1024]{1,0:T(8,128)(2,1)S(1)} %add_convert_fusion.1), channel_id=1, source_target_pairs={{0,0},{1,2},{2,1},{3,3},{4,4},{5,6},{6,5},{7,7},{8,8},{9,10},{10,9... | collective-permute-start | bytes 3145736 | tf_op jit(solution)/shard_map/ppermute | solution.py:452
  698.7 9.2 %collective-permute-start.49 = (bf16[64,1536]{1,0:T(8,128)(2,1)S(1)}, bf16[64,1536]{1,0:T(8,128)(2,1)S(1)}, u32[]{:S(2)}, u32[]{:S(2)}) collective-permute-start(bf16[64,1536]{1,0:T(8,128)(2,1)S(1)} %get-tuple-element.64), channel_id=1, source_target_pairs={{0,2},{3,1},{1,0},{2,3},{4,6},{7,5},{5,4},{6,7},{8,10},{11,9},{9,8... | collective-permute-start | bytes 589832 | tf_op jit(solution)/shard_map/ppermute | solution.py:510
  698.7 13.2 %collective-permute-start.50 = (bf16[64,1536]{1,0:T(8,128)(2,1)S(1)}, bf16[64,1536]{1,0:T(8,128)(2,1)S(1)}, u32[]{:S(2)}, u32[]{:S(2)}) collective-permute-start(bf16[64,1536]{1,0:T(8,128)(2,1)S(1)} %get-tuple-element.65), channel_id=1, source_target_pairs={{1,2},{2,1},{5,6},{6,5},{9,10},{10,9},{13,14},{14,13},{17,18},{18,... | collective-permute-start | bytes 589832 | tf_op jit(solution)/shard_map/ppermute | solution.py:515
  (97 other events, 1436.8 us)

commit v4 on v3

--- a/solution.py
+++ b/solution.py
@@ -438,8 +438,8 @@
 
 SWAP = [(0, 1), (1, 0)]
 TURN = [(0, 0), (1, 2), (2, 1), (3, 3)]
-RING_UP = [(0, 1), (1, 2), (2, 3), (3, 0)]
-RING_DOWN = [(1, 0), (2, 1), (3, 2), (0, 3)]
+FAR = [(0, 3), (3, 0), (1, 2), (2, 1)]
+NEAR = [(0, 1), (1, 0), (2, 3), (3, 2)]
 BF = jnp.bfloat16
 F32 = jnp.float32
 
@@ -454,14 +454,6 @@
 
 def swap(value, axis):
     return lax.ppermute(value, axis, SWAP)
-
-
-def up(value):
-    return lax.ppermute(value, "z", RING_UP)
-
-
-def down(value):
-    return lax.ppermute(value, "z", RING_DOWN)
 
 
 def pair_up(first, second, own_index, axis):
@@ -470,16 +462,18 @@
     )
 
 
-def gather_z(value, z):
-    below, above = up(value), down(value)
-    half = value.shape[-2] // 2
-    far_low = up(below[..., :half, :])
-    far_high = down(above[..., half:, :])
-    far = jnp.concatenate([far_low, far_high], axis=-2)
-    whole = jnp.zeros((4,) + value.shape, value.dtype)
-    for offset, part in ((0, value), (3, below), (1, above), (2, far)):
-        whole = lax.dynamic_update_index_in_dim(whole, part, (z + offset) % 4, 0)
-    return whole
+def gather_far(value, z):
+    far = lax.ppermute(value, "z", FAR)
+    return jnp.where(z < 2, jnp.stack([value, far]), jnp.stack([far, value]))
+
+
+def gather_near(pair, z):
+    other = lax.ppermute(pair, "z", NEAR)
+    return jnp.where(
+        (z == 0) | (z == 3),
+        jnp.stack([pair[0], other[0], other[1], pair[1]]),
+        jnp.stack([other[0], pair[0], pair[1], other[1]]),
+    )
 
 
 def gather_c(value, c, y, axis):
@@ -494,8 +488,15 @@
     return pair_up(value, swap(value, "x"), x, axis)
 
 
-def flat(value):
-    return value.reshape(-1, value.shape[-1])
+def gather_first(value, x, c, y):
+    half = value.shape[1] // 2
+    return (gather_x(value[:, :half], x, 1), gather_c(value[:, half:], c, y, 1))
+
+
+def gather_last(parts, x, c, y):
+    left = gather_c(parts[0], c, y, 2)
+    right = gather_x(parts[1], x, 1)
+    return jnp.concatenate([left, right], axis=3).reshape(-1, left.shape[-1])
 
 
 def tie(value, *others):
@@ -513,7 +514,7 @@
         [(0, 2), (3, 1), (1, 0), (2, 3)],
     )
     cross = lax.ppermute(other_low, ("c", "y"), [(1, 2), (2, 1)])
-    return got.astype(F32) + jnp.where(c == y, mine, cross.astype(F32))
+    return got.astype(F32) + jnp.where(c == y, mine.astype(F32), cross.astype(F32))
 
 
 def sum_x(blocks, x, axis):
@@ -522,33 +523,30 @@
     return mine.astype(F32) + swap(theirs.astype(BF), "x").astype(F32)
 
 
-def sum_ring(block_of, z):
-    far = block_of((z + 2) % 4).astype(BF)
-    half = far.shape[0] // 2
-    from_below = up(far[:half])
-    from_above = down(far[half:])
-    pad = ((0, half),) + ((0, 0),) * (far.ndim - 1)
-    pad_high = ((half, 0),) + ((0, 0),) * (far.ndim - 1)
-    after = block_of((z + 1) % 4) + jnp.pad(from_below, pad).astype(F32)
-    before = block_of((z + 3) % 4) + jnp.pad(from_above, pad_high).astype(F32)
-    got_up = up(after.astype(BF))
-    got_down = down(before.astype(BF))
-    return block_of(z) + got_up.astype(F32) + got_down.astype(F32)
-
-
-def weight_sum_z(left, right, z, x, c, y):
-    def block_of(place):
-        return contract_rows(lax.dynamic_slice_in_dim(left, place * 256, 256, 1), right)
-
-    own = sum_ring(block_of, z).reshape(2, 2, 64, right.shape[1])
-    return sum_c(sum_x(own, x, 0), c, y)
+def sum_z(blocks, z):
+    ends = (z == 0) | (z == 3)
+    outer, inner = jnp.stack([blocks[0], blocks[3]]), blocks[1:3]
+    pair = jnp.where(ends, outer, inner) + lax.ppermute(
+        jnp.where(ends, inner, outer).astype(BF), "z", NEAR
+    ).astype(F32)
+    given = lax.ppermute(jnp.where(z < 2, pair[1], pair[0]).astype(BF), "z", FAR)
+    return jnp.where(z < 2, pair[0], pair[1]) + given.astype(F32)
+
+
+def weight_sum(left, right, z, x, c, y):
+    blocks = contract_rows(left, right).astype(BF).reshape(4, 2, 2, 64, right.shape[1])
+    low = sum_x(blocks[..., :32, :], x, 1)
+    high = sum_c(blocks[..., 32:, :], c, y)
+    low = sum_c(low, c, y)
+    high = sum_x(high, x, 1)
+    return sum_z(jnp.concatenate([low, high], axis=1), z)
 
 
 def sum_other(value, step):
     if step == "0":
-        return lax.ppermute(value, "z", [(0, 1), (1, 0), (2, 3), (3, 2)])
+        return lax.ppermute(value, "z", NEAR)
     if step == "1":
-        return lax.ppermute(value, "z", [(0, 3), (3, 0), (1, 2), (2, 1)])
+        return lax.ppermute(value, "z", FAR)
     return swap(value, step)
 
 
@@ -792,32 +790,26 @@
     return (value * phi, phi + value * bell * 0.3989422804014327)
 
 
-def expand_kernel(left_tiles, x_ref, left_ref, right_ref, b_ref, act_ref, slope_ref):
-    def fill(w_ref):
-        rows = 256
-        for start in range(0, x_ref.shape[0], rows):
-            part = slice(start, start + rows)
-            value = exact(x_ref[part, :], w_ref[...], ((1,), (0,))) + b_ref[...]
-            active, slope = gelu_pair(value)
-            act_ref[part, :] = active.astype(BF)
-            slope_ref[part, :] = slope.astype(BF)
-
-    pl.when(pl.program_id(0) < left_tiles)(lambda: fill(left_ref))
-    pl.when(pl.program_id(0) >= left_tiles)(lambda: fill(right_ref))
-
-
-def expand(value, left, right, shift):
+def expand_kernel(x_ref, w_ref, b_ref, act_ref, slope_ref):
+    rows = 256
+    for start in range(0, x_ref.shape[0], rows):
+        part = slice(start, start + rows)
+        value = exact(x_ref[part, :], w_ref[...], ((1,), (0,))) + b_ref[...]
+        active, slope = gelu_pair(value)
+        act_ref[part, :] = active.astype(BF)
+        slope_ref[part, :] = slope.astype(BF)
+
+
+def expand(value, weight, shift):
     count, depth = value.shape
     width = shift.shape[1]
     tile = 256
-    left_tiles = left.shape[1] // tile
     return pl.pallas_call(
-        partial(expand_kernel, left_tiles),
+        expand_kernel,
         grid=(width // tile,),
         in_specs=[
             pl.BlockSpec((count, depth), lambda i: (0, 0)),
-            pl.BlockSpec((depth, tile), lambda i: (0, jnp.minimum(i, left_tiles - 1))),
-            pl.BlockSpec((depth, tile), lambda i: (0, jnp.maximum(i - left_tiles, 0))),
+            pl.BlockSpec((depth, tile), lambda i: (0, i)),
             pl.BlockSpec((1, tile), lambda i: (0, i)),
         ],
         out_specs=[pl.BlockSpec((count, tile), lambda i: (0, i))] * 2,
@@ -828,7 +820,7 @@
             transcendentals=3 * count * width,
             bytes_accessed=2 * (count * depth + depth * width + 2 * count * width),
         ),
-    )(value, left, right, shift)
+    )(value, weight, shift)
 
 
 def cut_levels(raw, cuts):
@@ -996,38 +988,30 @@
 
     half_width = w_qkv.shape[2]
     up_wide = w_up.shape[1]
-    left_wide = (up_wide + half_width) // 2
+    chip_count = lengths.shape[0]
+    half_queries = NQ_ROW // 2
+    query_total = chip_count * half_queries
     qkv_rows = jnp.concatenate([w_qkv[0], w_qkv[1], w_qkv[2]], axis=1)
-    mid_rows = jnp.concatenate([w_up, w_out.T], axis=1)
-    qkv_rows = gather_c(qkv_rows, c, y, 0)
-    mid_rows = gather_z(mid_rows, z)
-    down_rows = gather_c(w_down.T, c, y, 0)
-    qkv_rows = gather_x(qkv_rows, x, 0)
-    down_rows = gather_x(down_rows, x, 0)
-    mid_left = gather_x(mid_rows[..., :left_wide], x, 1)
-    mid_right = gather_c(mid_rows[..., left_wide:], c, y, 1)
-    full_qkv = flat(gather_z(qkv_rows, z))
-    mid_left = flat(gather_c(mid_left, c, y, 2))
-    mid_right = flat(gather_x(mid_right, x, 1))
-    full_out = mid_right[:, up_wide - left_wide :]
-    full_down = flat(gather_z(down_rows, z))
+    pair_rows = jnp.pad(pairing.astype(BF), ((0, 63), (0, 128 - half_queries)))
+    mid_rows = jnp.concatenate([w_up, w_out.T, pair_rows], axis=1)
+    qkv_pair = gather_far(qkv_rows, z)
+    mid_pair = gather_far(tie(mid_rows, qkv_pair), z)
+    qkv_line = gather_near(qkv_pair, z)
+    mid_line = gather_near(mid_pair, z)
+    qkv_parts = gather_first(qkv_line, x, c, y)
+    down_pair = gather_far(tie(w_down.T, mid_pair), z)
+    full_qkv = gather_last(qkv_parts, x, c, y)
+    mid_parts = gather_first(tie(mid_line, *qkv_parts), x, c, y)
+    down_line = gather_near(down_pair, z)
+    full_mid = gather_last(mid_parts, x, c, y)
+    down_parts = gather_first(tie(down_line, *mid_parts), x, c, y)
+    full_down = gather_last(down_parts, x, c, y)
+    full_out = full_mid[:, up_wide : up_wide + half_width]
+    pairs = full_mid[:, up_wide + half_width :].reshape(chip_count, 64, 128)
+    pairs = pairs[:, 0, :half_queries].astype(jnp.int32).reshape(1, query_total)
     row = jnp.where(c == y, tokens, swap(tokens, "c"))
     bias = jnp.concatenate([b_qv.reshape(-1), b_up])[None].astype(F32)
     bias = jnp.where(c == y, bias, swap(bias, "y"))
-    own_cot = turn(cot)
-    half_queries = NQ_ROW // 2
-    chip_count = lengths.shape[0]
-    query_total = chip_count * half_queries
-    pairs = lax.dynamic_update_slice_in_dim(
-        jnp.zeros((1, 2 * query_total), F32),
-        pairing.astype(F32),
-        ((4 * z + 2 * x + c) * 2 + y) * half_queries,
-        1,
-    )
-    pairs = sum_chips(pairs, "cxy01").reshape(chip_count, 2, half_queries)
-    pairs = lax.dynamic_index_in_dim(pairs, c, 1, keepdims=False).reshape(1, query_total)
-    pairs = pairs.astype(jnp.int32)
-
     row_lengths = lax.dynamic_index_in_dim(lengths, chip, 0, keepdims=False)
     segments = segments_of(row_lengths, token_count)
     seg_col, seg_row = segments[:, None], segments[None, :]
@@ -1039,7 +1023,7 @@
     )
     qkv = (dot(row, full_qkv) + qkv_bias).astype(BF)
     mixed, lse = attend(bounds, qkv, seg_col, seg_row)
-    mixed, own_cot, pairs = lax.optimization_barrier((mixed, own_cot, pairs))
+    own_cot = turn(tie(cot, qkv))
 
     def row_sum(left, weight_t, transposed):
         times = contract_cols if transposed else dot
@@ -1056,7 +1040,7 @@
     )
     normed_low = normed.astype(BF)
     normed_all = jnp.concatenate([normed_low, swap(normed_low, "c")], axis=0)
-    activation, slope = expand(normed_all, mid_left, mid_right, bias[:, 2 * half_width :])
+    activation, slope = expand(normed_all, full_mid, bias[:, 2 * half_width :])
     ffn_sum = row_sum(
         lambda which: activation[which * share : (which + 1) * share], full_down, True
     )
@@ -1064,7 +1048,6 @@
         normed + ffn_sum + b_down.astype(F32), gains[1], shifts[1]
     )
     result_low = result.astype(BF)
-    y_out = turn(result_low)
     embed = dot(result_low, w_proj).astype(BF)
 
     other_embed = swap(embed, "c")
@@ -1142,18 +1125,15 @@
     grad_ffn = grad_second.astype(BF)
     down_bias = jnp.sum(grad_ffn.astype(F32), axis=0)
     grad_ffn_all = jnp.concatenate([grad_ffn, swap(grad_ffn, "c")], axis=0)
-    down_part = weight_sum_z(grad_ffn_all, activation, z, x, c, y)
+    down_part = weight_sum(grad_ffn_all, activation, z, x, c, y)
     grad_up = (dot(grad_ffn_all, full_down) * slope.astype(F32)).astype(BF)
     up_bias = jnp.sum(grad_up.astype(F32), axis=0)
-    up_part = weight_sum_z(normed_all, grad_up, z, x, c, y)
-    def normed_terms(which):
-        part = grad_up[which * share : (which + 1) * share]
-        return contract_cols(part[:, :left_wide], mid_left) + contract_cols(
-            part[:, left_wide:], mid_right[:, : up_wide - left_wide]
-        )
-
-    other_terms = swap(normed_terms(1).astype(BF), "c")
-    grad_normed = normed_terms(0) + other_terms.astype(F32) + grad_second
+    up_part = weight_sum(normed_all, grad_up, z, x, c, y)
+    full_up = full_mid[:, :up_wide]
+    grad_normed = (
+        row_sum(lambda which: grad_up[which * share : (which + 1) * share], full_up, True)
+        + grad_second
+    )
     gain_one = jnp.sum(grad_normed * unit_one, axis=0)
     shift_one = jnp.sum(grad_normed, axis=0)
     grad_first = norm_backward(grad_normed, unit_one, rstd_one, gains[0])
@@ -1165,10 +1145,11 @@
         jnp.concatenate([grad_attn, other_attn], axis=0),
         jnp.concatenate([other_attn, grad_attn], axis=0),
     )
-    out_part = weight_sum_z(grad_attn_all, mixed, z, x, c, y)
+    out_part = weight_sum(grad_attn_all, mixed, z, x, c, y)
     grad_mixed = dot(grad_attn_all, full_out).astype(BF)
     grads, grad_sums = attend_back(bounds, qkv, mixed, grad_mixed, lse, seg_col, seg_row)
-    qkv_part = weight_sum_z(row, grads, z, x, c, y)
+    y_out = turn(tie(result_low, grads))
+    qkv_part = weight_sum(row, grads, z, x, c, y)
     grad_input = turn(
         (
             row_sum(

time: 727 us -> 672 us (0.924)
  waiting for transfers between devices: 293 us -> 233 us
  other arithmetic: 42.5 us -> 64.9 us
  matrix products: 75.4 us -> 60.5 us
  starting transfers between devices: 167 us -> 153 us
  local copies, waits for them, and re-layouts: 34.6 us -> 45.6 us
    ppermute x34 -> x18, waiting for transfers between devices: 235 us -> 63 us  [the longest x3 33.6 us: gather_far(): far = lax.ppermute(value, 'z', FAR)]
    ppermute x30 -> x33, waiting for transfers between devices: 22.3 us -> 86.1 us  [swap(): return lax.ppermute(value, axis, SWAP)]
    ppermute x34 -> x18, starting transfers between devices: 70.1 us -> 24.2 us  [the longest x4 7.6 us: sum_z(): lax.ppermute(jnp.where(ends, inner, outer).astype(BF), 'z', NEAR)]
    ppermute x4 -> x8, starting transfers between devices: 15.1 us -> 39.8 us  [sum_c(): cross = lax.ppermute(other_low, ('c', 'y'), [(1, 2), (2, 1)])]
    ppermute x4 -> x6, waiting for transfers between devices: 4.1 us -> 19.4 us  [gather_c(): got = lax.ppermute(value, ('c', 'y'), [(2, 0), (1, 3), (0, 1), (3, 2)])]
    dot_general x18 -> x6, matrix products: 35 us -> 19.8 us  [contract_rows(): lax.dot_general(left, right, (((0,), (0,)), ((), ())), precision=precisio...]
    ppermute x3, waiting for transfers between devices: 0.01 us -> 15.2 us  [turn(): return lax.ppermute(value, ('c', 'y'), TURN)]
    ppermute x4 -> x6, waiting for transfers between devices: 4.88 us -> 17.4 us  [gather_c(): cross = lax.ppermute(value, ('c', 'y'), [(2, 1), (1, 2)])]
  transfers between devices with their start and end apart: 85 -> 84, of which waited for: 41 -> 44; matrix products, arithmetic and copies ran while one was open for 18% -> 22% of each run, Pallas kernels for 6% -> 7%
where the time goes in v4:
time: 672 us; the launch traced here: 662 us
  waiting for transfers between devices  233 us (35%)
  starting transfers between devices  153 us (23%)
  Pallas kernels  89.2 us (13%)
  other arithmetic  64.9 us (10%)
  matrix products  60.5 us (9%)
  local copies, waits for them, and re-layouts  45.6 us (7%)
  blocking collectives  11.8 us (2%)
    ppermute x33, waiting for transfers between devices, swap(): return lax.ppermute(value, axis, SWAP)  86.1 us
    ppermute x33, starting transfers between devices, swap(): return lax.ppermute(value, axis, SWAP)  44.6 us
    ppermute x8, starting transfers between devices, sum_c(): cross = lax.ppermute(other_low, ('c', 'y'), [(1, 2), (2, 1)])  39.8 us
    ppermute x3, waiting for transfers between devices, gather_far(): far = lax.ppermute(value, 'z', FAR)  33.6 us
    pallas_call x1, Pallas kernels, attend_back(): pl.pallas_call(attend_back_kernel, grid=(pairs,), in_specs=[pl.BlockSpec(...  26.8 us
    dot_general x10, matrix products, contract_cols(): lax.dot_general(left, right, (((1,), (1,)), ((), ())), precision=precisio...  22.3 us
    dot_general x6, matrix products, contract_rows(): lax.dot_general(left, right, (((0,), (0,)), ((), ())), precision=precisio...  19.8 us
    ppermute x6, waiting for transfers between devices, gather_c(): got = lax.ppermute(value, ('c', 'y'), [(2, 0), (1, 3), (0, 1), (3, 2)])  19.4 us
  transfers between devices with their start and end apart: 84, of which 44 were waited for; matrix products, arithmetic and copies ran while one was open for 22% of the time, Pallas kernels for 7%

profile of v4, /device:TPU:1, one launch (start us, length us, event | category | flops | bytes accessed | tf_op | source)
XLA Modules:
  0.0 661.8 jit_solution(10350872938387483130)
XLA Ops:
  1.7 4.2 collective-permute-start.1
  23.2 16.4 %collective-permute-done.10 = bf16[64,2688]{1,0:T(8,128)(2,1)S(1)} collective-permute-done((bf16[64,2688]{1,0:T(8,128)(2,1)S(1)}, bf16[64,2688]{1,0:T(8,128)(2,1)S(1)}, u32[]{:S(2)}, u32[]{:S(2)}) %collective-permute-start.10) | collective-permute-done | bytes 344096 | tf_op jit(solution)/shard_map/ppermute | solution.py:466
  46.4 17.2 %collective-permute-done.20 = bf16[64,2048]{1,0:T(8,128)(2,1)S(1)} collective-permute-done((bf16[64,2048]{1,0:T(8,128)(2,1)}, bf16[64,2048]{1,0:T(8,128)(2,1)S(1)}, u32[]{:S(2)}, u32[]{:S(2)}) %collective-permute-start.20) | collective-permute-done | bytes 262176 | tf_op jit(solution)/shard_map/ppermute | solution.py:466
  66.3 7.0 %collective-permute-done.3 = bf16[4,32,1536]{2,1,0:T(8,128)(2,1)S(1)} collective-permute-done((bf16[4,32,1536]{2,1,0:T(8,128)(2,1)S(1)}, bf16[4,32,1536]{2,1,0:T(8,128)(2,1)S(1)}, u32[]{:S(2)}, u32[]{:S(2)}) %collective-permute-start.3) | collective-permute-done | bytes 393248 | tf_op jit(solution)/shard_map/ppermute | solution.py:456
  73.6 4.1 collective-permute-start.15
  80.0 10.3 %collective-permute-done.8 = bf16[4,2,32,1536]{3,2,1,0:T(8,128)(2,1)S(1)} collective-permute-done((bf16[4,2,32,1536]{3,2,1,0:T(8,128)(2,1)S(1)}, bf16[4,2,32,1536]{3,2,1,0:T(8,128)(2,1)S(1)}, u32[]{:S(2)}, u32[]{:S(2)}) %collective-permute-start.8) | collective-permute-done | bytes 786464 | tf_op jit(solution)/shard_map/ppermute | solution.py:456
  90.2 4.1 collective-permute-start.5
  94.6 3.1 collective-permute-done.16
  101.3 9.1 %collective-permute-done.5 = bf16[4,2,32,1536]{3,2,0,1:T(8,128)(2,1)S(1)} collective-permute-done((bf16[4,2,32,1536]{3,2,0,1:T(8,128)(2,1)S(1)}, bf16[4,2,32,1536]{3,2,0,1:T(8,128)(2,1)S(1)}, u32[]{:S(2)}, u32[]{:S(2)}) %collective-permute-start.5) | collective-permute-done | bytes 786464 | tf_op jit(solution)/shard_map/ppermute | solution.py:481
  111.1 4.5 collective-permute-done.12
  118.4 3.6 add_convert_fusion.q_ref.k_ref.v_ref
  122.1 3.6 collective-permute-start.14
  125.7 19.1 %shard_map.254 = (bf16[1024,512]{1,0:T(8,128)(2,1)S(1)}, f32[4,8,1024]{2,1,0:T(8,128)S(1)}) custom-call(s32[2,4]{1,0:T(2,128)S(1)} %pad_add_fusion.bounds, bf16[1024,1536]{1,0:T(8,128)(2,1)S(1)} %add_convert_fusion.q_ref.k_ref.v_ref, bf16[1024,1536]{1,0:T(8,128)(2,1)S(1)} %add_convert_fusion.q_ref.k_ref.v_ref, ...), custom_call_target="tpu_custom_call" | custom-call | flops 2147483648 | bytes 12582912 | tf_op jit(solution)/shard_map/pallas_call | solution.py:647
  147.3 5.1 collective-permute-start.27
  153.0 3.8 collective-permute-done.13
  163.8 23.0 %collective-permute-done.22 = bf16[4,32,2048]{2,1,0:T(8,128)(2,1)} collective-permute-done((bf16[4,32,2048]{2,1,0:T(8,128)(2,1)}, bf16[4,32,2048]{2,1,0:T(8,128)(2,1)}, u32[]{:S(2)}, u32[]{:S(2)}) %collective-permute-start.22) | collective-permute-done | bytes 524320 | tf_op jit(solution)/shard_map/ppermute | solution.py:456
  195.0 15.4 %collective-permute-done.23 = bf16[4,2,32,2048]{3,2,0,1:T(8,128)(2,1)S(1)} collective-permute-done((bf16[4,2,32,2048]{3,2,0,1:T(8,128)(2,1)S(1)}, bf16[4,2,32,2048]{3,2,0,1:T(8,128)(2,1)S(1)}, u32[]{:S(2)}, u32[]{:S(2)}) %collective-permute-start.23) | collective-permute-done | bytes 1048608 | tf_op jit(solution)/shard_map/ppermute | solution.py:480
  216.5 17.6 %shard_map.255 = (bf16[1024,2048]{1,0:T(8,128)(2,1)S(1)}, bf16[1024,2048]{1,0:T(8,128)(2,1)S(1)}) custom-call(bf16[1024,1024]{1,0:T(8,128)(2,1)S(1)} %pad_maximum_fusion.3.x_ref, bf16[1024,2688]{1,0:T(8,128)(2,1)S(1)} %bitcast.325, f32[1,2048]{1,0:T(1,128)S(1)} %slice.382.b_ref), custom_call_target="tpu_custom_call" | custom-call | flops 4294967296 | bytes 14680064 | tf_op jit(solution)/shard_map/pallas_call | solution.py:807
  239.4 2.9 fusion.145
  249.2 5.0 all-to-all-start
  262.2 4.6 all-to-all-done
  267.8 10.0 %shard_map.256 = f32[24,2048]{1,0:T(8,128)S(1)} custom-call(bf16[2048,128]{1,0:T(8,128)(2,1)} %bitcast.50.q_ref, bf16[1024,128]{1,0:T(8,128)(2,1)S(1)} %copy-done.8, s32[1,1024]{1,0:T(1,128)S(1)} %compare_select_fusion.seg_row.seg_ref), custom_call_target="tpu_custom_call" | custom-call | flops 3221225472 | bytes 786432 | tf_op jit(solution)/shard_map/pallas_call | solution.py:860
  278.5 11.8 %all_to_all.15 = f32[16,8,128]{2,1,0:T(8,128)S(1)} all-to-all(f32[16,8,128]{2,1,0:T(8,128)S(1)} %broadcast_in_dim.29), channel_id=1, replica_groups=mesh['z'=4,'x'=2,'c'=2,'y'=2] {'z','x','y'}, dimensions={0} | all-to-all | bytes 131072 | tf_op jit(solution)/shard_map/all_to_all | solution.py:1082
  291.7 15.8 %shard_map.257 = (bf16[2048,128]{1,0:T(8,128)(2,1)S(1)}, f32[768,128]{1,0:T(8,128)S(1)}) custom-call(bf16[2048,128]{1,0:T(8,128)(2,1)} %bitcast.50.q_ref, bf16[1024,128]{1,0:T(8,128)(2,1)S(1)} %copy-done.9, s32[1,1024]{1,0:T(1,128)S(1)} %compare_select_fusion.seg_row.seg_ref, f32[24,2048]{1,0:T(8,128)S(1)} %convolution_divide_fusion.coef_ref), custom_call_target="tpu_custom_call" | custom-call | flops 4831838208 | bytes 1572864 | tf_op jit(solution)/shard_map/pallas_call | solution.py:936
  309.1 4.2 all-to-all-start.2
  315.1 8.6 %all-to-all-done.2 = bf16[16,128,128]{2,1,0:T(8,128)(2,1)} async-done(((bf16[16,128,128]{2,1,0:T(8,128)(2,1)}), bf16[16,128,128]{2,1,0:T(8,128)(2,1)}, u32[]{:S(2)}, u32[]{:S(2)}) %all-to-all-start.2) | async-done | bytes 524320 | tf_op jit(solution)/shard_map/all_to_all | solution.py:1103
  326.6 5.7 collective-permute-start.31
  337.4 11.2 %collective-permute-done.29 = bf16[512,1024]{1,0:T(8,128)(2,1)S(1)} collective-permute-done((bf16[512,1024]{1,0:T(8,128)(2,1)}, bf16[512,1024]{1,0:T(8,128)(2,1)S(1)}, u32[]{:S(2)}, u32[]{:S(2)}) %collective-permute-start.29) | collective-permute-done | bytes 1048608 | tf_op jit(solution)/shard_map/ppermute | solution.py:452
  351.6 2.8 collective-permute-done.77
  354.6 2.9 convert_reduce_fusion.1
  361.0 3.5 collective-permute-done.79
  375.0 8.6 %convert_reduce_fusion = (f32[2048]{0:T(1024)S(1)}, bf16[1024,2048]{1,0:T(8,128)(2,1)S(1)}) fusion(bf16[1024,2048]{1,0:T(8,128)(2,1)} %copy-done.16, bf16[1024,2048]{1,0:T(8,128)(2,1)} %bitcast.335, bf16[512,1024]{1,0:T(8,128)(2,1)} %collective-permute-done.32, bf16[512,1024]{1,0:T(8,128)(2,1)} %get-tuple-element.65), kind=kOutput, calls=%fused_computation | convolution fusion | flops 4309645312 | bytes 14688256 | tf_op jit(solution)/shard_map/dot_general | solution.py:448
  383.6 4.7 fusion.21
  388.4 5.0 convolution_convert_fusion.2
  400.0 6.3 convolution_convert_fusion.1
  415.0 3.4 collective-permute-start.72
  435.6 6.6 %collective-permute-done.71 = bf16[4,2,32,2048]{3,2,0,1:T(8,128)(2,1)} collective-permute-done((bf16[4,2,32,2048]{3,2,0,1:T(8,128)(2,1)}, bf16[4,2,32,2048]{3,2,0,1:T(8,128)(2,1)}, u32[]{:S(2)}, u32[]{:S(2)}) %collective-permute-start.71) | collective-permute-done | bytes 1048608 | tf_op jit(solution)/shard_map/ppermute | solution.py:511
  450.0 4.6 collective-permute-start.70
  455.7 3.1 collective-permute-done.65
  460.6 9.5 %collective-permute-done.73 = bf16[4,32,2048]{2,1,0:T(8,128)(2,1)S(1)} collective-permute-done((bf16[4,32,2048]{2,1,0:T(8,128)(2,1)S(1)}, bf16[4,32,2048]{2,1,0:T(8,128)(2,1)S(1)}, u32[]{:S(2)}, u32[]{:S(2)}) %collective-permute-start.73) | collective-permute-done | bytes 524320 | tf_op jit(solution)/shard_map/ppermute | solution.py:456
  472.0 3.8 convolution_convert_fusion.4.grad_ref
  475.9 26.8 %shard_map.258 = (bf16[1024,1536]{1,0:T(8,128)(2,1)S(1)}, f32[4,8,128]{2,1,0:T(8,128)S(1)}) custom-call(s32[2,4]{1,0:T(2,128)S(1)} %pad_add_fusion.bounds, bf16[1024,1536]{1,0:T(8,128)(2,1)S(1)} %add_convert_fusion.q_ref.k_ref.v_ref, bf16[1024,1536]{1,0:T(8,128)(2,1)S(1)} %add_convert_fusion.q_ref.k_ref.v_ref, ...), custom_call_target="tpu_custom_call" | custom-call | flops 5368709120 | bytes 25165824 | tf_op jit(solution)/shard_map/pallas_call | solution.py:742
  502.7 2.8 fusion.15
  505.5 3.9 convolution_convert_fusion
  509.4 3.5 collective-permute-start.35
  517.8 3.6 convolution_convert_fusion.3
  523.2 5.6 collective-permute-start.47
  530.0 3.5 collective-permute-start.56
  534.5 3.3 collective-permute-done.48
  545.3 3.9 collective-permute-start.51
  554.9 5.9 collective-permute-done.67
  560.8 4.4 collective-permute-start.52
  567.3 3.9 collective-permute-done.52
  571.3 5.0 collective-permute-start.54
  585.4 5.9 collective-permute-done.75
  591.3 3.0 collective-permute-start.58
  595.2 3.0 collective-permute-done.58
  602.5 9.1 %collective-permute-done.39 = bf16[4,2,32,1536]{3,2,0,1:T(8,128)(2,1)S(1)} collective-permute-done((bf16[4,2,32,1536]{3,2,0,1:T(8,128)(2,1)S(1)}, bf16[4,2,32,1536]{3,2,0,1:T(8,128)(2,1)S(1)}, u32[]{:S(2)}, u32[]{:S(2)}) %collective-permute-start.39) | collective-permute-done | bytes 786464 | tf_op jit(solution)/shard_map/ppermute | solution.py:456
  612.0 16.2 %collective-permute-start.41 = (bf16[4,32,1536]{2,1,0:T(8,128)(2,1)S(1)}, bf16[4,32,1536]{2,1,0:T(8,128)(2,1)S(1)}, u32[]{:S(2)}, u32[]{:S(2)}) collective-permute-start(bf16[4,32,1536]{2,1,0:T(8,128)(2,1)S(1)} %get-tuple-element.71), channel_id=1, source_target_pairs={{1,2},{2,1},{5,6},{6,5},{9,10},{10,9},{13,14},{14,13},{17,18},{18,... | collective-permute-start | bytes 1179656 | tf_op jit(solution)/shard_map/ppermute | solution.py:516
  630.0 3.7 collective-permute-done.41
  633.7 3.5 collective-permute-done.40
  638.9 3.1 add_convert_fusion.1
  648.7 4.6 collective-permute-done.46
  654.1 4.0 collective-permute-done.38
  (495 shorter events, 210.7 us)
Async XLA Ops:
  1.7 19.9 %collective-permute-start.1 = (bf16[64,1536]{1,0:T(8,128)(2,1)S(1)}, bf16[64,1536]{1,0:T(8,128)(2,1)}, u32[]{:S(2)}, u32[]{:S(2)}) collective-permute-start(bf16[64,1536]{1,0:T(8,128)(2,1)S(1)} %get-tuple-element.153), channel_id=1, source_target_pairs={{0,24},{24,0},{8,16},{16,8},{1,25},{25,1},{9,17},{17,9},{2,26},{26... | collective-permute-start | bytes 589832 | tf_op jit(solution)/shard_map/ppermute | solution.py:466
  5.9 94.1 %collective-permute-start = (bf16[1024,1024]{1,0:T(8,128)(2,1)}, bf16[1024,1024]{1,0:T(8,128)(2,1)S(1)}, u32[]{:S(2)}, u32[]{:S(2)}) collective-permute-start(bf16[1024,1024]{1,0:T(8,128)(2,1)} %param.15), channel_id=1, source_target_pairs={{0,2},{2,0},{1,3},{3,1},{4,6},{6,4},{5,7},{7,5},{8,10},{10,8},{9,1... | collective-permute-start | bytes 6291464 | tf_op jit(solution)/shard_map/ppermute | solution.py:456
  8.9 12.0 %collective-permute-start.9 = (f32[1,3072]{1,0:T(1,128)}, f32[1,3072]{1,0:T(1,128)}, u32[]{:S(2)}, u32[]{:S(2)}) collective-permute-start(f32[1,3072]{1,0:T(1,128)} %maximum_convert_fusion), channel_id=1, source_target_pairs={{0,1},{1,0},{2,3},{3,2},{4,5},{5,4},{6,7},{7,6},{8,9},{9,8},{10,11... | collective-permute-start | bytes 36872 | tf_op jit(solution)/shard_map/ppermute | solution.py:456
  22.7 20.3 %collective-permute-start.2 = (bf16[2,64,1536]{2,1,0:T(8,128)(2,1)S(1)}, bf16[2,64,1536]{2,1,0:T(8,128)(2,1)S(1)}, u32[]{:S(2)}, u32[]{:S(2)}) collective-permute-start(bf16[2,64,1536]{2,1,0:T(8,128)(2,1)S(1)} %maximum_select_fusion.20), channel_id=1, source_target_pairs={{0,8},{8,0},{16,24},{24,16},{1,9},{9,1},{17,25},{25,17},{2,10},{10... | collective-permute-start | bytes 1179656 | tf_op jit(solution)/shard_map/ppermute | solution.py:471
  22.8 16.7 %collective-permute-start.10 = (bf16[64,2688]{1,0:T(8,128)(2,1)S(1)}, bf16[64,2688]{1,0:T(8,128)(2,1)S(1)}, u32[]{:S(2)}, u32[]{:S(2)}) collective-permute-start(bf16[64,2688]{1,0:T(8,128)(2,1)S(1)} %fusion.61), channel_id=1, source_target_pairs={{0,24},{24,0},{8,16},{16,8},{1,25},{25,1},{9,17},{17,9},{2,26},{26... | collective-permute-start | bytes 1032200 | tf_op jit(solution)/shard_map/ppermute | solution.py:466
  39.7 26.3 %collective-permute-start.11 = (bf16[2,64,2688]{2,1,0:T(8,128)(2,1)S(1)}, bf16[2,64,2688]{2,1,0:T(8,128)(2,1)S(1)}, u32[]{:S(2)}, u32[]{:S(2)}) collective-permute-start(bf16[2,64,2688]{2,1,0:T(8,128)(2,1)S(1)} %maximum_select_fusion.17), channel_id=1, source_target_pairs={{0,8},{8,0},{16,24},{24,16},{1,9},{9,1},{17,25},{25,17},{2,10},{10... | collective-permute-start | bytes 2064392 | tf_op jit(solution)/shard_map/ppermute | solution.py:471
  40.9 22.7 %collective-permute-start.20 = (bf16[64,2048]{1,0:T(8,128)(2,1)}, bf16[64,2048]{1,0:T(8,128)(2,1)S(1)}, u32[]{:S(2)}, u32[]{:S(2)}) collective-permute-start(bf16[64,2048]{1,0:T(8,128)(2,1)} %bitcast.357), channel_id=1, source_target_pairs={{0,24},{24,0},{8,16},{16,8},{1,25},{25,1},{9,17},{17,9},{2,26},{26... | collective-permute-start | bytes 786440 | tf_op jit(solution)/shard_map/ppermute | solution.py:466
  43.3 20.5 %collective-permute-start.6 = (bf16[4,32,1536]{2,1,0:T(8,128)(2,1)S(1)}, bf16[4,32,1536]{2,1,0:T(8,128)(2,1)S(1)}, u32[]{:S(2)}, u32[]{:S(2)}) collective-permute-start(bf16[4,32,1536]{2,1,0:T(8,128)(2,1)S(1)} %slice.372), channel_id=1, source_target_pairs={{2,0},{1,3},{0,1},{3,2},{6,4},{5,7},{4,5},{7,6},{10,8},{9,11},{8,9... | collective-permute-start | bytes 1179656 | tf_op jit(solution)/shard_map/ppermute | solution.py:480
  44.4 19.5 %collective-permute-start.7 = (bf16[4,32,1536]{2,1,0:T(8,128)(2,1)S(1)}, bf16[4,32,1536]{2,1,0:T(8,128)(2,1)S(1)}, u32[]{:S(2)}, u32[]{:S(2)}) collective-permute-start(bf16[4,32,1536]{2,1,0:T(8,128)(2,1)S(1)} %slice.372), channel_id=1, source_target_pairs={{2,1},{1,2},{6,5},{5,6},{10,9},{9,10},{14,13},{13,14},{18,17},{17,... | collective-permute-start | bytes 1179656 | tf_op jit(solution)/shard_map/ppermute | solution.py:481
  63.7 15.9 %collective-permute-start.21 = (bf16[2,64,2048]{2,1,0:T(8,128)(2,1)S(1)}, bf16[2,64,2048]{2,1,0:T(8,128)(2,1)S(1)}, u32[]{:S(2)}, u32[]{:S(2)}) collective-permute-start(bf16[2,64,2048]{2,1,0:T(8,128)(2,1)S(1)} %maximum_select_fusion.18), channel_id=1, source_target_pairs={{0,8},{8,0},{16,24},{24,16},{1,9},{9,1},{17,25},{25,17},{2,10},{10... | collective-permute-start | bytes 1572872 | tf_op jit(solution)/shard_map/ppermute | solution.py:471
  64.0 9.4 %collective-permute-start.3 = (bf16[4,32,1536]{2,1,0:T(8,128)(2,1)S(1)}, bf16[4,32,1536]{2,1,0:T(8,128)(2,1)S(1)}, u32[]{:S(2)}, u32[]{:S(2)}) collective-permute-start(bf16[4,32,1536]{2,1,0:T(8,128)(2,1)S(1)} %get-tuple-element.144), channel_id=1, source_target_pairs={{0,4},{4,0},{1,5},{5,1},{2,6},{6,2},{3,7},{7,3},{8,12},{12,8},{9,1... | collective-permute-start | bytes 1179656 | tf_op jit(solution)/shard_map/ppermute | solution.py:456
  65.4 24.9 %collective-permute-start.8 = (bf16[4,2,32,1536]{3,2,1,0:T(8,128)(2,1)S(1)}, bf16[4,2,32,1536]{3,2,1,0:T(8,128)(2,1)S(1)}, u32[]{:S(2)}, u32[]{:S(2)}) collective-permute-start(bf16[4,2,32,1536]{3,2,1,0:T(8,128)(2,1)S(1)} %maximum_select_fusion.16), channel_id=1, source_target_pairs={{0,4},{4,0},{1,5},{5,1},{2,6},{6,2},{3,7},{7,3},{8,12},{12,8},{9,1... | collective-permute-start | bytes 2359304 | tf_op jit(solution)/shard_map/ppermute | solution.py:456
  73.6 21.0 %collective-permute-start.15 = (bf16[4,32,2688]{2,1,0:T(8,128)(2,1)S(1)}, bf16[4,32,2688]{2,1,0:T(8,128)(2,1)S(1)}, u32[]{:S(2)}, u32[]{:S(2)}) collective-permute-start(bf16[4,32,2688]{2,1,0:T(8,128)(2,1)S(1)} %slice.299), channel_id=1, source_target_pairs={{2,0},{1,3},{0,1},{3,2},{6,4},{5,7},{4,5},{7,6},{10,8},{9,11},{8,9... | collective-permute-start | bytes 2064392 | tf_op jit(solution)/shard_map/ppermute | solution.py:480
  77.7 20.0 %collective-permute-start.16 = (bf16[4,32,2688]{2,1,0:T(8,128)(2,1)S(1)}, bf16[4,32,2688]{2,1,0:T(8,128)(2,1)S(1)}, u32[]{:S(2)}, u32[]{:S(2)}) collective-permute-start(bf16[4,32,2688]{2,1,0:T(8,128)(2,1)S(1)} %slice.299), channel_id=1, source_target_pairs={{2,1},{1,2},{6,5},{5,6},{10,9},{9,10},{14,13},{13,14},{18,17},{17,... | collective-permute-start | bytes 2064392 | tf_op jit(solution)/shard_map/ppermute | solution.py:481
  79.9 21.4 %collective-permute-start.4 = (bf16[4,2,32,1536]{3,2,0,1:T(8,128)(2,1)S(1)}, bf16[4,2,32,1536]{3,2,0,1:T(8,128)(2,1)S(1)}, u32[]{:S(2)}, u32[]{:S(2)}) collective-permute-start(bf16[4,2,32,1536]{3,2,0,1:T(8,128)(2,1)S(1)} %maximum_select_fusion.15), channel_id=1, source_target_pairs={{2,0},{1,3},{0,1},{3,2},{6,4},{5,7},{4,5},{7,6},{10,8},{9,11},{8,9... | collective-permute-start | bytes 2359304 | tf_op jit(solution)/shard_map/ppermute | solution.py:480
  90.2 20.2 %collective-permute-start.5 = (bf16[4,2,32,1536]{3,2,0,1:T(8,128)(2,1)S(1)}, bf16[4,2,32,1536]{3,2,0,1:T(8,128)(2,1)S(1)}, u32[]{:S(2)}, u32[]{:S(2)}) collective-permute-start(bf16[4,2,32,1536]{3,2,0,1:T(8,128)(2,1)S(1)} %maximum_select_fusion.15), channel_id=1, source_target_pairs={{2,1},{1,2},{6,5},{5,6},{10,9},{9,10},{14,13},{13,14},{18,17},{17,... | collective-permute-start | bytes 2359304 | tf_op jit(solution)/shard_map/ppermute | solution.py:481
  98.0 17.6 %collective-permute-start.12 = (bf16[4,32,2688]{2,1,0:T(8,128)(2,1)S(1)}, bf16[4,32,2688]{2,1,0:T(8,128)(2,1)S(1)}, u32[]{:S(2)}, u32[]{:S(2)}) collective-permute-start(bf16[4,32,2688]{2,1,0:T(8,128)(2,1)S(1)} %get-tuple-element.102), channel_id=1, source_target_pairs={{0,4},{4,0},{1,5},{5,1},{2,6},{6,2},{3,7},{7,3},{8,12},{12,8},{9,1... | collective-permute-start | bytes 2064392 | tf_op jit(solution)/shard_map/ppermute | solution.py:456
  99.5 53.0 %collective-permute-start.17 = (bf16[4,2,32,2688]{3,2,0,1:T(8,128)(2,1)S(1)}, bf16[4,2,32,2688]{3,2,0,1:T(8,128)(2,1)S(1)}, u32[]{:S(2)}, u32[]{:S(2)}) collective-permute-start(bf16[4,2,32,2688]{3,2,0,1:T(8,128)(2,1)S(1)} %maximum_select_fusion.10), channel_id=1, source_target_pairs={{0,4},{4,0},{1,5},{5,1},{2,6},{6,2},{3,7},{7,3},{8,12},{12,8},{9,1... | collective-permute-start | bytes 4128776 | tf_op jit(solution)/shard_map/ppermute | solution.py:456
  115.9 29.0 %collective-permute-start.25 = (bf16[4,32,2048]{2,1,0:T(8,128)(2,1)S(1)}, bf16[4,32,2048]{2,1,0:T(8,128)(2,1)S(1)}, u32[]{:S(2)}, u32[]{:S(2)}) collective-permute-start(bf16[4,32,2048]{2,1,0:T(8,128)(2,1)S(1)} %slice.310), channel_id=1, source_target_pairs={{2,0},{1,3},{0,1},{3,2},{6,4},{5,7},{4,5},{7,6},{10,8},{9,11},{8,9... | collective-permute-start | bytes 1572872 | tf_op jit(solution)/shard_map/ppermute | solution.py:480
  115.9 29.0 %collective-permute-start.26 = (bf16[4,32,2048]{2,1,0:T(8,128)(2,1)S(1)}, bf16[4,32,2048]{2,1,0:T(8,128)(2,1)S(1)}, u32[]{:S(2)}, u32[]{:S(2)}) collective-permute-start(bf16[4,32,2048]{2,1,0:T(8,128)(2,1)S(1)} %slice.310), channel_id=1, source_target_pairs={{2,1},{1,2},{6,5},{5,6},{10,9},{9,10},{14,13},{13,14},{18,17},{17,... | collective-permute-start | bytes 1572872 | tf_op jit(solution)/shard_map/ppermute | solution.py:481
  122.1 34.8 %collective-permute-start.13 = (bf16[4,2,32,2688]{3,2,0,1:T(8,128)(2,1)S(1)}, bf16[4,2,32,2688]{3,2,0,1:T(8,128)(2,1)S(1)}, u32[]{:S(2)}, u32[]{:S(2)}) collective-permute-start(bf16[4,2,32,2688]{3,2,0,1:T(8,128)(2,1)S(1)} %maximum_select_fusion.8), channel_id=1, source_target_pairs={{2,0},{1,3},{0,1},{3,2},{6,4},{5,7},{4,5},{7,6},{10,8},{9,11},{8,9... | collective-permute-start | bytes 4128776 | tf_op jit(solution)/shard_map/ppermute | solution.py:480
  122.1 37.3 %collective-permute-start.14 = (bf16[4,2,32,2688]{3,2,0,1:T(8,128)(2,1)S(1)}, bf16[4,2,32,2688]{3,2,0,1:T(8,128)(2,1)S(1)}, u32[]{:S(2)}, u32[]{:S(2)}) collective-permute-start(bf16[4,2,32,2688]{3,2,0,1:T(8,128)(2,1)S(1)} %maximum_select_fusion.8), channel_id=1, source_target_pairs={{2,1},{1,2},{6,5},{5,6},{10,9},{9,10},{14,13},{13,14},{18,17},{17,... | collective-permute-start | bytes 4128776 | tf_op jit(solution)/shard_map/ppermute | solution.py:481
  147.3 45.5 %collective-permute-start.27 = (bf16[4,2,32,2048]{3,2,1,0:T(8,128)(2,1)}, bf16[4,2,32,2048]{3,2,1,0:T(8,128)(2,1)}, u32[]{:S(2)}, u32[]{:S(2)}) collective-permute-start(bf16[4,2,32,2048]{3,2,1,0:T(8,128)(2,1)} %maximum_select_fusion.13), channel_id=1, source_target_pairs={{0,4},{4,0},{1,5},{5,1},{2,6},{6,2},{3,7},{7,3},{8,12},{12,8},{9,1... | collective-permute-start | bytes 3145736 | tf_op jit(solution)/shard_map/ppermute | solution.py:456
  152.4 34.4 %collective-permute-start.22 = (bf16[4,32,2048]{2,1,0:T(8,128)(2,1)}, bf16[4,32,2048]{2,1,0:T(8,128)(2,1)}, u32[]{:S(2)}, u32[]{:S(2)}) collective-permute-start(bf16[4,32,2048]{2,1,0:T(8,128)(2,1)} %get-tuple-element.112), channel_id=1, source_target_pairs={{0,4},{4,0},{1,5},{5,1},{2,6},{6,2},{3,7},{7,3},{8,12},{12,8},{9,1... | collective-permute-start | bytes 1572872 | tf_op jit(solution)/shard_map/ppermute | solution.py:456
  162.3 28.2 %collective-permute-start.18 = (bf16[512,1024]{1,0:T(8,128)(2,1)S(1)}, bf16[512,1024]{1,0:T(8,128)(2,1)S(1)}, u32[]{:S(2)}, u32[]{:S(2)}) collective-permute-start(bf16[512,1024]{1,0:T(8,128)(2,1)S(1)} %convolution_convert_fusion.5), channel_id=1, source_target_pairs={{0,2},{2,0},{1,3},{3,1},{4,6},{6,4},{5,7},{7,5},{8,10},{10,8},{9,1... | collective-permute-start | bytes 3145736 | tf_op jit(solution)/shard_map/ppermute | solution.py:456
  188.2 22.2 %collective-permute-start.23 = (bf16[4,2,32,2048]{3,2,0,1:T(8,128)(2,1)S(1)}, bf16[4,2,32,2048]{3,2,0,1:T(8,128)(2,1)S(1)}, u32[]{:S(2)}, u32[]{:S(2)}) collective-permute-start(bf16[4,2,32,2048]{3,2,0,1:T(8,128)(2,1)S(1)} %maximum_select_fusion.12), channel_id=1, source_target_pairs={{2,0},{1,3},{0,1},{3,2},{6,4},{5,7},{4,5},{7,6},{10,8},{9,11},{8,9... | collective-permute-start | bytes 3145736 | tf_op jit(solution)/shard_map/ppermute | solution.py:480
  188.4 24.7 %collective-permute-start.24 = (bf16[4,2,32,2048]{3,2,0,1:T(8,128)(2,1)S(1)}, bf16[4,2,32,2048]{3,2,0,1:T(8,128)(2,1)S(1)}, u32[]{:S(2)}, u32[]{:S(2)}) collective-permute-start(bf16[4,2,32,2048]{3,2,0,1:T(8,128)(2,1)S(1)} %maximum_select_fusion.12), channel_id=1, source_target_pairs={{2,1},{1,2},{6,5},{5,6},{10,9},{9,10},{14,13},{13,14},{18,17},{17,... | collective-permute-start | bytes 3145736 | tf_op jit(solution)/shard_map/ppermute | solution.py:481
  192.7 22.6 %collective-permute-start.19 = (bf16[512,1024]{1,0:T(8,128)(2,1)S(1)}, bf16[512,1024]{1,0:T(8,128)(2,1)S(1)}, u32[]{:S(2)}, u32[]{:S(2)}) collective-permute-start(bf16[512,1024]{1,0:T(8,128)(2,1)S(1)} %fusion.10), channel_id=1, source_target_pairs={{0,2},{2,0},{1,3},{3,1},{4,6},{6,4},{5,7},{7,5},{8,10},{10,8},{9,1... | collective-permute-start | bytes 3145736 | tf_op jit(solution)/shard_map/ppermute | solution.py:456
  249.2 17.6 %all-to-all-start = ((bf16[16,128,128]{2,1,0:T(8,128)(2,1)}), bf16[16,128,128]{2,1,0:T(8,128)(2,1)}, u32[]{:S(2)}, u32[]{:S(2)}) async-start(bf16[16,128,128]{2,1,0:T(8,128)(2,1)} %broadcast_in_dim.28), calls=%async_computation | async-start | bytes 1048576 | tf_op jit(solution)/shard_map/all_to_all | solution.py:1062
  309.1 14.7 %all-to-all-start.2 = ((bf16[16,128,128]{2,1,0:T(8,128)(2,1)}), bf16[16,128,128]{2,1,0:T(8,128)(2,1)}, u32[]{:S(2)}, u32[]{:S(2)}) async-start(bf16[16,128,128]{2,1,0:T(8,128)(2,1)} %bitcast.332), calls=%async_computation.2 | async-start | bytes 1048576 | tf_op jit(solution)/shard_map/all_to_all | solution.py:1103
  332.3 16.3 %collective-permute-start.29 = (bf16[512,1024]{1,0:T(8,128)(2,1)}, bf16[512,1024]{1,0:T(8,128)(2,1)S(1)}, u32[]{:S(2)}, u32[]{:S(2)}) collective-permute-start(bf16[512,1024]{1,0:T(8,128)(2,1)} %param.29), channel_id=1, source_target_pairs={{0,0},{1,2},{2,1},{3,3},{4,4},{5,6},{6,5},{7,7},{8,8},{9,10},{10,9... | collective-permute-start | bytes 3145736 | tf_op jit(solution)/shard_map/ppermute | solution.py:452
  336.9 13.6 %collective-permute-start.76 = (f32[512,128]{1,0:T(8,128)S(1)}, f32[512,128]{1,0:T(8,128)S(1)}, u32[]{:S(2)}, u32[]{:S(2)}) collective-permute-start(f32[512,128]{1,0:T(8,128)S(1)} %constant_dynamic-slice_fusion.1), channel_id=1, source_target_pairs={{0,2},{2,0},{1,3},{3,1},{4,6},{6,4},{5,7},{7,5},{8,10},{10,8},{9,1... | collective-permute-start | bytes 786440 | tf_op jit(solution)/shard_map/ppermute | solution.py:456
  357.5 17.5 %collective-permute-start.32 = (bf16[512,1024]{1,0:T(8,128)(2,1)}, bf16[512,1024]{1,0:T(8,128)(2,1)}, u32[]{:S(2)}, u32[]{:S(2)}) collective-permute-start(bf16[512,1024]{1,0:T(8,128)(2,1)} %get-tuple-element.65), channel_id=1, source_target_pairs={{0,2},{2,0},{1,3},{3,1},{4,6},{6,4},{5,7},{7,5},{8,10},{10,8},{9,1... | collective-permute-start | bytes 3145736 | tf_op jit(solution)/shard_map/ppermute | solution.py:456
  372.6 42.5 %collective-permute-start.81 = (f32[512,128]{1,0:T(8,128)S(1)}, f32[512,128]{1,0:T(8,128)S(1)}, u32[]{:S(2)}, u32[]{:S(2)}) collective-permute-start(f32[512,128]{1,0:T(8,128)S(1)} %convert_add_fusion.7), channel_id=1, source_target_pairs={{0,2},{2,0},{1,3},{3,1},{4,6},{6,4},{5,7},{7,5},{8,10},{10,8},{9,1... | collective-permute-start | bytes 786440 | tf_op jit(solution)/shard_map/ppermute | solution.py:456
  388.3 30.9 %collective-permute-start.33 = (bf16[512,1024]{1,0:T(8,128)(2,1)S(1)}, bf16[512,1024]{1,0:T(8,128)(2,1)S(1)}, u32[]{:S(2)}, u32[]{:S(2)}) collective-permute-start(bf16[512,1024]{1,0:T(8,128)(2,1)S(1)} %fusion.21), channel_id=1, source_target_pairs={{0,2},{2,0},{1,3},{3,1},{4,6},{6,4},{5,7},{7,5},{8,10},{10,8},{9,1... | collective-permute-start | bytes 3145736 | tf_op jit(solution)/shard_map/ppermute | solution.py:456
  394.2 28.9 %collective-permute-start.64 = (bf16[4,2,32,2048]{3,2,0,1:T(8,128)(2,1)S(1)}, bf16[4,2,32,2048]{3,2,0,1:T(8,128)(2,1)S(1)}, u32[]{:S(2)}, u32[]{:S(2)}) collective-permute-start(bf16[4,2,32,2048]{3,2,0,1:T(8,128)(2,1)S(1)} %bitcast.348), channel_id=1, source_target_pairs={{1,2},{2,1},{5,6},{6,5},{9,10},{10,9},{13,14},{14,13},{17,18},{18,... | collective-permute-start | bytes 3145736 | tf_op jit(solution)/shard_map/ppermute | solution.py:516
  396.8 26.8 %collective-permute-start.63 = (bf16[4,2,32,2048]{3,2,0,1:T(8,128)(2,1)S(1)}, bf16[4,2,32,2048]{3,2,0,1:T(8,128)(2,1)S(1)}, u32[]{:S(2)}, u32[]{:S(2)}) collective-permute-start(bf16[4,2,32,2048]{3,2,0,1:T(8,128)(2,1)S(1)} %bitcast_select_fusion.2), channel_id=1, source_target_pairs={{0,2},{3,1},{1,0},{2,3},{4,6},{7,5},{5,4},{6,7},{8,10},{11,9},{9,8... | collective-permute-start | bytes 3145736 | tf_op jit(solution)/shard_map/ppermute | solution.py:511
  399.0 28.6 %collective-permute-start.60 = (bf16[4,2,32,2048]{3,2,0,1:T(8,128)(2,1)}, bf16[4,2,32,2048]{3,2,0,1:T(8,128)(2,1)}, u32[]{:S(2)}, u32[]{:S(2)}) collective-permute-start(bf16[4,2,32,2048]{3,2,0,1:T(8,128)(2,1)} %bitcast.316), channel_id=1, source_target_pairs={{0,4},{4,0},{1,5},{5,1},{2,6},{6,2},{3,7},{7,3},{8,12},{12,8},{9,1... | collective-permute-start | bytes 3145736 | tf_op jit(solution)/shard_map/ppermute | solution.py:456
  415.0 18.2 %collective-permute-start.72 = (bf16[4,2,32,2048]{3,2,0,1:T(8,128)(2,1)}, bf16[4,2,32,2048]{3,2,0,1:T(8,128)(2,1)}, u32[]{:S(2)}, u32[]{:S(2)}) collective-permute-start(bf16[4,2,32,2048]{3,2,0,1:T(8,128)(2,1)} %bitcast.317), channel_id=1, source_target_pairs={{1,2},{2,1},{5,6},{6,5},{9,10},{10,9},{13,14},{14,13},{17,18},{18,... | collective-permute-start | bytes 3145736 | tf_op jit(solution)/shard_map/ppermute | solution.py:516
  419.3 22.9 %collective-permute-start.71 = (bf16[4,2,32,2048]{3,2,0,1:T(8,128)(2,1)}, bf16[4,2,32,2048]{3,2,0,1:T(8,128)(2,1)}, u32[]{:S(2)}, u32[]{:S(2)}) collective-permute-start(bf16[4,2,32,2048]{3,2,0,1:T(8,128)(2,1)} %bitcast_select_fusion), channel_id=1, source_target_pairs={{0,2},{3,1},{1,0},{2,3},{4,6},{7,5},{5,4},{6,7},{8,10},{11,9},{9,8... | collective-permute-start | bytes 3145736 | tf_op jit(solution)/shard_map/ppermute | solution.py:511
  423.1 24.6 %collective-permute-start.68 = (bf16[4,2,32,2048]{3,2,0,1:T(8,128)(2,1)}, bf16[4,2,32,2048]{3,2,0,1:T(8,128)(2,1)}, u32[]{:S(2)}, u32[]{:S(2)}) collective-permute-start(bf16[4,2,32,2048]{3,2,0,1:T(8,128)(2,1)} %bitcast.315), channel_id=1, source_target_pairs={{0,4},{4,0},{1,5},{5,1},{2,6},{6,2},{3,7},{7,3},{8,12},{12,8},{9,1... | collective-permute-start | bytes 3145736 | tf_op jit(solution)/shard_map/ppermute | solution.py:456
  423.6 48.4 %collective-permute-start.34 = (bf16[512,1024]{1,0:T(8,128)(2,1)}, bf16[512,1024]{1,0:T(8,128)(2,1)}, u32[]{:S(2)}, u32[]{:S(2)}) collective-permute-start(bf16[512,1024]{1,0:T(8,128)(2,1)} %get-tuple-element.68), channel_id=1, source_target_pairs={{0,2},{2,0},{1,3},{3,1},{4,6},{6,4},{5,7},{7,5},{8,10},{10,8},{9,1... | collective-permute-start | bytes 3145736 | tf_op jit(solution)/shard_map/ppermute | solution.py:456
  427.7 31.1 %collective-permute-start.65 = (bf16[4,32,2048]{2,1,0:T(8,128)(2,1)S(1)}, bf16[4,32,2048]{2,1,0:T(8,128)(2,1)S(1)}, u32[]{:S(2)}, u32[]{:S(2)}) collective-permute-start(bf16[4,32,2048]{2,1,0:T(8,128)(2,1)S(1)} %fusion.47), channel_id=1, source_target_pairs={{0,4},{4,0},{1,5},{5,1},{2,6},{6,2},{3,7},{7,3},{8,12},{12,8},{9,1... | collective-permute-start | bytes 1572872 | tf_op jit(solution)/shard_map/ppermute | solution.py:456
  433.2 16.7 %collective-permute-start.62 = (bf16[4,32,2048]{2,1,0:T(8,128)(2,1)S(1)}, bf16[4,32,2048]{2,1,0:T(8,128)(2,1)S(1)}, u32[]{:S(2)}, u32[]{:S(2)}) collective-permute-start(bf16[4,32,2048]{2,1,0:T(8,128)(2,1)S(1)} %get-tuple-element.61), channel_id=1, source_target_pairs={{1,2},{2,1},{5,6},{6,5},{9,10},{10,9},{13,14},{14,13},{17,18},{18,... | collective-permute-start | bytes 1572872 | tf_op jit(solution)/shard_map/ppermute | solution.py:516
  442.2 12.4 %collective-permute-start.61 = (bf16[4,32,2048]{2,1,0:T(8,128)(2,1)S(1)}, bf16[4,32,2048]{2,1,0:T(8,128)(2,1)S(1)}, u32[]{:S(2)}, u32[]{:S(2)}) collective-permute-start(bf16[4,32,2048]{2,1,0:T(8,128)(2,1)S(1)} %get-tuple-element.60), channel_id=1, source_target_pairs={{0,2},{3,1},{1,0},{2,3},{4,6},{7,5},{5,4},{6,7},{8,10},{11,9},{9,8... | collective-permute-start | bytes 1572872 | tf_op jit(solution)/shard_map/ppermute | solution.py:511
  447.7 22.4 %collective-permute-start.73 = (bf16[4,32,2048]{2,1,0:T(8,128)(2,1)S(1)}, bf16[4,32,2048]{2,1,0:T(8,128)(2,1)S(1)}, u32[]{:S(2)}, u32[]{:S(2)}) collective-permute-start(bf16[4,32,2048]{2,1,0:T(8,128)(2,1)S(1)} %fusion.49), channel_id=1, source_target_pairs={{0,4},{4,0},{1,5},{5,1},{2,6},{6,2},{3,7},{7,3},{8,12},{12,8},{9,1... | collective-permute-start | bytes 1572872 | tf_op jit(solution)/shard_map/ppermute | solution.py:456
  450.0 20.2 %collective-permute-start.70 = (bf16[4,32,2048]{2,1,0:T(8,128)(2,1)S(1)}, bf16[4,32,2048]{2,1,0:T(8,128)(2,1)S(1)}, u32[]{:S(2)}, u32[]{:S(2)}) collective-permute-start(bf16[4,32,2048]{2,1,0:T(8,128)(2,1)S(1)} %get-tuple-element.59), channel_id=1, source_target_pairs={{1,2},{2,1},{5,6},{6,5},{9,10},{10,9},{13,14},{14,13},{17,18},{18,... | collective-permute-start | bytes 1572872 | tf_op jit(solution)/shard_map/ppermute | solution.py:516
  454.6 15.6 %collective-permute-start.69 = (bf16[4,32,2048]{2,1,0:T(8,128)(2,1)S(1)}, bf16[4,32,2048]{2,1,0:T(8,128)(2,1)S(1)}, u32[]{:S(2)}, u32[]{:S(2)}) collective-permute-start(bf16[4,32,2048]{2,1,0:T(8,128)(2,1)S(1)} %get-tuple-element.58), channel_id=1, source_target_pairs={{0,2},{3,1},{1,0},{2,3},{4,6},{7,5},{5,4},{6,7},{8,10},{11,9},{9,8... | collective-permute-start | bytes 1572872 | tf_op jit(solution)/shard_map/ppermute | solution.py:511
  459.1 64.2 %collective-permute-start.66 = (bf16[2,64,2048]{2,1,0:T(8,128)(2,1)S(1)}, bf16[2,64,2048]{2,1,0:T(8,128)(2,1)S(1)}, u32[]{:S(2)}, u32[]{:S(2)}) collective-permute-start(bf16[2,64,2048]{2,1,0:T(8,128)(2,1)S(1)} %select_convert_fusion.1), channel_id=1, source_target_pairs={{0,8},{8,0},{16,24},{24,16},{1,9},{9,1},{17,25},{25,17},{2,10},{10... | collective-permute-start | bytes 1572872 | tf_op jit(solution)/shard_map/ppermute | solution.py:529
  470.5 59.5 %collective-permute-start.74 = (bf16[2,64,2048]{2,1,0:T(8,128)(2,1)S(1)}, bf16[2,64,2048]{2,1,0:T(8,128)(2,1)S(1)}, u32[]{:S(2)}, u32[]{:S(2)}) collective-permute-start(bf16[2,64,2048]{2,1,0:T(8,128)(2,1)S(1)} %select_convert_fusion), channel_id=1, source_target_pairs={{0,8},{8,0},{16,24},{24,16},{1,9},{9,1},{17,25},{25,17},{2,10},{10... | collective-permute-start | bytes 1572872 | tf_op jit(solution)/shard_map/ppermute | solution.py:529
  509.4 139.2 %collective-permute-start.35 = (bf16[512,1024]{1,0:T(8,128)(2,1)S(1)}, bf16[512,1024]{1,0:T(8,128)(2,1)}, u32[]{:S(2)}, u32[]{:S(2)}) collective-permute-start(bf16[512,1024]{1,0:T(8,128)(2,1)S(1)} %copy-done.23), channel_id=1, source_target_pairs={{0,0},{1,2},{2,1},{3,3},{4,4},{5,6},{6,5},{7,7},{8,8},{9,10},{10,9... | collective-permute-start | bytes 3145736 | tf_op jit(solution)/shard_map/ppermute | solution.py:452
  513.0 125.9 %collective-permute-start.37 = (bf16[512,1024]{1,0:T(8,128)(2,1)}, bf16[512,1024]{1,0:T(8,128)(2,1)}, u32[]{:S(2)}, u32[]{:S(2)}) collective-permute-start(bf16[512,1024]{1,0:T(8,128)(2,1)} %fusion.15), channel_id=1, source_target_pairs={{0,2},{2,0},{1,3},{3,1},{4,6},{6,4},{5,7},{7,5},{8,10},{10,8},{9,1... | collective-permute-start | bytes 3145736 | tf_op jit(solution)/shard_map/ppermute | solution.py:456
  514.5 85.3 %collective-permute-start.43 = (bf16[4,2,32,1536]{3,2,0,1:T(8,128)(2,1)}, bf16[4,2,32,1536]{3,2,0,1:T(8,128)(2,1)}, u32[]{:S(2)}, u32[]{:S(2)}) collective-permute-start(bf16[4,2,32,1536]{3,2,0,1:T(8,128)(2,1)} %bitcast.320), channel_id=1, source_target_pairs={{1,2},{2,1},{5,6},{6,5},{9,10},{10,9},{13,14},{14,13},{17,18},{18,... | collective-permute-start | bytes 2359304 | tf_op jit(solution)/shard_map/ppermute | solution.py:516
  523.2 10.4 %collective-permute-start.47 = (f32[72,128]{1,0:T(8,128)S(1)}, f32[72,128]{1,0:T(8,128)S(1)}, u32[]{:S(2)}, u32[]{:S(2)}) collective-permute-start(f32[72,128]{1,0:T(8,128)S(1)} %maximum_bitcast_fusion), channel_id=1, source_target_pairs={{0,4},{4,0},{1,5},{5,1},{2,6},{6,2},{3,7},{7,3},{8,12},{12,8},{9,1... | collective-permute-start | bytes 110600 | tf_op jit(solution)/shard_map/ppermute | solution.py:456
  530.0 41.3 %collective-permute-start.56 = (bf16[4,2,32,512]{3,2,0,1:T(8,128)(2,1)}, bf16[4,2,32,512]{3,2,0,1:T(8,128)(2,1)}, u32[]{:S(2)}, u32[]{:S(2)}) collective-permute-start(bf16[4,2,32,512]{3,2,0,1:T(8,128)(2,1)} %bitcast.322), channel_id=1, source_target_pairs={{1,2},{2,1},{5,6},{6,5},{9,10},{10,9},{13,14},{14,13},{17,18},{18,... | collective-permute-start | bytes 786440 | tf_op jit(solution)/shard_map/ppermute | solution.py:516
  550.7 10.1 %collective-permute-start.67 = (bf16[64,2048]{1,0:T(8,128)(2,1)}, bf16[64,2048]{1,0:T(8,128)(2,1)}, u32[]{:S(2)}, u32[]{:S(2)}) collective-permute-start(bf16[64,2048]{1,0:T(8,128)(2,1)} %fusion.66), channel_id=1, source_target_pairs={{0,24},{24,0},{8,16},{16,8},{1,25},{25,1},{9,17},{17,9},{2,26},{26... | collective-permute-start | bytes 786440 | tf_op jit(solution)/shard_map/ppermute | solution.py:532
  560.8 10.4 %collective-permute-start.52 = (bf16[4,2,32,512]{3,2,0,1:T(8,128)(2,1)}, bf16[4,2,32,512]{3,2,0,1:T(8,128)(2,1)S(1)}, u32[]{:S(2)}, u32[]{:S(2)}) collective-permute-start(bf16[4,2,32,512]{3,2,0,1:T(8,128)(2,1)} %bitcast.356), channel_id=1, source_target_pairs={{0,4},{4,0},{1,5},{5,1},{2,6},{6,2},{3,7},{7,3},{8,12},{12,8},{9,1... | collective-permute-start | bytes 786440 | tf_op jit(solution)/shard_map/ppermute | solution.py:456
  579.9 21.0 %collective-permute-start.42 = (bf16[4,2,32,1536]{3,2,0,1:T(8,128)(2,1)S(1)}, bf16[4,2,32,1536]{3,2,0,1:T(8,128)(2,1)S(1)}, u32[]{:S(2)}, u32[]{:S(2)}) collective-permute-start(bf16[4,2,32,1536]{3,2,0,1:T(8,128)(2,1)S(1)} %copy-done.49), channel_id=1, source_target_pairs={{0,2},{3,1},{1,0},{2,3},{4,6},{7,5},{5,4},{6,7},{8,10},{11,9},{9,8... | collective-permute-start | bytes 2359304 | tf_op jit(solution)/shard_map/ppermute | solution.py:511
  598.2 13.5 %collective-permute-start.39 = (bf16[4,2,32,1536]{3,2,0,1:T(8,128)(2,1)S(1)}, bf16[4,2,32,1536]{3,2,0,1:T(8,128)(2,1)S(1)}, u32[]{:S(2)}, u32[]{:S(2)}) collective-permute-start(bf16[4,2,32,1536]{3,2,0,1:T(8,128)(2,1)S(1)} %bitcast.351), channel_id=1, source_target_pairs={{0,4},{4,0},{1,5},{5,1},{2,6},{6,2},{3,7},{7,3},{8,12},{12,8},{9,1... | collective-permute-start | bytes 2359304 | tf_op jit(solution)/shard_map/ppermute | solution.py:456
  599.7 48.3 %collective-permute-start.59 = (bf16[64,512]{1,0:T(8,128)(2,1)S(1)}, bf16[64,512]{1,0:T(8,128)(2,1)S(1)}, u32[]{:S(2)}, u32[]{:S(2)}) collective-permute-start(bf16[64,512]{1,0:T(8,128)(2,1)S(1)} %fusion.91), channel_id=1, source_target_pairs={{0,24},{24,0},{8,16},{16,8},{1,25},{25,1},{9,17},{17,9},{2,26},{26... | collective-permute-start | bytes 196616 | tf_op jit(solution)/shard_map/ppermute | solution.py:532
  602.4 25.8 %collective-permute-start.44 = (bf16[4,32,1536]{2,1,0:T(8,128)(2,1)S(1)}, bf16[4,32,1536]{2,1,0:T(8,128)(2,1)S(1)}, u32[]{:S(2)}, u32[]{:S(2)}) collective-permute-start(bf16[4,32,1536]{2,1,0:T(8,128)(2,1)S(1)} %fusion.59), channel_id=1, source_target_pairs={{0,4},{4,0},{1,5},{5,1},{2,6},{6,2},{3,7},{7,3},{8,12},{12,8},{9,1... | collective-permute-start | bytes 1179656 | tf_op jit(solution)/shard_map/ppermute | solution.py:456
  612.0 21.7 %collective-permute-start.41 = (bf16[4,32,1536]{2,1,0:T(8,128)(2,1)S(1)}, bf16[4,32,1536]{2,1,0:T(8,128)(2,1)S(1)}, u32[]{:S(2)}, u32[]{:S(2)}) collective-permute-start(bf16[4,32,1536]{2,1,0:T(8,128)(2,1)S(1)} %get-tuple-element.71), channel_id=1, source_target_pairs={{1,2},{2,1},{5,6},{6,5},{9,10},{10,9},{13,14},{14,13},{17,18},{18,... | collective-permute-start | bytes 1179656 | tf_op jit(solution)/shard_map/ppermute | solution.py:516
  637.3 9.2 %collective-permute-start.45 = (bf16[2,64,1536]{2,1,0:T(8,128)(2,1)S(1)}, bf16[2,64,1536]{2,1,0:T(8,128)(2,1)S(1)}, u32[]{:S(2)}, u32[]{:S(2)}) collective-permute-start(bf16[2,64,1536]{2,1,0:T(8,128)(2,1)S(1)} %select_convert_fusion.2), channel_id=1, source_target_pairs={{0,8},{8,0},{16,24},{24,16},{1,9},{9,1},{17,25},{25,17},{2,10},{10... | collective-permute-start | bytes 1179656 | tf_op jit(solution)/shard_map/ppermute | solution.py:529
  642.0 16.1 %collective-permute-start.38 = (bf16[512,1024]{1,0:T(8,128)(2,1)S(1)}, bf16[512,1024]{1,0:T(8,128)(2,1)S(1)}, u32[]{:S(2)}, u32[]{:S(2)}) collective-permute-start(bf16[512,1024]{1,0:T(8,128)(2,1)S(1)} %add_convert_fusion.1), channel_id=1, source_target_pairs={{0,0},{1,2},{2,1},{3,3},{4,4},{5,6},{6,5},{7,7},{8,8},{9,10},{10,9... | collective-permute-start | bytes 3145736 | tf_op jit(solution)/shard_map/ppermute | solution.py:452
  (98 other events, 1170.6 us)

commit v5 on v4

--- a/solution.py
+++ b/solution.py
@@ -448,8 +448,24 @@
     return jnp.dot(left, right, preferred_element_type=F32)
 
 
+INTO_CORE = [(2, 0), (1, 3), (0, 1), (3, 2)]
+OUT_OF_CORE = [(0, 2), (3, 1), (1, 0), (2, 3)]
+CROSS = [(2, 1), (1, 2)]
+CORES = ("c", "y")
+
+
+def tie(value, *others):
+    return lax.optimization_barrier((value,) + others)[0]
+
+
+def exchange(*moves):
+    return lax.optimization_barrier(
+        tuple(lax.ppermute(value, axis, steps) for value, axis, steps in moves)
+    )
+
+
 def turn(value):
-    return lax.ppermute(value, ("c", "y"), TURN)
+    return lax.ppermute(value, CORES, TURN)
 
 
 def swap(value, axis):
@@ -462,13 +478,17 @@
     )
 
 
-def gather_far(value, z):
-    far = lax.ppermute(value, "z", FAR)
+def pair_core(value, got, cross, c, y, axis):
+    first = jnp.where(c == y, value, got)
+    second = jnp.where(c == y, got, cross)
+    return pair_up(first, second, c, axis)
+
+
+def far_pair(value, far, z):
     return jnp.where(z < 2, jnp.stack([value, far]), jnp.stack([far, value]))
 
 
-def gather_near(pair, z):
-    other = lax.ppermute(pair, "z", NEAR)
+def whole_line(pair, other, z):
     return jnp.where(
         (z == 0) | (z == 3),
         jnp.stack([pair[0], other[0], other[1], pair[1]]),
@@ -476,84 +496,96 @@
     )
 
 
-def gather_c(value, c, y, axis):
-    got = lax.ppermute(value, ("c", "y"), [(2, 0), (1, 3), (0, 1), (3, 2)])
-    cross = lax.ppermute(value, ("c", "y"), [(2, 1), (1, 2)])
-    first = jnp.where(c == y, value, got)
-    second = jnp.where(c == y, got, cross)
-    return pair_up(first, second, c, axis)
-
-
-def gather_x(value, x, axis):
-    return pair_up(value, swap(value, "x"), x, axis)
-
-
-def gather_first(value, x, c, y):
-    half = value.shape[1] // 2
-    return (gather_x(value[:, :half], x, 1), gather_c(value[:, half:], c, y, 1))
-
-
-def gather_last(parts, x, c, y):
-    left = gather_c(parts[0], c, y, 2)
-    right = gather_x(parts[1], x, 1)
-    return jnp.concatenate([left, right], axis=3).reshape(-1, left.shape[-1])
-
-
-def tie(value, *others):
-    return lax.optimization_barrier((value,) + others)[0]
-
-
-def sum_c(blocks, c, y):
+def first_moves(line):
+    half = line.shape[1] // 2
+    low, high = line[:, :half], line[:, half:]
+    return ((low, "x", SWAP), (high, CORES, INTO_CORE), (high, CORES, CROSS))
+
+
+def first_parts(line, moved, x, c, y):
+    half = line.shape[1] // 2
+    return (
+        pair_up(line[:, :half], moved[0], x, 1),
+        pair_core(line[:, half:], moved[1], moved[2], c, y, 1),
+    )
+
+
+def last_moves(parts):
+    return ((parts[1], "x", SWAP), (parts[0], CORES, INTO_CORE), (parts[0], CORES, CROSS))
+
+
+def full_rows(parts, moved, x, c, y):
+    low = pair_core(parts[0], moved[1], moved[2], c, y, 2)
+    high = pair_up(parts[1], moved[0], x, 1)
+    return jnp.concatenate([low, high], axis=3).reshape(-1, low.shape[-1])
+
+
+def at(blocks, index, axis):
+    return lax.dynamic_index_in_dim(blocks, index, axis, keepdims=False)
+
+
+def core_moves(blocks, c, y):
     axis = blocks.ndim - 3
-    mine = lax.dynamic_index_in_dim(blocks, c, axis, keepdims=False)
-    other = lax.dynamic_index_in_dim(blocks, 1 - c, axis, keepdims=False)
-    other_low = other.astype(BF)
-    got = lax.ppermute(
-        jnp.where(c == y, other_low, mine.astype(BF)),
-        ("c", "y"),
-        [(0, 2), (3, 1), (1, 0), (2, 3)],
-    )
-    cross = lax.ppermute(other_low, ("c", "y"), [(1, 2), (2, 1)])
+    mine, other = at(blocks, c, axis), at(blocks, 1 - c, axis)
+    given = jnp.where(c == y, other, mine).astype(BF)
+    return ((given, CORES, OUT_OF_CORE), (other.astype(BF), CORES, CROSS))
+
+
+def core_sum(blocks, got, cross, c, y):
+    mine = at(blocks, c, blocks.ndim - 3)
     return got.astype(F32) + jnp.where(c == y, mine.astype(F32), cross.astype(F32))
 
 
-def sum_x(blocks, x, axis):
-    theirs = lax.dynamic_index_in_dim(blocks, 1 - x, axis, keepdims=False)
-    mine = lax.dynamic_index_in_dim(blocks, x, axis, keepdims=False)
-    return mine.astype(F32) + swap(theirs.astype(BF), "x").astype(F32)
-
-
-def sum_z(blocks, z):
+def x_move(blocks, x):
+    return (at(blocks, 1 - x, 1).astype(BF), "x", SWAP)
+
+
+def x_sum(blocks, got, x):
+    return at(blocks, x, 1).astype(F32) + got.astype(F32)
+
+
+def near_move(line, z):
     ends = (z == 0) | (z == 3)
-    outer, inner = jnp.stack([blocks[0], blocks[3]]), blocks[1:3]
-    pair = jnp.where(ends, outer, inner) + lax.ppermute(
-        jnp.where(ends, inner, outer).astype(BF), "z", NEAR
-    ).astype(F32)
-    given = lax.ppermute(jnp.where(z < 2, pair[1], pair[0]).astype(BF), "z", FAR)
-    return jnp.where(z < 2, pair[0], pair[1]) + given.astype(F32)
-
-
-def weight_sum(left, right, z, x, c, y):
-    blocks = contract_rows(left, right).astype(BF).reshape(4, 2, 2, 64, right.shape[1])
-    low = sum_x(blocks[..., :32, :], x, 1)
-    high = sum_c(blocks[..., 32:, :], c, y)
-    low = sum_c(low, c, y)
-    high = sum_x(high, x, 1)
-    return sum_z(jnp.concatenate([low, high], axis=1), z)
-
-
-def sum_other(value, step):
-    if step == "0":
-        return lax.ppermute(value, "z", NEAR)
-    if step == "1":
-        return lax.ppermute(value, "z", FAR)
-    return swap(value, step)
-
-
-def sum_chips(value, steps):
-    for step in steps:
-        value = value + sum_other(value, step)
-    return value
+    outer, inner = jnp.stack([line[0], line[3]]), line[1:3]
+    return (jnp.where(ends, inner, outer).astype(BF), "z", NEAR)
+
+
+def near_sum(line, got, z):
+    ends = (z == 0) | (z == 3)
+    return jnp.where(ends, jnp.stack([line[0], line[3]]), line[1:3]) + got.astype(F32)
+
+
+def far_move(pair, z):
+    return (jnp.where(z < 2, pair[1], pair[0]).astype(BF), "z", FAR)
+
+
+def far_sum(pair, got, z):
+    return jnp.where(z < 2, pair[0], pair[1]) + got.astype(F32)
+
+
+def blocks_of(left, right):
+    return contract_rows(left, right).astype(BF).reshape(4, 2, 2, 64, right.shape[1])
+
+
+def sum_moves(blocks, x, c, y):
+    return (x_move(blocks[..., :32, :], x),) + core_moves(blocks[..., 32:, :], c, y)
+
+
+def sum_parts(blocks, moved, x, c, y):
+    return (
+        x_sum(blocks[..., :32, :], moved[0], x),
+        core_sum(blocks[..., 32:, :], moved[1], moved[2], c, y),
+    )
+
+
+def line_moves(parts, x, c, y):
+    return (x_move(parts[1], x),) + core_moves(parts[0], c, y)
+
+
+def line_of(parts, moved, x, c, y):
+    return jnp.concatenate(
+        [core_sum(parts[0], moved[1], moved[2], c, y), x_sum(parts[1], moved[0], x)], axis=1
+    )
 
 
 def tile_bounds(row_lengths, token_count):
@@ -642,7 +674,11 @@
 def attend(bounds, qkv, seg_col, seg_row):
     count, wide = qkv.shape
     pairs = wide // 3 // 128
-    column = lambda shift: pl.BlockSpec((count, 128), lambda i: (0, shift + i))
+    group = pairs // 2
+    column = lambda part: pl.BlockSpec(
+        (count, 128), lambda i: (0, (i // group) * 3 * group + part * group + i % group)
+    )
+    mixed_column = pl.BlockSpec((count, 128), lambda i: (0, i))
     whole = lambda shape: pl.BlockSpec(shape, lambda i: (0, 0))
     return pl.pallas_call(
         attend_kernel,
@@ -650,12 +686,12 @@
         in_specs=[
             pl.BlockSpec(memory_space=pltpu.SMEM),
             column(0),
-            column(pairs),
-            column(2 * pairs),
+            column(1),
+            column(2),
             whole((count, 1)),
             whole((1, count)),
         ],
-        out_specs=[column(0), pl.BlockSpec((1, 8, count), lambda i: (i, 0, 0))],
+        out_specs=[mixed_column, pl.BlockSpec((1, 8, count), lambda i: (i, 0, 0))],
         out_shape=[
             jax.ShapeDtypeStruct((count, wide // 3), BF),
             jax.ShapeDtypeStruct((pairs, 8, count), F32),
@@ -734,22 +770,24 @@
     sums_ref[0, 1:2, :] = jnp.sum(grad_value.astype(F32), axis=0, keepdims=True)
 
 
-def attend_back(bounds, qkv, mixed, grad_mixed, lse, seg_col, seg_row):
-    count, wide = qkv.shape
+def attend_back(bounds, group, qkv, mixed, grad_mixed, lse, seg_col, seg_row):
+    count = qkv.shape[0]
+    wide = qkv.shape[1] // 2
     pairs = wide // 3 // 128
     column = lambda shift: pl.BlockSpec((count, 128), lambda i: (0, shift + i))
     whole = lambda shape: pl.BlockSpec(shape, lambda i: (0, 0))
+    first = group * pairs
     return pl.pallas_call(
         attend_back_kernel,
         grid=(pairs,),
         in_specs=[
             pl.BlockSpec(memory_space=pltpu.SMEM),
-            column(0),
-            column(pairs),
-            column(2 * pairs),
-            column(0),
-            column(0),
-            pl.BlockSpec((1, 8, count), lambda i: (i, 0, 0)),
+            column(3 * first),
+            column(3 * first + pairs),
+            column(3 * first + 2 * pairs),
+            column(first),
+            column(first),
+            pl.BlockSpec((1, 8, count), lambda i: (first + i, 0, 0)),
             whole((count, 1)),
             whole((1, count)),
         ],
@@ -991,34 +1029,50 @@
     chip_count = lengths.shape[0]
     half_queries = NQ_ROW // 2
     query_total = chip_count * half_queries
-    qkv_rows = jnp.concatenate([w_qkv[0], w_qkv[1], w_qkv[2]], axis=1)
+    quarter = half_width // 2
+    qkv_rows = jnp.concatenate(
+        [w_qkv[k][:, g * quarter : (g + 1) * quarter] for g in range(2) for k in range(3)], axis=1
+    )
     pair_rows = jnp.pad(pairing.astype(BF), ((0, 63), (0, 128 - half_queries)))
     mid_rows = jnp.concatenate([w_up, w_out.T, pair_rows], axis=1)
-    qkv_pair = gather_far(qkv_rows, z)
-    mid_pair = gather_far(tie(mid_rows, qkv_pair), z)
-    qkv_line = gather_near(qkv_pair, z)
-    mid_line = gather_near(mid_pair, z)
-    qkv_parts = gather_first(qkv_line, x, c, y)
-    down_pair = gather_far(tie(w_down.T, mid_pair), z)
-    full_qkv = gather_last(qkv_parts, x, c, y)
-    mid_parts = gather_first(tie(mid_line, *qkv_parts), x, c, y)
-    down_line = gather_near(down_pair, z)
-    full_mid = gather_last(mid_parts, x, c, y)
-    down_parts = gather_first(tie(down_line, *mid_parts), x, c, y)
-    full_down = gather_last(down_parts, x, c, y)
+    bias = jnp.concatenate([b_qv.reshape(-1), b_up])[None].astype(F32)
+    down_rows = turn(w_down.T)
+    got = exchange((qkv_rows, "z", FAR), (tokens, "c", SWAP), (bias, "y", SWAP))
+    qkv_pair = far_pair(qkv_rows, got[0], z)
+    row = jnp.where(c == y, tokens, got[1])
+    bias = jnp.where(c == y, bias, got[2])
+    got = exchange((qkv_pair, "z", NEAR), (tie(mid_rows, qkv_pair), "z", FAR))
+    qkv_line = whole_line(qkv_pair, got[0], z)
+    mid_pair = far_pair(mid_rows, got[1], z)
+    full_down = lax.all_gather(tie(down_rows, qkv_line), ("z", "x", "y"), axis=0, tiled=True)
+    got = exchange(*first_moves(qkv_line), (mid_pair, "z", NEAR))
+    qkv_parts = first_parts(qkv_line, got, x, c, y)
+    mid_line = whole_line(mid_pair, got[3], z)
+    got = exchange(*last_moves(qkv_parts))
+    full_qkv = full_rows(qkv_parts, got, x, c, y)
+    got = exchange(*first_moves(tie(mid_line, full_qkv)))
+    mid_parts = first_parts(mid_line, got, x, c, y)
+    got = exchange(*last_moves(mid_parts))
+    full_mid = full_rows(mid_parts, got, x, c, y)
     full_out = full_mid[:, up_wide : up_wide + half_width]
     pairs = full_mid[:, up_wide + half_width :].reshape(chip_count, 64, 128)
     pairs = pairs[:, 0, :half_queries].astype(jnp.int32).reshape(1, query_total)
-    row = jnp.where(c == y, tokens, swap(tokens, "c"))
-    bias = jnp.concatenate([b_qv.reshape(-1), b_up])[None].astype(F32)
-    bias = jnp.where(c == y, bias, swap(bias, "y"))
     row_lengths = lax.dynamic_index_in_dim(lengths, chip, 0, keepdims=False)
     segments = segments_of(row_lengths, token_count)
     seg_col, seg_row = segments[:, None], segments[None, :]
     query_span = NQ_ROW * QLEN
     bounds = tile_bounds(row_lengths, token_count)
+    no_bias = jnp.zeros((1, quarter), F32)
     qkv_bias = jnp.concatenate(
-        [bias[:, :half_width], jnp.zeros_like(bias[:, :half_width]), bias[:, half_width : 2 * half_width]],
+        [
+            part
+            for g in range(2)
+            for part in (
+                bias[:, g * quarter : (g + 1) * quarter],
+                no_bias,
+                bias[:, half_width + g * quarter : half_width + (g + 1) * quarter],
+            )
+        ],
         axis=1,
     )
     qkv = (dot(row, full_qkv) + qkv_bias).astype(BF)
@@ -1125,10 +1179,15 @@
     grad_ffn = grad_second.astype(BF)
     down_bias = jnp.sum(grad_ffn.astype(F32), axis=0)
     grad_ffn_all = jnp.concatenate([grad_ffn, swap(grad_ffn, "c")], axis=0)
-    down_part = weight_sum(grad_ffn_all, activation, z, x, c, y)
+    down_blocks = contract_rows(grad_ffn_all, activation).astype(BF)
+    down_part = turn(
+        lax.psum_scatter(down_blocks, ("z", "x", "y"), scatter_dimension=0, tiled=True)
+    ).astype(F32)
     grad_up = (dot(grad_ffn_all, full_down) * slope.astype(F32)).astype(BF)
     up_bias = jnp.sum(grad_up.astype(F32), axis=0)
-    up_part = weight_sum(normed_all, grad_up, z, x, c, y)
+    up_blocks = blocks_of(normed_all, grad_up)
+    up_moved = exchange(*sum_moves(up_blocks, x, c, y))
+    up_parts = sum_parts(up_blocks, up_moved, x, c, y)
     full_up = full_mid[:, :up_wide]
     grad_normed = (
         row_sum(lambda which: grad_up[which * share : (which + 1) * share], full_up, True)
@@ -1145,43 +1204,81 @@
         jnp.concatenate([grad_attn, other_attn], axis=0),
         jnp.concatenate([other_attn, grad_attn], axis=0),
     )
-    out_part = weight_sum(grad_attn_all, mixed, z, x, c, y)
     grad_mixed = dot(grad_attn_all, full_out).astype(BF)
-    grads, grad_sums = attend_back(bounds, qkv, mixed, grad_mixed, lse, seg_col, seg_row)
-    y_out = turn(tie(result_low, grads))
-    qkv_part = weight_sum(row, grads, z, x, c, y)
-    grad_input = turn(
-        (
-            row_sum(
-                lambda which: rows_of(grads, other_start if which else own_start, share),
-                full_qkv,
-                True,
-            )
-            + grad_first
-        ).astype(BF)
-    )
-
+    out_blocks = blocks_of(grad_attn_all, mixed)
+    grad_mixed, *up_parts = lax.optimization_barrier((grad_mixed,) + tuple(up_parts))
+    up_moved = exchange(*line_moves(up_parts, x, c, y), x_move(out_blocks, x))
+    up_line = line_of(up_parts, up_moved, x, c, y)
+    out_line = x_sum(out_blocks, up_moved[3], x)
+    grads_one, sums_one = attend_back(bounds, 0, qkv, mixed, grad_mixed, lse, seg_col, seg_row)
+    grad_mixed, up_line, out_line = lax.optimization_barrier((grad_mixed, up_line, out_line))
+    up_moved = exchange(near_move(up_line, z), *core_moves(out_line, c, y))
+    up_pair = near_sum(up_line, up_moved[0], z)
+    out_line = core_sum(out_line, up_moved[1], up_moved[2], c, y)
+    grads_two, sums_two = attend_back(
+        bounds, 1, qkv, mixed, tie(grad_mixed, grads_one), lse, seg_col, seg_row
+    )
+    grads_one = tie(grads_one, grads_two)
+    proj_half = rows_of(proj_grad, own_start, share) + swap(
+        rows_of(proj_grad, other_start, share), "c"
+    )
     shared = jnp.stack([gain_one, gain_two, shift_one, shift_two, out_bias, down_bias])
     half_sums = jnp.concatenate(
-        [grad_sums[:, 0].reshape(-1), grad_sums[:, 1].reshape(-1), up_bias]
-    )
-    small = jnp.concatenate([shared.reshape(-1), half_sums]).reshape(-1, 128)
-    small = sum_chips(small, "xy01")
+        [
+            sums_one[:, 0].reshape(-1),
+            sums_two[:, 0].reshape(-1),
+            sums_one[:, 1].reshape(-1),
+            sums_two[:, 1].reshape(-1),
+            up_bias,
+        ]
+    )
+    small = jnp.concatenate([shared.reshape(-1, 128), half_sums.reshape(-1, 128), proj_half])
+
+    qkv_blocks = jnp.concatenate(
+        [blocks_of(row, grads_one), blocks_of(row, grads_two)], axis=4
+    )
+    qkv_blocks, up_pair, out_line = lax.optimization_barrier((qkv_blocks, up_pair, out_line))
+    moved = exchange(
+        *sum_moves(qkv_blocks, x, c, y), far_move(up_pair, z), near_move(out_line, z)
+    )
+    qkv_parts = sum_parts(qkv_blocks, moved, x, c, y)
+    up_part = far_sum(up_pair, moved[3], z)
+    out_pair = near_sum(out_line, moved[4], z)
+
+    def input_terms(start):
+        return contract_cols(
+            rows_of(grads_one, start, share), full_qkv[:, : 3 * quarter]
+        ) + contract_cols(rows_of(grads_two, start, share), full_qkv[:, 3 * quarter :])
+
+    other_terms = swap(input_terms(other_start).astype(BF), "c")
+    grad_input = (input_terms(own_start) + other_terms.astype(F32) + grad_first).astype(BF)
+    moved = exchange(*line_moves(qkv_parts, x, c, y), far_move(out_pair, z), (small, "y", SWAP))
+    qkv_line = line_of(qkv_parts, moved, x, c, y)
+    out_part = far_sum(out_pair, moved[3], z)
+    small = small + moved[4]
+    moved = exchange(near_move(qkv_line, z), (small, "x", SWAP))
+    qkv_pair = near_sum(qkv_line, moved[0], z)
+    small = small + moved[1]
+    y_out = turn(tie(result_low, grad_input, qkv_line))
+    grad_input = turn(tie(grad_input, qkv_line))
+    moved = exchange(far_move(qkv_pair, z), (small, "z", FAR))
+    qkv_part = far_sum(qkv_pair, moved[0], z)
+    small = small + moved[1]
+    small = small + lax.ppermute(small, "z", NEAR)
     other_small = swap(small, "c")
     shared_rows = 6 * width // 128
+    small_rows = small.shape[0] - share
     shared = (small[:shared_rows] + other_small[:shared_rows]).reshape(6, width)
-    half_sums = jnp.where(c == y, small[shared_rows:], other_small[shared_rows:]).reshape(-1)
-    proj_half = rows_of(proj_grad, own_start, share) + swap(
-        rows_of(proj_grad, other_start, share), "c"
-    )
-    for step in ("x", "y", "0", "1"):
-        proj_half = proj_half + sum_other(proj_half.astype(BF), step).astype(F32)
-    proj_sum = pair_up(proj_half, swap(proj_half, "c"), c, 0).reshape(width, -1)
+    half_sums = jnp.where(
+        c == y, small[shared_rows:small_rows], other_small[shared_rows:small_rows]
+    ).reshape(-1)
+    proj_sum = pair_up(small[small_rows:], other_small[small_rows:], c, 0).reshape(width, -1)
+    qkv_part = qkv_part.reshape(64, 2, 3, quarter).transpose(2, 0, 1, 3).reshape(3, 64, half_width)
     return (
         y_out,
         loss_out,
         grad_input,
-        jnp.stack([qkv_part[:, k * half_width : (k + 1) * half_width] for k in range(3)]),
+        qkv_part,
         half_sums[: 2 * half_width].reshape(2, half_width),
         out_part.T,
         shared[4],

time: 672 us -> 603 us (0.90)
  starting transfers between devices: 153 us -> 116 us
  waiting for transfers between devices: 233 us -> 198 us
  other arithmetic: 64.9 us -> 47.6 us
  between operations: 3.21 us -> 16.2 us
  matrix products: 60.5 us -> 70.7 us
    ppermute x33 -> x12, waiting for transfers between devices: 86.1 us -> 9.01 us  [swap(): return lax.ppermute(value, axis, SWAP)]
    ppermute x49 -> x48, waiting for transfers between devices: 134 us -> 181 us  [the longest x42 174 us: exchange(): lax.ppermute(value, axis, steps)]
    ppermute x33 -> x12, starting transfers between devices: 44.6 us -> 10.6 us  [swap(): return lax.ppermute(value, axis, SWAP)]
    dot_general x10 -> x12, matrix products: 22.3 us -> 34.2 us  [contract_cols(): lax.dot_general(left, right, (((1,), (1,)), ((), ())), precision=precisio...]
    add x27 -> x20, other arithmetic: 14.7 us -> 8.63 us  [the longest x5 2.88 us: core_sum(): got.astype(F32) + jnp.where(c == y, mine.astype(F32), cross.astype(F32))]
    unnamed x163 -> x167, local copies, waits for them, and re-layouts: 16.6 us -> 21.4 us
    ppermute x49 -> x48, starting transfers between devices: 99.6 us -> 96.6 us  [the longest x42 64.3 us: exchange(): lax.ppermute(value, axis, steps)]
    dot_general x6 -> x7, matrix products: 19.8 us -> 18.7 us  [contract_rows(): lax.dot_general(left, right, (((0,), (0,)), ((), ())), precision=precisio...]
  transfers between devices with their start and end apart: 84 -> 64, of which waited for: 44 -> 38; matrix products, arithmetic and copies ran while one was open for 22% -> 18% of each run, Pallas kernels for 7% -> 11%
where the time goes in v5:
time: 603 us; the launch traced here: 596 us
  waiting for transfers between devices  198 us (33%)
  starting transfers between devices  116 us (19%)
  Pallas kernels  90.1 us (15%)
  matrix products  70.7 us (12%)
  other arithmetic  47.6 us (8%)
  local copies, waits for them, and re-layouts  46.5 us (8%)
  between operations  16.2 us (3%)
  blocking collectives  11.4 us (2%)
    ppermute x42, waiting for transfers between devices, exchange(): lax.ppermute(value, axis, steps)  174 us
    ppermute x42, starting transfers between devices, exchange(): lax.ppermute(value, axis, steps)  64.3 us
    dot_general x12, matrix products, contract_cols(): lax.dot_general(left, right, (((1,), (1,)), ((), ())), precision=precisio...  34.2 us
    pallas_call x2, Pallas kernels, attend_back(): pl.pallas_call(attend_back_kernel, grid=(pairs,), in_specs=[pl.BlockSpec(...  27.5 us
    unnamed x167, local copies, waits for them, and re-layouts  21.4 us
    ppermute x5, starting transfers between devices, turn(): return lax.ppermute(value, CORES, TURN)  21.2 us
    pallas_call x1, Pallas kernels, attend(): pl.pallas_call(attend_kernel, grid=(pairs,), in_specs=[pl.BlockSpec(memor...  19.3 us
    dot_general x7, matrix products, contract_rows(): lax.dot_general(left, right, (((0,), (0,)), ((), ())), precision=precisio...  18.7 us
  transfers between devices with their start and end apart: 64, of which 38 were waited for; matrix products, arithmetic and copies ran while one was open for 18% of the time, Pallas kernels for 11%

profile of v5, /device:TPU:1, one launch (start us, length us, event | category | flops | bytes accessed | tf_op | source)
XLA Modules:
  0.0 596.5 jit_solution(6810208334758092692)
XLA Ops:
  8.3 4.2 collective-permute-start
  24.1 14.8 %collective-permute-done.4 = bf16[64,2688]{1,0:T(8,128)(2,1)S(1)} collective-permute-done((bf16[64,2688]{1,0:T(8,128)(2,1)}, bf16[64,2688]{1,0:T(8,128)(2,1)S(1)}, u32[]{:S(2)}, u32[]{:S(2)}) %collective-permute-start.4) | collective-permute-done | bytes 344096 | tf_op jit(solution)/shard_map/ppermute | solution.py:463
  39.2 3.6 collective-permute-start.6
  42.8 3.3 collective-permute-start.7
  49.9 3.7 collective-permute-done.7
  53.7 3.2 collective-permute-done.5
  56.9 7.9 %collective-permute-done.8 = bf16[2,64,2688]{2,1,0:T(8,128)(2,1)S(1)} collective-permute-done((bf16[2,64,2688]{2,1,0:T(8,128)(2,1)S(1)}, bf16[2,64,2688]{2,1,0:T(8,128)(2,1)S(1)}, u32[]{:S(2)}, u32[]{:S(2)}) %collective-permute-start.8) | collective-permute-done | bytes 688160 | tf_op jit(solution)/shard_map/ppermute | solution.py:463
  68.4 13.3 %collective-permute-done.10 = bf16[4,2,32,1536]{3,2,0,1:T(8,128)(2,1)S(1)} collective-permute-done((bf16[4,2,32,1536]{3,2,0,1:T(8,128)(2,1)S(1)}, bf16[4,2,32,1536]{3,2,0,1:T(8,128)(2,1)S(1)}, u32[]{:S(2)}, u32[]{:S(2)}) %collective-permute-start.10) | collective-permute-done | bytes 786464 | tf_op jit(solution)/shard_map/ppermute | solution.py:463
  81.7 2.9 collective-permute-done.11
  89.6 3.1 collective-permute-start.14
  93.1 3.1 broadcast_select_fusion
  96.2 15.9 %collective-permute-done.12 = bf16[4,32,2688]{2,1,0:T(8,128)(2,1)S(1)} collective-permute-done((bf16[4,32,2688]{2,1,0:T(8,128)(2,1)}, bf16[4,32,2688]{2,1,0:T(8,128)(2,1)S(1)}, u32[]{:S(2)}, u32[]{:S(2)}) %collective-permute-start.12) | collective-permute-done | bytes 688160 | tf_op jit(solution)/shard_map/ppermute | solution.py:463
  116.1 2.3 collective-permute-start.17
  119.1 3.6 add_convert_fusion.q_ref.k_ref.v_ref
  122.7 19.3 %shard_map.254 = (bf16[1024,512]{1,0:T(8,128)(2,1)S(1)}, f32[4,8,1024]{2,1,0:T(8,128)S(1)}) custom-call(s32[2,4]{1,0:T(2,128)S(1)} %pad_add_fusion.bounds, bf16[1024,1536]{1,0:T(8,128)(2,1)S(1)} %add_convert_fusion.q_ref.k_ref.v_ref, bf16[1024,1536]{1,0:T(8,128)(2,1)S(1)} %add_convert_fusion.q_ref.k_ref.v_ref, ...), custom_call_target="tpu_custom_call" | custom-call | flops 2147483648 | bytes 12582912 | tf_op jit(solution)/shard_map/pallas_call | solution.py:683
  142.2 6.3 %collective-permute-done.16 = bf16[4,2,32,2688]{3,2,0,1:T(8,128)(2,1)S(1)} collective-permute-done((bf16[4,2,32,2688]{3,2,0,1:T(8,128)(2,1)S(1)}, bf16[4,2,32,2688]{3,2,0,1:T(8,128)(2,1)S(1)}, u32[]{:S(2)}, u32[]{:S(2)}) %collective-permute-start.16) | collective-permute-done | bytes 1376288 | tf_op jit(solution)/shard_map/ppermute | solution.py:463
  148.5 3.2 collective-permute-done.17
  151.7 11.2 %collective-permute-done.15 = bf16[4,2,32,2688]{3,2,0,1:T(8,128)(2,1)S(1)} collective-permute-done((bf16[4,2,32,2688]{3,2,0,1:T(8,128)(2,1)S(1)}, bf16[4,2,32,2688]{3,2,0,1:T(8,128)(2,1)S(1)}, u32[]{:S(2)}, u32[]{:S(2)}) %collective-permute-start.15) | collective-permute-done | bytes 1376288 | tf_op jit(solution)/shard_map/ppermute | solution.py:463
  165.6 2.4 copy-done.4
  172.7 3.2 fusion.122
  181.2 17.7 %shard_map.255 = (bf16[1024,2048]{1,0:T(8,128)(2,1)S(1)}, bf16[1024,2048]{1,0:T(8,128)(2,1)S(1)}) custom-call(bf16[1024,1024]{1,0:T(8,128)(2,1)S(1)} %pad_maximum_fusion.4.x_ref, bf16[1024,2688]{1,0:T(8,128)(2,1)S(1)} %bitcast.249, f32[1,2048]{1,0:T(1,128)S(1)} %slice.392.b_ref), custom_call_target="tpu_custom_call" | custom-call | flops 4294967296 | bytes 14680064 | tf_op jit(solution)/shard_map/pallas_call | solution.py:845
  203.0 5.3 fusion.11
  208.6 2.4 collective-permute-done.21
  211.1 2.8 fusion.123
  220.8 4.2 all-to-all-start
  233.1 5.0 all-to-all-done
  239.1 10.0 %shard_map.256 = f32[24,2048]{1,0:T(8,128)S(1)} custom-call(bf16[2048,128]{1,0:T(8,128)(2,1)} %bitcast.38.q_ref, bf16[1024,128]{1,0:T(8,128)(2,1)S(1)} %copy-done.10, s32[1,1024]{1,0:T(1,128)S(1)} %compare_select_fusion.seg_row.seg_ref), custom_call_target="tpu_custom_call" | custom-call | flops 3221225472 | bytes 786432 | tf_op jit(solution)/shard_map/pallas_call | solution.py:898
  249.8 11.4 %all_to_all.15 = f32[16,8,128]{2,1,0:T(8,128)S(1)} all-to-all(f32[16,8,128]{2,1,0:T(8,128)S(1)} %broadcast_in_dim.29), channel_id=1, replica_groups=mesh['z'=4,'x'=2,'c'=2,'y'=2] {'z','x','y'}, dimensions={0} | all-to-all | bytes 131072 | tf_op jit(solution)/shard_map/all_to_all | solution.py:1136
  262.7 15.8 %shard_map.257 = (bf16[2048,128]{1,0:T(8,128)(2,1)S(1)}, f32[768,128]{1,0:T(8,128)S(1)}) custom-call(bf16[2048,128]{1,0:T(8,128)(2,1)} %bitcast.38.q_ref, bf16[1024,128]{1,0:T(8,128)(2,1)S(1)} %copy-done.11, s32[1,1024]{1,0:T(1,128)S(1)} %compare_select_fusion.seg_row.seg_ref, f32[24,2048]{1,0:T(8,128)S(1)} %convolution_divide_fusion.coef_ref), custom_call_target="tpu_custom_call" | custom-call | flops 4831838208 | bytes 1572864 | tf_op jit(solution)/shard_map/pallas_call | solution.py:974
  280.0 4.6 all-to-all-start.2
  284.7 6.0 %collective-permute-start.22 = (bf16[512,1024]{1,0:T(8,128)(2,1)}, bf16[512,1024]{1,0:T(8,128)(2,1)}, u32[]{:S(2)}, u32[]{:S(2)}) collective-permute-start(bf16[512,1024]{1,0:T(8,128)(2,1)} %param.29), channel_id=1, source_target_pairs={{0,0},{1,2},{2,1},{3,3},{4,4},{5,6},{6,5},{7,7},{8,8},{9,10},{10,9... | collective-permute-start | bytes 3145736 | tf_op jit(solution)/shard_map/ppermute | solution.py:468
  292.5 2.6 all-to-all-done.2
  297.9 5.8 collective-permute-start.24
  306.6 3.1 multiply_reduce_fusion
  309.8 2.9 convert_reduce_fusion.1
  320.2 9.2 %convert_reduce_fusion = (f32[2048]{0:T(1024)}, bf16[1024,2048]{1,0:T(8,128)(2,1)S(1)}) fusion(bf16[1024,2048]{1,0:T(8,128)(2,1)} %copy-done.15, bf16[1024,2048]{1,0:T(8,128)(2,1)} %all-gather.2.cloned.1.call-done, bf16[512,1024]{1,0:T(8,128)(2,1)} %collective-permute-done.25, bf16[512,1024]{1,0:T(8,128)(2,1)} %get-tuple-element.169), kind=kOutput, calls=%fused_computation | convolution fusion | flops 4309645312 | bytes 14688256 | tf_op jit(solution)/shard_map/dot_general | solution.py:448
  329.4 7.1 %fusion.14 = bf16[512,1024]{1,0:T(8,128)(2,1)} fusion(bf16[1024,2688]{1,0:T(8,128)(2,1)} %bitcast.244, bf16[1024,2048]{1,0:T(8,128)(2,1)S(1)} %get-tuple-element.249), kind=kOutput, calls=%fused_computation.68 | convolution fusion | flops 2148007936 | bytes 7340032 | tf_op jit(solution)/shard_map/dot_general | solution.py:43
  336.6 4.9 convolution_convert_fusion.1
  345.5 3.2 collective-permute-start.30
  351.3 7.8 %convolution_convert_fusion = bf16[1024,2048]{1,0:T(8,128)(2,1)} fusion(bf16[1024,2048]{1,0:T(8,128)(2,1)S(1)} %copy-done.14, bf16[512,1024]{1,0:T(8,128)(2,1)} %collective-permute-done.25, bf16[512,1024]{1,0:T(8,128)(2,1)} %get-tuple-element.169), kind=kOutput, calls=%fused_computation.4 | convolution fusion | flops 4301258752 | bytes 10485760 | tf_op jit(solution)/shard_map/dot_general | solution.py:33
  359.2 5.3 fusion.2
  364.5 2.5 multiply_reduce_fusion.1
  367.1 2.4 convert_reduce_fusion.2
  370.1 18.6 %collective-permute-done.30 = bf16[4,2,32,2048]{3,2,0,1:T(8,128)(2,1)} collective-permute-done((bf16[4,2,32,2048]{3,2,0,1:T(8,128)(2,1)}, bf16[4,2,32,2048]{3,2,0,1:T(8,128)(2,1)}, u32[]{:S(2)}, u32[]{:S(2)}) %collective-permute-start.30) | collective-permute-done | bytes 1048608 | tf_op jit(solution)/shard_map/ppermute | solution.py:463
  392.9 2.5 convolution_convert_fusion.5.grad_ref
  398.0 6.5 %collective-permute-start.34 = (bf16[4,2,64,512]{3,2,1,0:T(8,128)(2,1)S(1)}, bf16[4,2,64,512]{3,2,1,0:T(8,128)(2,1)S(1)}, u32[]{:S(2)}, u32[]{:S(2)}) collective-permute-start(bf16[4,2,64,512]{3,2,1,0:T(8,128)(2,1)S(1)} %dynamic-slice_bitcast_fusion.2), channel_id=1, source_target_pairs={{0,4},{4,0},{1,5},{5,1},{2,6},{6,2},{3,7},{7,3},{8,12},{12,8},{9,1... | collective-permute-start | bytes 1572872 | tf_op jit(solution)/shard_map/ppermute | solution.py:463
  406.9 13.6 %shard_map.258 = (bf16[1024,768]{1,0:T(8,128)(2,1)S(1)}, f32[2,8,128]{2,1,0:T(8,128)S(1)}) custom-call(s32[2,4]{1,0:T(2,128)S(1)} %pad_add_fusion.bounds, bf16[1024,1536]{1,0:T(8,128)(2,1)S(1)} %add_convert_fusion.q_ref.k_ref.v_ref, bf16[1024,1536]{1,0:T(8,128)(2,1)S(1)} %add_convert_fusion.q_ref.k_ref.v_ref, ...), custom_call_target="tpu_custom_call" | custom-call | flops 2684354560 | bytes 12582912 | tf_op jit(solution)/shard_map/pallas_call | solution.py:780
  422.4 9.9 %collective-permute-done.32 = bf16[4,32,2048]{2,1,0:T(8,128)(2,1)S(1)} collective-permute-done((bf16[4,32,2048]{2,1,0:T(8,128)(2,1)S(1)}, bf16[4,32,2048]{2,1,0:T(8,128)(2,1)S(1)}, u32[]{:S(2)}, u32[]{:S(2)}) %collective-permute-start.32) | collective-permute-done | bytes 524320 | tf_op jit(solution)/shard_map/ppermute | solution.py:463
  433.3 27.8 %collective-permute-done.33 = bf16[4,32,2048]{2,1,0:T(8,128)(2,1)S(1)} collective-permute-done((bf16[4,32,2048]{2,1,0:T(8,128)(2,1)S(1)}, bf16[4,32,2048]{2,1,0:T(8,128)(2,1)S(1)}, u32[]{:S(2)}, u32[]{:S(2)}) %collective-permute-start.33) | collective-permute-done | bytes 524320 | tf_op jit(solution)/shard_map/ppermute | solution.py:463
  461.9 13.9 %shard_map.259 = (bf16[1024,768]{1,0:T(8,128)(2,1)S(1)}, f32[2,8,128]{2,1,0:T(8,128)S(1)}) custom-call(s32[2,4]{1,0:T(2,128)S(1)} %pad_add_fusion.bounds, bf16[1024,1536]{1,0:T(8,128)(2,1)S(1)} %add_convert_fusion.q_ref.k_ref.v_ref, bf16[1024,1536]{1,0:T(8,128)(2,1)S(1)} %add_convert_fusion.q_ref.k_ref.v_ref, ...), custom_call_target="tpu_custom_call" | custom-call | flops 2684354560 | bytes 12582912 | tf_op jit(solution)/shard_map/pallas_call | solution.py:780
  482.4 4.8 collective-permute-start.38
  488.6 3.6 collective-permute-done.38
  493.2 2.9 collective-permute-start.41
  496.2 3.1 collective-permute-start.39
  500.3 9.8 %collective-permute-done.43 = bf16[2,64,512]{2,1,0:T(8,128)(2,1)S(1)} collective-permute-done((bf16[2,64,512]{2,1,0:T(8,128)(2,1)S(1)}, bf16[2,64,512]{2,1,0:T(8,128)(2,1)S(1)}, u32[]{:S(2)}, u32[]{:S(2)}) %collective-permute-start.43) | collective-permute-done | bytes 131104 | tf_op jit(solution)/shard_map/ppermute | solution.py:463
  512.1 2.5 collective-permute-done.39
  514.9 3.7 collective-permute-start.46
  523.3 2.5 collective-permute-done.47
  536.9 3.5 collective-permute-done.53
  541.1 3.0 collective-permute-start.55
  544.1 7.3 %collective-permute-start.52 = (bf16[512,1024]{1,0:T(8,128)(2,1)}, bf16[512,1024]{1,0:T(8,128)(2,1)}, u32[]{:S(2)}, u32[]{:S(2)}) collective-permute-start(bf16[512,1024]{1,0:T(8,128)(2,1)} %add_convert_fusion.1), channel_id=1, source_target_pairs={{0,0},{1,2},{2,1},{3,3},{4,4},{5,6},{6,5},{7,7},{8,8},{9,10},{10,9... | collective-permute-start | bytes 3145736 | tf_op jit(solution)/shard_map/ppermute | solution.py:468
  553.4 11.2 %collective-permute-start.57 = (f32[584,128]{1,0:T(8,128)S(1)}, f32[584,128]{1,0:T(8,128)S(1)}, u32[]{:S(2)}, u32[]{:S(2)}) collective-permute-start(f32[584,128]{1,0:T(8,128)S(1)} %add.472), channel_id=1, source_target_pairs={{0,8},{8,0},{16,24},{24,16},{1,9},{9,1},{17,25},{25,17},{2,10},{10... | collective-permute-start | bytes 897032 | tf_op jit(solution)/shard_map/ppermute | solution.py:1267
  566.2 4.3 collective-permute-done.57
  576.1 3.6 collective-permute-start.59
  (439 shorter events, 148.9 us)
Async XLA Ops:
  7.2 195.7 %all-gather.2.cloned.1.call-start = ((), (), s32[]{:S(2)}) async-start(), calls=%async_computation.4 | async-start | bytes 4456448 | tf_op jit(solution)/shard_map/all_gather | solution.py:1047
  8.3 15.2 %collective-permute-start = (bf16[64,1536]{1,0:T(8,128)(2,1)S(1)}, bf16[64,1536]{1,0:T(8,128)(2,1)S(1)}, u32[]{:S(2)}, u32[]{:S(2)}) collective-permute-start(bf16[64,1536]{1,0:T(8,128)(2,1)S(1)} %slice_dynamic-update-slice_fusion), channel_id=1, source_target_pairs={{0,24},{24,0},{8,16},{16,8},{1,25},{25,1},{9,17},{17,9},{2,26},{26... | collective-permute-start | bytes 589832 | tf_op jit(solution)/shard_map/ppermute | solution.py:463
  12.5 10.9 %collective-permute-start.1 = (bf16[1024,1024]{1,0:T(8,128)(2,1)}, bf16[1024,1024]{1,0:T(8,128)(2,1)S(1)}, u32[]{:S(2)}, u32[]{:S(2)}) collective-permute-start(bf16[1024,1024]{1,0:T(8,128)(2,1)} %param.15), channel_id=1, source_target_pairs={{0,2},{2,0},{1,3},{3,1},{4,6},{6,4},{5,7},{7,5},{8,10},{10,8},{9,1... | collective-permute-start | bytes 6291464 | tf_op jit(solution)/shard_map/ppermute | solution.py:463
  14.8 8.6 %collective-permute-start.2 = (f32[1,3072]{1,0:T(1,128)S(1)}, f32[1,3072]{1,0:T(1,128)S(1)}, u32[]{:S(2)}, u32[]{:S(2)}) collective-permute-start(f32[1,3072]{1,0:T(1,128)S(1)} %maximum_convert_fusion), channel_id=1, source_target_pairs={{0,1},{1,0},{2,3},{3,2},{4,5},{5,4},{6,7},{7,6},{8,9},{9,8},{10,11... | collective-permute-start | bytes 36872 | tf_op jit(solution)/shard_map/ppermute | solution.py:463
  16.1 80.0 %collective-permute-start.20 = (bf16[64,2048]{1,0:T(8,128)(2,1)}, bf16[64,2048]{1,0:T(8,128)(2,1)}, u32[]{:S(2)}, u32[]{:S(2)}) collective-permute-start(bf16[64,2048]{1,0:T(8,128)(2,1)} %bitcast.305), channel_id=1, source_target_pairs={{0,0},{1,2},{2,1},{3,3},{4,4},{5,6},{6,5},{7,7},{8,8},{9,10},{10,9... | collective-permute-start | bytes 786440 | tf_op jit(solution)/shard_map/ppermute | solution.py:468
  23.5 15.4 %collective-permute-start.3 = (bf16[2,64,1536]{2,1,0:T(8,128)(2,1)S(1)}, bf16[2,64,1536]{2,1,0:T(8,128)(2,1)S(1)}, u32[]{:S(2)}, u32[]{:S(2)}) collective-permute-start(bf16[2,64,1536]{2,1,0:T(8,128)(2,1)S(1)} %maximum_select_fusion.14), channel_id=1, source_target_pairs={{0,8},{8,0},{16,24},{24,16},{1,9},{9,1},{17,25},{25,17},{2,10},{10... | collective-permute-start | bytes 1179656 | tf_op jit(solution)/shard_map/ppermute | solution.py:463
  23.6 15.3 %collective-permute-start.4 = (bf16[64,2688]{1,0:T(8,128)(2,1)}, bf16[64,2688]{1,0:T(8,128)(2,1)S(1)}, u32[]{:S(2)}, u32[]{:S(2)}) collective-permute-start(bf16[64,2688]{1,0:T(8,128)(2,1)} %get-tuple-element.85), channel_id=1, source_target_pairs={{0,24},{24,0},{8,16},{16,8},{1,25},{25,1},{9,17},{17,9},{2,26},{26... | collective-permute-start | bytes 1032200 | tf_op jit(solution)/shard_map/ppermute | solution.py:463
  39.2 10.7 %collective-permute-start.6 = (bf16[4,32,1536]{2,1,0:T(8,128)(2,1)S(1)}, bf16[4,32,1536]{2,1,0:T(8,128)(2,1)S(1)}, u32[]{:S(2)}, u32[]{:S(2)}) collective-permute-start(bf16[4,32,1536]{2,1,0:T(8,128)(2,1)S(1)} %get-tuple-element.207), channel_id=1, source_target_pairs={{2,0},{1,3},{0,1},{3,2},{6,4},{5,7},{4,5},{7,6},{10,8},{9,11},{8,9... | collective-permute-start | bytes 1179656 | tf_op jit(solution)/shard_map/ppermute | solution.py:463
  42.8 10.9 %collective-permute-start.7 = (bf16[4,32,1536]{2,1,0:T(8,128)(2,1)S(1)}, bf16[4,32,1536]{2,1,0:T(8,128)(2,1)S(1)}, u32[]{:S(2)}, u32[]{:S(2)}) collective-permute-start(bf16[4,32,1536]{2,1,0:T(8,128)(2,1)S(1)} %get-tuple-element.207), channel_id=1, source_target_pairs={{2,1},{1,2},{6,5},{5,6},{10,9},{9,10},{14,13},{13,14},{18,17},{17,... | collective-permute-start | bytes 1179656 | tf_op jit(solution)/shard_map/ppermute | solution.py:463
  46.1 10.8 %collective-permute-start.5 = (bf16[4,32,1536]{2,1,0:T(8,128)(2,1)S(1)}, bf16[4,32,1536]{2,1,0:T(8,128)(2,1)S(1)}, u32[]{:S(2)}, u32[]{:S(2)}) collective-permute-start(bf16[4,32,1536]{2,1,0:T(8,128)(2,1)S(1)} %get-tuple-element.208), channel_id=1, source_target_pairs={{0,4},{4,0},{1,5},{5,1},{2,6},{6,2},{3,7},{7,3},{8,12},{12,8},{9,1... | collective-permute-start | bytes 1179656 | tf_op jit(solution)/shard_map/ppermute | solution.py:463
  47.5 17.3 %collective-permute-start.8 = (bf16[2,64,2688]{2,1,0:T(8,128)(2,1)S(1)}, bf16[2,64,2688]{2,1,0:T(8,128)(2,1)S(1)}, u32[]{:S(2)}, u32[]{:S(2)}) collective-permute-start(bf16[2,64,2688]{2,1,0:T(8,128)(2,1)S(1)} %maximum_select_fusion.12), channel_id=1, source_target_pairs={{0,8},{8,0},{16,24},{24,16},{1,9},{9,1},{17,25},{25,17},{2,10},{10... | collective-permute-start | bytes 2064392 | tf_op jit(solution)/shard_map/ppermute | solution.py:463
  65.1 16.7 %collective-permute-start.10 = (bf16[4,2,32,1536]{3,2,0,1:T(8,128)(2,1)S(1)}, bf16[4,2,32,1536]{3,2,0,1:T(8,128)(2,1)S(1)}, u32[]{:S(2)}, u32[]{:S(2)}) collective-permute-start(bf16[4,2,32,1536]{3,2,0,1:T(8,128)(2,1)S(1)} %maximum_select_fusion.10), channel_id=1, source_target_pairs={{2,0},{1,3},{0,1},{3,2},{6,4},{5,7},{4,5},{7,6},{10,8},{9,11},{8,9... | collective-permute-start | bytes 2359304 | tf_op jit(solution)/shard_map/ppermute | solution.py:463
  65.5 19.2 %collective-permute-start.11 = (bf16[4,2,32,1536]{3,2,0,1:T(8,128)(2,1)S(1)}, bf16[4,2,32,1536]{3,2,0,1:T(8,128)(2,1)S(1)}, u32[]{:S(2)}, u32[]{:S(2)}) collective-permute-start(bf16[4,2,32,1536]{3,2,0,1:T(8,128)(2,1)S(1)} %maximum_select_fusion.10), channel_id=1, source_target_pairs={{2,1},{1,2},{6,5},{5,6},{10,9},{9,10},{14,13},{13,14},{18,17},{17,... | collective-permute-start | bytes 2359304 | tf_op jit(solution)/shard_map/ppermute | solution.py:463
  67.5 18.6 %collective-permute-start.9 = (bf16[4,2,32,1536]{3,2,1,0:T(8,128)(2,1)S(1)}, bf16[4,2,32,1536]{3,2,1,0:T(8,128)(2,1)S(1)}, u32[]{:S(2)}, u32[]{:S(2)}) collective-permute-start(bf16[4,2,32,1536]{3,2,1,0:T(8,128)(2,1)S(1)} %maximum_select_fusion.11), channel_id=1, source_target_pairs={{0,4},{4,0},{1,5},{5,1},{2,6},{6,2},{3,7},{7,3},{8,12},{12,8},{9,1... | collective-permute-start | bytes 2359304 | tf_op jit(solution)/shard_map/ppermute | solution.py:463
  89.6 22.5 %collective-permute-start.13 = (bf16[4,32,2688]{2,1,0:T(8,128)(2,1)}, bf16[4,32,2688]{2,1,0:T(8,128)(2,1)S(1)}, u32[]{:S(2)}, u32[]{:S(2)}) collective-permute-start(bf16[4,32,2688]{2,1,0:T(8,128)(2,1)} %get-tuple-element.196), channel_id=1, source_target_pairs={{2,0},{1,3},{0,1},{3,2},{6,4},{5,7},{4,5},{7,6},{10,8},{9,11},{8,9... | collective-permute-start | bytes 2064392 | tf_op jit(solution)/shard_map/ppermute | solution.py:463
  89.6 24.2 %collective-permute-start.14 = (bf16[4,32,2688]{2,1,0:T(8,128)(2,1)}, bf16[4,32,2688]{2,1,0:T(8,128)(2,1)}, u32[]{:S(2)}, u32[]{:S(2)}) collective-permute-start(bf16[4,32,2688]{2,1,0:T(8,128)(2,1)} %get-tuple-element.196), channel_id=1, source_target_pairs={{2,1},{1,2},{6,5},{5,6},{10,9},{9,10},{14,13},{13,14},{18,17},{17,... | collective-permute-start | bytes 2064392 | tf_op jit(solution)/shard_map/ppermute | solution.py:463
  92.7 19.4 %collective-permute-start.12 = (bf16[4,32,2688]{2,1,0:T(8,128)(2,1)}, bf16[4,32,2688]{2,1,0:T(8,128)(2,1)S(1)}, u32[]{:S(2)}, u32[]{:S(2)}) collective-permute-start(bf16[4,32,2688]{2,1,0:T(8,128)(2,1)} %get-tuple-element.197), channel_id=1, source_target_pairs={{0,4},{4,0},{1,5},{5,1},{2,6},{6,2},{3,7},{7,3},{8,12},{12,8},{9,1... | collective-permute-start | bytes 2064392 | tf_op jit(solution)/shard_map/ppermute | solution.py:463
  115.7 32.8 %collective-permute-start.16 = (bf16[4,2,32,2688]{3,2,0,1:T(8,128)(2,1)S(1)}, bf16[4,2,32,2688]{3,2,0,1:T(8,128)(2,1)S(1)}, u32[]{:S(2)}, u32[]{:S(2)}) collective-permute-start(bf16[4,2,32,2688]{3,2,0,1:T(8,128)(2,1)S(1)} %maximum_select_fusion.6), channel_id=1, source_target_pairs={{2,0},{1,3},{0,1},{3,2},{6,4},{5,7},{4,5},{7,6},{10,8},{9,11},{8,9... | collective-permute-start | bytes 4128776 | tf_op jit(solution)/shard_map/ppermute | solution.py:463
  116.1 35.6 %collective-permute-start.17 = (bf16[4,2,32,2688]{3,2,0,1:T(8,128)(2,1)S(1)}, bf16[4,2,32,2688]{3,2,0,1:T(8,128)(2,1)S(1)}, u32[]{:S(2)}, u32[]{:S(2)}) collective-permute-start(bf16[4,2,32,2688]{3,2,0,1:T(8,128)(2,1)S(1)} %maximum_select_fusion.6), channel_id=1, source_target_pairs={{2,1},{1,2},{6,5},{5,6},{10,9},{9,10},{14,13},{13,14},{18,17},{17,... | collective-permute-start | bytes 4128776 | tf_op jit(solution)/shard_map/ppermute | solution.py:463
  118.7 44.2 %collective-permute-start.15 = (bf16[4,2,32,2688]{3,2,0,1:T(8,128)(2,1)S(1)}, bf16[4,2,32,2688]{3,2,0,1:T(8,128)(2,1)S(1)}, u32[]{:S(2)}, u32[]{:S(2)}) collective-permute-start(bf16[4,2,32,2688]{3,2,0,1:T(8,128)(2,1)S(1)} %maximum_select_fusion.7), channel_id=1, source_target_pairs={{0,4},{4,0},{1,5},{5,1},{2,6},{6,2},{3,7},{7,3},{8,12},{12,8},{9,1... | collective-permute-start | bytes 4128776 | tf_op jit(solution)/shard_map/ppermute | solution.py:463
  169.7 3.0 collective-permute-start.18
  177.3 2.7 collective-permute-start.19
  208.3 2.7 collective-permute-start.21
  216.3 1.7 collective-permute-start.23
  220.8 17.3 %all-to-all-start = ((bf16[16,128,128]{2,1,0:T(8,128)(2,1)}), bf16[16,128,128]{2,1,0:T(8,128)(2,1)}, u32[]{:S(2)}, u32[]{:S(2)}) async-start(bf16[16,128,128]{2,1,0:T(8,128)(2,1)} %broadcast_in_dim.28), calls=%async_computation | async-start | bytes 1048576 | tf_op jit(solution)/shard_map/all_to_all | solution.py:1116
  280.0 15.2 %all-to-all-start.2 = ((bf16[16,128,128]{2,1,0:T(8,128)(2,1)}), bf16[16,128,128]{2,1,0:T(8,128)(2,1)}, u32[]{:S(2)}, u32[]{:S(2)}) async-start(bf16[16,128,128]{2,1,0:T(8,128)(2,1)} %bitcast.250), calls=%async_computation.2 | async-start | bytes 1048576 | tf_op jit(solution)/shard_map/all_to_all | solution.py:1157
  284.6 291.4 %reduce-scatter.2.cloned.1.call-start = ((), (), s32[]{:S(2)}) async-start(), calls=%async_computation.5 | async-start | bytes 4456448 | tf_op jit(solution)/shard_map/reduce_scatter | solution.py:1184
  284.7 22.0 %collective-permute-start.22 = (bf16[512,1024]{1,0:T(8,128)(2,1)}, bf16[512,1024]{1,0:T(8,128)(2,1)}, u32[]{:S(2)}, u32[]{:S(2)}) collective-permute-start(bf16[512,1024]{1,0:T(8,128)(2,1)} %param.29), channel_id=1, source_target_pairs={{0,0},{1,2},{2,1},{3,3},{4,4},{5,6},{6,5},{7,7},{8,8},{9,10},{10,9... | collective-permute-start | bytes 3145736 | tf_op jit(solution)/shard_map/ppermute | solution.py:468
  297.9 6.9 %collective-permute-start.24 = (f32[512,128]{1,0:T(8,128)S(1)}, f32[512,128]{1,0:T(8,128)S(1)}, u32[]{:S(2)}, u32[]{:S(2)}) collective-permute-start(f32[512,128]{1,0:T(8,128)S(1)} %constant_dynamic-slice_fusion.7), channel_id=1, source_target_pairs={{0,2},{2,0},{1,3},{3,1},{4,6},{6,4},{5,7},{7,5},{8,10},{10,8},{9,1... | collective-permute-start | bytes 786440 | tf_op jit(solution)/shard_map/ppermute | solution.py:472
  312.7 7.5 %collective-permute-start.25 = (bf16[512,1024]{1,0:T(8,128)(2,1)}, bf16[512,1024]{1,0:T(8,128)(2,1)}, u32[]{:S(2)}, u32[]{:S(2)}) collective-permute-start(bf16[512,1024]{1,0:T(8,128)(2,1)} %get-tuple-element.169), channel_id=1, source_target_pairs={{0,2},{2,0},{1,3},{3,1},{4,6},{6,4},{5,7},{7,5},{8,10},{10,8},{9,1... | collective-permute-start | bytes 3145736 | tf_op jit(solution)/shard_map/ppermute | solution.py:472
  314.5 3.9 collective-permute-start.48
  315.7 1.5 collective-permute-start.51
  336.5 28.0 %collective-permute-start.26 = (bf16[512,1024]{1,0:T(8,128)(2,1)}, bf16[512,1024]{1,0:T(8,128)(2,1)}, u32[]{:S(2)}, u32[]{:S(2)}) collective-permute-start(bf16[512,1024]{1,0:T(8,128)(2,1)} %fusion.14), channel_id=1, source_target_pairs={{0,2},{2,0},{1,3},{3,1},{4,6},{6,4},{5,7},{7,5},{8,10},{10,8},{9,1... | collective-permute-start | bytes 3145736 | tf_op jit(solution)/shard_map/ppermute | solution.py:472
  344.7 25.4 %collective-permute-start.29 = (bf16[4,2,32,2048]{3,2,0,1:T(8,128)(2,1)}, bf16[4,2,32,2048]{3,2,0,1:T(8,128)(2,1)}, u32[]{:S(2)}, u32[]{:S(2)}) collective-permute-start(bf16[4,2,32,2048]{3,2,0,1:T(8,128)(2,1)} %bitcast_select_fusion.2), channel_id=1, source_target_pairs={{0,2},{3,1},{1,0},{2,3},{4,6},{7,5},{5,4},{6,7},{8,10},{11,9},{9,8... | collective-permute-start | bytes 3145736 | tf_op jit(solution)/shard_map/ppermute | solution.py:463
  345.5 43.3 %collective-permute-start.30 = (bf16[4,2,32,2048]{3,2,0,1:T(8,128)(2,1)}, bf16[4,2,32,2048]{3,2,0,1:T(8,128)(2,1)}, u32[]{:S(2)}, u32[]{:S(2)}) collective-permute-start(bf16[4,2,32,2048]{3,2,0,1:T(8,128)(2,1)} %bitcast.239), channel_id=1, source_target_pairs={{2,1},{1,2},{6,5},{5,6},{10,9},{9,10},{14,13},{13,14},{18,17},{17,... | collective-permute-start | bytes 3145736 | tf_op jit(solution)/shard_map/ppermute | solution.py:463
  349.8 39.0 %collective-permute-start.28 = (bf16[4,2,32,2048]{3,2,1,0:T(8,128)(2,1)}, bf16[4,2,32,2048]{3,2,1,0:T(8,128)(2,1)}, u32[]{:S(2)}, u32[]{:S(2)}) collective-permute-start(bf16[4,2,32,2048]{3,2,1,0:T(8,128)(2,1)} %dynamic-slice_bitcast_fusion), channel_id=1, source_target_pairs={{0,4},{4,0},{1,5},{5,1},{2,6},{6,2},{3,7},{7,3},{8,12},{12,8},{9,1... | collective-permute-start | bytes 3145736 | tf_op jit(solution)/shard_map/ppermute | solution.py:463
  370.1 22.8 %collective-permute-start.27 = (bf16[512,1024]{1,0:T(8,128)(2,1)}, bf16[512,1024]{1,0:T(8,128)(2,1)S(1)}, u32[]{:S(2)}, u32[]{:S(2)}) collective-permute-start(bf16[512,1024]{1,0:T(8,128)(2,1)} %get-tuple-element.172), channel_id=1, source_target_pairs={{0,2},{2,0},{1,3},{3,1},{4,6},{6,4},{5,7},{7,5},{8,10},{10,8},{9,1... | collective-permute-start | bytes 3145736 | tf_op jit(solution)/shard_map/ppermute | solution.py:472
  398.0 24.4 %collective-permute-start.34 = (bf16[4,2,64,512]{3,2,1,0:T(8,128)(2,1)S(1)}, bf16[4,2,64,512]{3,2,1,0:T(8,128)(2,1)S(1)}, u32[]{:S(2)}, u32[]{:S(2)}) collective-permute-start(bf16[4,2,64,512]{3,2,1,0:T(8,128)(2,1)S(1)} %dynamic-slice_bitcast_fusion.2), channel_id=1, source_target_pairs={{0,4},{4,0},{1,5},{5,1},{2,6},{6,2},{3,7},{7,3},{8,12},{12,8},{9,1... | collective-permute-start | bytes 1572872 | tf_op jit(solution)/shard_map/ppermute | solution.py:463
  404.6 27.7 %collective-permute-start.32 = (bf16[4,32,2048]{2,1,0:T(8,128)(2,1)S(1)}, bf16[4,32,2048]{2,1,0:T(8,128)(2,1)S(1)}, u32[]{:S(2)}, u32[]{:S(2)}) collective-permute-start(bf16[4,32,2048]{2,1,0:T(8,128)(2,1)S(1)} %fusion.27), channel_id=1, source_target_pairs={{0,2},{3,1},{1,0},{2,3},{4,6},{7,5},{5,4},{6,7},{8,10},{11,9},{9,8... | collective-permute-start | bytes 1572872 | tf_op jit(solution)/shard_map/ppermute | solution.py:463
  404.6 28.7 %collective-permute-start.31 = (bf16[4,32,2048]{2,1,0:T(8,128)(2,1)S(1)}, bf16[4,32,2048]{2,1,0:T(8,128)(2,1)S(1)}, u32[]{:S(2)}, u32[]{:S(2)}) collective-permute-start(bf16[4,32,2048]{2,1,0:T(8,128)(2,1)S(1)} %fusion.46), channel_id=1, source_target_pairs={{0,4},{4,0},{1,5},{5,1},{2,6},{6,2},{3,7},{7,3},{8,12},{12,8},{9,1... | collective-permute-start | bytes 1572872 | tf_op jit(solution)/shard_map/ppermute | solution.py:463
  404.7 56.4 %collective-permute-start.33 = (bf16[4,32,2048]{2,1,0:T(8,128)(2,1)S(1)}, bf16[4,32,2048]{2,1,0:T(8,128)(2,1)S(1)}, u32[]{:S(2)}, u32[]{:S(2)}) collective-permute-start(bf16[4,32,2048]{2,1,0:T(8,128)(2,1)S(1)} %bitcast_convert_fusion), channel_id=1, source_target_pairs={{2,1},{1,2},{6,5},{5,6},{10,9},{9,10},{14,13},{13,14},{18,17},{17,... | collective-permute-start | bytes 1572872 | tf_op jit(solution)/shard_map/ppermute | solution.py:463
  480.8 11.4 %collective-permute-start.36 = (bf16[2,64,2048]{2,1,0:T(8,128)(2,1)S(1)}, bf16[2,64,2048]{2,1,0:T(8,128)(2,1)S(1)}, u32[]{:S(2)}, u32[]{:S(2)}) collective-permute-start(bf16[2,64,2048]{2,1,0:T(8,128)(2,1)S(1)} %select_convert_fusion), channel_id=1, source_target_pairs={{0,8},{8,0},{16,24},{24,16},{1,9},{9,1},{17,25},{25,17},{2,10},{10... | collective-permute-start | bytes 1572872 | tf_op jit(solution)/shard_map/ppermute | solution.py:463
  482.4 6.2 %collective-permute-start.37 = (bf16[4,64,512]{2,1,0:T(8,128)(2,1)S(1)}, bf16[4,64,512]{2,1,0:T(8,128)(2,1)S(1)}, u32[]{:S(2)}, u32[]{:S(2)}) collective-permute-start(bf16[4,64,512]{2,1,0:T(8,128)(2,1)S(1)} %fusion.47), channel_id=1, source_target_pairs={{0,2},{3,1},{1,0},{2,3},{4,6},{7,5},{5,4},{6,7},{8,10},{11,9},{9,8... | collective-permute-start | bytes 786440 | tf_op jit(solution)/shard_map/ppermute | solution.py:463
  482.4 9.8 %collective-permute-start.38 = (bf16[4,64,512]{2,1,0:T(8,128)(2,1)S(1)}, bf16[4,64,512]{2,1,0:T(8,128)(2,1)S(1)}, u32[]{:S(2)}, u32[]{:S(2)}) collective-permute-start(bf16[4,64,512]{2,1,0:T(8,128)(2,1)S(1)} %bitcast_convert_fusion.2), channel_id=1, source_target_pairs={{2,1},{1,2},{6,5},{5,6},{10,9},{9,10},{14,13},{13,14},{18,17},{17,... | collective-permute-start | bytes 786440 | tf_op jit(solution)/shard_map/ppermute | solution.py:463
  493.2 16.8 %collective-permute-start.40 = (bf16[4,2,32,1536]{3,2,0,1:T(8,128)(2,1)S(1)}, bf16[4,2,32,1536]{3,2,0,1:T(8,128)(2,1)S(1)}, u32[]{:S(2)}, u32[]{:S(2)}) collective-permute-start(bf16[4,2,32,1536]{3,2,0,1:T(8,128)(2,1)S(1)} %bitcast_select_fusion.5), channel_id=1, source_target_pairs={{0,2},{3,1},{1,0},{2,3},{4,6},{7,5},{5,4},{6,7},{8,10},{11,9},{9,8... | collective-permute-start | bytes 2359304 | tf_op jit(solution)/shard_map/ppermute | solution.py:463
  493.2 18.9 %collective-permute-start.41 = (bf16[4,2,32,1536]{3,2,0,1:T(8,128)(2,1)S(1)}, bf16[4,2,32,1536]{3,2,0,1:T(8,128)(2,1)S(1)}, u32[]{:S(2)}, u32[]{:S(2)}) collective-permute-start(bf16[4,2,32,1536]{3,2,0,1:T(8,128)(2,1)S(1)} %bitcast.267), channel_id=1, source_target_pairs={{2,1},{1,2},{6,5},{5,6},{10,9},{9,10},{14,13},{13,14},{18,17},{17,... | collective-permute-start | bytes 2359304 | tf_op jit(solution)/shard_map/ppermute | solution.py:463
  496.2 18.4 %collective-permute-start.39 = (bf16[4,2,32,1536]{3,2,1,0:T(8,128)(2,1)S(1)}, bf16[4,2,32,1536]{3,2,1,0:T(8,128)(2,1)S(1)}, u32[]{:S(2)}, u32[]{:S(2)}) collective-permute-start(bf16[4,2,32,1536]{3,2,1,0:T(8,128)(2,1)S(1)} %dynamic-slice_bitcast_fusion.1), channel_id=1, source_target_pairs={{0,4},{4,0},{1,5},{5,1},{2,6},{6,2},{3,7},{7,3},{8,12},{12,8},{9,1... | collective-permute-start | bytes 2359304 | tf_op jit(solution)/shard_map/ppermute | solution.py:463
  499.3 10.7 %collective-permute-start.42 = (bf16[64,2048]{1,0:T(8,128)(2,1)S(1)}, bf16[64,2048]{1,0:T(8,128)(2,1)S(1)}, u32[]{:S(2)}, u32[]{:S(2)}) collective-permute-start(bf16[64,2048]{1,0:T(8,128)(2,1)S(1)} %fusion.60), channel_id=1, source_target_pairs={{0,24},{24,0},{8,16},{16,8},{1,25},{25,1},{9,17},{17,9},{2,26},{26... | collective-permute-start | bytes 786440 | tf_op jit(solution)/shard_map/ppermute | solution.py:463
  499.8 10.2 %collective-permute-start.43 = (bf16[2,64,512]{2,1,0:T(8,128)(2,1)S(1)}, bf16[2,64,512]{2,1,0:T(8,128)(2,1)S(1)}, u32[]{:S(2)}, u32[]{:S(2)}) collective-permute-start(bf16[2,64,512]{2,1,0:T(8,128)(2,1)S(1)} %select_convert_fusion.4), channel_id=1, source_target_pairs={{0,8},{8,0},{16,24},{24,16},{1,9},{9,1},{17,25},{25,17},{2,10},{10... | collective-permute-start | bytes 393224 | tf_op jit(solution)/shard_map/ppermute | solution.py:463
  510.0 12.1 %collective-permute-start.49 = (f32[584,128]{1,0:T(8,128)S(1)}, f32[584,128]{1,0:T(8,128)S(1)}, u32[]{:S(2)}, u32[]{:S(2)}) collective-permute-start(f32[584,128]{1,0:T(8,128)S(1)} %pad_maximum_fusion.13), channel_id=1, source_target_pairs={{0,1},{1,0},{2,3},{3,2},{4,5},{5,4},{6,7},{7,6},{8,9},{9,8},{10,11... | collective-permute-start | bytes 897032 | tf_op jit(solution)/shard_map/ppermute | solution.py:463
  514.9 10.9 %collective-permute-start.46 = (bf16[4,32,1536]{2,1,0:T(8,128)(2,1)S(1)}, bf16[4,32,1536]{2,1,0:T(8,128)(2,1)S(1)}, u32[]{:S(2)}, u32[]{:S(2)}) collective-permute-start(bf16[4,32,1536]{2,1,0:T(8,128)(2,1)S(1)} %bitcast_convert_fusion.1), channel_id=1, source_target_pairs={{2,1},{1,2},{6,5},{5,6},{10,9},{9,10},{14,13},{13,14},{18,17},{17,... | collective-permute-start | bytes 1179656 | tf_op jit(solution)/shard_map/ppermute | solution.py:463
  518.7 8.8 %collective-permute-start.45 = (bf16[4,32,1536]{2,1,0:T(8,128)(2,1)S(1)}, bf16[4,32,1536]{2,1,0:T(8,128)(2,1)S(1)}, u32[]{:S(2)}, u32[]{:S(2)}) collective-permute-start(bf16[4,32,1536]{2,1,0:T(8,128)(2,1)S(1)} %fusion.36), channel_id=1, source_target_pairs={{0,2},{3,1},{1,0},{2,3},{4,6},{7,5},{5,4},{6,7},{8,10},{11,9},{9,8... | collective-permute-start | bytes 1179656 | tf_op jit(solution)/shard_map/ppermute | solution.py:463
  519.1 10.4 %collective-permute-start.44 = (bf16[4,32,1536]{2,1,0:T(8,128)(2,1)S(1)}, bf16[4,32,1536]{2,1,0:T(8,128)(2,1)S(1)}, u32[]{:S(2)}, u32[]{:S(2)}) collective-permute-start(bf16[4,32,1536]{2,1,0:T(8,128)(2,1)S(1)} %fusion.54), channel_id=1, source_target_pairs={{0,4},{4,0},{1,5},{5,1},{2,6},{6,2},{3,7},{7,3},{8,12},{12,8},{9,1... | collective-permute-start | bytes 1179656 | tf_op jit(solution)/shard_map/ppermute | solution.py:463
  520.8 5.0 collective-permute-start.47
  522.2 10.4 %collective-permute-start.35 = (bf16[512,1024]{1,0:T(8,128)(2,1)S(1)}, bf16[512,1024]{1,0:T(8,128)(2,1)S(1)}, u32[]{:S(2)}, u32[]{:S(2)}) collective-permute-start(bf16[512,1024]{1,0:T(8,128)(2,1)S(1)} %add_convert_fusion.2), channel_id=1, source_target_pairs={{0,2},{2,0},{1,3},{3,1},{4,6},{6,4},{5,7},{7,5},{8,10},{10,8},{9,1... | collective-permute-start | bytes 3145736 | tf_op jit(solution)/shard_map/ppermute | solution.py:472
  529.5 7.4 %collective-permute-start.54 = (f32[584,128]{1,0:T(8,128)S(1)}, f32[584,128]{1,0:T(8,128)S(1)}, u32[]{:S(2)}, u32[]{:S(2)}) collective-permute-start(f32[584,128]{1,0:T(8,128)S(1)} %fusion.104), channel_id=1, source_target_pairs={{0,4},{4,0},{1,5},{5,1},{2,6},{6,2},{3,7},{7,3},{8,12},{12,8},{9,1... | collective-permute-start | bytes 897032 | tf_op jit(solution)/shard_map/ppermute | solution.py:463
  531.4 9.0 %collective-permute-start.53 = (bf16[2,64,1536]{2,1,0:T(8,128)(2,1)S(1)}, bf16[2,64,1536]{2,1,0:T(8,128)(2,1)S(1)}, u32[]{:S(2)}, u32[]{:S(2)}) collective-permute-start(bf16[2,64,1536]{2,1,0:T(8,128)(2,1)S(1)} %select_convert_fusion.1), channel_id=1, source_target_pairs={{0,8},{8,0},{16,24},{24,16},{1,9},{9,1},{17,25},{25,17},{2,10},{10... | collective-permute-start | bytes 1179656 | tf_op jit(solution)/shard_map/ppermute | solution.py:463
  540.5 12.8 %collective-permute-start.56 = (f32[584,128]{1,0:T(8,128)S(1)}, f32[584,128]{1,0:T(8,128)S(1)}, u32[]{:S(2)}, u32[]{:S(2)}) collective-permute-start(f32[584,128]{1,0:T(8,128)S(1)} %add.470), channel_id=1, source_target_pairs={{0,24},{24,0},{8,16},{16,8},{1,25},{25,1},{9,17},{17,9},{2,26},{26... | collective-permute-start | bytes 897032 | tf_op jit(solution)/shard_map/ppermute | solution.py:463
  541.1 12.2 %collective-permute-start.55 = (bf16[64,1536]{1,0:T(8,128)(2,1)S(1)}, bf16[64,1536]{1,0:T(8,128)(2,1)S(1)}, u32[]{:S(2)}, u32[]{:S(2)}) collective-permute-start(bf16[64,1536]{1,0:T(8,128)(2,1)S(1)} %fusion.61), channel_id=1, source_target_pairs={{0,24},{24,0},{8,16},{16,8},{1,25},{25,1},{9,17},{17,9},{2,26},{26... | collective-permute-start | bytes 589832 | tf_op jit(solution)/shard_map/ppermute | solution.py:463
  544.1 30.3 %collective-permute-start.52 = (bf16[512,1024]{1,0:T(8,128)(2,1)}, bf16[512,1024]{1,0:T(8,128)(2,1)}, u32[]{:S(2)}, u32[]{:S(2)}) collective-permute-start(bf16[512,1024]{1,0:T(8,128)(2,1)} %add_convert_fusion.1), channel_id=1, source_target_pairs={{0,0},{1,2},{2,1},{3,3},{4,4},{5,6},{6,5},{7,7},{8,8},{9,10},{10,9... | collective-permute-start | bytes 3145736 | tf_op jit(solution)/shard_map/ppermute | solution.py:468
  551.4 24.0 %collective-permute-start.50 = (bf16[512,1024]{1,0:T(8,128)(2,1)S(1)}, bf16[512,1024]{1,0:T(8,128)(2,1)}, u32[]{:S(2)}, u32[]{:S(2)}) collective-permute-start(bf16[512,1024]{1,0:T(8,128)(2,1)S(1)} %copy-done.23), channel_id=1, source_target_pairs={{0,0},{1,2},{2,1},{3,3},{4,4},{5,6},{6,5},{7,7},{8,8},{9,10},{10,9... | collective-permute-start | bytes 3145736 | tf_op jit(solution)/shard_map/ppermute | solution.py:468
  553.4 17.1 %collective-permute-start.57 = (f32[584,128]{1,0:T(8,128)S(1)}, f32[584,128]{1,0:T(8,128)S(1)}, u32[]{:S(2)}, u32[]{:S(2)}) collective-permute-start(f32[584,128]{1,0:T(8,128)S(1)} %add.472), channel_id=1, source_target_pairs={{0,8},{8,0},{16,24},{24,16},{1,9},{9,1},{17,25},{25,17},{2,10},{10... | collective-permute-start | bytes 897032 | tf_op jit(solution)/shard_map/ppermute | solution.py:1267
  570.5 4.9 collective-permute-start.58
  576.1 7.9 %collective-permute-start.59 = (bf16[64,2048]{1,0:T(8,128)(2,1)}, bf16[64,2048]{1,0:T(8,128)(2,1)S(1)}, u32[]{:S(2)}, u32[]{:S(2)}) collective-permute-start(bf16[64,2048]{1,0:T(8,128)(2,1)} %reduce-scatter.2.cloned.1.call-done), channel_id=1, source_target_pairs={{0,0},{1,2},{2,1},{3,3},{4,4},{5,6},{6,5},{7,7},{8,8},{9,10},{10,9... | collective-permute-start | bytes 786440 | tf_op jit(solution)/shard_map/ppermute | solution.py:468
  (75 other events, 681.8 us)
Sparse Core Ops, SparseCore 0:
  96.3 86.2 all-gather.1
  359.2 109.2 reduce-scatter.1

commit v6 on v5

--- a/solution.py
+++ b/solution.py
@@ -448,9 +448,6 @@
     return jnp.dot(left, right, preferred_element_type=F32)
 
 
-INTO_CORE = [(2, 0), (1, 3), (0, 1), (3, 2)]
-OUT_OF_CORE = [(0, 2), (3, 1), (1, 0), (2, 3)]
-CROSS = [(2, 1), (1, 2)]
 CORES = ("c", "y")
 
 
@@ -464,10 +461,6 @@
     )
 
 
-def turn(value):
-    return lax.ppermute(value, CORES, TURN)
-
-
 def swap(value, axis):
     return lax.ppermute(value, axis, SWAP)
 
@@ -476,12 +469,6 @@
     return jnp.where(
         own_index == 0, jnp.stack([first, second], axis), jnp.stack([second, first], axis)
     )
-
-
-def pair_core(value, got, cross, c, y, axis):
-    first = jnp.where(c == y, value, got)
-    second = jnp.where(c == y, got, cross)
-    return pair_up(first, second, c, axis)
 
 
 def far_pair(value, far, z):
@@ -498,25 +485,21 @@
 
 def first_moves(line):
     half = line.shape[1] // 2
-    low, high = line[:, :half], line[:, half:]
-    return ((low, "x", SWAP), (high, CORES, INTO_CORE), (high, CORES, CROSS))
-
-
-def first_parts(line, moved, x, c, y):
+    return ((line[:, :half], "x", SWAP), (line[:, half:], "y", SWAP))
+
+
+def first_parts(line, moved, x, y):
     half = line.shape[1] // 2
-    return (
-        pair_up(line[:, :half], moved[0], x, 1),
-        pair_core(line[:, half:], moved[1], moved[2], c, y, 1),
-    )
+    return (pair_up(line[:, :half], moved[0], x, 1), pair_up(line[:, half:], moved[1], y, 1))
 
 
 def last_moves(parts):
-    return ((parts[1], "x", SWAP), (parts[0], CORES, INTO_CORE), (parts[0], CORES, CROSS))
-
-
-def full_rows(parts, moved, x, c, y):
-    low = pair_core(parts[0], moved[1], moved[2], c, y, 2)
-    high = pair_up(parts[1], moved[0], x, 1)
+    return ((parts[0], "y", SWAP), (parts[1], "x", SWAP))
+
+
+def full_rows(parts, moved, x, y):
+    low = pair_up(parts[0], moved[0], y, 2)
+    high = pair_up(parts[1], moved[1], x, 1)
     return jnp.concatenate([low, high], axis=3).reshape(-1, low.shape[-1])
 
 
@@ -524,24 +507,12 @@
     return lax.dynamic_index_in_dim(blocks, index, axis, keepdims=False)
 
 
-def core_moves(blocks, c, y):
-    axis = blocks.ndim - 3
-    mine, other = at(blocks, c, axis), at(blocks, 1 - c, axis)
-    given = jnp.where(c == y, other, mine).astype(BF)
-    return ((given, CORES, OUT_OF_CORE), (other.astype(BF), CORES, CROSS))
-
-
-def core_sum(blocks, got, cross, c, y):
-    mine = at(blocks, c, blocks.ndim - 3)
-    return got.astype(F32) + jnp.where(c == y, mine.astype(F32), cross.astype(F32))
-
-
-def x_move(blocks, x):
-    return (at(blocks, 1 - x, 1).astype(BF), "x", SWAP)
-
-
-def x_sum(blocks, got, x):
-    return at(blocks, x, 1).astype(F32) + got.astype(F32)
+def side_move(blocks, axis_name, own_index, axis):
+    return (at(blocks, 1 - own_index, axis).astype(BF), axis_name, SWAP)
+
+
+def side_sum(blocks, got, own_index, axis):
+    return at(blocks, own_index, axis).astype(F32) + got.astype(F32)
 
 
 def near_move(line, z):
@@ -567,24 +538,29 @@
     return contract_rows(left, right).astype(BF).reshape(4, 2, 2, 64, right.shape[1])
 
 
-def sum_moves(blocks, x, c, y):
-    return (x_move(blocks[..., :32, :], x),) + core_moves(blocks[..., 32:, :], c, y)
-
-
-def sum_parts(blocks, moved, x, c, y):
+def sum_moves(blocks, x, y):
+    half = blocks.shape[3] // 2
     return (
-        x_sum(blocks[..., :32, :], moved[0], x),
-        core_sum(blocks[..., 32:, :], moved[1], moved[2], c, y),
-    )
-
-
-def line_moves(parts, x, c, y):
-    return (x_move(parts[1], x),) + core_moves(parts[0], c, y)
-
-
-def line_of(parts, moved, x, c, y):
+        side_move(blocks[..., :half, :], "x", x, 1),
+        side_move(blocks[..., half:, :], "y", y, 2),
+    )
+
+
+def sum_parts(blocks, moved, x, y):
+    half = blocks.shape[3] // 2
+    return (
+        side_sum(blocks[..., :half, :], moved[0], x, 1),
+        side_sum(blocks[..., half:, :], moved[1], y, 2),
+    )
+
+
+def line_moves(parts, x, y):
+    return (side_move(parts[0], "y", y, 1), side_move(parts[1], "x", x, 1))
+
+
+def line_of(parts, moved, x, y):
     return jnp.concatenate(
-        [core_sum(parts[0], moved[1], moved[2], c, y), x_sum(parts[1], moved[0], x)], axis=1
+        [side_sum(parts[0], moved[0], y, 1), side_sum(parts[1], moved[1], x, 1)], axis=1
     )
 
 
@@ -1036,24 +1012,38 @@
     pair_rows = jnp.pad(pairing.astype(BF), ((0, 63), (0, 128 - half_queries)))
     mid_rows = jnp.concatenate([w_up, w_out.T, pair_rows], axis=1)
     bias = jnp.concatenate([b_qv.reshape(-1), b_up])[None].astype(F32)
-    down_rows = turn(w_down.T)
-    got = exchange((qkv_rows, "z", FAR), (tokens, "c", SWAP), (bias, "y", SWAP))
-    qkv_pair = far_pair(qkv_rows, got[0], z)
+    got = exchange(
+        (qkv_rows, CORES, TURN), (tokens, "c", SWAP), (bias, "y", SWAP)
+    )
+    qkv_rows = got[0]
     row = jnp.where(c == y, tokens, got[1])
     bias = jnp.where(c == y, bias, got[2])
-    got = exchange((qkv_pair, "z", NEAR), (tie(mid_rows, qkv_pair), "z", FAR))
+    (rest_rows,) = exchange(
+        (tie(jnp.concatenate([mid_rows, w_down.T], axis=1), row), CORES, TURN)
+    )
+    (far,) = exchange((qkv_rows, "z", FAR))
+    qkv_pair = far_pair(qkv_rows, far, z)
+    mid_wide = mid_rows.shape[1]
+    rest_rows = tie(rest_rows, qkv_pair)
+    mid_rows, down_rows = rest_rows[:, :mid_wide], rest_rows[:, mid_wide:]
+    got = exchange((qkv_pair, "z", NEAR), (mid_rows, "z", FAR))
     qkv_line = whole_line(qkv_pair, got[0], z)
     mid_pair = far_pair(mid_rows, got[1], z)
-    full_down = lax.all_gather(tie(down_rows, qkv_line), ("z", "x", "y"), axis=0, tiled=True)
     got = exchange(*first_moves(qkv_line), (mid_pair, "z", NEAR))
-    qkv_parts = first_parts(qkv_line, got, x, c, y)
-    mid_line = whole_line(mid_pair, got[3], z)
-    got = exchange(*last_moves(qkv_parts))
-    full_qkv = full_rows(qkv_parts, got, x, c, y)
-    got = exchange(*first_moves(tie(mid_line, full_qkv)))
-    mid_parts = first_parts(mid_line, got, x, c, y)
-    got = exchange(*last_moves(mid_parts))
-    full_mid = full_rows(mid_parts, got, x, c, y)
+    qkv_parts = first_parts(qkv_line, got, x, y)
+    mid_line = whole_line(mid_pair, got[2], z)
+    last = last_moves(qkv_parts)
+    got = exchange(*last, (tie(down_rows, mid_line), "z", FAR), *first_moves(mid_line))
+    full_qkv = full_rows(qkv_parts, got, x, y)
+    down_pair = far_pair(down_rows, got[2], z)
+    mid_parts = first_parts(mid_line, got[3:], x, y)
+    (near,) = exchange((down_pair, "z", NEAR))
+    down_line = whole_line(down_pair, near, z)
+    got = exchange(*last_moves(mid_parts), *first_moves(down_line))
+    full_mid = full_rows(mid_parts, got, x, y)
+    down_parts = first_parts(down_line, got[2:], x, y)
+    got = exchange(*last_moves(down_parts))
+    full_down = full_rows(down_parts, got, x, y)
     full_out = full_mid[:, up_wide : up_wide + half_width]
     pairs = full_mid[:, up_wide + half_width :].reshape(chip_count, 64, 128)
     pairs = pairs[:, 0, :half_queries].astype(jnp.int32).reshape(1, query_total)
@@ -1077,7 +1067,6 @@
     )
     qkv = (dot(row, full_qkv) + qkv_bias).astype(BF)
     mixed, lse = attend(bounds, qkv, seg_col, seg_row)
-    own_cot = turn(tie(cot, qkv))
 
     def row_sum(left, weight_t, transposed):
         times = contract_cols if transposed else dot
@@ -1153,7 +1142,8 @@
     )
     losses = jnp.where(c == y, losses, swap(losses, "c"))
     loss_out = rows_of(losses, 4 * z + 2 * x + c, 1)
-    query_grad, doc_grad = pool_back(cuts, query_span, queries, row_embed, seg_row, coefficient)
+    y_out, own_cot = exchange((result_low, CORES, TURN), (tie(cot, queries), CORES, TURN))
+    query_grad, doc_grad = pool_back(cuts, query_span, tie(queries, y_out, own_cot), row_embed, seg_row, coefficient)
     grad_blocks = lax.all_to_all(
         query_grad.reshape(chip_count, half_span, proj_width), chips, 0, 0
     )
@@ -1179,15 +1169,16 @@
     grad_ffn = grad_second.astype(BF)
     down_bias = jnp.sum(grad_ffn.astype(F32), axis=0)
     grad_ffn_all = jnp.concatenate([grad_ffn, swap(grad_ffn, "c")], axis=0)
-    down_blocks = contract_rows(grad_ffn_all, activation).astype(BF)
-    down_part = turn(
-        lax.psum_scatter(down_blocks, ("z", "x", "y"), scatter_dimension=0, tiled=True)
-    ).astype(F32)
+    down_blocks = blocks_of(grad_ffn_all, activation)
+    grad_ffn_all = tie(grad_ffn_all, down_blocks)
+    down_moved = exchange(*sum_moves(down_blocks, x, y))
     grad_up = (dot(grad_ffn_all, full_down) * slope.astype(F32)).astype(BF)
     up_bias = jnp.sum(grad_up.astype(F32), axis=0)
-    up_blocks = blocks_of(normed_all, grad_up)
-    up_moved = exchange(*sum_moves(up_blocks, x, c, y))
-    up_parts = sum_parts(up_blocks, up_moved, x, c, y)
+    up_blocks = blocks_of(normed_all, tie(grad_up, *down_moved))
+    down_parts = sum_parts(down_blocks, down_moved, x, y)
+    moved = exchange(*line_moves(down_parts, x, y), *sum_moves(up_blocks, x, y))
+    down_line = line_of(down_parts, moved, x, y)
+    up_parts = sum_parts(up_blocks, moved[2:], x, y)
     full_up = full_mid[:, :up_wide]
     grad_normed = (
         row_sum(lambda which: grad_up[which * share : (which + 1) * share], full_up, True)
@@ -1206,19 +1197,31 @@
     )
     grad_mixed = dot(grad_attn_all, full_out).astype(BF)
     out_blocks = blocks_of(grad_attn_all, mixed)
-    grad_mixed, *up_parts = lax.optimization_barrier((grad_mixed,) + tuple(up_parts))
-    up_moved = exchange(*line_moves(up_parts, x, c, y), x_move(out_blocks, x))
-    up_line = line_of(up_parts, up_moved, x, c, y)
-    out_line = x_sum(out_blocks, up_moved[3], x)
+    grad_mixed, out_blocks, down_line, *up_parts = lax.optimization_barrier(
+        (grad_mixed, out_blocks, down_line) + tuple(up_parts)
+    )
+    moved = exchange(
+        near_move(down_line, z), *line_moves(up_parts, x, y), *sum_moves(out_blocks, x, y)
+    )
     grads_one, sums_one = attend_back(bounds, 0, qkv, mixed, grad_mixed, lse, seg_col, seg_row)
-    grad_mixed, up_line, out_line = lax.optimization_barrier((grad_mixed, up_line, out_line))
-    up_moved = exchange(near_move(up_line, z), *core_moves(out_line, c, y))
-    up_pair = near_sum(up_line, up_moved[0], z)
-    out_line = core_sum(out_line, up_moved[1], up_moved[2], c, y)
+    down_pair = near_sum(down_line, moved[0], z)
+    up_line = line_of(up_parts, moved[1:], x, y)
+    out_parts = sum_parts(out_blocks, moved[3:], x, y)
+    grad_mixed, down_pair, up_line, *out_parts = lax.optimization_barrier(
+        (grad_mixed, down_pair, up_line) + tuple(out_parts)
+    )
+    moved = exchange(
+        far_move(down_pair, z), near_move(up_line, z), *line_moves(out_parts, x, y)
+    )
     grads_two, sums_two = attend_back(
         bounds, 1, qkv, mixed, tie(grad_mixed, grads_one), lse, seg_col, seg_row
     )
-    grads_one = tie(grads_one, grads_two)
+    down_part = far_sum(down_pair, moved[0], z)
+    up_pair = near_sum(up_line, moved[1], z)
+    out_line = line_of(out_parts, moved[2:], x, y)
+    grads_one, grads_two, down_part, up_pair, out_line = lax.optimization_barrier(
+        (grads_one, grads_two, down_part, up_pair, out_line)
+    )
     proj_half = rows_of(proj_grad, own_start, share) + swap(
         rows_of(proj_grad, other_start, share), "c"
     )
@@ -1237,13 +1240,12 @@
     qkv_blocks = jnp.concatenate(
         [blocks_of(row, grads_one), blocks_of(row, grads_two)], axis=4
     )
-    qkv_blocks, up_pair, out_line = lax.optimization_barrier((qkv_blocks, up_pair, out_line))
     moved = exchange(
-        *sum_moves(qkv_blocks, x, c, y), far_move(up_pair, z), near_move(out_line, z)
-    )
-    qkv_parts = sum_parts(qkv_blocks, moved, x, c, y)
-    up_part = far_sum(up_pair, moved[3], z)
-    out_pair = near_sum(out_line, moved[4], z)
+        *sum_moves(qkv_blocks, x, y), far_move(up_pair, z), near_move(out_line, z)
+    )
+    qkv_parts = sum_parts(qkv_blocks, moved, x, y)
+    up_part = far_sum(up_pair, moved[2], z)
+    out_pair = near_sum(out_line, moved[3], z)
 
     def input_terms(start):
         return contract_cols(
@@ -1252,19 +1254,30 @@
 
     other_terms = swap(input_terms(other_start).astype(BF), "c")
     grad_input = (input_terms(own_start) + other_terms.astype(F32) + grad_first).astype(BF)
-    moved = exchange(*line_moves(qkv_parts, x, c, y), far_move(out_pair, z), (small, "y", SWAP))
-    qkv_line = line_of(qkv_parts, moved, x, c, y)
-    out_part = far_sum(out_pair, moved[3], z)
-    small = small + moved[4]
-    moved = exchange(near_move(qkv_line, z), (small, "x", SWAP))
+    moved = exchange(*line_moves(qkv_parts, x, y), far_move(out_pair, z), (small, "y", SWAP))
+    qkv_line = line_of(qkv_parts, moved, x, y)
+    out_part = far_sum(out_pair, moved[2], z)
+    small = small + moved[3]
+    rest_part = jnp.concatenate([down_part, up_part, out_part], axis=1).astype(BF)
+    moved = exchange(
+        near_move(qkv_line, z), (small, "x", SWAP), (rest_part, CORES, TURN),
+        (tie(grad_input, qkv_line), CORES, TURN),
+    )
     qkv_pair = near_sum(qkv_line, moved[0], z)
     small = small + moved[1]
-    y_out = turn(tie(result_low, grad_input, qkv_line))
-    grad_input = turn(tie(grad_input, qkv_line))
+    rest_part = moved[2].astype(F32)
+    grad_input = moved[3]
+    down_part, up_part, out_part = (
+        rest_part[:, :up_wide],
+        rest_part[:, up_wide : 2 * up_wide],
+        rest_part[:, 2 * up_wide :],
+    )
     moved = exchange(far_move(qkv_pair, z), (small, "z", FAR))
-    qkv_part = far_sum(qkv_pair, moved[0], z)
+    qkv_part = far_sum(qkv_pair, moved[0], z).astype(BF)
     small = small + moved[1]
-    small = small + lax.ppermute(small, "z", NEAR)
+    moved = exchange((qkv_part, CORES, TURN), (small, "z", NEAR))
+    qkv_part = moved[0].astype(F32)
+    small = small + moved[1]
     other_small = swap(small, "c")
     shared_rows = 6 * width // 128
     small_rows = small.shape[0] - share

time: 603 us -> 553 us (0.917)
  waiting for transfers between devices: 198 us -> 154 us
  matrix products: 70.7 us -> 53.9 us
  between operations: 16.2 us -> 3.36 us
  local copies, waits for them, and re-layouts: 46.5 us -> 56 us
  starting transfers between devices: 116 us -> 123 us
    ppermute x42 -> x55, waiting for transfers between devices: 174 us -> 136 us  [exchange(): lax.ppermute(value, axis, steps)]
    ppermute x6 -> x0, starting transfers between devices: 32.4 us -> none  [the longest x5 21.2 us: turn(): return lax.ppermute(value, CORES, TURN)]
    ppermute x42 -> x55, starting transfers between devices: 64.3 us -> 93.5 us  [exchange(): lax.ppermute(value, axis, steps)]
    dot_general x12, matrix products: 34.2 us -> 21.8 us  [contract_cols(): lax.dot_general(left, right, (((1,), (1,)), ((), ())), precision=precisio...]
    ppermute x12, starting transfers between devices: 10.6 us -> 19.4 us  [swap(): return lax.ppermute(value, axis, SWAP)]
    all_to_all x1, waiting for transfers between devices: 2.64 us -> 10.3 us  [local_chip(): lax.all_to_all(query_grad.reshape(chip_count, half_span, proj_width), chi...]
    ppermute x6 -> x0, waiting for transfers between devices: 6.65 us -> none  [the longest x1 4.32 us: local_chip(): small = small + lax.ppermute(small, 'z', NEAR)]
    unnamed x167 -> x175, local copies, waits for them, and re-layouts: 21.4 us -> 25.6 us
  transfers between devices with their start and end apart: 64 -> 69, of which waited for: 38 -> 33; matrix products, arithmetic and copies ran while one was open for 18% -> 17% of each run, Pallas kernels for 11% -> 10%
where the time goes in v6:
time: 553 us; the launch traced here: 546 us
  waiting for transfers between devices  154 us (28%)
  starting transfers between devices  123 us (22%)
  Pallas kernels  90.3 us (16%)
  local copies, waits for them, and re-layouts  56 us (10%)
  matrix products  53.9 us (10%)
  other arithmetic  50.5 us (9%)
  blocking collectives  14.7 us (3%)
    ppermute x55, waiting for transfers between devices, exchange(): lax.ppermute(value, axis, steps)  136 us
    ppermute x55, starting transfers between devices, exchange(): lax.ppermute(value, axis, steps)  93.5 us
    pallas_call x2, Pallas kernels, attend_back(): pl.pallas_call(attend_back_kernel, grid=(pairs,), in_specs=[pl.BlockSpec(...  27.6 us
    unnamed x175, local copies, waits for them, and re-layouts  25.6 us
    dot_general x12, matrix products, contract_cols(): lax.dot_general(left, right, (((1,), (1,)), ((), ())), precision=precisio...  21.8 us
    ppermute x12, starting transfers between devices, swap(): return lax.ppermute(value, axis, SWAP)  19.4 us
    pallas_call x1, Pallas kernels, attend(): pl.pallas_call(attend_kernel, grid=(pairs,), in_specs=[pl.BlockSpec(memor...  19.2 us
    dot_general x7, matrix products, contract_rows(): lax.dot_general(left, right, (((0,), (0,)), ((), ())), precision=precisio...  18.5 us
  transfers between devices with their start and end apart: 69, of which 33 were waited for; matrix products, arithmetic and copies ran while one was open for 17% of the time, Pallas kernels for 10%

profile of v6, /device:TPU:1, one launch (start us, length us, event | category | flops | bytes accessed | tf_op | source)
XLA Modules:
  0.0 546.1 jit_solution(17681065525918108239)
XLA Ops:
  2.2 2.1 collective-permute-start.2
  9.0 2.5 collective-permute-start
  16.2 3.3 broadcast_select_fusion
  19.6 3.7 collective-permute-start.3
  23.3 2.9 collective-permute-start.5
  27.5 3.9 collective-permute-start.4
  31.4 3.6 collective-permute-done.5
  35.1 5.7 %collective-permute-done.4 = bf16[2,64,1536]{2,1,0:T(8,128)(2,1)S(1)} collective-permute-done((bf16[2,64,1536]{2,1,0:T(8,128)(2,1)S(1)}, bf16[2,64,1536]{2,1,0:T(8,128)(2,1)S(1)}, u32[]{:S(2)}, u32[]{:S(2)}) %collective-permute-start.4) | collective-permute-done | bytes 393248 | tf_op jit(solution)/shard_map/ppermute | solution.py:460
  40.8 9.5 %collective-permute-done.6 = bf16[64,2688]{1,0:T(8,128)(2,1)S(1)} collective-permute-done((bf16[64,2688]{1,0:T(8,128)(2,1)S(1)}, bf16[64,2688]{1,0:T(8,128)(2,1)S(1)}, u32[]{:S(2)}, u32[]{:S(2)}) %collective-permute-start.6) | collective-permute-done | bytes 344096 | tf_op jit(solution)/shard_map/ppermute | solution.py:460
  52.4 8.6 %collective-permute-done.8 = bf16[4,32,1536]{2,1,0:T(8,128)(2,1)S(1)} collective-permute-done((bf16[4,32,1536]{2,1,0:T(8,128)(2,1)S(1)}, bf16[4,32,1536]{2,1,0:T(8,128)(2,1)S(1)}, u32[]{:S(2)}, u32[]{:S(2)}) %collective-permute-start.8) | collective-permute-done | bytes 393248 | tf_op jit(solution)/shard_map/ppermute | solution.py:460
  61.1 5.7 %collective-permute-done.9 = bf16[2,64,2688]{2,1,0:T(8,128)(2,1)S(1)} collective-permute-done((bf16[2,64,2688]{2,1,0:T(8,128)(2,1)S(1)}, bf16[2,64,2688]{2,1,0:T(8,128)(2,1)S(1)}, u32[]{:S(2)}, u32[]{:S(2)}) %collective-permute-start.9) | collective-permute-done | bytes 688160 | tf_op jit(solution)/shard_map/ppermute | solution.py:460
  72.1 3.6 collective-permute-done.12
  75.7 24.6 %collective-permute-done.14 = bf16[4,32,2688]{2,1,0:T(8,128)(2,1)S(1)} collective-permute-done((bf16[4,32,2688]{2,1,0:T(8,128)(2,1)S(1)}, bf16[4,32,2688]{2,1,0:T(8,128)(2,1)S(1)}, u32[]{:S(2)}, u32[]{:S(2)}) %collective-permute-start.14) | collective-permute-done | bytes 688160 | tf_op jit(solution)/shard_map/ppermute | solution.py:460
  105.9 3.6 add_convert_fusion.q_ref.k_ref.v_ref
  115.7 19.2 %shard_map.254 = (bf16[1024,512]{1,0:T(8,128)(2,1)S(1)}, f32[4,8,1024]{2,1,0:T(8,128)S(1)}) custom-call(s32[2,4]{1,0:T(2,128)S(1)} %pad_add_fusion.bounds, bf16[1024,1536]{1,0:T(8,128)(2,1)S(1)} %add_convert_fusion.q_ref.k_ref.v_ref, bf16[1024,1536]{1,0:T(8,128)(2,1)S(1)} %add_convert_fusion.q_ref.k_ref.v_ref, ...), custom_call_target="tpu_custom_call" | custom-call | flops 2147483648 | bytes 12582912 | tf_op jit(solution)/shard_map/pallas_call | solution.py:659
  135.2 5.9 %collective-permute-done.19 = bf16[4,32,2048]{2,1,0:T(8,128)(2,1)S(1)} collective-permute-done((bf16[4,32,2048]{2,1,0:T(8,128)(2,1)S(1)}, bf16[4,32,2048]{2,1,0:T(8,128)(2,1)S(1)}, u32[]{:S(2)}, u32[]{:S(2)}) %collective-permute-start.19) | collective-permute-done | bytes 524320 | tf_op jit(solution)/shard_map/ppermute | solution.py:460
  144.7 2.4 copy-done.4
  148.8 4.2 collective-permute-start.20
  162.5 2.5 fusion.120
  167.6 15.0 %collective-permute-done.22 = bf16[4,2,32,2048]{3,2,0,1:T(8,128)(2,1)S(1)} collective-permute-done((bf16[4,2,32,2048]{3,2,0,1:T(8,128)(2,1)S(1)}, bf16[4,2,32,2048]{3,2,0,1:T(8,128)(2,1)S(1)}, u32[]{:S(2)}, u32[]{:S(2)}) %collective-permute-start.22) | collective-permute-done | bytes 1048608 | tf_op jit(solution)/shard_map/ppermute | solution.py:460
  185.3 17.6 %shard_map.255 = (bf16[1024,2048]{1,0:T(8,128)(2,1)S(1)}, bf16[1024,2048]{1,0:T(8,128)(2,1)S(1)}) custom-call(bf16[1024,1024]{1,0:T(8,128)(2,1)S(1)} %pad_maximum_fusion.4.x_ref, bf16[1024,2688]{1,0:T(8,128)(2,1)S(1)} %bitcast.290, f32[1,2048]{1,0:T(1,128)S(1)} %slice.489.b_ref), custom_call_target="tpu_custom_call" | custom-call | flops 4294967296 | bytes 14680064 | tf_op jit(solution)/shard_map/pallas_call | solution.py:821
  203.0 2.4 fusion.12
  206.5 2.3 collective-permute-done.24
  208.8 2.8 fusion.121
  218.5 6.0 %all-to-all-start = ((bf16[16,128,128]{2,1,0:T(8,128)(2,1)}), bf16[16,128,128]{2,1,0:T(8,128)(2,1)}, u32[]{:S(2)}, u32[]{:S(2)}) async-start(bf16[16,128,128]{2,1,0:T(8,128)(2,1)} %broadcast_in_dim.28), calls=%async_computation | async-start | bytes 1048576 | tf_op jit(solution)/shard_map/all_to_all | solution.py:1105
  233.7 4.0 collective-permute-start.25
  238.7 10.0 %shard_map.256 = f32[24,2048]{1,0:T(8,128)S(1)} custom-call(bf16[2048,128]{1,0:T(8,128)(2,1)} %bitcast.53.q_ref, bf16[1024,128]{1,0:T(8,128)(2,1)S(1)} %copy-done.12, s32[1,1024]{1,0:T(1,128)S(1)} %compare_select_fusion.seg_row.seg_ref), custom_call_target="tpu_custom_call" | custom-call | flops 3221225472 | bytes 786432 | tf_op jit(solution)/shard_map/pallas_call | solution.py:874
  248.7 5.0 collective-permute-start.27
  254.5 14.7 %all_to_all.15 = f32[16,8,128]{2,1,0:T(8,128)S(1)} all-to-all(f32[16,8,128]{2,1,0:T(8,128)S(1)} %broadcast_in_dim.29), channel_id=1, replica_groups=mesh['z'=4,'x'=2,'c'=2,'y'=2] {'z','x','y'}, dimensions={0} | all-to-all | bytes 131072 | tf_op jit(solution)/shard_map/all_to_all | solution.py:1125
  270.6 15.8 %shard_map.257 = (bf16[2048,128]{1,0:T(8,128)(2,1)S(1)}, f32[768,128]{1,0:T(8,128)S(1)}) custom-call(bf16[2048,128]{1,0:T(8,128)(2,1)} %bitcast.53.q_ref, bf16[1024,128]{1,0:T(8,128)(2,1)S(1)} %copy-done.13, s32[1,1024]{1,0:T(1,128)S(1)} %compare_select_fusion.seg_row.seg_ref, f32[24,2048]{1,0:T(8,128)S(1)} %convolution_divide_fusion.coef_ref), custom_call_target="tpu_custom_call" | custom-call | flops 4831838208 | bytes 1572864 | tf_op jit(solution)/shard_map/pallas_call | solution.py:950
  287.9 4.7 all-to-all-start.2
  294.4 10.3 %all-to-all-done.2 = bf16[16,128,128]{2,1,0:T(8,128)(2,1)} async-done(((bf16[16,128,128]{2,1,0:T(8,128)(2,1)}), bf16[16,128,128]{2,1,0:T(8,128)(2,1)}, u32[]{:S(2)}, u32[]{:S(2)}) %all-to-all-start.2) | async-done | bytes 524320 | tf_op jit(solution)/shard_map/all_to_all | solution.py:1147
  307.5 4.0 collective-permute-start.29
  314.1 3.1 multiply_reduce_fusion
  317.3 2.9 convert_reduce_fusion.1
  325.8 7.4 %convolution_convert_fusion.1 = bf16[1024,2048]{1,0:T(8,128)(2,1)S(1)} fusion(bf16[1024,2048]{1,0:T(8,128)(2,1)} %copy-done.14, bf16[512,1024]{1,0:T(8,128)(2,1)} %collective-permute-done.30, bf16[512,1024]{1,0:T(8,128)(2,1)} %get-tuple-element.201), kind=kOutput, calls=%fused_computation.6 | convolution fusion | flops 4301258752 | bytes 10485760 | tf_op jit(solution)/shard_map/dot_general | solution.py:33
  339.3 4.9 convert_reduce_fusion
  344.2 2.4 fusion.15
  346.8 2.4 fusion.2
  349.1 11.5 %collective-permute-done.34 = bf16[4,2,32,2048]{3,2,0,1:T(8,128)(2,1)S(1)} collective-permute-done((bf16[4,2,32,2048]{3,2,0,1:T(8,128)(2,1)S(1)}, bf16[4,2,32,2048]{3,2,0,1:T(8,128)(2,1)S(1)}, u32[]{:S(2)}, u32[]{:S(2)}) %collective-permute-start.34) | collective-permute-done | bytes 1048608 | tf_op jit(solution)/shard_map/ppermute | solution.py:460
  366.3 5.0 convolution_convert_fusion
  378.8 2.3 convert_reduce_fusion.2
  381.3 2.2 collective-permute-start.32
  383.5 15.9 %collective-permute-done.38 = bf16[4,2,32,2048]{3,2,0,1:T(8,128)(2,1)} collective-permute-done((bf16[4,2,32,2048]{3,2,0,1:T(8,128)(2,1)}, bf16[4,2,32,2048]{3,2,0,1:T(8,128)(2,1)}, u32[]{:S(2)}, u32[]{:S(2)}) %collective-permute-start.38) | collective-permute-done | bytes 1048608 | tf_op jit(solution)/shard_map/ppermute | solution.py:460
  406.8 2.6 convolution_convert_fusion.5.grad_ref
  415.6 13.7 %shard_map.258 = (bf16[1024,768]{1,0:T(8,128)(2,1)S(1)}, f32[2,8,128]{2,1,0:T(8,128)S(1)}) custom-call(s32[2,4]{1,0:T(2,128)S(1)} %pad_add_fusion.bounds, bf16[1024,1536]{1,0:T(8,128)(2,1)S(1)} %add_convert_fusion.q_ref.k_ref.v_ref, bf16[1024,1536]{1,0:T(8,128)(2,1)S(1)} %add_convert_fusion.q_ref.k_ref.v_ref, ...), custom_call_target="tpu_custom_call" | custom-call | flops 2684354560 | bytes 12582912 | tf_op jit(solution)/shard_map/pallas_call | solution.py:756
  431.7 2.3 collective-permute-start.46
  435.6 14.0 %shard_map.259 = (bf16[1024,768]{1,0:T(8,128)(2,1)S(1)}, f32[2,8,128]{2,1,0:T(8,128)S(1)}) custom-call(s32[2,4]{1,0:T(2,128)S(1)} %pad_add_fusion.bounds, bf16[1024,1536]{1,0:T(8,128)(2,1)S(1)} %add_convert_fusion.q_ref.k_ref.v_ref, bf16[1024,1536]{1,0:T(8,128)(2,1)S(1)} %add_convert_fusion.q_ref.k_ref.v_ref, ...), custom_call_target="tpu_custom_call" | custom-call | flops 2684354560 | bytes 12582912 | tf_op jit(solution)/shard_map/pallas_call | solution.py:756
  449.7 2.6 collective-permute-start.56
  462.2 3.0 collective-permute-start.50
  467.2 5.9 %collective-permute-start.60 = (bf16[512,1024]{1,0:T(8,128)(2,1)S(1)}, bf16[512,1024]{1,0:T(8,128)(2,1)S(1)}, u32[]{:S(2)}, u32[]{:S(2)}) collective-permute-start(bf16[512,1024]{1,0:T(8,128)(2,1)S(1)} %add_convert_fusion.2), channel_id=1, source_target_pairs={{0,2},{2,0},{1,3},{3,1},{4,6},{6,4},{5,7},{7,5},{8,10},{10,8},{9,1... | collective-permute-start | bytes 3145736 | tf_op jit(solution)/shard_map/ppermute | solution.py:465
  473.1 2.2 collective-permute-done.49
  475.9 2.8 collective-permute-start.54
  482.0 9.4 %collective-permute-start.61 = (bf16[512,1024]{1,0:T(8,128)(2,1)S(1)}, bf16[512,1024]{1,0:T(8,128)(2,1)S(1)}, u32[]{:S(2)}, u32[]{:S(2)}) collective-permute-start(bf16[512,1024]{1,0:T(8,128)(2,1)S(1)} %add_convert_fusion.1), channel_id=1, source_target_pairs={{0,0},{1,2},{2,1},{3,3},{4,4},{5,6},{6,5},{7,7},{8,8},{9,10},{10,9... | collective-permute-start | bytes 3145736 | tf_op jit(solution)/shard_map/ppermute | solution.py:460
  491.7 7.2 %collective-permute-start.59 = (bf16[64,4608]{1,0:T(8,128)(2,1)S(1)}, bf16[64,4608]{1,0:T(8,128)(2,1)S(1)}, u32[]{:S(2)}, u32[]{:S(2)}) collective-permute-start(bf16[64,4608]{1,0:T(8,128)(2,1)S(1)} %pad_maximum_fusion.15), channel_id=1, source_target_pairs={{0,0},{1,2},{2,1},{3,3},{4,4},{5,6},{6,5},{7,7},{8,8},{9,10},{10,9... | collective-permute-start | bytes 1769480 | tf_op jit(solution)/shard_map/ppermute | solution.py:460
  499.5 1.9 collective-permute-start.58
  501.4 4.2 collective-permute-done.58
  506.6 3.9 collective-permute-done.59
  511.4 2.7 collective-permute-start.62
  516.0 4.4 collective-permute-done.62
  520.5 5.9 %collective-permute-start.64 = (bf16[64,1536]{1,0:T(8,128)(2,1)S(1)}, bf16[64,1536]{1,0:T(8,128)(2,1)S(1)}, u32[]{:S(2)}, u32[]{:S(2)}) collective-permute-start(bf16[64,1536]{1,0:T(8,128)(2,1)S(1)} %fusion.62), channel_id=1, source_target_pairs={{0,0},{1,2},{2,1},{3,3},{4,4},{5,6},{6,5},{7,7},{8,8},{9,10},{10,9... | collective-permute-start | bytes 589832 | tf_op jit(solution)/shard_map/ppermute | solution.py:460
  526.4 4.0 collective-permute-start.65
  531.2 4.0 collective-permute-done.65
  542.3 2.3 copy.194
  (488 shorter events, 151.9 us)
Async XLA Ops:
  2.2 13.5 %collective-permute-start.2 = (f32[1,3072]{1,0:T(1,128)S(1)}, f32[1,3072]{1,0:T(1,128)S(1)}, u32[]{:S(2)}, u32[]{:S(2)}) collective-permute-start(f32[1,3072]{1,0:T(1,128)S(1)} %maximum_convert_fusion), channel_id=1, source_target_pairs={{0,1},{1,0},{2,3},{3,2},{4,5},{5,4},{6,7},{7,6},{8,9},{9,8},{10,11... | collective-permute-start | bytes 36872 | tf_op jit(solution)/shard_map/ppermute | solution.py:460
  9.0 7.2 %collective-permute-start = (bf16[64,1536]{1,0:T(8,128)(2,1)}, bf16[64,1536]{1,0:T(8,128)(2,1)S(1)}, u32[]{:S(2)}, u32[]{:S(2)}) collective-permute-start(bf16[64,1536]{1,0:T(8,128)(2,1)} %slice_dynamic-update-slice_fusion), channel_id=1, source_target_pairs={{0,0},{1,2},{2,1},{3,3},{4,4},{5,6},{6,5},{7,7},{8,8},{9,10},{10,9... | collective-permute-start | bytes 589832 | tf_op jit(solution)/shard_map/ppermute | solution.py:460
  11.5 4.7 collective-permute-start.1
  19.6 7.8 %collective-permute-start.3 = (bf16[64,1536]{1,0:T(8,128)(2,1)S(1)}, bf16[64,1536]{1,0:T(8,128)(2,1)S(1)}, u32[]{:S(2)}, u32[]{:S(2)}) collective-permute-start(bf16[64,1536]{1,0:T(8,128)(2,1)S(1)} %collective-permute-done), channel_id=1, source_target_pairs={{0,24},{24,0},{8,16},{16,8},{1,25},{25,1},{9,17},{17,9},{2,26},{26... | collective-permute-start | bytes 589832 | tf_op jit(solution)/shard_map/ppermute | solution.py:460
  23.3 11.7 %collective-permute-start.5 = (bf16[64,4736]{1,0:T(8,128)(2,1)S(1)}, bf16[64,4736]{1,0:T(8,128)(2,1)S(1)}, u32[]{:S(2)}, u32[]{:S(2)}) collective-permute-start(bf16[64,4736]{1,0:T(8,128)(2,1)S(1)} %fusion.44), channel_id=1, source_target_pairs={{0,0},{1,2},{2,1},{3,3},{4,4},{5,6},{6,5},{7,7},{8,8},{9,10},{10,9... | collective-permute-start | bytes 1818632 | tf_op jit(solution)/shard_map/ppermute | solution.py:460
  27.5 13.3 %collective-permute-start.4 = (bf16[2,64,1536]{2,1,0:T(8,128)(2,1)S(1)}, bf16[2,64,1536]{2,1,0:T(8,128)(2,1)S(1)}, u32[]{:S(2)}, u32[]{:S(2)}) collective-permute-start(bf16[2,64,1536]{2,1,0:T(8,128)(2,1)S(1)} %maximum_select_fusion.23), channel_id=1, source_target_pairs={{0,8},{8,0},{16,24},{24,16},{1,9},{9,1},{17,25},{25,17},{2,10},{10... | collective-permute-start | bytes 1179656 | tf_op jit(solution)/shard_map/ppermute | solution.py:460
  35.0 15.3 %collective-permute-start.6 = (bf16[64,2688]{1,0:T(8,128)(2,1)S(1)}, bf16[64,2688]{1,0:T(8,128)(2,1)S(1)}, u32[]{:S(2)}, u32[]{:S(2)}) collective-permute-start(bf16[64,2688]{1,0:T(8,128)(2,1)S(1)} %get-tuple-element.264), channel_id=1, source_target_pairs={{0,24},{24,0},{8,16},{16,8},{1,25},{25,1},{9,17},{17,9},{2,26},{26... | collective-permute-start | bytes 1032200 | tf_op jit(solution)/shard_map/ppermute | solution.py:460
  50.5 16.4 %collective-permute-start.9 = (bf16[2,64,2688]{2,1,0:T(8,128)(2,1)S(1)}, bf16[2,64,2688]{2,1,0:T(8,128)(2,1)S(1)}, u32[]{:S(2)}, u32[]{:S(2)}) collective-permute-start(bf16[2,64,2688]{2,1,0:T(8,128)(2,1)S(1)} %maximum_select_fusion.20), channel_id=1, source_target_pairs={{0,8},{8,0},{16,24},{24,16},{1,9},{9,1},{17,25},{25,17},{2,10},{10... | collective-permute-start | bytes 2064392 | tf_op jit(solution)/shard_map/ppermute | solution.py:460
  51.0 10.0 %collective-permute-start.8 = (bf16[4,32,1536]{2,1,0:T(8,128)(2,1)S(1)}, bf16[4,32,1536]{2,1,0:T(8,128)(2,1)S(1)}, u32[]{:S(2)}, u32[]{:S(2)}) collective-permute-start(bf16[4,32,1536]{2,1,0:T(8,128)(2,1)S(1)} %get-tuple-element.253), channel_id=1, source_target_pairs={{0,1},{1,0},{2,3},{3,2},{4,5},{5,4},{6,7},{7,6},{8,9},{9,8},{10,11... | collective-permute-start | bytes 1179656 | tf_op jit(solution)/shard_map/ppermute | solution.py:460
  51.0 10.0 %collective-permute-start.7 = (bf16[4,32,1536]{2,1,0:T(8,128)(2,1)S(1)}, bf16[4,32,1536]{2,1,0:T(8,128)(2,1)S(1)}, u32[]{:S(2)}, u32[]{:S(2)}) collective-permute-start(bf16[4,32,1536]{2,1,0:T(8,128)(2,1)S(1)} %get-tuple-element.254), channel_id=1, source_target_pairs={{0,4},{4,0},{1,5},{5,1},{2,6},{6,2},{3,7},{7,3},{8,12},{12,8},{9,1... | collective-permute-start | bytes 1179656 | tf_op jit(solution)/shard_map/ppermute | solution.py:460
  67.5 8.2 %collective-permute-start.12 = (bf16[64,2048]{1,0:T(8,128)(2,1)S(1)}, bf16[64,2048]{1,0:T(8,128)(2,1)S(1)}, u32[]{:S(2)}, u32[]{:S(2)}) collective-permute-start(bf16[64,2048]{1,0:T(8,128)(2,1)S(1)} %get-tuple-element.109), channel_id=1, source_target_pairs={{0,24},{24,0},{8,16},{16,8},{1,25},{25,1},{9,17},{17,9},{2,26},{26... | collective-permute-start | bytes 786440 | tf_op jit(solution)/shard_map/ppermute | solution.py:460
  68.5 32.1 %collective-permute-start.10 = (bf16[4,2,32,1536]{3,2,0,1:T(8,128)(2,1)S(1)}, bf16[4,2,32,1536]{3,2,0,1:T(8,128)(2,1)S(1)}, u32[]{:S(2)}, u32[]{:S(2)}) collective-permute-start(bf16[4,2,32,1536]{3,2,0,1:T(8,128)(2,1)S(1)} %maximum_select_fusion.18), channel_id=1, source_target_pairs={{0,1},{1,0},{2,3},{3,2},{4,5},{5,4},{6,7},{7,6},{8,9},{9,8},{10,11... | collective-permute-start | bytes 2359304 | tf_op jit(solution)/shard_map/ppermute | solution.py:460
  68.6 31.9 %collective-permute-start.11 = (bf16[4,2,32,1536]{3,2,1,0:T(8,128)(2,1)S(1)}, bf16[4,2,32,1536]{3,2,1,0:T(8,128)(2,1)S(1)}, u32[]{:S(2)}, u32[]{:S(2)}) collective-permute-start(bf16[4,2,32,1536]{3,2,1,0:T(8,128)(2,1)S(1)} %maximum_select_fusion.19), channel_id=1, source_target_pairs={{0,4},{4,0},{1,5},{5,1},{2,6},{6,2},{3,7},{7,3},{8,12},{12,8},{9,1... | collective-permute-start | bytes 2359304 | tf_op jit(solution)/shard_map/ppermute | solution.py:460
  70.2 30.1 %collective-permute-start.14 = (bf16[4,32,2688]{2,1,0:T(8,128)(2,1)S(1)}, bf16[4,32,2688]{2,1,0:T(8,128)(2,1)S(1)}, u32[]{:S(2)}, u32[]{:S(2)}) collective-permute-start(bf16[4,32,2688]{2,1,0:T(8,128)(2,1)S(1)} %get-tuple-element.239), channel_id=1, source_target_pairs={{0,1},{1,0},{2,3},{3,2},{4,5},{5,4},{6,7},{7,6},{8,9},{9,8},{10,11... | collective-permute-start | bytes 2064392 | tf_op jit(solution)/shard_map/ppermute | solution.py:460
  71.6 28.9 %collective-permute-start.13 = (bf16[4,32,2688]{2,1,0:T(8,128)(2,1)S(1)}, bf16[4,32,2688]{2,1,0:T(8,128)(2,1)S(1)}, u32[]{:S(2)}, u32[]{:S(2)}) collective-permute-start(bf16[4,32,2688]{2,1,0:T(8,128)(2,1)S(1)} %get-tuple-element.240), channel_id=1, source_target_pairs={{0,4},{4,0},{1,5},{5,1},{2,6},{6,2},{3,7},{7,3},{8,12},{12,8},{9,1... | collective-permute-start | bytes 2064392 | tf_op jit(solution)/shard_map/ppermute | solution.py:460
  100.6 10.6 %collective-permute-start.17 = (bf16[2,64,2048]{2,1,0:T(8,128)(2,1)S(1)}, bf16[2,64,2048]{2,1,0:T(8,128)(2,1)S(1)}, u32[]{:S(2)}, u32[]{:S(2)}) collective-permute-start(bf16[2,64,2048]{2,1,0:T(8,128)(2,1)S(1)} %maximum_select_fusion.21), channel_id=1, source_target_pairs={{0,8},{8,0},{16,24},{24,16},{1,9},{9,1},{17,25},{25,17},{2,10},{10... | collective-permute-start | bytes 1572872 | tf_op jit(solution)/shard_map/ppermute | solution.py:460
  101.0 41.3 %collective-permute-start.15 = (bf16[4,2,32,2688]{3,2,0,1:T(8,128)(2,1)S(1)}, bf16[4,2,32,2688]{3,2,0,1:T(8,128)(2,1)S(1)}, u32[]{:S(2)}, u32[]{:S(2)}) collective-permute-start(bf16[4,2,32,2688]{3,2,0,1:T(8,128)(2,1)S(1)} %maximum_select_fusion.9), channel_id=1, source_target_pairs={{0,1},{1,0},{2,3},{3,2},{4,5},{5,4},{6,7},{7,6},{8,9},{9,8},{10,11... | collective-permute-start | bytes 4128776 | tf_op jit(solution)/shard_map/ppermute | solution.py:460
  102.4 39.8 %collective-permute-start.16 = (bf16[4,2,32,2688]{3,2,0,1:T(8,128)(2,1)S(1)}, bf16[4,2,32,2688]{3,2,0,1:T(8,128)(2,1)S(1)}, u32[]{:S(2)}, u32[]{:S(2)}) collective-permute-start(bf16[4,2,32,2688]{3,2,0,1:T(8,128)(2,1)S(1)} %maximum_select_fusion.10), channel_id=1, source_target_pairs={{0,4},{4,0},{1,5},{5,1},{2,6},{6,2},{3,7},{7,3},{8,12},{12,8},{9,1... | collective-permute-start | bytes 4128776 | tf_op jit(solution)/shard_map/ppermute | solution.py:460
  113.1 28.0 %collective-permute-start.19 = (bf16[4,32,2048]{2,1,0:T(8,128)(2,1)S(1)}, bf16[4,32,2048]{2,1,0:T(8,128)(2,1)S(1)}, u32[]{:S(2)}, u32[]{:S(2)}) collective-permute-start(bf16[4,32,2048]{2,1,0:T(8,128)(2,1)S(1)} %get-tuple-element.245), channel_id=1, source_target_pairs={{0,1},{1,0},{2,3},{3,2},{4,5},{5,4},{6,7},{7,6},{8,9},{9,8},{10,11... | collective-permute-start | bytes 1572872 | tf_op jit(solution)/shard_map/ppermute | solution.py:460
  114.0 28.3 %collective-permute-start.18 = (bf16[4,32,2048]{2,1,0:T(8,128)(2,1)S(1)}, bf16[4,32,2048]{2,1,0:T(8,128)(2,1)S(1)}, u32[]{:S(2)}, u32[]{:S(2)}) collective-permute-start(bf16[4,32,2048]{2,1,0:T(8,128)(2,1)S(1)} %get-tuple-element.246), channel_id=1, source_target_pairs={{0,4},{4,0},{1,5},{5,1},{2,6},{6,2},{3,7},{7,3},{8,12},{12,8},{9,1... | collective-permute-start | bytes 1572872 | tf_op jit(solution)/shard_map/ppermute | solution.py:460
  148.8 13.6 %collective-permute-start.20 = (bf16[512,1024]{1,0:T(8,128)(2,1)}, bf16[512,1024]{1,0:T(8,128)(2,1)}, u32[]{:S(2)}, u32[]{:S(2)}) collective-permute-start(bf16[512,1024]{1,0:T(8,128)(2,1)} %convolution_convert_fusion.6), channel_id=1, source_target_pairs={{0,2},{2,0},{1,3},{3,1},{4,6},{6,4},{5,7},{7,5},{8,10},{10,8},{9,1... | collective-permute-start | bytes 3145736 | tf_op jit(solution)/shard_map/ppermute | solution.py:465
  157.7 24.9 %collective-permute-start.22 = (bf16[4,2,32,2048]{3,2,0,1:T(8,128)(2,1)S(1)}, bf16[4,2,32,2048]{3,2,0,1:T(8,128)(2,1)S(1)}, u32[]{:S(2)}, u32[]{:S(2)}) collective-permute-start(bf16[4,2,32,2048]{3,2,0,1:T(8,128)(2,1)S(1)} %maximum_select_fusion.14), channel_id=1, source_target_pairs={{0,1},{1,0},{2,3},{3,2},{4,5},{5,4},{6,7},{7,6},{8,9},{9,8},{10,11... | collective-permute-start | bytes 3145736 | tf_op jit(solution)/shard_map/ppermute | solution.py:460
  159.5 24.6 %collective-permute-start.23 = (bf16[4,2,32,2048]{3,2,1,0:T(8,128)(2,1)S(1)}, bf16[4,2,32,2048]{3,2,1,0:T(8,128)(2,1)S(1)}, u32[]{:S(2)}, u32[]{:S(2)}) collective-permute-start(bf16[4,2,32,2048]{3,2,1,0:T(8,128)(2,1)S(1)} %maximum_select_fusion.15), channel_id=1, source_target_pairs={{0,4},{4,0},{1,5},{5,1},{2,6},{6,2},{3,7},{7,3},{8,12},{12,8},{9,1... | collective-permute-start | bytes 3145736 | tf_op jit(solution)/shard_map/ppermute | solution.py:460
  165.8 19.2 %collective-permute-start.21 = (bf16[512,1024]{1,0:T(8,128)(2,1)S(1)}, bf16[512,1024]{1,0:T(8,128)(2,1)S(1)}, u32[]{:S(2)}, u32[]{:S(2)}) collective-permute-start(bf16[512,1024]{1,0:T(8,128)(2,1)S(1)} %fusion.10), channel_id=1, source_target_pairs={{0,2},{2,0},{1,3},{3,1},{4,6},{6,4},{5,7},{7,5},{8,10},{10,8},{9,1... | collective-permute-start | bytes 3145736 | tf_op jit(solution)/shard_map/ppermute | solution.py:465
  218.5 19.2 %all-to-all-start = ((bf16[16,128,128]{2,1,0:T(8,128)(2,1)}), bf16[16,128,128]{2,1,0:T(8,128)(2,1)}, u32[]{:S(2)}, u32[]{:S(2)}) async-start(bf16[16,128,128]{2,1,0:T(8,128)(2,1)} %broadcast_in_dim.28), calls=%async_computation | async-start | bytes 1048576 | tf_op jit(solution)/shard_map/all_to_all | solution.py:1105
  233.7 36.9 %collective-permute-start.25 = (bf16[512,1024]{1,0:T(8,128)(2,1)}, bf16[512,1024]{1,0:T(8,128)(2,1)}, u32[]{:S(2)}, u32[]{:S(2)}) collective-permute-start(bf16[512,1024]{1,0:T(8,128)(2,1)} %copy-done.21), channel_id=1, source_target_pairs={{0,0},{1,2},{2,1},{3,3},{4,4},{5,6},{6,5},{7,7},{8,8},{9,10},{10,9... | collective-permute-start | bytes 3145736 | tf_op jit(solution)/shard_map/ppermute | solution.py:460
  248.7 21.9 %collective-permute-start.27 = (bf16[512,1024]{1,0:T(8,128)(2,1)S(1)}, bf16[512,1024]{1,0:T(8,128)(2,1)}, u32[]{:S(2)}, u32[]{:S(2)}) collective-permute-start(bf16[512,1024]{1,0:T(8,128)(2,1)S(1)} %copy-done.73), channel_id=1, source_target_pairs={{0,0},{1,2},{2,1},{3,3},{4,4},{5,6},{6,5},{7,7},{8,8},{9,10},{10,9... | collective-permute-start | bytes 3145736 | tf_op jit(solution)/shard_map/ppermute | solution.py:460
  287.9 16.8 %all-to-all-start.2 = ((bf16[16,128,128]{2,1,0:T(8,128)(2,1)}), bf16[16,128,128]{2,1,0:T(8,128)(2,1)}, u32[]{:S(2)}, u32[]{:S(2)}) async-start(bf16[16,128,128]{2,1,0:T(8,128)(2,1)} %bitcast.295), calls=%async_computation.2 | async-start | bytes 1048576 | tf_op jit(solution)/shard_map/all_to_all | solution.py:1147
  307.5 5.2 collective-permute-start.29
  320.2 5.6 %collective-permute-start.30 = (bf16[512,1024]{1,0:T(8,128)(2,1)}, bf16[512,1024]{1,0:T(8,128)(2,1)}, u32[]{:S(2)}, u32[]{:S(2)}) collective-permute-start(bf16[512,1024]{1,0:T(8,128)(2,1)} %get-tuple-element.201), channel_id=1, source_target_pairs={{0,2},{2,0},{1,3},{3,1},{4,6},{6,4},{5,7},{7,5},{8,10},{10,8},{9,1... | collective-permute-start | bytes 3145736 | tf_op jit(solution)/shard_map/ppermute | solution.py:465
  335.9 24.7 %collective-permute-start.34 = (bf16[4,2,32,2048]{3,2,0,1:T(8,128)(2,1)S(1)}, bf16[4,2,32,2048]{3,2,0,1:T(8,128)(2,1)S(1)}, u32[]{:S(2)}, u32[]{:S(2)}) collective-permute-start(bf16[4,2,32,2048]{3,2,0,1:T(8,128)(2,1)S(1)} %bitcast.329), channel_id=1, source_target_pairs={{0,1},{1,0},{2,3},{3,2},{4,5},{5,4},{6,7},{7,6},{8,9},{9,8},{10,11... | collective-permute-start | bytes 3145736 | tf_op jit(solution)/shard_map/ppermute | solution.py:460
  336.6 24.4 %collective-permute-start.33 = (bf16[4,2,32,2048]{3,2,0,1:T(8,128)(2,1)S(1)}, bf16[4,2,32,2048]{3,2,0,1:T(8,128)(2,1)S(1)}, u32[]{:S(2)}, u32[]{:S(2)}) collective-permute-start(bf16[4,2,32,2048]{3,2,0,1:T(8,128)(2,1)S(1)} %bitcast.330), channel_id=1, source_target_pairs={{0,4},{4,0},{1,5},{5,1},{2,6},{6,2},{3,7},{7,3},{8,12},{12,8},{9,1... | collective-permute-start | bytes 3145736 | tf_op jit(solution)/shard_map/ppermute | solution.py:460
  346.5 30.5 %collective-permute-start.31 = (bf16[512,1024]{1,0:T(8,128)(2,1)S(1)}, bf16[512,1024]{1,0:T(8,128)(2,1)S(1)}, u32[]{:S(2)}, u32[]{:S(2)}) collective-permute-start(bf16[512,1024]{1,0:T(8,128)(2,1)S(1)} %fusion.15), channel_id=1, source_target_pairs={{0,2},{2,0},{1,3},{3,1},{4,6},{6,4},{5,7},{7,5},{8,10},{10,8},{9,1... | collective-permute-start | bytes 3145736 | tf_op jit(solution)/shard_map/ppermute | solution.py:465
  362.3 21.2 %collective-permute-start.35 = (bf16[4,32,2048]{2,1,0:T(8,128)(2,1)}, bf16[4,32,2048]{2,1,0:T(8,128)(2,1)}, u32[]{:S(2)}, u32[]{:S(2)}) collective-permute-start(bf16[4,32,2048]{2,1,0:T(8,128)(2,1)} %fusion.48), channel_id=1, source_target_pairs={{0,1},{1,0},{2,3},{3,2},{4,5},{5,4},{6,7},{7,6},{8,9},{9,8},{10,11... | collective-permute-start | bytes 1572872 | tf_op jit(solution)/shard_map/ppermute | solution.py:460
  365.4 18.1 %collective-permute-start.36 = (bf16[4,32,2048]{2,1,0:T(8,128)(2,1)}, bf16[4,32,2048]{2,1,0:T(8,128)(2,1)}, u32[]{:S(2)}, u32[]{:S(2)}) collective-permute-start(bf16[4,32,2048]{2,1,0:T(8,128)(2,1)} %fusion.49), channel_id=1, source_target_pairs={{0,4},{4,0},{1,5},{5,1},{2,6},{6,2},{3,7},{7,3},{8,12},{12,8},{9,1... | collective-permute-start | bytes 1572872 | tf_op jit(solution)/shard_map/ppermute | solution.py:460
  376.3 23.1 %collective-permute-start.38 = (bf16[4,2,32,2048]{3,2,0,1:T(8,128)(2,1)}, bf16[4,2,32,2048]{3,2,0,1:T(8,128)(2,1)}, u32[]{:S(2)}, u32[]{:S(2)}) collective-permute-start(bf16[4,2,32,2048]{3,2,0,1:T(8,128)(2,1)} %bitcast.280), channel_id=1, source_target_pairs={{0,1},{1,0},{2,3},{3,2},{4,5},{5,4},{6,7},{7,6},{8,9},{9,8},{10,11... | collective-permute-start | bytes 3145736 | tf_op jit(solution)/shard_map/ppermute | solution.py:460
  376.6 22.9 %collective-permute-start.37 = (bf16[4,2,32,2048]{3,2,0,1:T(8,128)(2,1)}, bf16[4,2,32,2048]{3,2,0,1:T(8,128)(2,1)}, u32[]{:S(2)}, u32[]{:S(2)}) collective-permute-start(bf16[4,2,32,2048]{3,2,0,1:T(8,128)(2,1)} %bitcast.281), channel_id=1, source_target_pairs={{0,4},{4,0},{1,5},{5,1},{2,6},{6,2},{3,7},{7,3},{8,12},{12,8},{9,1... | collective-permute-start | bytes 3145736 | tf_op jit(solution)/shard_map/ppermute | solution.py:460
  381.3 25.5 %collective-permute-start.32 = (bf16[512,1024]{1,0:T(8,128)(2,1)}, bf16[512,1024]{1,0:T(8,128)(2,1)S(1)}, u32[]{:S(2)}, u32[]{:S(2)}) collective-permute-start(bf16[512,1024]{1,0:T(8,128)(2,1)} %get-tuple-element.204), channel_id=1, source_target_pairs={{0,2},{2,0},{1,3},{3,1},{4,6},{6,4},{5,7},{7,5},{8,10},{10,8},{9,1... | collective-permute-start | bytes 3145736 | tf_op jit(solution)/shard_map/ppermute | solution.py:465
  411.1 18.3 %collective-permute-start.41 = (bf16[4,32,2048]{2,1,0:T(8,128)(2,1)S(1)}, bf16[4,32,2048]{2,1,0:T(8,128)(2,1)S(1)}, u32[]{:S(2)}, u32[]{:S(2)}) collective-permute-start(bf16[4,32,2048]{2,1,0:T(8,128)(2,1)S(1)} %fusion.51), channel_id=1, source_target_pairs={{0,4},{4,0},{1,5},{5,1},{2,6},{6,2},{3,7},{7,3},{8,12},{12,8},{9,1... | collective-permute-start | bytes 1572872 | tf_op jit(solution)/shard_map/ppermute | solution.py:460
  412.6 16.8 %collective-permute-start.40 = (bf16[4,32,2048]{2,1,0:T(8,128)(2,1)S(1)}, bf16[4,32,2048]{2,1,0:T(8,128)(2,1)S(1)}, u32[]{:S(2)}, u32[]{:S(2)}) collective-permute-start(bf16[4,32,2048]{2,1,0:T(8,128)(2,1)S(1)} %fusion.50), channel_id=1, source_target_pairs={{0,1},{1,0},{2,3},{3,2},{4,5},{5,4},{6,7},{7,6},{8,9},{9,8},{10,11... | collective-permute-start | bytes 1572872 | tf_op jit(solution)/shard_map/ppermute | solution.py:460
  412.9 16.4 %collective-permute-start.43 = (bf16[4,2,32,512]{3,2,0,1:T(8,128)(2,1)S(1)}, bf16[4,2,32,512]{3,2,0,1:T(8,128)(2,1)S(1)}, u32[]{:S(2)}, u32[]{:S(2)}) collective-permute-start(bf16[4,2,32,512]{3,2,0,1:T(8,128)(2,1)S(1)} %dynamic-slice_bitcast_fusion), channel_id=1, source_target_pairs={{0,1},{1,0},{2,3},{3,2},{4,5},{5,4},{6,7},{7,6},{8,9},{9,8},{10,11... | collective-permute-start | bytes 786440 | tf_op jit(solution)/shard_map/ppermute | solution.py:460
  414.3 15.1 %collective-permute-start.42 = (bf16[4,2,32,512]{3,2,0,1:T(8,128)(2,1)S(1)}, bf16[4,2,32,512]{3,2,0,1:T(8,128)(2,1)S(1)}, u32[]{:S(2)}, u32[]{:S(2)}) collective-permute-start(bf16[4,2,32,512]{3,2,0,1:T(8,128)(2,1)S(1)} %dynamic-slice_bitcast_fusion.1), channel_id=1, source_target_pairs={{0,4},{4,0},{1,5},{5,1},{2,6},{6,2},{3,7},{7,3},{8,12},{12,8},{9,1... | collective-permute-start | bytes 786440 | tf_op jit(solution)/shard_map/ppermute | solution.py:460
  414.6 14.8 %collective-permute-start.39 = (bf16[2,64,2048]{2,1,0:T(8,128)(2,1)S(1)}, bf16[2,64,2048]{2,1,0:T(8,128)(2,1)S(1)}, u32[]{:S(2)}, u32[]{:S(2)}) collective-permute-start(bf16[2,64,2048]{2,1,0:T(8,128)(2,1)S(1)} %select_convert_fusion.1), channel_id=1, source_target_pairs={{0,8},{8,0},{16,24},{24,16},{1,9},{9,1},{17,25},{25,17},{2,10},{10... | collective-permute-start | bytes 1572872 | tf_op jit(solution)/shard_map/ppermute | solution.py:460
  430.3 22.0 %collective-permute-start.47 = (bf16[4,32,512]{2,1,0:T(8,128)(2,1)S(1)}, bf16[4,32,512]{2,1,0:T(8,128)(2,1)S(1)}, u32[]{:S(2)}, u32[]{:S(2)}) collective-permute-start(bf16[4,32,512]{2,1,0:T(8,128)(2,1)S(1)} %fusion.70), channel_id=1, source_target_pairs={{0,4},{4,0},{1,5},{5,1},{2,6},{6,2},{3,7},{7,3},{8,12},{12,8},{9,1... | collective-permute-start | bytes 393224 | tf_op jit(solution)/shard_map/ppermute | solution.py:460
  431.7 20.5 %collective-permute-start.46 = (bf16[4,32,512]{2,1,0:T(8,128)(2,1)S(1)}, bf16[4,32,512]{2,1,0:T(8,128)(2,1)S(1)}, u32[]{:S(2)}, u32[]{:S(2)}) collective-permute-start(bf16[4,32,512]{2,1,0:T(8,128)(2,1)S(1)} %fusion.69), channel_id=1, source_target_pairs={{0,1},{1,0},{2,3},{3,2},{4,5},{5,4},{6,7},{7,6},{8,9},{9,8},{10,11... | collective-permute-start | bytes 393224 | tf_op jit(solution)/shard_map/ppermute | solution.py:460
  434.0 18.2 %collective-permute-start.44 = (bf16[64,2048]{1,0:T(8,128)(2,1)S(1)}, bf16[64,2048]{1,0:T(8,128)(2,1)S(1)}, u32[]{:S(2)}, u32[]{:S(2)}) collective-permute-start(bf16[64,2048]{1,0:T(8,128)(2,1)S(1)} %fusion.63), channel_id=1, source_target_pairs={{0,24},{24,0},{8,16},{16,8},{1,25},{25,1},{9,17},{17,9},{2,26},{26... | collective-permute-start | bytes 786440 | tf_op jit(solution)/shard_map/ppermute | solution.py:460
  435.5 16.8 %collective-permute-start.45 = (bf16[2,64,2048]{2,1,0:T(8,128)(2,1)S(1)}, bf16[2,64,2048]{2,1,0:T(8,128)(2,1)S(1)}, u32[]{:S(2)}, u32[]{:S(2)}) collective-permute-start(bf16[2,64,2048]{2,1,0:T(8,128)(2,1)S(1)} %select_convert_fusion), channel_id=1, source_target_pairs={{0,8},{8,0},{16,24},{24,16},{1,9},{9,1},{17,25},{25,17},{2,10},{10... | collective-permute-start | bytes 1572872 | tf_op jit(solution)/shard_map/ppermute | solution.py:460
  449.7 41.7 %collective-permute-start.56 = (f32[584,128]{1,0:T(8,128)S(1)}, f32[584,128]{1,0:T(8,128)S(1)}, u32[]{:S(2)}, u32[]{:S(2)}) collective-permute-start(f32[584,128]{1,0:T(8,128)S(1)} %pad_maximum_fusion.17), channel_id=1, source_target_pairs={{0,1},{1,0},{2,3},{3,2},{4,5},{5,4},{6,7},{7,6},{8,9},{9,8},{10,11... | collective-permute-start | bytes 897032 | tf_op jit(solution)/shard_map/ppermute | solution.py:460
  461.4 14.0 %collective-permute-start.49 = (bf16[4,2,32,1536]{3,2,0,1:T(8,128)(2,1)S(1)}, bf16[4,2,32,1536]{3,2,0,1:T(8,128)(2,1)S(1)}, u32[]{:S(2)}, u32[]{:S(2)}) collective-permute-start(bf16[4,2,32,1536]{3,2,0,1:T(8,128)(2,1)S(1)} %bitcast.333), channel_id=1, source_target_pairs={{0,1},{1,0},{2,3},{3,2},{4,5},{5,4},{6,7},{7,6},{8,9},{9,8},{10,11... | collective-permute-start | bytes 2359304 | tf_op jit(solution)/shard_map/ppermute | solution.py:460
  461.7 14.1 %collective-permute-start.48 = (bf16[4,2,32,1536]{3,2,0,1:T(8,128)(2,1)S(1)}, bf16[4,2,32,1536]{3,2,0,1:T(8,128)(2,1)S(1)}, u32[]{:S(2)}, u32[]{:S(2)}) collective-permute-start(bf16[4,2,32,1536]{3,2,0,1:T(8,128)(2,1)S(1)} %bitcast.332), channel_id=1, source_target_pairs={{0,4},{4,0},{1,5},{5,1},{2,6},{6,2},{3,7},{7,3},{8,12},{12,8},{9,1... | collective-permute-start | bytes 2359304 | tf_op jit(solution)/shard_map/ppermute | solution.py:460
  462.1 5.1 collective-permute-start.51
  462.2 11.0 %collective-permute-start.50 = (bf16[64,2048]{1,0:T(8,128)(2,1)S(1)}, bf16[64,2048]{1,0:T(8,128)(2,1)S(1)}, u32[]{:S(2)}, u32[]{:S(2)}) collective-permute-start(bf16[64,2048]{1,0:T(8,128)(2,1)S(1)} %fusion.64), channel_id=1, source_target_pairs={{0,24},{24,0},{8,16},{16,8},{1,25},{25,1},{9,17},{17,9},{2,26},{26... | collective-permute-start | bytes 786440 | tf_op jit(solution)/shard_map/ppermute | solution.py:460
  467.2 13.5 %collective-permute-start.60 = (bf16[512,1024]{1,0:T(8,128)(2,1)S(1)}, bf16[512,1024]{1,0:T(8,128)(2,1)S(1)}, u32[]{:S(2)}, u32[]{:S(2)}) collective-permute-start(bf16[512,1024]{1,0:T(8,128)(2,1)S(1)} %add_convert_fusion.2), channel_id=1, source_target_pairs={{0,2},{2,0},{1,3},{3,1},{4,6},{6,4},{5,7},{7,5},{8,10},{10,8},{9,1... | collective-permute-start | bytes 3145736 | tf_op jit(solution)/shard_map/ppermute | solution.py:465
  475.9 15.5 %collective-permute-start.54 = (bf16[64,512]{1,0:T(8,128)(2,1)S(1)}, bf16[64,512]{1,0:T(8,128)(2,1)S(1)}, u32[]{:S(2)}, u32[]{:S(2)}) collective-permute-start(bf16[64,512]{1,0:T(8,128)(2,1)S(1)} %fusion.75), channel_id=1, source_target_pairs={{0,24},{24,0},{8,16},{16,8},{1,25},{25,1},{9,17},{17,9},{2,26},{26... | collective-permute-start | bytes 196616 | tf_op jit(solution)/shard_map/ppermute | solution.py:460
  479.0 12.4 %collective-permute-start.52 = (bf16[4,32,1536]{2,1,0:T(8,128)(2,1)S(1)}, bf16[4,32,1536]{2,1,0:T(8,128)(2,1)S(1)}, u32[]{:S(2)}, u32[]{:S(2)}) collective-permute-start(bf16[4,32,1536]{2,1,0:T(8,128)(2,1)S(1)} %fusion.58), channel_id=1, source_target_pairs={{0,1},{1,0},{2,3},{3,2},{4,5},{5,4},{6,7},{7,6},{8,9},{9,8},{10,11... | collective-permute-start | bytes 1179656 | tf_op jit(solution)/shard_map/ppermute | solution.py:460
  479.4 12.0 %collective-permute-start.53 = (bf16[4,32,1536]{2,1,0:T(8,128)(2,1)S(1)}, bf16[4,32,1536]{2,1,0:T(8,128)(2,1)S(1)}, u32[]{:S(2)}, u32[]{:S(2)}) collective-permute-start(bf16[4,32,1536]{2,1,0:T(8,128)(2,1)S(1)} %fusion.59), channel_id=1, source_target_pairs={{0,4},{4,0},{1,5},{5,1},{2,6},{6,2},{3,7},{7,3},{8,12},{12,8},{9,1... | collective-permute-start | bytes 1179656 | tf_op jit(solution)/shard_map/ppermute | solution.py:460
  482.0 28.5 %collective-permute-start.61 = (bf16[512,1024]{1,0:T(8,128)(2,1)S(1)}, bf16[512,1024]{1,0:T(8,128)(2,1)S(1)}, u32[]{:S(2)}, u32[]{:S(2)}) collective-permute-start(bf16[512,1024]{1,0:T(8,128)(2,1)S(1)} %add_convert_fusion.1), channel_id=1, source_target_pairs={{0,0},{1,2},{2,1},{3,3},{4,4},{5,6},{6,5},{7,7},{8,8},{9,10},{10,9... | collective-permute-start | bytes 3145736 | tf_op jit(solution)/shard_map/ppermute | solution.py:460
  491.7 18.8 %collective-permute-start.59 = (bf16[64,4608]{1,0:T(8,128)(2,1)S(1)}, bf16[64,4608]{1,0:T(8,128)(2,1)S(1)}, u32[]{:S(2)}, u32[]{:S(2)}) collective-permute-start(bf16[64,4608]{1,0:T(8,128)(2,1)S(1)} %pad_maximum_fusion.15), channel_id=1, source_target_pairs={{0,0},{1,2},{2,1},{3,3},{4,4},{5,6},{6,5},{7,7},{8,8},{9,10},{10,9... | collective-permute-start | bytes 1769480 | tf_op jit(solution)/shard_map/ppermute | solution.py:460
  499.0 7.5 %collective-permute-start.57 = (bf16[2,64,1536]{2,1,0:T(8,128)(2,1)S(1)}, bf16[2,64,1536]{2,1,0:T(8,128)(2,1)S(1)}, u32[]{:S(2)}, u32[]{:S(2)}) collective-permute-start(bf16[2,64,1536]{2,1,0:T(8,128)(2,1)S(1)} %select_convert_fusion.2), channel_id=1, source_target_pairs={{0,8},{8,0},{16,24},{24,16},{1,9},{9,1},{17,25},{25,17},{2,10},{10... | collective-permute-start | bytes 1179656 | tf_op jit(solution)/shard_map/ppermute | solution.py:460
  499.5 6.1 %collective-permute-start.58 = (f32[584,128]{1,0:T(8,128)S(1)}, f32[584,128]{1,0:T(8,128)S(1)}, u32[]{:S(2)}, u32[]{:S(2)}) collective-permute-start(f32[584,128]{1,0:T(8,128)S(1)} %fusion.102), channel_id=1, source_target_pairs={{0,4},{4,0},{1,5},{5,1},{2,6},{6,2},{3,7},{7,3},{8,12},{12,8},{9,1... | collective-permute-start | bytes 897032 | tf_op jit(solution)/shard_map/ppermute | solution.py:460
  510.7 9.7 %collective-permute-start.63 = (f32[584,128]{1,0:T(8,128)S(1)}, f32[584,128]{1,0:T(8,128)S(1)}, u32[]{:S(2)}, u32[]{:S(2)}) collective-permute-start(f32[584,128]{1,0:T(8,128)S(1)} %add.510), channel_id=1, source_target_pairs={{0,24},{24,0},{8,16},{16,8},{1,25},{25,1},{9,17},{17,9},{2,26},{26... | collective-permute-start | bytes 897032 | tf_op jit(solution)/shard_map/ppermute | solution.py:460
  511.4 8.9 %collective-permute-start.62 = (bf16[64,1536]{1,0:T(8,128)(2,1)S(1)}, bf16[64,1536]{1,0:T(8,128)(2,1)S(1)}, u32[]{:S(2)}, u32[]{:S(2)}) collective-permute-start(bf16[64,1536]{1,0:T(8,128)(2,1)S(1)} %fusion.65), channel_id=1, source_target_pairs={{0,24},{24,0},{8,16},{16,8},{1,25},{25,1},{9,17},{17,9},{2,26},{26... | collective-permute-start | bytes 589832 | tf_op jit(solution)/shard_map/ppermute | solution.py:460
  520.5 10.7 %collective-permute-start.64 = (bf16[64,1536]{1,0:T(8,128)(2,1)S(1)}, bf16[64,1536]{1,0:T(8,128)(2,1)S(1)}, u32[]{:S(2)}, u32[]{:S(2)}) collective-permute-start(bf16[64,1536]{1,0:T(8,128)(2,1)S(1)} %fusion.62), channel_id=1, source_target_pairs={{0,0},{1,2},{2,1},{3,3},{4,4},{5,6},{6,5},{7,7},{8,8},{9,10},{10,9... | collective-permute-start | bytes 589832 | tf_op jit(solution)/shard_map/ppermute | solution.py:460
  526.4 8.8 %collective-permute-start.65 = (f32[584,128]{1,0:T(8,128)S(1)}, f32[584,128]{1,0:T(8,128)S(1)}, u32[]{:S(2)}, u32[]{:S(2)}) collective-permute-start(f32[584,128]{1,0:T(8,128)S(1)} %add.512), channel_id=1, source_target_pairs={{0,8},{8,0},{16,24},{24,16},{1,9},{9,1},{17,25},{25,17},{2,10},{10... | collective-permute-start | bytes 897032 | tf_op jit(solution)/shard_map/ppermute | solution.py:460
  (81 other events, 860.4 us)

commit v7 on v6

--- a/solution.py
+++ b/solution.py
@@ -455,6 +455,10 @@
     return lax.optimization_barrier((value,) + others)[0]
 
 
+def tie_all(values, *others):
+    return lax.optimization_barrier(tuple(values) + others)[: len(values)]
+
+
 def exchange(*moves):
     return lax.optimization_barrier(
         tuple(lax.ppermute(value, axis, steps) for value, axis, steps in moves)
@@ -576,11 +580,25 @@
     return jnp.stack([low, high]).astype(jnp.int32)
 
 
+def token_spans(row_lengths, token_count):
+    ends = jnp.cumsum(row_lengths)[:, None]
+    span = NQ_ROW * QLEN
+    place = jnp.arange(token_count, dtype=jnp.int32)[None, :]
+    doc = place - span
+    begin = jnp.max(jnp.where(ends <= doc, ends, 0), axis=0) + span
+    end = jnp.min(jnp.where(ends > doc, ends, token_count), axis=0) + span
+    query = place[0] // QLEN * QLEN
+    return jnp.stack(
+        [jnp.where(doc[0] < 0, query, begin), jnp.where(doc[0] < 0, query + QLEN, end)]
+    ).astype(jnp.int32)
+
+
 def rows_of(value, start, count):
     return lax.dynamic_slice_in_dim(value, start, count, 0)
 
 
 TILE = 256
+KEYS = 256
 NEG = -1e30
 
 
@@ -594,196 +612,203 @@
     return (jnp.where(lane < HEAD_DIM, value, zero), jnp.where(lane < HEAD_DIM, zero, value))
 
 
-def fill_bias(seg_col, seg_row, bias):
-    for start in range(0, bias.shape[0], TILE):
-        rows = slice(start, start + TILE)
-        bias[rows, :] = jnp.where(seg_col[rows, :] == seg_row[...], 0.0, NEG)
-
-
-def attend_kernel(bounds, q_ref, k_ref, v_ref, seg_col, seg_row, out_ref, lse_ref, bias, held):
-    @pl.when(pl.program_id(0) == 0)
-    def _():
-        fill_bias(seg_col, seg_row, bias)
-
-    for block in range(q_ref.shape[0] // TILE):
-        own = slice(block * TILE, (block + 1) * TILE)
-        queries = head_masks(q_ref[own, :] * HEAD_DIM**-0.5)
-
-        def score(step, highest):
-            rows = pl.ds(pl.multiple_of(step * TILE, TILE), TILE)
-            keys, shift = k_ref[rows, :], bias[rows, own]
-            fresh = []
-            for head in range(2):
-                scores = exact(keys, queries[head], ((1,), (1,))) + shift
-                held[head, rows, :] = scores
-                fresh.append(jnp.maximum(highest[head], jnp.max(scores, axis=0, keepdims=True)))
-            return tuple(fresh)
-
-        low = jnp.full((1, TILE), NEG, F32)
-        highest = lax.fori_loop(bounds[0, block], bounds[1, block], score, (low, low))
-
-        def mix(step, carried):
-            rows = pl.ds(pl.multiple_of(step * TILE, TILE), TILE)
-            values = v_ref[rows, :]
-            fresh = []
-            for head in range(2):
-                total, mixed = carried[head]
-                expo = jnp.exp(held[head, rows, :] - highest[head])
-                fresh.append(
-                    (
-                        total + jnp.sum(expo, axis=0, keepdims=True),
-                        mixed + exact(values, expo.astype(BF), ((0,), (0,))),
-                    )
+def key_shift(step, spans):
+    place = step * KEYS + lax.broadcasted_iota(jnp.int32, (KEYS, TILE), 0)
+    inside = (place >= spans[0:1, :]) & (place < spans[1:2, :])
+    return jnp.where(inside, 0.0, NEG)
+
+
+def attend_kernel(bounds, own_ref, qkv_ref, spans, out_ref, lse_ref, held):
+    block = pl.program_id(0)
+    groups = 2
+    pairs = out_ref.shape[1] // 128
+    per_group = pairs // groups
+
+    def column(pair, part):
+        start = ((pair // per_group) * 3 + part) * per_group + pair % per_group
+        return slice(start * 128, (start + 1) * 128)
+
+    queries = [head_masks(own_ref[:, column(pair, 0)] * HEAD_DIM**-0.5) for pair in range(pairs)]
+    heads = [(pair, head) for pair in range(pairs) for head in range(2)]
+
+    def score(step, highest):
+        rows = pl.ds(pl.multiple_of(step * KEYS, KEYS), KEYS)
+        shift = key_shift(step, spans)
+        fresh = []
+        for index, (pair, head) in enumerate(heads):
+            keys = qkv_ref[rows, column(pair, 1)]
+            scores = exact(keys, queries[pair][head], ((1,), (1,))) + shift
+            held[index, rows, :] = scores
+            fresh.append(jnp.maximum(highest[index], jnp.max(scores, axis=0, keepdims=True)))
+        return tuple(fresh)
+
+    low = jnp.full((1, TILE), NEG, F32)
+    highest = lax.fori_loop(bounds[0, block], bounds[1, block], score, (low,) * len(heads))
+
+    def mix(step, carried):
+        rows = pl.ds(pl.multiple_of(step * KEYS, KEYS), KEYS)
+        fresh = []
+        for index, (pair, head) in enumerate(heads):
+            values = qkv_ref[rows, column(pair, 2)]
+            total, mixed = carried[index]
+            expo = jnp.exp(held[index, rows, :] - highest[index])
+            product = exact(values, expo.astype(BF), ((0,), (0,)))
+            fresh.append(
+                (
+                    total + jnp.sum(expo, axis=0, keepdims=True),
+                    mixed + product[head * HEAD_DIM : (head + 1) * HEAD_DIM],
                 )
-            return tuple(fresh)
-
-        start = (jnp.zeros((1, TILE), F32), jnp.zeros((2 * HEAD_DIM, TILE), F32))
-        parts = lax.fori_loop(bounds[0, block], bounds[1, block], mix, (start, start))
-        mixed = jnp.concatenate(
-            [parts[0][1][:HEAD_DIM] / parts[0][0], parts[1][1][HEAD_DIM:] / parts[1][0]], axis=0
-        )
-        out_ref[own, :] = jnp.transpose(mixed).astype(BF)
-        for head in range(2):
-            lse_ref[0, head : head + 1, own] = highest[head] + jnp.log(parts[head][0])
-
-
-def attend(bounds, qkv, seg_col, seg_row):
+            )
+        return tuple(fresh)
+
+    start = (jnp.zeros((1, TILE), F32), jnp.zeros((HEAD_DIM, TILE), F32))
+    parts = lax.fori_loop(bounds[0, block], bounds[1, block], mix, (start,) * len(heads))
+    for pair in range(pairs):
+        both = [parts[2 * pair + head][1] / parts[2 * pair + head][0] for head in range(2)]
+        mixed = jnp.transpose(jnp.concatenate(both, axis=0))
+        out_ref[:, pair * 128 : (pair + 1) * 128] = mixed.astype(BF)
+    for index in range(len(heads)):
+        lse_ref[index : index + 1, :] = highest[index] + jnp.log(parts[index][0])
+
+
+def attend(bounds, qkv, spans):
     count, wide = qkv.shape
-    pairs = wide // 3 // 128
-    group = pairs // 2
-    column = lambda part: pl.BlockSpec(
-        (count, 128), lambda i: (0, (i // group) * 3 * group + part * group + i % group)
-    )
-    mixed_column = pl.BlockSpec((count, 128), lambda i: (0, i))
+    heads = wide // 3 // HEAD_DIM
     whole = lambda shape: pl.BlockSpec(shape, lambda i: (0, 0))
     return pl.pallas_call(
         attend_kernel,
-        grid=(pairs,),
+        grid=(count // TILE,),
         in_specs=[
             pl.BlockSpec(memory_space=pltpu.SMEM),
-            column(0),
-            column(1),
-            column(2),
-            whole((count, 1)),
-            whole((1, count)),
+            pl.BlockSpec((TILE, wide), lambda i: (i, 0)),
+            whole((count, wide)),
+            pl.BlockSpec((2, TILE), lambda i: (0, i)),
         ],
-        out_specs=[mixed_column, pl.BlockSpec((1, 8, count), lambda i: (i, 0, 0))],
+        out_specs=[
+            pl.BlockSpec((TILE, wide // 3), lambda i: (i, 0)),
+            pl.BlockSpec((heads, TILE), lambda i: (0, i)),
+        ],
         out_shape=[
             jax.ShapeDtypeStruct((count, wide // 3), BF),
-            jax.ShapeDtypeStruct((pairs, 8, count), F32),
+            jax.ShapeDtypeStruct((heads, count), F32),
         ],
-        scratch_shapes=[pltpu.VMEM((count, count), F32), pltpu.VMEM((2, count, TILE), F32)],
+        scratch_shapes=[pltpu.VMEM((heads, count, TILE), F32)],
         compiler_params=pltpu.CompilerParams(vmem_limit_bytes=40 << 20),
         cost_estimate=pl.CostEstimate(
-            flops=4 * pairs * count * count * 128,
-            transcendentals=pairs * count * count,
+            flops=4 * heads * count * count * 64,
+            transcendentals=heads * count * count // 2,
             bytes_accessed=4 * count * wide * 2,
         ),
-    )(bounds, qkv, qkv, qkv, seg_col, seg_row)
+    )(bounds, qkv, qkv, spans)
 
 
 def attend_back_kernel(
-    bounds, q_ref, k_ref, v_ref, out_ref, grad_ref, lse_ref, seg_col, seg_row,
-    grads_ref, sums_ref, bias, key_sum, value_sum,
+    first, bounds, own_ref, qkv_ref, out_ref, grad_ref, lse_ref, spans,
+    grads_ref, sums_ref, key_sum, value_sum,
 ):
-    pair = pl.program_id(0)
-
-    @pl.when(pair == 0)
+    block = pl.program_id(0)
+    pairs = out_ref.shape[1] // 128
+    heads = [(pair, head) for pair in range(pairs) for head in range(2)]
+    cut = lambda index: slice(index * 128, (index + 1) * 128)
+
+    @pl.when(block == 0)
     def _():
-        fill_bias(seg_col, seg_row, bias)
-
-    key_sum[...] = jnp.zeros_like(key_sum)
-    value_sum[...] = jnp.zeros_like(value_sum)
-    columns = [
-        pl.ds(pl.multiple_of(part * (grads_ref.shape[1] // 3) + pair * 128, 128), 128) for part in range(3)
-    ]
-    query_total = jnp.zeros((1, 128), F32)
+        key_sum[...] = jnp.zeros_like(key_sum)
+        value_sum[...] = jnp.zeros_like(value_sum)
+        sums_ref[...] = jnp.zeros_like(sums_ref)
+
+    queries = [head_masks(own_ref[:, cut(pair)] * HEAD_DIM**-0.5) for pair in range(pairs)]
+    grads = [head_masks(grad_ref[:, cut(pair)]) for pair in range(pairs)]
     picks = head_masks(jnp.ones((8, 128), BF))
-    for block in range(q_ref.shape[0] // TILE):
-        own = slice(block * TILE, (block + 1) * TILE)
-        queries = head_masks(q_ref[own, :] * HEAD_DIM**-0.5)
-        grads = head_masks(grad_ref[own, :])
-        product = grad_ref[own, :].astype(F32) * out_ref[own, :].astype(F32)
-        product_high = product.astype(BF)
-        product_low = (product - product_high.astype(F32)).astype(BF)
-        inner = [
+    inner = []
+    for pair, head in heads:
+        product = grad_ref[:, cut(pair)].astype(F32) * out_ref[:, cut(pair)].astype(F32)
+        high = product.astype(BF)
+        rest = (product - high.astype(F32)).astype(BF)
+        inner.append(
             (
-                exact(picks[head], product_high, ((1,), (1,)))
-                + exact(picks[head], product_low, ((1,), (1,)))
+                exact(picks[head], high, ((1,), (1,))) + exact(picks[head], rest, ((1,), (1,)))
             )[0:1]
-            for head in range(2)
-        ]
-        lse = [lse_ref[0, head : head + 1, own] for head in range(2)]
-
-        def step_of(step, carried):
-            rows = pl.ds(pl.multiple_of(step * TILE, TILE), TILE)
-            keys, values, shift = k_ref[rows, :], v_ref[rows, :], bias[rows, own]
-            fresh = []
-            key_add = jnp.zeros((TILE, 128), F32)
-            value_add = jnp.zeros((TILE, 128), F32)
+        )
+    lse = [lse_ref[first + index : first + index + 1, :] for index in range(len(heads))]
+
+    def step_of(step, carried):
+        rows = pl.ds(pl.multiple_of(step * KEYS, KEYS), KEYS)
+        shift = key_shift(step, spans)
+        fresh = []
+        for pair in range(pairs):
+            keys = qkv_ref[rows, cut(pairs + pair)]
+            values = qkv_ref[rows, cut(2 * pairs + pair)]
+            key_add = jnp.zeros((KEYS, 128), F32)
+            value_add = jnp.zeros((KEYS, 128), F32)
             for head in range(2):
-                scores = exact(keys, queries[head], ((1,), (1,))) + shift
-                probs = jnp.exp(scores - lse[head])
-                grad_probs = exact(values, grads[head], ((1,), (1,)))
-                grad_scores = (probs * (grad_probs - inner[head])).astype(BF)
-                value_add = value_add + exact(probs.astype(BF), grads[head], ((1,), (0,)))
-                key_add = key_add + exact(grad_scores, queries[head], ((1,), (0,)))
-                fresh.append(carried[head] + exact(keys, grad_scores, ((0,), (0,))))
-            key_sum[rows, :] += key_add
-            value_sum[rows, :] += value_add
-            return tuple(fresh)
-
-        start = jnp.zeros((2 * HEAD_DIM, TILE), F32)
-        parts = lax.fori_loop(bounds[0, block], bounds[1, block], step_of, (start, start))
-        grad_query = jnp.concatenate([parts[0][:HEAD_DIM], parts[1][HEAD_DIM:]], axis=0)
+                index = 2 * pair + head
+                scores = exact(keys, queries[pair][head], ((1,), (1,))) + shift
+                probs = jnp.exp(scores - lse[index])
+                grad_probs = exact(values, grads[pair][head], ((1,), (1,)))
+                grad_scores = (probs * (grad_probs - inner[index])).astype(BF)
+                value_add = value_add + exact(probs.astype(BF), grads[pair][head], ((1,), (0,)))
+                key_add = key_add + exact(grad_scores, queries[pair][head], ((1,), (0,)))
+                product = exact(keys, grad_scores, ((0,), (0,)))
+                fresh.append(carried[index] + product[head * HEAD_DIM : (head + 1) * HEAD_DIM])
+            key_sum[rows, cut(pair)] += key_add
+            value_sum[rows, cut(pair)] += value_add
+        return tuple(fresh)
+
+    start = jnp.zeros((HEAD_DIM, TILE), F32)
+    parts = lax.fori_loop(bounds[0, block], bounds[1, block], step_of, (start,) * len(heads))
+    own = pl.ds(pl.multiple_of(block * TILE, TILE), TILE)
+    for pair in range(pairs):
+        grad_query = jnp.concatenate([parts[2 * pair], parts[2 * pair + 1]], axis=0)
         grad_query = jnp.transpose(grad_query * HEAD_DIM**-0.5).astype(BF)
-        grads_ref[own, columns[0]] = grad_query
-        query_total = query_total + jnp.sum(grad_query.astype(F32), axis=0, keepdims=True)
-    grad_value = value_sum[...].astype(BF)
-    grads_ref[:, columns[1]] = key_sum[...].astype(BF)
-    grads_ref[:, columns[2]] = grad_value
-    sums_ref[0, 0:1, :] = query_total
-    sums_ref[0, 1:2, :] = jnp.sum(grad_value.astype(F32), axis=0, keepdims=True)
-
-
-def attend_back(bounds, group, qkv, mixed, grad_mixed, lse, seg_col, seg_row):
+        grads_ref[own, cut(pair)] = grad_query
+        sums_ref[0:1, cut(pair)] += jnp.sum(grad_query.astype(F32), axis=0, keepdims=True)
+
+    @pl.when(block == pl.num_programs(0) - 1)
+    def _():
+        wide = pairs * 128
+        grad_value = value_sum[...].astype(BF)
+        grads_ref[:, wide : 2 * wide] = key_sum[...].astype(BF)
+        grads_ref[:, 2 * wide :] = grad_value
+        sums_ref[1:2, :] = jnp.sum(grad_value.astype(F32), axis=0, keepdims=True)
+
+
+def attend_back(bounds, group, qkv, mixed, grad_mixed, lse, spans):
     count = qkv.shape[0]
     wide = qkv.shape[1] // 2
-    pairs = wide // 3 // 128
-    column = lambda shift: pl.BlockSpec((count, 128), lambda i: (0, shift + i))
+    heads = wide // 3 // HEAD_DIM
     whole = lambda shape: pl.BlockSpec(shape, lambda i: (0, 0))
-    first = group * pairs
     return pl.pallas_call(
-        attend_back_kernel,
-        grid=(pairs,),
+        partial(attend_back_kernel, group * heads),
+        grid=(count // TILE,),
         in_specs=[
             pl.BlockSpec(memory_space=pltpu.SMEM),
-            column(3 * first),
-            column(3 * first + pairs),
-            column(3 * first + 2 * pairs),
-            column(first),
-            column(first),
-            pl.BlockSpec((1, 8, count), lambda i: (first + i, 0, 0)),
-            whole((count, 1)),
-            whole((1, count)),
+            pl.BlockSpec((TILE, wide), lambda i: (i, group)),
+            pl.BlockSpec((count, wide), lambda i: (0, group)),
+            pl.BlockSpec((TILE, wide // 3), lambda i: (i, group)),
+            pl.BlockSpec((TILE, wide // 3), lambda i: (i, group)),
+            pl.BlockSpec((2 * heads, TILE), lambda i: (0, i)),
+            pl.BlockSpec((2, TILE), lambda i: (0, i)),
         ],
-        out_specs=[whole((count, wide)), pl.BlockSpec((1, 8, 128), lambda i: (i, 0, 0))],
+        out_specs=[whole((count, wide)), whole((8, wide // 3))],
         out_shape=[
             jax.ShapeDtypeStruct((count, wide), BF),
-            jax.ShapeDtypeStruct((pairs, 8, 128), F32),
+            jax.ShapeDtypeStruct((8, wide // 3), F32),
         ],
         scratch_shapes=[
-            pltpu.VMEM((count, count), F32),
-            pltpu.VMEM((count, 128), F32),
-            pltpu.VMEM((count, 128), F32),
+            pltpu.VMEM((count, wide // 3), F32),
+            pltpu.VMEM((count, wide // 3), F32),
         ],
         compiler_params=pltpu.CompilerParams(vmem_limit_bytes=40 << 20),
         cost_estimate=pl.CostEstimate(
-            flops=10 * pairs * count * count * 128,
-            transcendentals=pairs * count * count,
+            flops=10 * heads * count * count * 64,
+            transcendentals=heads * count * count // 2,
             bytes_accessed=8 * count * wide * 2,
         ),
-    )(bounds, qkv, qkv, qkv, mixed, grad_mixed, lse, seg_col, seg_row)
+    )(
+        bounds, qkv, qkv, mixed, grad_mixed,
+        lse, spans,
+    )
 
 
 ERFC = (
@@ -830,7 +855,7 @@
         out_shape=[jax.ShapeDtypeStruct((count, width), BF)] * 2,
         compiler_params=pltpu.CompilerParams(vmem_limit_bytes=32 << 20),
         cost_estimate=pl.CostEstimate(
-            flops=2 * count * depth * width,
+            flops=10 * count * depth * width,
             transcendentals=3 * count * width,
             bytes_accessed=2 * (count * depth + depth * width + 2 * count * width),
         ),
@@ -1026,7 +1051,8 @@
     mid_wide = mid_rows.shape[1]
     rest_rows = tie(rest_rows, qkv_pair)
     mid_rows, down_rows = rest_rows[:, :mid_wide], rest_rows[:, mid_wide:]
-    got = exchange((qkv_pair, "z", NEAR), (mid_rows, "z", FAR))
+    got = exchange((qkv_pair, "z", NEAR), (mid_rows, "z", FAR), (tie(cot, qkv_pair), CORES, TURN))
+    own_cot = got[2]
     qkv_line = whole_line(qkv_pair, got[0], z)
     mid_pair = far_pair(mid_rows, got[1], z)
     got = exchange(*first_moves(qkv_line), (mid_pair, "z", NEAR))
@@ -1042,14 +1068,13 @@
     got = exchange(*last_moves(mid_parts), *first_moves(down_line))
     full_mid = full_rows(mid_parts, got, x, y)
     down_parts = first_parts(down_line, got[2:], x, y)
-    got = exchange(*last_moves(down_parts))
-    full_down = full_rows(down_parts, got, x, y)
+    down_got = exchange(*last_moves(down_parts))
     full_out = full_mid[:, up_wide : up_wide + half_width]
     pairs = full_mid[:, up_wide + half_width :].reshape(chip_count, 64, 128)
     pairs = pairs[:, 0, :half_queries].astype(jnp.int32).reshape(1, query_total)
     row_lengths = lax.dynamic_index_in_dim(lengths, chip, 0, keepdims=False)
     segments = segments_of(row_lengths, token_count)
-    seg_col, seg_row = segments[:, None], segments[None, :]
+    seg_row, spans = segments[None, :], token_spans(row_lengths, token_count)
     query_span = NQ_ROW * QLEN
     bounds = tile_bounds(row_lengths, token_count)
     no_bias = jnp.zeros((1, quarter), F32)
@@ -1066,7 +1091,7 @@
         axis=1,
     )
     qkv = (dot(row, full_qkv) + qkv_bias).astype(BF)
-    mixed, lse = attend(bounds, qkv, seg_col, seg_row)
+    mixed, lse = attend(bounds, tie(qkv, down_line), spans)
 
     def row_sum(left, weight_t, transposed):
         times = contract_cols if transposed else dot
@@ -1084,6 +1109,8 @@
     normed_low = normed.astype(BF)
     normed_all = jnp.concatenate([normed_low, swap(normed_low, "c")], axis=0)
     activation, slope = expand(normed_all, full_mid, bias[:, 2 * half_width :])
+    down_got = tie_all(down_got, activation)
+    full_down = full_rows(down_parts, down_got, x, y)
     ffn_sum = row_sum(
         lambda which: activation[which * share : (which + 1) * share], full_down, True
     )
@@ -1140,10 +1167,7 @@
         )
         / sums
     )
-    losses = jnp.where(c == y, losses, swap(losses, "c"))
-    loss_out = rows_of(losses, 4 * z + 2 * x + c, 1)
-    y_out, own_cot = exchange((result_low, CORES, TURN), (tie(cot, queries), CORES, TURN))
-    query_grad, doc_grad = pool_back(cuts, query_span, tie(queries, y_out, own_cot), row_embed, seg_row, coefficient)
+    query_grad, doc_grad = pool_back(cuts, query_span, queries, row_embed, seg_row, coefficient)
     grad_blocks = lax.all_to_all(
         query_grad.reshape(chip_count, half_span, proj_width), chips, 0, 0
     )
@@ -1168,17 +1192,18 @@
     grad_second = norm_backward(grad_result, unit_two, rstd_two, gains[1])
     grad_ffn = grad_second.astype(BF)
     down_bias = jnp.sum(grad_ffn.astype(F32), axis=0)
-    grad_ffn_all = jnp.concatenate([grad_ffn, swap(grad_ffn, "c")], axis=0)
+    other_ffn, other_losses = exchange((grad_ffn, "c", SWAP), (losses, "c", SWAP))
+    losses = jnp.where(c == y, losses, other_losses)
+    loss_out = rows_of(losses, 4 * z + 2 * x + c, 1)
+    grad_ffn_all = jnp.concatenate([grad_ffn, other_ffn], axis=0)
     down_blocks = blocks_of(grad_ffn_all, activation)
-    grad_ffn_all = tie(grad_ffn_all, down_blocks)
     down_moved = exchange(*sum_moves(down_blocks, x, y))
     grad_up = (dot(grad_ffn_all, full_down) * slope.astype(F32)).astype(BF)
     up_bias = jnp.sum(grad_up.astype(F32), axis=0)
-    up_blocks = blocks_of(normed_all, tie(grad_up, *down_moved))
+    up_blocks = blocks_of(normed_all, grad_up)
     down_parts = sum_parts(down_blocks, down_moved, x, y)
-    moved = exchange(*line_moves(down_parts, x, y), *sum_moves(up_blocks, x, y))
+    moved = exchange(*line_moves(down_parts, x, y))
     down_line = line_of(down_parts, moved, x, y)
-    up_parts = sum_parts(up_blocks, moved[2:], x, y)
     full_up = full_mid[:, :up_wide]
     grad_normed = (
         row_sum(lambda which: grad_up[which * share : (which + 1) * share], full_up, True)
@@ -1197,41 +1222,49 @@
     )
     grad_mixed = dot(grad_attn_all, full_out).astype(BF)
     out_blocks = blocks_of(grad_attn_all, mixed)
-    grad_mixed, out_blocks, down_line, *up_parts = lax.optimization_barrier(
-        (grad_mixed, out_blocks, down_line) + tuple(up_parts)
+    grad_mixed, out_blocks, down_line, up_blocks = lax.optimization_barrier(
+        (grad_mixed, out_blocks, down_line, up_blocks)
+    )
+    moved = exchange(near_move(down_line, z), *sum_moves(up_blocks, x, y))
+    grads_one, sums_one = attend_back(bounds, 0, qkv, mixed, grad_mixed, lse, spans)
+    down_pair = near_sum(down_line, moved[0], z)
+    up_parts = sum_parts(up_blocks, moved[1:], x, y)
+    grad_mixed, down_pair, out_blocks, *up_parts = lax.optimization_barrier(
+        (grad_mixed, down_pair, out_blocks) + tuple(up_parts)
+    )
+    moves = line_moves(up_parts, x, y) + sum_moves(out_blocks, x, y)
+    grad_mixed, *given = lax.optimization_barrier(
+        (grad_mixed,) + tuple(value for value, _, _ in moves)
+    )
+    moved = exchange(*((value,) + move[1:] for value, move in zip(given, moves)))
+    grads_two, sums_two = attend_back(
+        bounds, 1, qkv, mixed, tie(grad_mixed, grads_one), lse, spans
+    )
+    up_line = line_of(up_parts, moved, x, y)
+    out_parts = sum_parts(out_blocks, moved[2:], x, y)
+    grads_one, grads_two, down_pair, up_line, *out_parts = lax.optimization_barrier(
+        (grads_one, grads_two, down_pair, up_line) + tuple(out_parts)
     )
     moved = exchange(
-        near_move(down_line, z), *line_moves(up_parts, x, y), *sum_moves(out_blocks, x, y)
-    )
-    grads_one, sums_one = attend_back(bounds, 0, qkv, mixed, grad_mixed, lse, seg_col, seg_row)
-    down_pair = near_sum(down_line, moved[0], z)
-    up_line = line_of(up_parts, moved[1:], x, y)
-    out_parts = sum_parts(out_blocks, moved[3:], x, y)
-    grad_mixed, down_pair, up_line, *out_parts = lax.optimization_barrier(
-        (grad_mixed, down_pair, up_line) + tuple(out_parts)
-    )
-    moved = exchange(
-        far_move(down_pair, z), near_move(up_line, z), *line_moves(out_parts, x, y)
-    )
-    grads_two, sums_two = attend_back(
-        bounds, 1, qkv, mixed, tie(grad_mixed, grads_one), lse, seg_col, seg_row
-    )
-    down_part = far_sum(down_pair, moved[0], z)
-    up_pair = near_sum(up_line, moved[1], z)
-    out_line = line_of(out_parts, moved[2:], x, y)
-    grads_one, grads_two, down_part, up_pair, out_line = lax.optimization_barrier(
-        (grads_one, grads_two, down_part, up_pair, out_line)
-    )
+        near_move(up_line, z),
+        *line_moves(out_parts, x, y),
+        (tie(result_low, up_line), CORES, TURN),
+        far_move(down_pair, z),
+    )
+    down_part = far_sum(down_pair, moved[4], z)
+    up_pair = near_sum(up_line, moved[0], z)
+    out_line = line_of(out_parts, moved[1:3], x, y)
+    y_out = moved[3]
     proj_half = rows_of(proj_grad, own_start, share) + swap(
         rows_of(proj_grad, other_start, share), "c"
     )
     shared = jnp.stack([gain_one, gain_two, shift_one, shift_two, out_bias, down_bias])
     half_sums = jnp.concatenate(
         [
-            sums_one[:, 0].reshape(-1),
-            sums_two[:, 0].reshape(-1),
-            sums_one[:, 1].reshape(-1),
-            sums_two[:, 1].reshape(-1),
+            sums_one[0],
+            sums_two[0],
+            sums_one[1],
+            sums_two[1],
             up_bias,
         ]
     )
@@ -1240,12 +1273,19 @@
     qkv_blocks = jnp.concatenate(
         [blocks_of(row, grads_one), blocks_of(row, grads_two)], axis=4
     )
+    qkv_blocks, up_pair, out_line, down_part, small = lax.optimization_barrier(
+        (qkv_blocks, up_pair, out_line, down_part, small)
+    )
     moved = exchange(
-        *sum_moves(qkv_blocks, x, y), far_move(up_pair, z), near_move(out_line, z)
+        *sum_moves(qkv_blocks, x, y),
+        far_move(up_pair, z),
+        near_move(out_line, z),
+        (small, "y", SWAP),
     )
     qkv_parts = sum_parts(qkv_blocks, moved, x, y)
     up_part = far_sum(up_pair, moved[2], z)
     out_pair = near_sum(out_line, moved[3], z)
+    small = small + moved[4]
 
     def input_terms(start):
         return contract_cols(
@@ -1254,31 +1294,29 @@
 
     other_terms = swap(input_terms(other_start).astype(BF), "c")
     grad_input = (input_terms(own_start) + other_terms.astype(F32) + grad_first).astype(BF)
-    moved = exchange(*line_moves(qkv_parts, x, y), far_move(out_pair, z), (small, "y", SWAP))
+    moved = exchange(*line_moves(qkv_parts, x, y), far_move(out_pair, z), (small, "x", SWAP))
     qkv_line = line_of(qkv_parts, moved, x, y)
     out_part = far_sum(out_pair, moved[2], z)
     small = small + moved[3]
-    rest_part = jnp.concatenate([down_part, up_part, out_part], axis=1).astype(BF)
     moved = exchange(
-        near_move(qkv_line, z), (small, "x", SWAP), (rest_part, CORES, TURN),
+        near_move(qkv_line, z),
+        (small, "z", FAR),
         (tie(grad_input, qkv_line), CORES, TURN),
     )
     qkv_pair = near_sum(qkv_line, moved[0], z)
     small = small + moved[1]
-    rest_part = moved[2].astype(F32)
-    grad_input = moved[3]
-    down_part, up_part, out_part = (
-        rest_part[:, :up_wide],
-        rest_part[:, up_wide : 2 * up_wide],
-        rest_part[:, 2 * up_wide :],
-    )
-    moved = exchange(far_move(qkv_pair, z), (small, "z", FAR))
-    qkv_part = far_sum(qkv_pair, moved[0], z).astype(BF)
+    grad_input = moved[2]
+    ffn_part = jnp.concatenate([down_part, up_part], axis=1).astype(BF)
+    moved = exchange(
+        far_move(qkv_pair, z), (small, "z", NEAR), (tie(ffn_part, qkv_pair), CORES, TURN)
+    )
+    attn_part = jnp.concatenate([far_sum(qkv_pair, moved[0], z), out_part], axis=1).astype(BF)
     small = small + moved[1]
-    moved = exchange((qkv_part, CORES, TURN), (small, "z", NEAR))
-    qkv_part = moved[0].astype(F32)
-    small = small + moved[1]
-    other_small = swap(small, "c")
+    ffn_part = moved[2].astype(F32)
+    down_part, up_part = ffn_part[:, :up_wide], ffn_part[:, up_wide:]
+    attn_part, other_small = exchange((attn_part, CORES, TURN), (small, "c", SWAP))
+    attn_part = attn_part.astype(F32)
+    qkv_part, out_part = attn_part[:, : 3 * half_width], attn_part[:, 3 * half_width :]
     shared_rows = 6 * width // 128
     small_rows = small.shape[0] - share
     shared = (small[:shared_rows] + other_small[:shared_rows]).reshape(6, width)

time: 553 us -> 549 us (level)
  waiting for transfers between devices: 154 us -> 222 us
  local copies, waits for them, and re-layouts: 56 us -> 35.2 us
  starting transfers between devices: 123 us -> 106 us
  other arithmetic: 50.5 us -> 34.7 us
  Pallas kernels: 90.3 us -> 76.1 us
    ppermute x55 -> x58, waiting for transfers between devices: 136 us -> 195 us  [exchange(): lax.ppermute(value, axis, steps)]
    ppermute x55 -> x58, starting transfers between devices: 93.5 us -> 79.5 us  [exchange(): lax.ppermute(value, axis, steps)]
    unnamed x175 -> x119, local copies, waits for them, and re-layouts: 25.6 us -> 12.4 us
    pallas_call x3, Pallas kernels: 46.9 us -> 34 us  [the longest x2 23.6 us: attend_back(): pl.pallas_call(partial(attend_back_kernel, group * heads), grid=(count //...]
    all_to_all x1, waiting for transfers between devices: 0.01 us -> 11.4 us  [local_chip(): lax.all_to_all(jnp.broadcast_to(own_queries[None], (chip_count,) + own_qu...]
    ppermute x12 -> x9, starting transfers between devices: 19.4 us -> 15.7 us  [swap(): return lax.ppermute(value, axis, SWAP)]
  transfers between devices with their start and end apart: 69 -> 69, of which waited for: 33 -> 44; matrix products, arithmetic and copies ran while one was open for 17% -> 10% of each run, Pallas kernels for 10% -> 4%
where the time goes in v7:
time: 549 us; the launch traced here: 544 us
  waiting for transfers between devices  222 us (40%)
  starting transfers between devices  106 us (19%)
  Pallas kernels  76.1 us (14%)
  matrix products  54.8 us (10%)
  local copies, waits for them, and re-layouts  35.2 us (6%)
  other arithmetic  34.7 us (6%)
  blocking collectives  11.8 us (2%)
    ppermute x58, waiting for transfers between devices, exchange(): lax.ppermute(value, axis, steps)  195 us
    ppermute x58, starting transfers between devices, exchange(): lax.ppermute(value, axis, steps)  79.5 us
    pallas_call x2, Pallas kernels, attend_back(): pl.pallas_call(partial(attend_back_kernel, group * heads), grid=(count //...  23.6 us
    dot_general x12, matrix products, contract_cols(): lax.dot_general(left, right, (((1,), (1,)), ((), ())), precision=precisio...  20.1 us
    dot_general x7, matrix products, contract_rows(): lax.dot_general(left, right, (((0,), (0,)), ((), ())), precision=precisio...  19.8 us
    pallas_call x1, Pallas kernels, expand(): pl.pallas_call(expand_kernel, grid=(width // tile,), in_specs=[pl.BlockSp...  17.5 us
    ppermute x9, starting transfers between devices, swap(): return lax.ppermute(value, axis, SWAP)  15.7 us
    pallas_call x1, Pallas kernels, pool_back(): pl.pallas_call(partial(pool_back_kernel, cuts, span), grid=(count // TILE...  15.6 us
  transfers between devices with their start and end apart: 69, of which 44 were waited for; matrix products, arithmetic and copies ran while one was open for 10% of the time, Pallas kernels for 4%

profile of v7, /device:TPU:1, one launch (start us, length us, event | category | flops | bytes accessed | tf_op | source)
XLA Modules:
  0.0 543.7 jit_solution(15334008972588869528)
XLA Ops:
  1.8 4.5 collective-permute-start
  12.4 3.3 collective-permute-start.3
  15.7 3.3 broadcast_select_fusion
  19.1 3.6 collective-permute-start.5
  24.2 4.6 collective-permute-start.7
  32.9 9.9 %collective-permute-done.6 = bf16[64,2688]{1,0:T(8,128)(2,1)S(1)} collective-permute-done((bf16[64,2688]{1,0:T(8,128)(2,1)S(1)}, bf16[64,2688]{1,0:T(8,128)(2,1)S(1)}, u32[]{:S(2)}, u32[]{:S(2)}) %collective-permute-start.6) | collective-permute-done | bytes 344096 | tf_op jit(solution)/shard_map/ppermute | solution.py:464
  47.5 5.8 %collective-permute-done.8 = bf16[4,32,1536]{2,1,0:T(8,128)(2,1)S(1)} collective-permute-done((bf16[4,32,1536]{2,1,0:T(8,128)(2,1)S(1)}, bf16[4,32,1536]{2,1,0:T(8,128)(2,1)S(1)}, u32[]{:S(2)}, u32[]{:S(2)}) %collective-permute-start.8) | collective-permute-done | bytes 393248 | tf_op jit(solution)/shard_map/ppermute | solution.py:464
  54.2 6.2 %collective-permute-done.10 = bf16[2,64,2688]{2,1,0:T(8,128)(2,1)S(1)} collective-permute-done((bf16[2,64,2688]{2,1,0:T(8,128)(2,1)S(1)}, bf16[2,64,2688]{2,1,0:T(8,128)(2,1)S(1)}, u32[]{:S(2)}, u32[]{:S(2)}) %collective-permute-start.10) | collective-permute-done | bytes 688160 | tf_op jit(solution)/shard_map/ppermute | solution.py:464
  61.5 3.3 collective-permute-start.15
  64.8 3.0 collective-permute-start.13
  69.8 2.6 collective-permute-done.13
  72.4 2.4 collective-permute-done.14
  74.8 3.7 collective-permute-done.15
  78.4 13.2 %collective-permute-done.12 = bf16[4,2,32,1536]{3,2,1,0:T(8,128)(2,1)S(1)} collective-permute-done((bf16[4,2,32,1536]{3,2,1,0:T(8,128)(2,1)S(1)}, bf16[4,2,32,1536]{3,2,1,0:T(8,128)(2,1)S(1)}, u32[]{:S(2)}, u32[]{:S(2)}) %collective-permute-start.12) | collective-permute-done | bytes 786464 | tf_op jit(solution)/shard_map/ppermute | solution.py:464
  91.6 3.7 collective-permute-done.11
  98.7 3.0 collective-permute-start.16
  103.5 3.6 add_convert_fusion.own_ref.qkv_ref
  107.5 3.9 collective-permute-done.16
  113.9 10.4 %shard_map.254 = (bf16[1024,512]{1,0:T(8,128)(2,1)S(1)}, f32[8,1024]{1,0:T(8,128)S(1)}) custom-call(s32[2,4]{1,0:T(2,128)S(1)} %pad_add_fusion.1.bounds, bf16[1024,1536]{1,0:T(8,128)(2,1)S(1)} %add_convert_fusion.own_ref.qkv_ref, bf16[1024,1536]{1,0:T(8,128)(2,1)S(1)} %add_convert_fusion.own_ref.qkv_ref, s32[2,1024]{1,0:T(2,128)S(1)} %pad_add_fusion.spans), custom_call_target="tpu_custom_call" | custom-call | flops 2147483648 | bytes 12582912 | tf_op jit(solution)/shard_map/pallas_call | solution.py:678
  124.3 11.4 %collective-permute-done.19 = bf16[4,32,2048]{2,1,0:T(8,128)(2,1)S(1)} collective-permute-done((bf16[4,32,2048]{2,1,0:T(8,128)(2,1)S(1)}, bf16[4,32,2048]{2,1,0:T(8,128)(2,1)S(1)}, u32[]{:S(2)}, u32[]{:S(2)}) %collective-permute-start.19) | collective-permute-done | bytes 524320 | tf_op jit(solution)/shard_map/ppermute | solution.py:464
  139.5 2.4 copy-done.2
  143.6 3.9 collective-permute-start.21
  151.5 2.5 fusion.115
  156.8 17.5 %collective-permute-done.24 = bf16[4,2,32,2048]{3,2,1,0:T(8,128)(2,1)S(1)} collective-permute-done((bf16[4,2,32,2048]{3,2,1,0:T(8,128)(2,1)S(1)}, bf16[4,2,32,2048]{3,2,1,0:T(8,128)(2,1)S(1)}, u32[]{:S(2)}, u32[]{:S(2)}) %collective-permute-start.24) | collective-permute-done | bytes 1048608 | tf_op jit(solution)/shard_map/ppermute | solution.py:464
  175.8 17.5 %shard_map.255 = (bf16[1024,2048]{1,0:T(8,128)(2,1)S(1)}, bf16[1024,2048]{1,0:T(8,128)(2,1)S(1)}) custom-call(bf16[1024,1024]{1,0:T(8,128)(2,1)S(1)} %pad_maximum_fusion.5.x_ref, bf16[1024,2688]{1,0:T(8,128)(2,1)S(1)} %bitcast.280, f32[1,2048]{1,0:T(1,128)S(1)} %slice.493.b_ref), custom_call_target="tpu_custom_call" | custom-call | flops 21474836480 | bytes 14680064 | tf_op jit(solution)/shard_map/pallas_call | solution.py:846
  196.8 2.4 fusion.11
  200.3 2.3 collective-permute-done.25
  202.6 2.8 fusion.116
  209.6 7.3 %all-to-all-start = ((bf16[16,128,128]{2,1,0:T(8,128)(2,1)}), bf16[16,128,128]{2,1,0:T(8,128)(2,1)S(1)}, u32[]{:S(2)}, u32[]{:S(2)}) async-start(bf16[16,128,128]{2,1,0:T(8,128)(2,1)} %broadcast_in_dim.46), calls=%async_computation | async-start | bytes 1048576 | tf_op jit(solution)/shard_map/all_to_all | solution.py:1132
  218.1 11.4 %all-to-all-done = bf16[16,128,128]{2,1,0:T(8,128)(2,1)S(1)} async-done(((bf16[16,128,128]{2,1,0:T(8,128)(2,1)}), bf16[16,128,128]{2,1,0:T(8,128)(2,1)S(1)}, u32[]{:S(2)}, u32[]{:S(2)}) %all-to-all-start) | async-done | bytes 524320 | tf_op jit(solution)/shard_map/all_to_all | solution.py:1132
  229.5 9.1 %shard_map.256 = f32[24,2048]{1,0:T(8,128)S(1)} custom-call(bf16[2048,128]{1,0:T(8,128)(2,1)S(1)} %bitcast.285, bf16[1024,128]{1,0:T(8,128)(2,1)S(1)} %maximum_select_fusion.26.d_ref, s32[1,1024]{1,0:T(1,128)S(1)} %compare_select_fusion.seg_ref), custom_call_target="tpu_custom_call" | custom-call | flops 3221225472 | bytes 786432 | tf_op jit(solution)/shard_map/pallas_call | solution.py:899
  239.3 11.8 %all_to_all.15 = f32[16,8,128]{2,1,0:T(8,128)S(1)} all-to-all(f32[16,8,128]{2,1,0:T(8,128)S(1)} %broadcast_in_dim.47), channel_id=1, replica_groups=mesh['z'=4,'x'=2,'c'=2,'y'=2] {'z','x','y'}, dimensions={0} | all-to-all | bytes 131072 | tf_op jit(solution)/shard_map/all_to_all | solution.py:1152
  252.1 15.6 %shard_map.257 = (bf16[2048,128]{1,0:T(8,128)(2,1)}, f32[768,128]{1,0:T(8,128)S(1)}) custom-call(bf16[2048,128]{1,0:T(8,128)(2,1)S(1)} %bitcast.286, bf16[1024,128]{1,0:T(8,128)(2,1)S(1)} %maximum_select_fusion.26.d_ref, s32[1,1024]{1,0:T(1,128)S(1)} %compare_select_fusion.seg_ref, f32[24,2048]{1,0:T(8,128)S(1)} %convolution_divide_fusion.coef_ref), custom_call_target="tpu_custom_call" | custom-call | flops 4831838208 | bytes 1572864 | tf_op jit(solution)/shard_map/pallas_call | solution.py:975
  267.6 3.8 all-to-all-start.2
  271.4 10.2 %all-to-all-done.2 = bf16[16,128,128]{2,1,0:T(8,128)(2,1)S(1)} async-done(((bf16[16,128,128]{2,1,0:T(8,128)(2,1)}), bf16[16,128,128]{2,1,0:T(8,128)(2,1)S(1)}, u32[]{:S(2)}, u32[]{:S(2)}) %all-to-all-start.2) | async-done | bytes 524320 | tf_op jit(solution)/shard_map/all_to_all | solution.py:1171
  281.8 5.7 %collective-permute-start.27 = (f32[512,128]{1,0:T(8,128)S(1)}, f32[512,128]{1,0:T(8,128)S(1)}, u32[]{:S(2)}, u32[]{:S(2)}) collective-permute-start(f32[512,128]{1,0:T(8,128)S(1)} %constant_dynamic-slice_fusion.6), channel_id=1, source_target_pairs={{0,2},{2,0},{1,3},{3,1},{4,6},{6,4},{5,7},{7,5},{8,10},{10,8},{9,1... | collective-permute-start | bytes 786440 | tf_op jit(solution)/shard_map/ppermute | solution.py:469
  290.5 2.3 convert_reduce_fusion.1
  296.6 7.5 %convolution_convert_fusion.1 = bf16[1024,2048]{1,0:T(8,128)(2,1)S(1)} fusion(bf16[1024,2048]{1,0:T(8,128)(2,1)} %copy-done.5, bf16[512,1024]{1,0:T(8,128)(2,1)} %collective-permute-done.28, bf16[512,1024]{1,0:T(8,128)(2,1)} %get-tuple-element.233), kind=kOutput, calls=%fused_computation.6 | convolution fusion | flops 4301258752 | bytes 10485760 | tf_op jit(solution)/shard_map/dot_general | solution.py:33
  304.2 6.8 %convert_reduce_fusion = (f32[2048]{0:T(1024)S(1)}, bf16[1024,2048]{1,0:T(8,128)(2,1)S(1)}) fusion(bf16[1024,2048]{1,0:T(8,128)(2,1)S(1)} %copy-done.7, bf16[1024,2048]{1,0:T(8,128)(2,1)S(1)} %bitcast.296, bf16[512,1024]{1,0:T(8,128)(2,1)} %collective-permute-done.28, bf16[512,1024]{1,0:T(8,128)(2,1)} %get-tuple-element.233), kind=kOutput, calls=%fused_computation | convolution fusion | flops 4309645312 | bytes 14688256 | tf_op jit(solution)/shard_map/dot_general | solution.py:448
  311.0 2.4 fusion.14
  316.6 6.2 %convolution_convert_fusion = bf16[1024,2048]{1,0:T(8,128)(2,1)} fusion(bf16[1024,2048]{1,0:T(8,128)(2,1)S(1)} %get-tuple-element.320, bf16[512,1024]{1,0:T(8,128)(2,1)S(1)} %copy-done.40, bf16[512,1024]{1,0:T(8,128)(2,1)S(1)} %copy-done.25), kind=kOutput, calls=%fused_computation.5 | convolution fusion | flops 4301258752 | bytes 10485760 | tf_op jit(solution)/shard_map/dot_general | solution.py:33
  322.8 2.4 fusion.2
  327.1 12.1 %collective-permute-done.33 = bf16[4,2,32,2048]{3,2,0,1:T(8,128)(2,1)S(1)} collective-permute-done((bf16[4,2,32,2048]{3,2,0,1:T(8,128)(2,1)S(1)}, bf16[4,2,32,2048]{3,2,0,1:T(8,128)(2,1)S(1)}, u32[]{:S(2)}, u32[]{:S(2)}) %collective-permute-start.33) | collective-permute-done | bytes 1048608 | tf_op jit(solution)/shard_map/ppermute | solution.py:464
  348.9 4.4 collective-permute-done.35
  353.3 2.5 collective-permute-done.34
  360.1 2.6 convolution_convert_fusion.5.grad_ref
  367.3 11.7 %shard_map.258 = (bf16[1024,768]{1,0:T(8,128)(2,1)S(1)}, f32[8,256]{1,0:T(8,128)S(1)}) custom-call(s32[2,4]{1,0:T(2,128)S(1)} %pad_add_fusion.1.bounds, bf16[1024,1536]{1,0:T(8,128)(2,1)S(1)} %copy-done.4, bf16[1024,1536]{1,0:T(8,128)(2,1)S(1)} %copy-done.4, bf16[1024,512]{1,0:T(8,128)(2,1)S(1)} %get-tuple-element.131.out_ref, ...), custom_call_target="tpu_custom_call" | custom-call | flops 2684354560 | bytes 12582912 | tf_op jit(solution)/shard_map/pallas_call | solution.py:781
  379.1 7.1 %collective-permute-done.37 = bf16[4,2,32,2048]{3,2,0,1:T(8,128)(2,1)S(1)} collective-permute-done((bf16[4,2,32,2048]{3,2,0,1:T(8,128)(2,1)S(1)}, bf16[4,2,32,2048]{3,2,0,1:T(8,128)(2,1)S(1)}, u32[]{:S(2)}, u32[]{:S(2)}) %collective-permute-start.37) | collective-permute-done | bytes 1048608 | tf_op jit(solution)/shard_map/ppermute | solution.py:464
  388.2 11.9 %shard_map.259 = (bf16[1024,768]{1,0:T(8,128)(2,1)S(1)}, f32[8,256]{1,0:T(8,128)S(1)}) custom-call(s32[2,4]{1,0:T(2,128)S(1)} %pad_add_fusion.1.bounds, bf16[1024,1536]{1,0:T(8,128)(2,1)S(1)} %copy-done.4, bf16[1024,1536]{1,0:T(8,128)(2,1)S(1)} %copy-done.4, bf16[1024,512]{1,0:T(8,128)(2,1)S(1)} %get-tuple-element.131.out_ref, ...), custom_call_target="tpu_custom_call" | custom-call | flops 2684354560 | bytes 12582912 | tf_op jit(solution)/shard_map/pallas_call | solution.py:781
  400.2 3.4 collective-permute-start.39
  405.2 13.5 %collective-permute-done.41 = bf16[4,2,32,512]{3,2,0,1:T(8,128)(2,1)S(1)} collective-permute-done((bf16[4,2,32,512]{3,2,0,1:T(8,128)(2,1)S(1)}, bf16[4,2,32,512]{3,2,0,1:T(8,128)(2,1)S(1)}, u32[]{:S(2)}, u32[]{:S(2)}) %collective-permute-start.41) | collective-permute-done | bytes 262176 | tf_op jit(solution)/shard_map/ppermute | solution.py:464
  419.5 6.9 %collective-permute-start.46 = (bf16[512,1024]{1,0:T(8,128)(2,1)S(1)}, bf16[512,1024]{1,0:T(8,128)(2,1)S(1)}, u32[]{:S(2)}, u32[]{:S(2)}) collective-permute-start(bf16[512,1024]{1,0:T(8,128)(2,1)S(1)} %copy-done.14), channel_id=1, source_target_pairs={{0,0},{1,2},{2,1},{3,3},{4,4},{5,6},{6,5},{7,7},{8,8},{9,10},{10,9... | collective-permute-start | bytes 3145736 | tf_op jit(solution)/shard_map/ppermute | solution.py:464
  437.0 3.9 collective-permute-done.44
  440.9 4.1 collective-permute-done.47
  451.2 2.1 collective-permute-start.61
  453.3 3.4 collective-permute-done.51
  456.7 15.4 %collective-permute-done.53 = f32[584,128]{1,0:T(8,128)S(1)} collective-permute-done((f32[584,128]{1,0:T(8,128)S(1)}, f32[584,128]{1,0:T(8,128)S(1)}, u32[]{:S(2)}, u32[]{:S(2)}) %collective-permute-start.53) | collective-permute-done | bytes 299040 | tf_op jit(solution)/shard_map/ppermute | solution.py:464
  477.3 3.1 collective-permute-done.57
  480.4 8.4 %collective-permute-done.55 = bf16[4,32,1536]{2,1,0:T(8,128)(2,1)S(1)} collective-permute-done((bf16[4,32,1536]{2,1,0:T(8,128)(2,1)S(1)}, bf16[4,32,1536]{2,1,0:T(8,128)(2,1)S(1)}, u32[]{:S(2)}, u32[]{:S(2)}) %collective-permute-start.55) | collective-permute-done | bytes 393248 | tf_op jit(solution)/shard_map/ppermute | solution.py:464
  492.3 4.9 collective-permute-done.59
  497.1 11.6 %collective-permute-done.58 = bf16[2,64,1536]{2,1,0:T(8,128)(2,1)S(1)} collective-permute-done((bf16[2,64,1536]{2,1,0:T(8,128)(2,1)S(1)}, bf16[2,64,1536]{2,1,0:T(8,128)(2,1)S(1)}, u32[]{:S(2)}, u32[]{:S(2)}) %collective-permute-start.58) | collective-permute-done | bytes 393248 | tf_op jit(solution)/shard_map/ppermute | solution.py:464
  508.9 4.3 collective-permute-start.64
  515.1 8.7 %collective-permute-done.62 = bf16[64,1536]{1,0:T(8,128)(2,1)S(1)} collective-permute-done((bf16[64,1536]{1,0:T(8,128)(2,1)S(1)}, bf16[64,1536]{1,0:T(8,128)(2,1)S(1)}, u32[]{:S(2)}, u32[]{:S(2)}) %collective-permute-start.62) | collective-permute-done | bytes 196640 | tf_op jit(solution)/shard_map/ppermute | solution.py:464
  524.0 3.7 collective-permute-start.65
  (443 shorter events, 131.8 us)
Async XLA Ops:
  1.8 9.7 %collective-permute-start = (bf16[64,1536]{1,0:T(8,128)(2,1)S(1)}, bf16[64,1536]{1,0:T(8,128)(2,1)S(1)}, u32[]{:S(2)}, u32[]{:S(2)}) collective-permute-start(bf16[64,1536]{1,0:T(8,128)(2,1)S(1)} %slice_dynamic-update-slice_fusion), channel_id=1, source_target_pairs={{0,0},{1,2},{2,1},{3,3},{4,4},{5,6},{6,5},{7,7},{8,8},{9,10},{10,9... | collective-permute-start | bytes 589832 | tf_op jit(solution)/shard_map/ppermute | solution.py:464
  7.8 4.6 collective-permute-start.1
  12.4 10.4 %collective-permute-start.3 = (bf16[64,1536]{1,0:T(8,128)(2,1)S(1)}, bf16[64,1536]{1,0:T(8,128)(2,1)S(1)}, u32[]{:S(2)}, u32[]{:S(2)}) collective-permute-start(bf16[64,1536]{1,0:T(8,128)(2,1)S(1)} %collective-permute-done), channel_id=1, source_target_pairs={{0,24},{24,0},{8,16},{16,8},{1,25},{25,1},{9,17},{17,9},{2,26},{26... | collective-permute-start | bytes 589832 | tf_op jit(solution)/shard_map/ppermute | solution.py:464
  19.1 11.7 %collective-permute-start.5 = (bf16[64,4736]{1,0:T(8,128)(2,1)S(1)}, bf16[64,4736]{1,0:T(8,128)(2,1)S(1)}, u32[]{:S(2)}, u32[]{:S(2)}) collective-permute-start(bf16[64,4736]{1,0:T(8,128)(2,1)S(1)} %fusion.42), channel_id=1, source_target_pairs={{0,0},{1,2},{2,1},{3,3},{4,4},{5,6},{6,5},{7,7},{8,8},{9,10},{10,9... | collective-permute-start | bytes 1818632 | tf_op jit(solution)/shard_map/ppermute | solution.py:464
  22.9 10.0 %collective-permute-start.4 = (bf16[2,64,1536]{2,1,0:T(8,128)(2,1)S(1)}, bf16[2,64,1536]{2,1,0:T(8,128)(2,1)S(1)}, u32[]{:S(2)}, u32[]{:S(2)}) collective-permute-start(bf16[2,64,1536]{2,1,0:T(8,128)(2,1)S(1)} %maximum_select_fusion.23), channel_id=1, source_target_pairs={{0,8},{8,0},{16,24},{24,16},{1,9},{9,1},{17,25},{25,17},{2,10},{10... | collective-permute-start | bytes 1179656 | tf_op jit(solution)/shard_map/ppermute | solution.py:464
  24.2 18.6 %collective-permute-start.7 = (bf16[512,1024]{1,0:T(8,128)(2,1)}, bf16[512,1024]{1,0:T(8,128)(2,1)S(1)}, u32[]{:S(2)}, u32[]{:S(2)}) collective-permute-start(bf16[512,1024]{1,0:T(8,128)(2,1)} %param.29), channel_id=1, source_target_pairs={{0,0},{1,2},{2,1},{3,3},{4,4},{5,6},{6,5},{7,7},{8,8},{9,10},{10,9... | collective-permute-start | bytes 3145736 | tf_op jit(solution)/shard_map/ppermute | solution.py:464
  30.8 12.1 %collective-permute-start.6 = (bf16[64,2688]{1,0:T(8,128)(2,1)S(1)}, bf16[64,2688]{1,0:T(8,128)(2,1)S(1)}, u32[]{:S(2)}, u32[]{:S(2)}) collective-permute-start(bf16[64,2688]{1,0:T(8,128)(2,1)S(1)} %get-tuple-element.286), channel_id=1, source_target_pairs={{0,24},{24,0},{8,16},{16,8},{1,25},{25,1},{9,17},{17,9},{2,26},{26... | collective-permute-start | bytes 1032200 | tf_op jit(solution)/shard_map/ppermute | solution.py:464
  43.8 9.5 %collective-permute-start.8 = (bf16[4,32,1536]{2,1,0:T(8,128)(2,1)S(1)}, bf16[4,32,1536]{2,1,0:T(8,128)(2,1)S(1)}, u32[]{:S(2)}, u32[]{:S(2)}) collective-permute-start(bf16[4,32,1536]{2,1,0:T(8,128)(2,1)S(1)} %get-tuple-element.276), channel_id=1, source_target_pairs={{0,4},{4,0},{1,5},{5,1},{2,6},{6,2},{3,7},{7,3},{8,12},{12,8},{9,1... | collective-permute-start | bytes 1179656 | tf_op jit(solution)/shard_map/ppermute | solution.py:464
  45.0 9.2 %collective-permute-start.9 = (bf16[4,32,1536]{2,1,0:T(8,128)(2,1)S(1)}, bf16[4,32,1536]{2,1,0:T(8,128)(2,1)S(1)}, u32[]{:S(2)}, u32[]{:S(2)}) collective-permute-start(bf16[4,32,1536]{2,1,0:T(8,128)(2,1)S(1)} %get-tuple-element.275), channel_id=1, source_target_pairs={{0,1},{1,0},{2,3},{3,2},{4,5},{5,4},{6,7},{7,6},{8,9},{9,8},{10,11... | collective-permute-start | bytes 1179656 | tf_op jit(solution)/shard_map/ppermute | solution.py:464
  45.9 14.5 %collective-permute-start.10 = (bf16[2,64,2688]{2,1,0:T(8,128)(2,1)S(1)}, bf16[2,64,2688]{2,1,0:T(8,128)(2,1)S(1)}, u32[]{:S(2)}, u32[]{:S(2)}) collective-permute-start(bf16[2,64,2688]{2,1,0:T(8,128)(2,1)S(1)} %maximum_select_fusion.20), channel_id=1, source_target_pairs={{0,8},{8,0},{16,24},{24,16},{1,9},{9,1},{17,25},{25,17},{2,10},{10... | collective-permute-start | bytes 2064392 | tf_op jit(solution)/shard_map/ppermute | solution.py:464
  61.2 13.6 %collective-permute-start.14 = (bf16[4,32,2688]{2,1,0:T(8,128)(2,1)S(1)}, bf16[4,32,2688]{2,1,0:T(8,128)(2,1)S(1)}, u32[]{:S(2)}, u32[]{:S(2)}) collective-permute-start(bf16[4,32,2688]{2,1,0:T(8,128)(2,1)S(1)} %get-tuple-element.262), channel_id=1, source_target_pairs={{0,4},{4,0},{1,5},{5,1},{2,6},{6,2},{3,7},{7,3},{8,12},{12,8},{9,1... | collective-permute-start | bytes 2064392 | tf_op jit(solution)/shard_map/ppermute | solution.py:464
  61.5 16.9 %collective-permute-start.15 = (bf16[4,32,2688]{2,1,0:T(8,128)(2,1)S(1)}, bf16[4,32,2688]{2,1,0:T(8,128)(2,1)S(1)}, u32[]{:S(2)}, u32[]{:S(2)}) collective-permute-start(bf16[4,32,2688]{2,1,0:T(8,128)(2,1)S(1)} %get-tuple-element.261), channel_id=1, source_target_pairs={{0,1},{1,0},{2,3},{3,2},{4,5},{5,4},{6,7},{7,6},{8,9},{9,8},{10,11... | collective-permute-start | bytes 2064392 | tf_op jit(solution)/shard_map/ppermute | solution.py:464
  64.8 7.6 %collective-permute-start.13 = (bf16[64,2048]{1,0:T(8,128)(2,1)S(1)}, bf16[64,2048]{1,0:T(8,128)(2,1)S(1)}, u32[]{:S(2)}, u32[]{:S(2)}) collective-permute-start(bf16[64,2048]{1,0:T(8,128)(2,1)S(1)} %get-tuple-element.125), channel_id=1, source_target_pairs={{0,24},{24,0},{8,16},{16,8},{1,25},{25,1},{9,17},{17,9},{2,26},{26... | collective-permute-start | bytes 786440 | tf_op jit(solution)/shard_map/ppermute | solution.py:464
  67.9 23.7 %collective-permute-start.12 = (bf16[4,2,32,1536]{3,2,1,0:T(8,128)(2,1)S(1)}, bf16[4,2,32,1536]{3,2,1,0:T(8,128)(2,1)S(1)}, u32[]{:S(2)}, u32[]{:S(2)}) collective-permute-start(bf16[4,2,32,1536]{3,2,1,0:T(8,128)(2,1)S(1)} %maximum_select_fusion.19), channel_id=1, source_target_pairs={{0,4},{4,0},{1,5},{5,1},{2,6},{6,2},{3,7},{7,3},{8,12},{12,8},{9,1... | collective-permute-start | bytes 2359304 | tf_op jit(solution)/shard_map/ppermute | solution.py:464
  69.3 26.0 %collective-permute-start.11 = (bf16[4,2,32,1536]{3,2,0,1:T(8,128)(2,1)S(1)}, bf16[4,2,32,1536]{3,2,0,1:T(8,128)(2,1)S(1)}, u32[]{:S(2)}, u32[]{:S(2)}) collective-permute-start(bf16[4,2,32,1536]{3,2,0,1:T(8,128)(2,1)S(1)} %maximum_select_fusion.18), channel_id=1, source_target_pairs={{0,1},{1,0},{2,3},{3,2},{4,5},{5,4},{6,7},{7,6},{8,9},{9,8},{10,11... | collective-permute-start | bytes 2359304 | tf_op jit(solution)/shard_map/ppermute | solution.py:464
  95.5 41.5 %collective-permute-start.18 = (bf16[4,2,32,2688]{3,2,0,1:T(8,128)(2,1)S(1)}, bf16[4,2,32,2688]{3,2,0,1:T(8,128)(2,1)S(1)}, u32[]{:S(2)}, u32[]{:S(2)}) collective-permute-start(bf16[4,2,32,2688]{3,2,0,1:T(8,128)(2,1)S(1)} %maximum_select_fusion.10), channel_id=1, source_target_pairs={{0,4},{4,0},{1,5},{5,1},{2,6},{6,2},{3,7},{7,3},{8,12},{12,8},{9,1... | collective-permute-start | bytes 4128776 | tf_op jit(solution)/shard_map/ppermute | solution.py:464
  97.1 40.0 %collective-permute-start.17 = (bf16[4,2,32,2688]{3,2,0,1:T(8,128)(2,1)S(1)}, bf16[4,2,32,2688]{3,2,0,1:T(8,128)(2,1)S(1)}, u32[]{:S(2)}, u32[]{:S(2)}) collective-permute-start(bf16[4,2,32,2688]{3,2,0,1:T(8,128)(2,1)S(1)} %maximum_select_fusion.9), channel_id=1, source_target_pairs={{0,1},{1,0},{2,3},{3,2},{4,5},{5,4},{6,7},{7,6},{8,9},{9,8},{10,11... | collective-permute-start | bytes 4128776 | tf_op jit(solution)/shard_map/ppermute | solution.py:464
  98.7 12.7 %collective-permute-start.16 = (bf16[2,64,2048]{2,1,0:T(8,128)(2,1)S(1)}, bf16[2,64,2048]{2,1,0:T(8,128)(2,1)S(1)}, u32[]{:S(2)}, u32[]{:S(2)}) collective-permute-start(bf16[2,64,2048]{2,1,0:T(8,128)(2,1)S(1)} %maximum_select_fusion.21), channel_id=1, source_target_pairs={{0,8},{8,0},{16,24},{24,16},{1,9},{9,1},{17,25},{25,17},{2,10},{10... | collective-permute-start | bytes 1572872 | tf_op jit(solution)/shard_map/ppermute | solution.py:464
  113.3 22.5 %collective-permute-start.19 = (bf16[4,32,2048]{2,1,0:T(8,128)(2,1)S(1)}, bf16[4,32,2048]{2,1,0:T(8,128)(2,1)S(1)}, u32[]{:S(2)}, u32[]{:S(2)}) collective-permute-start(bf16[4,32,2048]{2,1,0:T(8,128)(2,1)S(1)} %get-tuple-element.268), channel_id=1, source_target_pairs={{0,4},{4,0},{1,5},{5,1},{2,6},{6,2},{3,7},{7,3},{8,12},{12,8},{9,1... | collective-permute-start | bytes 1572872 | tf_op jit(solution)/shard_map/ppermute | solution.py:464
  113.7 23.4 %collective-permute-start.20 = (bf16[4,32,2048]{2,1,0:T(8,128)(2,1)S(1)}, bf16[4,32,2048]{2,1,0:T(8,128)(2,1)S(1)}, u32[]{:S(2)}, u32[]{:S(2)}) collective-permute-start(bf16[4,32,2048]{2,1,0:T(8,128)(2,1)S(1)} %get-tuple-element.267), channel_id=1, source_target_pairs={{0,1},{1,0},{2,3},{3,2},{4,5},{5,4},{6,7},{7,6},{8,9},{9,8},{10,11... | collective-permute-start | bytes 1572872 | tf_op jit(solution)/shard_map/ppermute | solution.py:464
  143.6 7.9 %collective-permute-start.21 = (bf16[512,1024]{1,0:T(8,128)(2,1)}, bf16[512,1024]{1,0:T(8,128)(2,1)}, u32[]{:S(2)}, u32[]{:S(2)}) collective-permute-start(bf16[512,1024]{1,0:T(8,128)(2,1)} %convolution_convert_fusion.6), channel_id=1, source_target_pairs={{0,2},{2,0},{1,3},{3,1},{4,6},{6,4},{5,7},{7,5},{8,10},{10,8},{9,1... | collective-permute-start | bytes 3145736 | tf_op jit(solution)/shard_map/ppermute | solution.py:469
  149.4 24.8 %collective-permute-start.24 = (bf16[4,2,32,2048]{3,2,1,0:T(8,128)(2,1)S(1)}, bf16[4,2,32,2048]{3,2,1,0:T(8,128)(2,1)S(1)}, u32[]{:S(2)}, u32[]{:S(2)}) collective-permute-start(bf16[4,2,32,2048]{3,2,1,0:T(8,128)(2,1)S(1)} %maximum_select_fusion.15), channel_id=1, source_target_pairs={{0,4},{4,0},{1,5},{5,1},{2,6},{6,2},{3,7},{7,3},{8,12},{12,8},{9,1... | collective-permute-start | bytes 3145736 | tf_op jit(solution)/shard_map/ppermute | solution.py:464
  149.9 24.5 %collective-permute-start.23 = (bf16[4,2,32,2048]{3,2,0,1:T(8,128)(2,1)S(1)}, bf16[4,2,32,2048]{3,2,0,1:T(8,128)(2,1)S(1)}, u32[]{:S(2)}, u32[]{:S(2)}) collective-permute-start(bf16[4,2,32,2048]{3,2,0,1:T(8,128)(2,1)S(1)} %maximum_select_fusion.14), channel_id=1, source_target_pairs={{0,1},{1,0},{2,3},{3,2},{4,5},{5,4},{6,7},{7,6},{8,9},{9,8},{10,11... | collective-permute-start | bytes 3145736 | tf_op jit(solution)/shard_map/ppermute | solution.py:464
  154.8 19.6 %collective-permute-start.22 = (bf16[512,1024]{1,0:T(8,128)(2,1)S(1)}, bf16[512,1024]{1,0:T(8,128)(2,1)S(1)}, u32[]{:S(2)}, u32[]{:S(2)}) collective-permute-start(bf16[512,1024]{1,0:T(8,128)(2,1)S(1)} %fusion.10), channel_id=1, source_target_pairs={{0,2},{2,0},{1,3},{3,1},{4,6},{6,4},{5,7},{7,5},{8,10},{10,8},{9,1... | collective-permute-start | bytes 3145736 | tf_op jit(solution)/shard_map/ppermute | solution.py:469
  209.6 19.9 %all-to-all-start = ((bf16[16,128,128]{2,1,0:T(8,128)(2,1)}), bf16[16,128,128]{2,1,0:T(8,128)(2,1)S(1)}, u32[]{:S(2)}, u32[]{:S(2)}) async-start(bf16[16,128,128]{2,1,0:T(8,128)(2,1)} %broadcast_in_dim.46), calls=%async_computation | async-start | bytes 1048576 | tf_op jit(solution)/shard_map/all_to_all | solution.py:1132
  267.6 14.0 %all-to-all-start.2 = ((bf16[16,128,128]{2,1,0:T(8,128)(2,1)}), bf16[16,128,128]{2,1,0:T(8,128)(2,1)S(1)}, u32[]{:S(2)}, u32[]{:S(2)}) async-start(bf16[16,128,128]{2,1,0:T(8,128)(2,1)} %bitcast.59), calls=%async_computation.2 | async-start | bytes 1048576 | tf_op jit(solution)/shard_map/all_to_all | solution.py:1171
  281.8 6.9 %collective-permute-start.27 = (f32[512,128]{1,0:T(8,128)S(1)}, f32[512,128]{1,0:T(8,128)S(1)}, u32[]{:S(2)}, u32[]{:S(2)}) collective-permute-start(f32[512,128]{1,0:T(8,128)S(1)} %constant_dynamic-slice_fusion.6), channel_id=1, source_target_pairs={{0,2},{2,0},{1,3},{3,1},{4,6},{6,4},{5,7},{7,5},{8,10},{10,8},{9,1... | collective-permute-start | bytes 786440 | tf_op jit(solution)/shard_map/ppermute | solution.py:469
  292.8 3.8 collective-permute-start.28
  313.4 12.3 %collective-permute-start.30 = (bf16[512,1024]{1,0:T(8,128)(2,1)S(1)}, bf16[512,1024]{1,0:T(8,128)(2,1)S(1)}, u32[]{:S(2)}, u32[]{:S(2)}) collective-permute-start(bf16[512,1024]{1,0:T(8,128)(2,1)S(1)} %fusion.14), channel_id=1, source_target_pairs={{0,2},{2,0},{1,3},{3,1},{4,6},{6,4},{5,7},{7,5},{8,10},{10,8},{9,1... | collective-permute-start | bytes 3145736 | tf_op jit(solution)/shard_map/ppermute | solution.py:469
  314.5 24.7 %collective-permute-start.33 = (bf16[4,2,32,2048]{3,2,0,1:T(8,128)(2,1)S(1)}, bf16[4,2,32,2048]{3,2,0,1:T(8,128)(2,1)S(1)}, u32[]{:S(2)}, u32[]{:S(2)}) collective-permute-start(bf16[4,2,32,2048]{3,2,0,1:T(8,128)(2,1)S(1)} %bitcast.319), channel_id=1, source_target_pairs={{0,1},{1,0},{2,3},{3,2},{4,5},{5,4},{6,7},{7,6},{8,9},{9,8},{10,11... | collective-permute-start | bytes 3145736 | tf_op jit(solution)/shard_map/ppermute | solution.py:464
  315.2 24.4 %collective-permute-start.32 = (bf16[4,2,32,2048]{3,2,0,1:T(8,128)(2,1)S(1)}, bf16[4,2,32,2048]{3,2,0,1:T(8,128)(2,1)S(1)}, u32[]{:S(2)}, u32[]{:S(2)}) collective-permute-start(bf16[4,2,32,2048]{3,2,0,1:T(8,128)(2,1)S(1)} %bitcast.320), channel_id=1, source_target_pairs={{0,4},{4,0},{1,5},{5,1},{2,6},{6,2},{3,7},{7,3},{8,12},{12,8},{9,1... | collective-permute-start | bytes 3145736 | tf_op jit(solution)/shard_map/ppermute | solution.py:464
  340.8 12.5 %collective-permute-start.35 = (bf16[4,32,2048]{2,1,0:T(8,128)(2,1)}, bf16[4,32,2048]{2,1,0:T(8,128)(2,1)}, u32[]{:S(2)}, u32[]{:S(2)}) collective-permute-start(bf16[4,32,2048]{2,1,0:T(8,128)(2,1)} %fusion.44), channel_id=1, source_target_pairs={{0,4},{4,0},{1,5},{5,1},{2,6},{6,2},{3,7},{7,3},{8,12},{12,8},{9,1... | collective-permute-start | bytes 1572872 | tf_op jit(solution)/shard_map/ppermute | solution.py:464
  343.7 12.2 %collective-permute-start.34 = (bf16[4,32,2048]{2,1,0:T(8,128)(2,1)}, bf16[4,32,2048]{2,1,0:T(8,128)(2,1)}, u32[]{:S(2)}, u32[]{:S(2)}) collective-permute-start(bf16[4,32,2048]{2,1,0:T(8,128)(2,1)} %fusion.43), channel_id=1, source_target_pairs={{0,1},{1,0},{2,3},{3,2},{4,5},{5,4},{6,7},{7,6},{8,9},{9,8},{10,11... | collective-permute-start | bytes 1572872 | tf_op jit(solution)/shard_map/ppermute | solution.py:464
  347.0 11.8 %collective-permute-start.31 = (bf16[512,1024]{1,0:T(8,128)(2,1)S(1)}, bf16[512,1024]{1,0:T(8,128)(2,1)S(1)}, u32[]{:S(2)}, u32[]{:S(2)}) collective-permute-start(bf16[512,1024]{1,0:T(8,128)(2,1)S(1)} %get-tuple-element.236), channel_id=1, source_target_pairs={{0,2},{2,0},{1,3},{3,1},{4,6},{6,4},{5,7},{7,5},{8,10},{10,8},{9,1... | collective-permute-start | bytes 3145736 | tf_op jit(solution)/shard_map/ppermute | solution.py:469
  363.9 22.2 %collective-permute-start.37 = (bf16[4,2,32,2048]{3,2,0,1:T(8,128)(2,1)S(1)}, bf16[4,2,32,2048]{3,2,0,1:T(8,128)(2,1)S(1)}, u32[]{:S(2)}, u32[]{:S(2)}) collective-permute-start(bf16[4,2,32,2048]{3,2,0,1:T(8,128)(2,1)S(1)} %dynamic-slice_bitcast_fusion.1), channel_id=1, source_target_pairs={{0,4},{4,0},{1,5},{5,1},{2,6},{6,2},{3,7},{7,3},{8,12},{12,8},{9,1... | collective-permute-start | bytes 3145736 | tf_op jit(solution)/shard_map/ppermute | solution.py:464
  364.8 22.0 %collective-permute-start.38 = (bf16[4,2,32,2048]{3,2,0,1:T(8,128)(2,1)S(1)}, bf16[4,2,32,2048]{3,2,0,1:T(8,128)(2,1)S(1)}, u32[]{:S(2)}, u32[]{:S(2)}) collective-permute-start(bf16[4,2,32,2048]{3,2,0,1:T(8,128)(2,1)S(1)} %dynamic-slice_bitcast_fusion), channel_id=1, source_target_pairs={{0,1},{1,0},{2,3},{3,2},{4,5},{5,4},{6,7},{7,6},{8,9},{9,8},{10,11... | collective-permute-start | bytes 3145736 | tf_op jit(solution)/shard_map/ppermute | solution.py:464
  366.3 12.8 %collective-permute-start.36 = (bf16[2,64,2048]{2,1,0:T(8,128)(2,1)S(1)}, bf16[2,64,2048]{2,1,0:T(8,128)(2,1)S(1)}, u32[]{:S(2)}, u32[]{:S(2)}) collective-permute-start(bf16[2,64,2048]{2,1,0:T(8,128)(2,1)S(1)} %select_convert_fusion.1), channel_id=1, source_target_pairs={{0,8},{8,0},{16,24},{24,16},{1,9},{9,1},{17,25},{25,17},{2,10},{10... | collective-permute-start | bytes 1572872 | tf_op jit(solution)/shard_map/ppermute | solution.py:464
  400.2 18.5 %collective-permute-start.39 = (bf16[4,32,2048]{2,1,0:T(8,128)(2,1)S(1)}, bf16[4,32,2048]{2,1,0:T(8,128)(2,1)S(1)}, u32[]{:S(2)}, u32[]{:S(2)}) collective-permute-start(bf16[4,32,2048]{2,1,0:T(8,128)(2,1)S(1)} %fusion.45), channel_id=1, source_target_pairs={{0,1},{1,0},{2,3},{3,2},{4,5},{5,4},{6,7},{7,6},{8,9},{9,8},{10,11... | collective-permute-start | bytes 1572872 | tf_op jit(solution)/shard_map/ppermute | solution.py:464
  403.6 15.1 %collective-permute-start.40 = (bf16[4,32,2048]{2,1,0:T(8,128)(2,1)S(1)}, bf16[4,32,2048]{2,1,0:T(8,128)(2,1)S(1)}, u32[]{:S(2)}, u32[]{:S(2)}) collective-permute-start(bf16[4,32,2048]{2,1,0:T(8,128)(2,1)S(1)} %fusion.46), channel_id=1, source_target_pairs={{0,4},{4,0},{1,5},{5,1},{2,6},{6,2},{3,7},{7,3},{8,12},{12,8},{9,1... | collective-permute-start | bytes 1572872 | tf_op jit(solution)/shard_map/ppermute | solution.py:464
  403.6 15.1 %collective-permute-start.41 = (bf16[4,2,32,512]{3,2,0,1:T(8,128)(2,1)S(1)}, bf16[4,2,32,512]{3,2,0,1:T(8,128)(2,1)S(1)}, u32[]{:S(2)}, u32[]{:S(2)}) collective-permute-start(bf16[4,2,32,512]{3,2,0,1:T(8,128)(2,1)S(1)} %dynamic-slice_bitcast_fusion.5), channel_id=1, source_target_pairs={{0,4},{4,0},{1,5},{5,1},{2,6},{6,2},{3,7},{7,3},{8,12},{12,8},{9,1... | collective-permute-start | bytes 786440 | tf_op jit(solution)/shard_map/ppermute | solution.py:464
  405.1 13.6 %collective-permute-start.42 = (bf16[4,2,32,512]{3,2,0,1:T(8,128)(2,1)S(1)}, bf16[4,2,32,512]{3,2,0,1:T(8,128)(2,1)S(1)}, u32[]{:S(2)}, u32[]{:S(2)}) collective-permute-start(bf16[4,2,32,512]{3,2,0,1:T(8,128)(2,1)S(1)} %dynamic-slice_bitcast_fusion.4), channel_id=1, source_target_pairs={{0,1},{1,0},{2,3},{3,2},{4,5},{5,4},{6,7},{7,6},{8,9},{9,8},{10,11... | collective-permute-start | bytes 786440 | tf_op jit(solution)/shard_map/ppermute | solution.py:464
  419.5 25.6 %collective-permute-start.46 = (bf16[512,1024]{1,0:T(8,128)(2,1)S(1)}, bf16[512,1024]{1,0:T(8,128)(2,1)S(1)}, u32[]{:S(2)}, u32[]{:S(2)}) collective-permute-start(bf16[512,1024]{1,0:T(8,128)(2,1)S(1)} %copy-done.14), channel_id=1, source_target_pairs={{0,0},{1,2},{2,1},{3,3},{4,4},{5,6},{6,5},{7,7},{8,8},{9,10},{10,9... | collective-permute-start | bytes 3145736 | tf_op jit(solution)/shard_map/ppermute | solution.py:464
  426.5 18.6 %collective-permute-start.43 = (bf16[2,64,2048]{2,1,0:T(8,128)(2,1)S(1)}, bf16[2,64,2048]{2,1,0:T(8,128)(2,1)S(1)}, u32[]{:S(2)}, u32[]{:S(2)}) collective-permute-start(bf16[2,64,2048]{2,1,0:T(8,128)(2,1)S(1)} %select_convert_fusion), channel_id=1, source_target_pairs={{0,8},{8,0},{16,24},{24,16},{1,9},{9,1},{17,25},{25,17},{2,10},{10... | collective-permute-start | bytes 1572872 | tf_op jit(solution)/shard_map/ppermute | solution.py:464
  426.6 18.4 %collective-permute-start.47 = (bf16[64,2048]{1,0:T(8,128)(2,1)S(1)}, bf16[64,2048]{1,0:T(8,128)(2,1)S(1)}, u32[]{:S(2)}, u32[]{:S(2)}) collective-permute-start(bf16[64,2048]{1,0:T(8,128)(2,1)S(1)} %fusion.57), channel_id=1, source_target_pairs={{0,24},{24,0},{8,16},{16,8},{1,25},{25,1},{9,17},{17,9},{2,26},{26... | collective-permute-start | bytes 786440 | tf_op jit(solution)/shard_map/ppermute | solution.py:464
  428.2 7.6 %collective-permute-start.45 = (bf16[4,32,512]{2,1,0:T(8,128)(2,1)S(1)}, bf16[4,32,512]{2,1,0:T(8,128)(2,1)S(1)}, u32[]{:S(2)}, u32[]{:S(2)}) collective-permute-start(bf16[4,32,512]{2,1,0:T(8,128)(2,1)S(1)} %fusion.64), channel_id=1, source_target_pairs={{0,4},{4,0},{1,5},{5,1},{2,6},{6,2},{3,7},{7,3},{8,12},{12,8},{9,1... | collective-permute-start | bytes 393224 | tf_op jit(solution)/shard_map/ppermute | solution.py:464
  428.3 12.6 %collective-permute-start.44 = (bf16[4,32,512]{2,1,0:T(8,128)(2,1)S(1)}, bf16[4,32,512]{2,1,0:T(8,128)(2,1)S(1)}, u32[]{:S(2)}, u32[]{:S(2)}) collective-permute-start(bf16[4,32,512]{2,1,0:T(8,128)(2,1)S(1)} %fusion.63), channel_id=1, source_target_pairs={{0,1},{1,0},{2,3},{3,2},{4,5},{5,4},{6,7},{7,6},{8,9},{9,8},{10,11... | collective-permute-start | bytes 393224 | tf_op jit(solution)/shard_map/ppermute | solution.py:464
  435.8 12.2 %collective-permute-start.60 = (bf16[512,1024]{1,0:T(8,128)(2,1)S(1)}, bf16[512,1024]{1,0:T(8,128)(2,1)S(1)}, u32[]{:S(2)}, u32[]{:S(2)}) collective-permute-start(bf16[512,1024]{1,0:T(8,128)(2,1)S(1)} %add_convert_fusion.2), channel_id=1, source_target_pairs={{0,2},{2,0},{1,3},{3,1},{4,6},{6,4},{5,7},{7,5},{8,10},{10,8},{9,1... | collective-permute-start | bytes 3145736 | tf_op jit(solution)/shard_map/ppermute | solution.py:469
  445.6 5.5 %collective-permute-start.52 = (bf16[2,64,512]{2,1,0:T(8,128)(2,1)S(1)}, bf16[2,64,512]{2,1,0:T(8,128)(2,1)S(1)}, u32[]{:S(2)}, u32[]{:S(2)}) collective-permute-start(bf16[2,64,512]{2,1,0:T(8,128)(2,1)S(1)} %select_convert_fusion.6), channel_id=1, source_target_pairs={{0,8},{8,0},{16,24},{24,16},{1,9},{9,1},{17,25},{25,17},{2,10},{10... | collective-permute-start | bytes 393224 | tf_op jit(solution)/shard_map/ppermute | solution.py:464
  446.1 26.0 %collective-permute-start.50 = (bf16[4,2,32,1536]{3,2,0,1:T(8,128)(2,1)S(1)}, bf16[4,2,32,1536]{3,2,0,1:T(8,128)(2,1)S(1)}, u32[]{:S(2)}, u32[]{:S(2)}) collective-permute-start(bf16[4,2,32,1536]{3,2,0,1:T(8,128)(2,1)S(1)} %dynamic-slice_bitcast_fusion.2), channel_id=1, source_target_pairs={{0,1},{1,0},{2,3},{3,2},{4,5},{5,4},{6,7},{7,6},{8,9},{9,8},{10,11... | collective-permute-start | bytes 2359304 | tf_op jit(solution)/shard_map/ppermute | solution.py:464
  446.3 25.8 %collective-permute-start.49 = (bf16[4,2,32,1536]{3,2,0,1:T(8,128)(2,1)S(1)}, bf16[4,2,32,1536]{3,2,0,1:T(8,128)(2,1)S(1)}, u32[]{:S(2)}, u32[]{:S(2)}) collective-permute-start(bf16[4,2,32,1536]{3,2,0,1:T(8,128)(2,1)S(1)} %dynamic-slice_bitcast_fusion.3), channel_id=1, source_target_pairs={{0,4},{4,0},{1,5},{5,1},{2,6},{6,2},{3,7},{7,3},{8,12},{12,8},{9,1... | collective-permute-start | bytes 2359304 | tf_op jit(solution)/shard_map/ppermute | solution.py:464
  446.4 10.3 %collective-permute-start.51 = (bf16[64,2048]{1,0:T(8,128)(2,1)S(1)}, bf16[64,2048]{1,0:T(8,128)(2,1)S(1)}, u32[]{:S(2)}, u32[]{:S(2)}) collective-permute-start(bf16[64,2048]{1,0:T(8,128)(2,1)S(1)} %fusion.58), channel_id=1, source_target_pairs={{0,24},{24,0},{8,16},{16,8},{1,25},{25,1},{9,17},{17,9},{2,26},{26... | collective-permute-start | bytes 786440 | tf_op jit(solution)/shard_map/ppermute | solution.py:464
  448.0 24.1 %collective-permute-start.53 = (f32[584,128]{1,0:T(8,128)S(1)}, f32[584,128]{1,0:T(8,128)S(1)}, u32[]{:S(2)}, u32[]{:S(2)}) collective-permute-start(f32[584,128]{1,0:T(8,128)S(1)} %pad_maximum_fusion.22), channel_id=1, source_target_pairs={{0,1},{1,0},{2,3},{3,2},{4,5},{5,4},{6,7},{7,6},{8,9},{9,8},{10,11... | collective-permute-start | bytes 897032 | tf_op jit(solution)/shard_map/ppermute | solution.py:464
  451.2 41.1 %collective-permute-start.61 = (bf16[512,1024]{1,0:T(8,128)(2,1)S(1)}, bf16[512,1024]{1,0:T(8,128)(2,1)S(1)}, u32[]{:S(2)}, u32[]{:S(2)}) collective-permute-start(bf16[512,1024]{1,0:T(8,128)(2,1)S(1)} %add_convert_fusion.1), channel_id=1, source_target_pairs={{0,0},{1,2},{2,1},{3,3},{4,4},{5,6},{6,5},{7,7},{8,8},{9,10},{10,9... | collective-permute-start | bytes 3145736 | tf_op jit(solution)/shard_map/ppermute | solution.py:464
  472.1 8.3 %collective-permute-start.57 = (f32[584,128]{1,0:T(8,128)S(1)}, f32[584,128]{1,0:T(8,128)S(1)}, u32[]{:S(2)}, u32[]{:S(2)}) collective-permute-start(f32[584,128]{1,0:T(8,128)S(1)} %add.548), channel_id=1, source_target_pairs={{0,4},{4,0},{1,5},{5,1},{2,6},{6,2},{3,7},{7,3},{8,12},{12,8},{9,1... | collective-permute-start | bytes 897032 | tf_op jit(solution)/shard_map/ppermute | solution.py:464
  472.3 5.0 collective-permute-start.56
  474.1 14.8 %collective-permute-start.55 = (bf16[4,32,1536]{2,1,0:T(8,128)(2,1)S(1)}, bf16[4,32,1536]{2,1,0:T(8,128)(2,1)S(1)}, u32[]{:S(2)}, u32[]{:S(2)}) collective-permute-start(bf16[4,32,1536]{2,1,0:T(8,128)(2,1)S(1)} %fusion.53), channel_id=1, source_target_pairs={{0,4},{4,0},{1,5},{5,1},{2,6},{6,2},{3,7},{7,3},{8,12},{12,8},{9,1... | collective-permute-start | bytes 1179656 | tf_op jit(solution)/shard_map/ppermute | solution.py:464
  475.9 13.5 %collective-permute-start.54 = (bf16[4,32,1536]{2,1,0:T(8,128)(2,1)S(1)}, bf16[4,32,1536]{2,1,0:T(8,128)(2,1)S(1)}, u32[]{:S(2)}, u32[]{:S(2)}) collective-permute-start(bf16[4,32,1536]{2,1,0:T(8,128)(2,1)S(1)} %fusion.52), channel_id=1, source_target_pairs={{0,1},{1,0},{2,3},{3,2},{4,5},{5,4},{6,7},{7,6},{8,9},{9,8},{10,11... | collective-permute-start | bytes 1179656 | tf_op jit(solution)/shard_map/ppermute | solution.py:464
  489.4 7.7 %collective-permute-start.59 = (f32[584,128]{1,0:T(8,128)S(1)}, f32[584,128]{1,0:T(8,128)S(1)}, u32[]{:S(2)}, u32[]{:S(2)}) collective-permute-start(f32[584,128]{1,0:T(8,128)S(1)} %add.551), channel_id=1, source_target_pairs={{0,24},{24,0},{8,16},{16,8},{1,25},{25,1},{9,17},{17,9},{2,26},{26... | collective-permute-start | bytes 897032 | tf_op jit(solution)/shard_map/ppermute | solution.py:464
  491.5 17.2 %collective-permute-start.58 = (bf16[2,64,1536]{2,1,0:T(8,128)(2,1)S(1)}, bf16[2,64,1536]{2,1,0:T(8,128)(2,1)S(1)}, u32[]{:S(2)}, u32[]{:S(2)}) collective-permute-start(bf16[2,64,1536]{2,1,0:T(8,128)(2,1)S(1)} %select_convert_fusion.2), channel_id=1, source_target_pairs={{0,8},{8,0},{16,24},{24,16},{1,9},{9,1},{17,25},{25,17},{2,10},{10... | collective-permute-start | bytes 1179656 | tf_op jit(solution)/shard_map/ppermute | solution.py:464
  508.9 14.9 %collective-permute-start.64 = (bf16[64,4096]{1,0:T(8,128)(2,1)S(1)}, bf16[64,4096]{1,0:T(8,128)(2,1)S(1)}, u32[]{:S(2)}, u32[]{:S(2)}) collective-permute-start(bf16[64,4096]{1,0:T(8,128)(2,1)S(1)} %pad_maximum_fusion.21), channel_id=1, source_target_pairs={{0,0},{1,2},{2,1},{3,3},{4,4},{5,6},{6,5},{7,7},{8,8},{9,10},{10,9... | collective-permute-start | bytes 1572872 | tf_op jit(solution)/shard_map/ppermute | solution.py:464
  513.2 10.6 %collective-permute-start.63 = (f32[584,128]{1,0:T(8,128)S(1)}, f32[584,128]{1,0:T(8,128)S(1)}, u32[]{:S(2)}, u32[]{:S(2)}) collective-permute-start(f32[584,128]{1,0:T(8,128)S(1)} %add.557), channel_id=1, source_target_pairs={{0,8},{8,0},{16,24},{24,16},{1,9},{9,1},{17,25},{25,17},{2,10},{10... | collective-permute-start | bytes 897032 | tf_op jit(solution)/shard_map/ppermute | solution.py:464
  513.4 10.4 %collective-permute-start.62 = (bf16[64,1536]{1,0:T(8,128)(2,1)S(1)}, bf16[64,1536]{1,0:T(8,128)(2,1)S(1)}, u32[]{:S(2)}, u32[]{:S(2)}) collective-permute-start(bf16[64,1536]{1,0:T(8,128)(2,1)S(1)} %fusion.59), channel_id=1, source_target_pairs={{0,24},{24,0},{8,16},{16,8},{1,25},{25,1},{9,17},{17,9},{2,26},{26... | collective-permute-start | bytes 589832 | tf_op jit(solution)/shard_map/ppermute | solution.py:464
  523.9 7.9 %collective-permute-start.66 = (f32[584,128]{1,0:T(8,128)S(1)}, f32[584,128]{1,0:T(8,128)S(1)}, u32[]{:S(2)}, u32[]{:S(2)}) collective-permute-start(f32[584,128]{1,0:T(8,128)S(1)} %add.561), channel_id=1, source_target_pairs={{0,2},{2,0},{1,3},{3,1},{4,6},{6,4},{5,7},{7,5},{8,10},{10,8},{9,1... | collective-permute-start | bytes 897032 | tf_op jit(solution)/shard_map/ppermute | solution.py:464
  524.0 7.7 %collective-permute-start.65 = (bf16[64,2048]{1,0:T(8,128)(2,1)S(1)}, bf16[64,2048]{1,0:T(8,128)(2,1)S(1)}, u32[]{:S(2)}, u32[]{:S(2)}) collective-permute-start(bf16[64,2048]{1,0:T(8,128)(2,1)S(1)} %pad_maximum_fusion.24), channel_id=1, source_target_pairs={{0,0},{1,2},{2,1},{3,3},{4,4},{5,6},{6,5},{7,7},{8,8},{9,10},{10,9... | collective-permute-start | bytes 786440 | tf_op jit(solution)/shard_map/ppermute | solution.py:464
  (55 other events, 535.4 us)
